TPU v7x, 32 devices: a whole 2x2x4 slice. The times are simulated.
32 devices in a mesh: samp: 4 (over y, x), probe: 8 (over z, core).
Axes of the slice: x: 2, y: 2, z: 4, core: 2. Of those that a mesh axis runs over, the one named last changes fastest.
Arguments:
- methyl: bfloat16 [4096, 16384], P('samp', 'probe'), may hold values from -0.25 to 1.25
- atlas: bfloat16 [64, 16384], P(None, 'probe'), may hold values from 0 to 1, as said below
- panel_ids: int32 [64], replicated, may hold values from 0 to 63, each once
Outputs:
- relmat: float32 [3, 4096, 1024], P(None, 'samp', 'probe')
- scores: float32 [32, 4096], P(None, ('samp', 'probe'))
Inputs may be any that keep to these rules, and one draw needn't show every extreme that they name: atlas values are beta values between 0 and 1.
All inputs are finite; a program needn't handle non-finite values.
Results may differ from a plain program's by a relative error of at most 0.003.
Values may be sent and summed in bfloat16 or wider, within the bound.
No kernel may reach another device: no remote copies, remote signals or barrier semaphores. Data moves between devices by JAX's collectives and lax.ppermute only.
A program may use at most 128 MiB of HBM per device.

v0:
```python
import functools

import jax
import jax.numpy as jnp
from jax import lax
from jax.experimental import pallas as pl
from jax.experimental.pallas import tpu as pltpu
from jax.sharding import PartitionSpec as P


K = 32
ITERS = 128
F32, BF16 = jnp.float32, jnp.bfloat16
HIGHEST = lax.Precision.HIGHEST
LANES = 128
VMEM_LIMIT = 60 * 1024 * 1024


def nt(a, b):
    return lax.dot_general(a, b, (((1,), (1,)), ((), ())), preferred_element_type=F32)


def tn(a, b):
    return lax.dot_general(a, b, (((0,), (0,)), ((), ())), preferred_element_type=F32)


def params(*semantics):
    return pltpu.CompilerParams(dimension_semantics=semantics, vmem_limit_bytes=VMEM_LIMIT)


def cost(flops, nbytes):
    return pl.CostEstimate(flops=int(flops), bytes_accessed=int(nbytes), transcendentals=0)


def three_terms(value):
    high = value.astype(BF16)
    rest = value - high.astype(F32)
    mid = rest.astype(BF16)
    low = (rest - mid.astype(F32)).astype(BF16)
    return jnp.concatenate([high, mid, low], axis=0)


def project_kernel(core_ref, ids_ref, atlas_ref, methyl_ref, out_ref, panel_ref, same_ref, other_ref, gram_ref):
    kk = panel_ref.shape[0]
    blocks, _, share = out_ref.shape
    core = core_ref[0]

    @pl.when(pl.program_id(0) == 0)
    def _():
        rows = atlas_ref.shape[0]
        row = lax.broadcasted_iota(jnp.int32, (kk, rows), 0)
        wanted = jnp.zeros((kk, rows), jnp.int32)
        for k in range(kk):
            wanted = jnp.where(row == k, ids_ref[k], wanted)
        pick = wanted == lax.broadcasted_iota(jnp.int32, (kk, rows), 1)
        chosen = jnp.where(pick, 1.0, 0.0).astype(BF16)
        panel = jnp.dot(chosen, atlas_ref[...], preferred_element_type=F32).astype(BF16)
        panel_ref[...] = panel
        gram_ref[...] = nt(panel, panel)

    proj = nt(methyl_ref[...], panel_ref[...]).T
    for b in range(blocks):
        out_ref[b, :kk, :] = proj[:, b * share : (b + 1) * share]
        out_ref[b, kk:, :] = jnp.zeros((kk, share), F32)
        out_ref[b, kk:, :kk] = gram_ref[...]
    for b in range(blocks // 2):
        same = pl.multiple_of((2 * b + core) * share, share)
        other = pl.multiple_of((2 * b + 1 - core) * share, share)
        same_ref[b * share : (b + 1) * share, :] = methyl_ref[pl.ds(same, share), :]
        other_ref[b * share : (b + 1) * share, :] = methyl_ref[pl.ds(other, share), :]


def project(core, panel_ids, atlas, methyl, shares):
    rows, probes = methyl.shape
    share = rows // shares
    chunk = row_chunk(share)
    half = pl.BlockSpec((chunk // 2, probes), lambda i: (i, 0))
    return pl.pallas_call(
        project_kernel,
        grid=(rows // chunk,),
        in_specs=[
            pl.BlockSpec(memory_space=pltpu.SMEM),
            pl.BlockSpec(memory_space=pltpu.SMEM),
            pl.BlockSpec(atlas.shape, lambda i: (0, 0)),
            pl.BlockSpec((chunk, probes), lambda i: (i, 0)),
        ],
        out_specs=(
            pl.BlockSpec((chunk // share, 2 * K, share), lambda i: (i, 0, 0)),
            pl.BlockSpec((K, probes), lambda i: (0, 0)),
            half,
            half,
        ),
        out_shape=(
            jax.ShapeDtypeStruct((shares, 2 * K, share), F32),
            jax.ShapeDtypeStruct((K, probes), BF16),
            jax.ShapeDtypeStruct((rows // 2, probes), BF16),
            jax.ShapeDtypeStruct((rows // 2, probes), BF16),
        ),
        scratch_shapes=[pltpu.VMEM((K, K), F32)],
        compiler_params=params("arbitrary"),
        cost_estimate=cost(2 * K * rows * probes, 4 * rows * probes),
        name="project",
    )(core, panel_ids, atlas, methyl)


def row_chunk(share):
    return 2 * share * max(1, 128 // share)


def descend_kernel(parts_ref, scores_ref, design_ref, spread_ref, w_ref):
    kk, share = w_ref.shape
    total = parts_ref[0]
    for peer in range(1, parts_ref.shape[0]):
        total = total + parts_ref[peer]
    gram = total[kk:, :kk]
    row = lax.broadcasted_iota(jnp.int32, (kk, kk), 0)
    col = lax.broadcasted_iota(jnp.int32, (kk, kk), 1)
    trace = jnp.sum(jnp.where(row == col, gram, 0.0), axis=(0, 1), keepdims=True)
    rate = 1.0 / trace
    step = jnp.where(row == col, 1.0, 0.0) - rate * gram
    pull = rate * total[:kk, :]
    for k in range(kk):
        spread_ref[k] = jnp.broadcast_to(step[:, k : k + 1], (kk, share))
    w_ref[...] = jnp.full((kk, share), 1.0 / kk, F32)

    def descend(_, carry):
        acc = [pull, None, None, None]
        for k in range(kk):
            term = spread_ref[k] * w_ref[k : k + 1, :]
            acc[k % 4] = term if acc[k % 4] is None else acc[k % 4] + term
        w_ref[...] = jnp.maximum((acc[0] + acc[1]) + (acc[2] + acc[3]), 0.0)
        return carry

    lax.fori_loop(0, ITERS, descend, 0)
    weights = w_ref[...]
    scores_ref[...] = kk * weights
    design = weights.astype(BF16)
    for peer in range(design_ref.shape[0]):
        design_ref[peer] = design


def descend(parts):
    shares, _, share = parts.shape
    return pl.pallas_call(
        descend_kernel,
        out_shape=(
            jax.ShapeDtypeStruct((K, share), F32),
            jax.ShapeDtypeStruct((shares, K, share), BF16),
        ),
        scratch_shapes=[pltpu.VMEM((K, K, share), F32), pltpu.VMEM((K, share), F32)],
        compiler_params=params(),
        cost_estimate=cost(2 * ITERS * K * K * share, 4 * K * share),
        name="descend",
    )(parts)


def cross_kernel(design_ref, methyl_ref, panel_ref, out_ref):
    blocks, kk, _ = design_ref.shape
    probes = methyl_ref.shape[1]
    design = jnp.concatenate([design_ref[b] for b in range(blocks)], axis=1)

    @pl.when(pl.program_id(0) == 0)
    def _():
        out_ref[...] = jnp.zeros_like(out_ref)

    out_ref[:, probes : probes + kk] += nt(design, design)
    width = min(probes, 512)
    for at in range(0, probes, width):
        cols = slice(at, at + width)
        out_ref[:, cols] += jnp.dot(design, methyl_ref[:, cols], preferred_element_type=F32)
        left = methyl_ref[:, cols].astype(F32) - tn(design, panel_ref[:, cols])
        squares = jnp.sum(left * left, axis=0, keepdims=True)
        for b in range(0, width, LANES):
            row = (at + b) // LANES
            out_ref[row : row + 1, probes + LANES :] += squares[:, b : b + LANES]


def cross_products(design, methyl, panel):
    _, _, share = design.shape
    rows, probes = methyl.shape
    chunk = row_chunk(share)
    return pl.pallas_call(
        cross_kernel,
        grid=(rows // chunk,),
        in_specs=[
            pl.BlockSpec((chunk // share, K, share), lambda i: (i, 0, 0)),
            pl.BlockSpec((chunk, probes), lambda i: (i, 0)),
            pl.BlockSpec((K, probes), lambda i: (0, 0)),
        ],
        out_specs=pl.BlockSpec((K, probes + 2 * LANES), lambda i: (0, 0)),
        out_shape=jax.ShapeDtypeStruct((K, probes + 2 * LANES), F32),
        compiler_params=params("arbitrary"),
        cost_estimate=cost(4 * K * rows * probes, 2 * rows * probes),
        name="cross",
    )(design, methyl, panel)


def ridge_inverse(matrix):
    kk = matrix.shape[0]
    row = lax.broadcasted_iota(jnp.int32, (kk, kk), 0)
    col = lax.broadcasted_iota(jnp.int32, (kk, kk), 1)
    work = jnp.concatenate([matrix, jnp.where(row == col, 1.0, 0.0)], axis=1)
    which = lax.broadcasted_iota(jnp.int32, (kk, 1), 0)
    for k in range(kk):
        pivot_row = work[k : k + 1, :] / work[k : k + 1, k : k + 1]
        factor = jnp.where(which == k, 0.0, work[:, k : k + 1])
        work = jnp.where(which == k, pivot_row, work - factor * pivot_row)
    return work[:, kk:]


def solve_kernel(ridge, samples, mine_ref, peer_ref, panel_ref, out_ref):
    kk, probes = panel_ref.shape
    total = mine_ref[...] + peer_ref[...]
    cross = total[:, :probes]
    wgram = total[:, probes : probes + kk]
    start = jnp.concatenate(
        [total[r : r + 1, probes + LANES :] for r in range(probes // LANES)], axis=1
    )
    row = lax.broadcasted_iota(jnp.int32, (kk, kk), 0)
    col = lax.broadcasted_iota(jnp.int32, (kk, kk), 1)
    system = wgram + jnp.where(row == col, ridge, 0.0)
    inverse = ridge_inverse(system)
    loadings = jnp.dot(inverse, cross, precision=HIGHEST)
    short = cross - jnp.dot(system, loadings, precision=HIGHEST)
    loadings = loadings + jnp.dot(inverse, short, precision=HIGHEST)
    panel = panel_ref[...].astype(F32)
    slope = jnp.dot(wgram, loadings + panel, precision=HIGHEST) - 2.0 * cross
    spread = start + jnp.sum((loadings - panel) * slope, axis=0, keepdims=True)
    rate = lax.rsqrt(jnp.maximum(spread, 0.0) / samples + 1e-06)
    out_ref[:kk, :] = loadings
    out_ref[kk:, :] = jnp.broadcast_to(rate, (out_ref.shape[0] - kk, probes))


def solve(mine, peer, panel, ridge, samples):
    probes = panel.shape[1]
    return pl.pallas_call(
        functools.partial(solve_kernel, ridge, samples),
        out_shape=jax.ShapeDtypeStruct((K + 8, probes), F32),
        compiler_params=params(),
        cost_estimate=cost(50 * K * K * probes, 20 * K * probes),
        name="solve",
    )(mine, peer, panel)


def standardise(design, methyl_ref, terms_ref, rate, store):
    probes = methyl_ref.shape[1]
    stacked = jnp.concatenate([design] * 3, axis=0)
    width = min(probes, 512)
    for at in range(0, probes, width):
        cols = slice(at, at + width)
        fitted = tn(stacked, terms_ref[:, cols])
        left = methyl_ref[:, cols].astype(F32) - fitted
        store(at, width, (left * rate[:, cols]).astype(BF16))


def put_tile(left, right, slots_ref, sends_ref, keep_ref):
    share = keep_ref.shape[1]
    part = nt(left, right)
    for p in range(right.shape[0] // share):
        block = part[:, p * share : (p + 1) * share]
        slot = slots_ref[p]

        @pl.when(slot < 0)
        def _():
            keep_ref[...] = block

        @pl.when(slot >= 0)
        def _():
            sends_ref[jnp.maximum(slot, 0)] = block.astype(BF16)


def own_kernel(
    steps, slots_ref, core_ref, design_ref, mine_ref, theirs_ref, facts_ref, more_ref,
    zscore_ref, sends_ref, keep_ref, z_ref, half_ref, terms_ref, moreterms_ref,
):
    step = pl.program_id(0)
    blocks, kk, share = design_ref.shape
    chunk, probes = mine_ref.shape
    core = core_ref[0]

    @pl.when(step == 0)
    def _():
        terms_ref[...] = three_terms(facts_ref[:kk, :])
        moreterms_ref[...] = three_terms(more_ref[:kk, :])

    @pl.when(step < steps)
    def _():
        design = jnp.concatenate([design_ref[b] for b in range(blocks)], axis=1)
        rows = pl.ds(pl.multiple_of(step * chunk, chunk), chunk)

        def store(base, at, width, value):
            zscore_ref[:, base + at : base + at + width] = value
            z_ref[rows, base + at : base + at + width] = value

        standardise(design, mine_ref, terms_ref, facts_ref[kk : kk + 1, :], functools.partial(store, 0))
        standardise(
            design, theirs_ref, moreterms_ref, more_ref[kk : kk + 1, :], functools.partial(store, probes)
        )
        for b in range(blocks // 2):
            here = pl.ds(pl.multiple_of((2 * b + core) * share, share), share)
            there = pl.ds(pl.multiple_of(step * (chunk // 2) + b * share, share), share)
            half_ref[there, :] = zscore_ref[here, :]

    @pl.when(step >= steps)
    def _():
        rows = pl.ds(pl.multiple_of((step - steps) * chunk, chunk), chunk)
        put_tile(z_ref[rows, :], half_ref[...], slots_ref, sends_ref, keep_ref)


def own_tile(slots, core, rounds, design, mine, theirs, facts, more):
    _, _, share = design.shape
    rows, probes = mine.shape
    chunk = row_chunk(share)
    steps = rows // chunk

    def first(i, *_):
        return (jnp.minimum(i, steps - 1), 0)

    def second(i, *_):
        return (jnp.maximum(i - steps, 0), 0)

    whole = pl.BlockSpec((K + 8, probes), lambda i, *_: (0, 0))
    return pl.pallas_call(
        functools.partial(own_kernel, steps),
        grid_spec=pltpu.PrefetchScalarGridSpec(
            num_scalar_prefetch=2,
            grid=(2 * steps,),
            in_specs=[
                pl.BlockSpec((chunk // share, K, share), lambda i, *_: (*first(i), 0)),
                pl.BlockSpec((chunk, probes), first),
                pl.BlockSpec((chunk, probes), first),
                whole,
                whole,
            ],
            out_specs=[
                pl.BlockSpec((chunk, 2 * probes), first),
                pl.BlockSpec((rounds, chunk, share), lambda i, *_: (0, *second(i))),
                pl.BlockSpec((chunk, share), second),
            ],
            scratch_shapes=[
                pltpu.VMEM((rows, 2 * probes), BF16),
                pltpu.VMEM((rows // 2, 2 * probes), BF16),
                pltpu.VMEM((3 * K, probes), BF16),
                pltpu.VMEM((3 * K, probes), BF16),
            ],
        ),
        out_shape=(
            jax.ShapeDtypeStruct((rows, 2 * probes), BF16),
            jax.ShapeDtypeStruct((rounds, rows, share), BF16),
            jax.ShapeDtypeStruct((rows, share), F32),
        ),
        compiler_params=params("arbitrary"),
        cost_estimate=cost(2 * rows * rows * probes, 12 * rows * probes),
        name="own",
    )(slots, core, design, mine, theirs, facts, more)


def pair_kernel(
    steps, slots_ref, design_ref, mine_ref, theirs_ref, facts_ref, more_ref, zscore_ref,
    sends_ref, keep_ref, z_ref, terms_ref, moreterms_ref,
):
    step = pl.program_id(0)
    blocks, kk, _ = design_ref.shape
    chunk, probes = mine_ref.shape

    @pl.when(step == 0)
    def _():
        terms_ref[...] = three_terms(facts_ref[:kk, :])
        moreterms_ref[...] = three_terms(more_ref[:kk, :])

    @pl.when(step < steps)
    def _():
        design = jnp.concatenate([design_ref[b] for b in range(blocks)], axis=1)
        rows = pl.ds(pl.multiple_of(step * chunk, chunk), chunk)

        def store(base, at, width, value):
            z_ref[rows, base + at : base + at + width] = value

        standardise(design, mine_ref, terms_ref, facts_ref[kk : kk + 1, :], functools.partial(store, 0))
        standardise(
            design, theirs_ref, moreterms_ref, more_ref[kk : kk + 1, :], functools.partial(store, probes)
        )

    @pl.when(step >= steps)
    def _():
        put_tile(zscore_ref[...], z_ref[...], slots_ref, sends_ref, keep_ref)


def pair_tile(slots, rounds, design, mine, theirs, facts, more, zscore):
    _, _, share = design.shape
    half, probes = mine.shape
    rows = zscore.shape[0]
    chunk = row_chunk(share)
    steps = half // chunk

    def first(i, *_):
        return (jnp.minimum(i, steps - 1), 0)

    def second(i, *_):
        return (jnp.maximum(i - steps, 0), 0)

    whole = pl.BlockSpec((K + 8, probes), lambda i, *_: (0, 0))
    return pl.pallas_call(
        functools.partial(pair_kernel, steps),
        grid_spec=pltpu.PrefetchScalarGridSpec(
            num_scalar_prefetch=1,
            grid=(steps + rows // chunk,),
            in_specs=[
                pl.BlockSpec((chunk // share, K, share), lambda i, *_: (*first(i), 0)),
                pl.BlockSpec((chunk, probes), first),
                pl.BlockSpec((chunk, probes), first),
                whole,
                whole,
                pl.BlockSpec((chunk, 2 * probes), second),
            ],
            out_specs=[
                pl.BlockSpec((rounds, chunk, share), lambda i, *_: (0, *second(i))),
                pl.BlockSpec((chunk, share), second),
            ],
            scratch_shapes=[
                pltpu.VMEM((half, 2 * probes), BF16),
                pltpu.VMEM((3 * K, probes), BF16),
                pltpu.VMEM((3 * K, probes), BF16),
            ],
        ),
        out_shape=(
            jax.ShapeDtypeStruct((rounds, rows, share), BF16),
            jax.ShapeDtypeStruct((rows, share), F32),
        ),
        compiler_params=params("arbitrary"),
        cost_estimate=cost(2 * rows * rows * probes, 8 * rows * probes),
        name="pair",
    )(slots, design, mine, theirs, facts, more, zscore)


def line_rounds(line):
    far = line > 3
    rounds = [[(0, 1), (line - 1, line - 2)] if far else []]
    slots = [[-1] * line for _ in range(line)]
    for j in range(1, line):
        pairs = []
        for i in range(line):
            to = (i + j) % line
            if far and abs(to - i) == line - 1:
                slots[i][to] = 0
            else:
                pairs.append((i, to))
                slots[i][to] = j
        rounds.append(pairs)
    return rounds, slots


def body(methyl, atlas, panel_ids):
    panels, shares = lax.axis_size("samp"), lax.axis_size("probe")
    rows = methyl.shape[0]
    samples = rows * panels
    probes = methyl.shape[1] * shares
    share = rows // shares
    line = shares // 2
    position = lax.axis_index("probe")
    place, core = position // 2, position % 2
    core_only = core[None]

    def to_sibling(value):
        return lax.ppermute(value, "probe", [(i, i ^ 1) for i in range(shares)])

    def to_panel(value, by):
        return lax.ppermute(value, "samp", [(i, (i + by) % panels) for i in range(panels)])

    def to_panel_sibling(value, by):
        pairs = [
            (s * shares + i, ((s + by) % panels) * shares + (i ^ 1))
            for s in range(panels)
            for i in range(shares)
        ]
        return lax.ppermute(value, ("samp", "probe"), pairs)

    def swap_panels(value, bit):
        return lax.ppermute(value, "samp", [(i, i ^ bit) for i in range(panels)])

    theirs = to_sibling(methyl)
    parts, panel, same, other = project(core_only, panel_ids, atlas, methyl, shares)
    before_mine = to_panel(same, 1)
    parts = lax.all_to_all(parts, "probe", 0, 0)
    scores, copies = descend(parts)
    design = lax.all_to_all(copies, "probe", 0, 0)
    part = cross_products(design, methyl, panel)
    bit = panels // 2
    while bit > 1:
        part = part + swap_panels(part, bit)
        bit //= 2
    peer = swap_panels(part, 1)
    half = lax.dynamic_index_in_dim(design.reshape(line, 2, K, share), core, 1, False)
    design_before = to_panel(half, 1)
    before_theirs = to_panel_sibling(other, 1)
    facts = solve(part, peer, panel, 0.0001 * samples, samples)
    more = to_sibling(facts)

    rounds, table = line_rounds(line)
    slots = jnp.take(jnp.array(table, jnp.int32), place, axis=0)

    def reduced(sends, keep):
        def send(value, pairs):
            return lax.ppermute(
                value, "probe", [(2 * i + c, 2 * to + c) for i, to in pairs for c in (0, 1)]
            )

        relay = send(sends[0], rounds[0]) if rounds[0] else None
        total = keep
        for j in [*range(1, 2), *range(line - 1, 1, -1)]:
            value = sends[j]
            if relay is not None and j in (2, line - 2):
                at = (place == line - 2) & (j == 2) | (place == 1) & (j == line - 2)
                value = jnp.where(at, value.astype(F32) + relay.astype(F32), value.astype(F32)).astype(BF16)
            total = total + send(value, rounds[j]).astype(F32)
        return total

    zscore, sends, keep = own_tile(slots, core_only, line, design, methyl, theirs, facts, more)
    own = reduced(sends, keep)
    sends, keep = pair_tile(
        slots, line, design_before, before_mine, before_theirs, facts, more, zscore
    )
    left = reduced(sends, keep)
    blocks = lax.all_to_all(left.astype(BF16).reshape(shares, share, share), "probe", 0, 0)
    blocks = to_panel(blocks, -1)
    after = jnp.swapaxes(blocks.astype(F32), 1, 2).reshape(rows, share)
    return jnp.stack([own, left, after]) / probes, scores


def solution(mesh):
    placed = (P("samp", "probe"), P(None, "probe"), P())
    return jax.shard_map(
        body,
        mesh=mesh,
        in_specs=placed,
        out_specs=(P(None, "samp", "probe"), P(None, ("samp", "probe"))),
        check_vma=False,
    )
```

profile of v0, /device:TPU:0, one launch (start us, length us, event | category | flops | bytes accessed | tf_op | source)
XLA Modules:
  0.0 216.4 jit_solution(13975265000940407646)
XLA Ops:
  1.2 5.9 %project.1 = (f32[8,64,128]{2,1,0:T(8,128)}, bf16[32,2048]{1,0:T(8,128)(2,1)}, bf16[512,2048]{1,0:T(8,128)(2,1)}, bf16[512,2048]{1,0:T(8,128)(2,1)}) custom-call(s32[1]{0:T(128)} %bitcast.1.core_ref, s32[64]{0:T(128)} %ids_ref.1, bf16[64,2048]{1,0:T(8,128)(2,1)} %atlas_ref.1, bf16[1024,2048]{1,0:T(8,128)(2,1)} %mine_ref.1), custom_call_target="tpu_custom_call" | custom-call | flops 134217728 | bytes 8388608 | tf_op jit(solution)/shard_map/project/pallas_call | solution.py:78
  7.1 2.6 %collective-permute-start.10 = (bf16[512,2048]{1,0:T(8,128)(2,1)}, bf16[512,2048]{1,0:T(8,128)(2,1)S(1)}, u32[]{:S(2)}, u32[]{:S(2)}) collective-permute-start(bf16[512,2048]{1,0:T(8,128)(2,1)} %get-tuple-element.19), channel_id=1, source_target_pairs={{0,9},{1,8},{2,11},{3,10},{4,13},{5,12},{6,15},{7,14},{8,17},{9,16... | collective-permute-start | bytes 6291464 | tf_op jit(solution)/shard_map/ppermute | solution.py:476
  9.7 1.5 collective-permute-start.9
  11.2 14.7 %all_to_all.15.parts_ref = f32[8,64,128]{2,1,0:T(8,128)} all-to-all(f32[8,64,128]{2,1,0:T(8,128)} %get-tuple-element.13), channel_id=1, replica_groups=mesh['samp'=4,'probe'=8] {'probe'}, dimensions={0} | all-to-all | bytes 524288 | tf_op jit(solution)/shard_map/all_to_all | solution.py:484
  25.9 7.6 %descend.1 = (f32[32,128]{1,0:T(8,128)}, bf16[8,32,128]{2,1,0:T(8,128)(2,1)}) custom-call(f32[8,64,128]{2,1,0:T(8,128)} %all_to_all.15.parts_ref), custom_call_target="tpu_custom_call" | custom-call | flops 33554432 | bytes 16384 | tf_op jit(solution)/shard_map/descend/pallas_call | solution.py:144
  33.5 9.9 %all_to_all.16.design_ref = bf16[8,32,128]{2,1,0:T(8,128)(2,1)} all-to-all(bf16[8,32,128]{2,1,0:T(8,128)(2,1)} %get-tuple-element.14), channel_id=1, replica_groups=mesh['samp'=4,'probe'=8] {'probe'}, dimensions={0} | all-to-all | bytes 131072 | tf_op jit(solution)/shard_map/all_to_all | solution.py:486
  43.3 4.8 %cross.1 = f32[32,2304]{1,0:T(8,128)} custom-call(bf16[8,32,128]{2,1,0:T(8,128)(2,1)} %all_to_all.16.design_ref, bf16[1024,2048]{1,0:T(8,128)(2,1)} %mine_ref.1, bf16[32,2048]{1,0:T(8,128)(2,1)} %get-tuple-element.15.panel_ref), custom_call_target="tpu_custom_call" | custom-call | flops 268435456 | bytes 4194304 | tf_op jit(solution)/shard_map/cross/pallas_call | solution.py:182
  48.7 59.6 %collective-permute-done.1 = f32[32,2304]{1,0:T(8,128)S(1)} collective-permute-done((f32[32,2304]{1,0:T(8,128)}, f32[32,2304]{1,0:T(8,128)S(1)}, u32[]{:S(2)}, u32[]{:S(2)}) %collective-permute-start.1) | collective-permute-done | bytes 294944 | tf_op jit(solution)/shard_map/ppermute | solution.py:479
  109.4 8.9 %collective-permute-done.2.peer_ref = f32[32,2304]{1,0:T(8,128)S(1)} collective-permute-done((f32[32,2304]{1,0:T(8,128)S(1)}, f32[32,2304]{1,0:T(8,128)S(1)}, u32[]{:S(2)}, u32[]{:S(2)}) %collective-permute-start.2) | collective-permute-done | bytes 294944 | tf_op jit(solution)/shard_map/ppermute | solution.py:479
  119.1 5.6 %solve.1.facts_ref = f32[40,2048]{1,0:T(8,128)} custom-call(f32[32,2304]{1,0:T(8,128)} %copy-done, f32[32,2304]{1,0:T(8,128)} %copy-done.5, bf16[32,2048]{1,0:T(8,128)(2,1)} %get-tuple-element.15.panel_ref), custom_call_target="tpu_custom_call" | custom-call | flops 104857600 | bytes 1310720 | tf_op jit(solution)/shard_map/solve/pallas_call | solution.py:236
  124.7 1.2 fusion.4.slots_ref
  127.3 15.9 %own.1 = (bf16[1024,4096]{1,0:T(8,128)(2,1)}, bf16[4,1024,128]{2,1,0:T(8,128)(2,1)}, f32[1024,128]{1,0:T(8,128)}) custom-call(s32[4]{0:T(128)} %fusion.4.slots_ref, s32[1]{0:T(128)} %bitcast.1.core_ref, bf16[8,32,128]{2,1,0:T(8,128)(2,1)} %all_to_all.16.design_ref, bf16[1024,2048]{1,0:T(8,128)(2,1)} %mine_ref.1, ...), custom_call_target="tpu_custom_call" | custom-call | flops 4294967296 | bytes 25165824 | tf_op jit(solution)/shard_map/own/pallas_call | solution.py:323
  144.6 11.9 %pair.1 = (bf16[4,1024,128]{2,1,0:T(8,128)(2,1)}, f32[1024,128]{1,0:T(8,128)}) custom-call(s32[4]{0:T(128)} %fusion.4.slots_ref, bf16[4,32,128]{2,1,0:T(8,128)(2,1)} %copy-done.8, bf16[512,2048]{1,0:T(8,128)(2,1)} %collective-permute-done.9.mine_ref, bf16[512,2048]{1,0:T(8,128)(2,1)} %copy-done.6, f32[40,2048]{1,0:T(8,128)} %solve.1.facts_ref, ...), custom_call_target="tpu_custom_call" | custom-call | flops 4294967296 | bytes 16777216 | tf_op jit(solution)/shard_map/pair/pallas_call | solution.py:403
  156.5 1.2 slice_bitcast_fusion.2
  157.7 3.8 %collective-permute-start.13 = (bf16[1024,128]{1,0:T(8,128)(2,1)S(1)}, bf16[1024,128]{1,0:T(8,128)(2,1)S(1)}, u32[]{:S(2)}, u32[]{:S(2)}) collective-permute-start(bf16[1024,128]{1,0:T(8,128)(2,1)S(1)} %get-tuple-element.50), channel_id=1, source_target_pairs={{0,2},{1,3},{6,4},{7,5},{8,10},{9,11},{14,12},{15,13},{16,18},{17,... | collective-permute-start | bytes 786440 | tf_op jit(solution)/shard_map/ppermute | solution.py:504
  161.5 1.3 collective-permute-start.11
  162.8 1.3 collective-permute-start.12
  164.1 4.0 %collective-permute-done.13 = bf16[1024,128]{1,0:T(8,128)(2,1)S(1)} collective-permute-done((bf16[1024,128]{1,0:T(8,128)(2,1)S(1)}, bf16[1024,128]{1,0:T(8,128)(2,1)S(1)}, u32[]{:S(2)}, u32[]{:S(2)}) %collective-permute-start.13) | collective-permute-done | bytes 262176 | tf_op jit(solution)/shard_map/ppermute | solution.py:504
  168.2 1.0 fusion.1
  169.2 3.0 %collective-permute-start.14 = (bf16[1024,128]{1,0:T(8,128)(2,1)S(1)}, bf16[1024,128]{1,0:T(8,128)(2,1)S(1)}, u32[]{:S(2)}, u32[]{:S(2)}) collective-permute-start(bf16[1024,128]{1,0:T(8,128)(2,1)S(1)} %fusion.1), channel_id=1, source_target_pairs={{0,4},{1,5},{2,6},{3,7},{4,0},{5,1},{6,2},{7,3},{8,12},{9,13},{10,... | collective-permute-start | bytes 786440 | tf_op jit(solution)/shard_map/ppermute | solution.py:504
  173.1 2.2 %collective-permute-start.6 = (bf16[1024,128]{1,0:T(8,128)(2,1)}, bf16[1024,128]{1,0:T(8,128)(2,1)}, u32[]{:S(2)}, u32[]{:S(2)}) collective-permute-start(bf16[1024,128]{1,0:T(8,128)(2,1)} %get-tuple-element.47), channel_id=1, source_target_pairs={{0,2},{1,3},{6,4},{7,5},{8,10},{9,11},{14,12},{15,13},{16,18},{17,... | collective-permute-start | bytes 786440 | tf_op jit(solution)/shard_map/ppermute | solution.py:504
  175.3 1.3 collective-permute-start.4
  176.6 1.3 collective-permute-start.5
  177.9 8.9 %collective-permute-done.14 = bf16[1024,128]{1,0:T(8,128)(2,1)S(1)} collective-permute-done((bf16[1024,128]{1,0:T(8,128)(2,1)S(1)}, bf16[1024,128]{1,0:T(8,128)(2,1)S(1)}, u32[]{:S(2)}, u32[]{:S(2)}) %collective-permute-start.14) | collective-permute-done | bytes 262176 | tf_op jit(solution)/shard_map/ppermute | solution.py:504
  187.6 3.4 %all-to-all-start.2 = ((bf16[8,128,128]{2,1,0:T(8,128)(2,1)}), bf16[8,128,128]{2,1,0:T(8,128)(2,1)S(1)}, u32[]{:S(2)}, u32[]{:S(2)}) async-start(bf16[8,128,128]{2,1,0:T(8,128)(2,1)} %bitcast.14), calls=%async_computation.2 | async-start | bytes 524288 | tf_op jit(solution)/shard_map/all_to_all | solution.py:524
  191.1 1.0 fusion
  192.1 2.9 %collective-permute-start.7 = (bf16[1024,128]{1,0:T(8,128)(2,1)S(1)}, bf16[1024,128]{1,0:T(8,128)(2,1)S(1)}, u32[]{:S(2)}, u32[]{:S(2)}) collective-permute-start(bf16[1024,128]{1,0:T(8,128)(2,1)S(1)} %fusion), channel_id=1, source_target_pairs={{0,4},{1,5},{2,6},{3,7},{4,0},{5,1},{6,2},{7,3},{8,12},{9,13},{10,... | collective-permute-start | bytes 786440 | tf_op jit(solution)/shard_map/ppermute | solution.py:504
  195.0 11.9 %all-to-all-done.2 = bf16[8,128,128]{2,1,0:T(8,128)(2,1)S(1)} async-done(((bf16[8,128,128]{2,1,0:T(8,128)(2,1)}), bf16[8,128,128]{2,1,0:T(8,128)(2,1)S(1)}, u32[]{:S(2)}, u32[]{:S(2)}) %all-to-all-start.2) | async-done | bytes 262176 | tf_op jit(solution)/shard_map/all_to_all | solution.py:524
  206.9 2.4 %collective-permute-start.15 = (bf16[8,128,128]{2,1,0:T(8,128)(2,1)S(1)}, bf16[8,128,128]{2,1,0:T(8,128)(2,1)S(1)}, u32[]{:S(2)}, u32[]{:S(2)}) collective-permute-start(bf16[8,128,128]{2,1,0:T(8,128)(2,1)S(1)} %all-to-all-done.2), channel_id=1, source_target_pairs={{0,24},{8,0},{16,8},{24,16},{1,25},{9,1},{17,9},{25,17},{2,26},{10... | collective-permute-start | bytes 786440 | tf_op jit(solution)/shard_map/ppermute | solution.py:468
  209.2 2.7 %collective-permute-done.7 = bf16[1024,128]{1,0:T(8,128)(2,1)S(1)} collective-permute-done((bf16[1024,128]{1,0:T(8,128)(2,1)S(1)}, bf16[1024,128]{1,0:T(8,128)(2,1)S(1)}, u32[]{:S(2)}, u32[]{:S(2)}) %collective-permute-start.7) | collective-permute-done | bytes 262176 | tf_op jit(solution)/shard_map/ppermute | solution.py:504
  212.0 2.8 %collective-permute-done.15 = bf16[8,128,128]{2,1,0:T(8,128)(2,1)S(1)} collective-permute-done((bf16[8,128,128]{2,1,0:T(8,128)(2,1)S(1)}, bf16[8,128,128]{2,1,0:T(8,128)(2,1)S(1)}, u32[]{:S(2)}, u32[]{:S(2)}) %collective-permute-start.15) | collective-permute-done | bytes 262176 | tf_op jit(solution)/shard_map/ppermute | solution.py:468
  215.1 1.2 maximum_multiply_fusion
  (40 shorter events, 7.6 us)
Async XLA Ops:
  0.6 125.9 %collective-permute-start = (bf16[1024,2048]{1,0:T(8,128)(2,1)}, bf16[1024,2048]{1,0:T(8,128)(2,1)}, u32[]{:S(2)}, u32[]{:S(2)}) collective-permute-start(bf16[1024,2048]{1,0:T(8,128)(2,1)} %mine_ref.1), channel_id=1, source_target_pairs={{0,1},{1,0},{2,3},{3,2},{4,5},{5,4},{6,7},{7,6},{8,9},{9,8},{10,11... | collective-permute-start | bytes 12582920 | tf_op jit(solution)/shard_map/ppermute | solution.py:465
  7.1 136.1 %collective-permute-start.10 = (bf16[512,2048]{1,0:T(8,128)(2,1)}, bf16[512,2048]{1,0:T(8,128)(2,1)S(1)}, u32[]{:S(2)}, u32[]{:S(2)}) collective-permute-start(bf16[512,2048]{1,0:T(8,128)(2,1)} %get-tuple-element.19), channel_id=1, source_target_pairs={{0,9},{1,8},{2,11},{3,10},{4,13},{5,12},{6,15},{7,14},{8,17},{9,16... | collective-permute-start | bytes 6291464 | tf_op jit(solution)/shard_map/ppermute | solution.py:476
  9.7 133.5 %collective-permute-start.9 = (bf16[512,2048]{1,0:T(8,128)(2,1)}, bf16[512,2048]{1,0:T(8,128)(2,1)}, u32[]{:S(2)}, u32[]{:S(2)}) collective-permute-start(bf16[512,2048]{1,0:T(8,128)(2,1)} %get-tuple-element.18), channel_id=1, source_target_pairs={{0,8},{8,16},{16,24},{24,0},{1,9},{9,17},{17,25},{25,1},{2,10},{10... | collective-permute-start | bytes 6291464 | tf_op jit(solution)/shard_map/ppermute | solution.py:468
  48.2 77.8 %copy-start.4 = (bf16[8,32,128]{2,1,0:T(8,128)(2,1)S(1)}, bf16[8,32,128]{2,1,0:T(8,128)(2,1)}, u32[]{:S(2)}) copy-start(bf16[8,32,128]{2,1,0:T(8,128)(2,1)} %all_to_all.16.design_ref) | copy-start | bytes 196612
  48.2 60.1 %collective-permute-start.1 = (f32[32,2304]{1,0:T(8,128)}, f32[32,2304]{1,0:T(8,128)S(1)}, u32[]{:S(2)}, u32[]{:S(2)}) collective-permute-start(f32[32,2304]{1,0:T(8,128)} %cross.1), channel_id=1, source_target_pairs={{0,16},{8,24},{16,0},{24,8},{1,17},{9,25},{17,1},{25,9},{2,18},{10... | collective-permute-start | bytes 884744 | tf_op jit(solution)/shard_map/ppermute | solution.py:479
  109.3 9.0 %copy-start = (f32[32,2304]{1,0:T(8,128)}, f32[32,2304]{1,0:T(8,128)S(1)}, u32[]{:S(2)}) copy-start(f32[32,2304]{1,0:T(8,128)S(1)} %add.42.mine_ref) | copy-start | bytes 884740
  109.3 9.0 %collective-permute-start.2 = (f32[32,2304]{1,0:T(8,128)S(1)}, f32[32,2304]{1,0:T(8,128)S(1)}, u32[]{:S(2)}, u32[]{:S(2)}) collective-permute-start(f32[32,2304]{1,0:T(8,128)S(1)} %add.42.mine_ref), channel_id=1, source_target_pairs={{0,8},{8,0},{16,24},{24,16},{1,9},{9,1},{17,25},{25,17},{2,10},{10... | collective-permute-start | bytes 884744 | tf_op jit(solution)/shard_map/ppermute | solution.py:479
  118.3 0.7 copy-start.5
  124.7 1.8 collective-permute-start.3
  125.9 17.3 %collective-permute-start.8 = (bf16[4,32,128]{2,1,0:T(8,128)(2,1)S(1)}, bf16[4,32,128]{2,1,0:T(8,128)(2,1)S(1)}, u32[]{:S(2)}, u32[]{:S(2)}) collective-permute-start(bf16[4,32,128]{2,1,0:T(8,128)(2,1)S(1)} %dynamic-slice_bitcast_fusion), channel_id=1, source_target_pairs={{0,8},{8,16},{16,24},{24,0},{1,9},{9,17},{17,25},{25,1},{2,10},{10... | collective-permute-start | bytes 98312 | tf_op jit(solution)/shard_map/ppermute | solution.py:468
  126.5 0.7 copy-start.7
  143.2 0.6 copy-start.8
  143.2 1.4 copy-start.6
  156.5 15.8 %copy-start.1 = (bf16[4,1024,128]{2,1,0:T(8,128)(2,1)S(1)}, bf16[4,1024,128]{2,1,0:T(8,128)(2,1)}, u32[]{:S(2)}) copy-start(bf16[4,1024,128]{2,1,0:T(8,128)(2,1)} %get-tuple-element.17) | copy-start | bytes 3145732
  157.7 29.1 %copy-start.3 = (f32[1024,128]{1,0:T(8,128)S(1)}, f32[1024,128]{1,0:T(8,128)}, u32[]{:S(2)}) copy-start(f32[1024,128]{1,0:T(8,128)} %get-tuple-element.21) | copy-start | bytes 1572868
  157.7 10.4 %collective-permute-start.13 = (bf16[1024,128]{1,0:T(8,128)(2,1)S(1)}, bf16[1024,128]{1,0:T(8,128)(2,1)S(1)}, u32[]{:S(2)}, u32[]{:S(2)}) collective-permute-start(bf16[1024,128]{1,0:T(8,128)(2,1)S(1)} %get-tuple-element.50), channel_id=1, source_target_pairs={{0,2},{1,3},{6,4},{7,5},{8,10},{9,11},{14,12},{15,13},{16,18},{17,... | collective-permute-start | bytes 786440 | tf_op jit(solution)/shard_map/ppermute | solution.py:504
  161.5 15.1 %collective-permute-start.11 = (bf16[1024,128]{1,0:T(8,128)(2,1)S(1)}, bf16[1024,128]{1,0:T(8,128)(2,1)S(1)}, u32[]{:S(2)}, u32[]{:S(2)}) collective-permute-start(bf16[1024,128]{1,0:T(8,128)(2,1)S(1)} %get-tuple-element.49), channel_id=1, source_target_pairs={{0,2},{1,3},{2,4},{3,5},{4,6},{5,7},{8,10},{9,11},{10,12},{11,13},... | collective-permute-start | bytes 786440 | tf_op jit(solution)/shard_map/ppermute | solution.py:504
  162.8 15.1 %collective-permute-start.12 = (bf16[1024,128]{1,0:T(8,128)(2,1)S(1)}, bf16[1024,128]{1,0:T(8,128)(2,1)S(1)}, u32[]{:S(2)}, u32[]{:S(2)}) collective-permute-start(bf16[1024,128]{1,0:T(8,128)(2,1)S(1)} %get-tuple-element.51), channel_id=1, source_target_pairs={{2,0},{3,1},{4,2},{5,3},{6,4},{7,5},{10,8},{11,9},{12,10},{13,11},... | collective-permute-start | bytes 786440 | tf_op jit(solution)/shard_map/ppermute | solution.py:504
  169.2 17.6 %collective-permute-start.14 = (bf16[1024,128]{1,0:T(8,128)(2,1)S(1)}, bf16[1024,128]{1,0:T(8,128)(2,1)S(1)}, u32[]{:S(2)}, u32[]{:S(2)}) collective-permute-start(bf16[1024,128]{1,0:T(8,128)(2,1)S(1)} %fusion.1), channel_id=1, source_target_pairs={{0,4},{1,5},{2,6},{3,7},{4,0},{5,1},{6,2},{7,3},{8,12},{9,13},{10,... | collective-permute-start | bytes 786440 | tf_op jit(solution)/shard_map/ppermute | solution.py:504
  173.1 17.9 %collective-permute-start.6 = (bf16[1024,128]{1,0:T(8,128)(2,1)}, bf16[1024,128]{1,0:T(8,128)(2,1)}, u32[]{:S(2)}, u32[]{:S(2)}) collective-permute-start(bf16[1024,128]{1,0:T(8,128)(2,1)} %get-tuple-element.47), channel_id=1, source_target_pairs={{0,2},{1,3},{6,4},{7,5},{8,10},{9,11},{14,12},{15,13},{16,18},{17,... | collective-permute-start | bytes 786440 | tf_op jit(solution)/shard_map/ppermute | solution.py:504
  175.3 33.9 %collective-permute-start.4 = (bf16[1024,128]{1,0:T(8,128)(2,1)}, bf16[1024,128]{1,0:T(8,128)(2,1)S(1)}, u32[]{:S(2)}, u32[]{:S(2)}) collective-permute-start(bf16[1024,128]{1,0:T(8,128)(2,1)} %get-tuple-element.46), channel_id=1, source_target_pairs={{0,2},{1,3},{2,4},{3,5},{4,6},{5,7},{8,10},{9,11},{10,12},{11,13},... | collective-permute-start | bytes 786440 | tf_op jit(solution)/shard_map/ppermute | solution.py:504
  176.6 32.6 %collective-permute-start.5 = (bf16[1024,128]{1,0:T(8,128)(2,1)S(1)}, bf16[1024,128]{1,0:T(8,128)(2,1)S(1)}, u32[]{:S(2)}, u32[]{:S(2)}) collective-permute-start(bf16[1024,128]{1,0:T(8,128)(2,1)S(1)} %get-tuple-element.48), channel_id=1, source_target_pairs={{2,0},{3,1},{4,2},{5,3},{6,4},{7,5},{10,8},{11,9},{12,10},{13,11},... | collective-permute-start | bytes 786440 | tf_op jit(solution)/shard_map/ppermute | solution.py:504
  186.8 25.1 %copy-start.2 = (f32[1024,128]{1,0:T(8,128)S(1)}, f32[1024,128]{1,0:T(8,128)}, u32[]{:S(2)}) copy-start(f32[1024,128]{1,0:T(8,128)} %get-tuple-element.16) | copy-start | bytes 1572868
  187.6 19.2 %all-to-all-start.2 = ((bf16[8,128,128]{2,1,0:T(8,128)(2,1)}), bf16[8,128,128]{2,1,0:T(8,128)(2,1)S(1)}, u32[]{:S(2)}, u32[]{:S(2)}) async-start(bf16[8,128,128]{2,1,0:T(8,128)(2,1)} %bitcast.14), calls=%async_computation.2 | async-start | bytes 524288 | tf_op jit(solution)/shard_map/all_to_all | solution.py:524
  192.1 19.8 %collective-permute-start.7 = (bf16[1024,128]{1,0:T(8,128)(2,1)S(1)}, bf16[1024,128]{1,0:T(8,128)(2,1)S(1)}, u32[]{:S(2)}, u32[]{:S(2)}) collective-permute-start(bf16[1024,128]{1,0:T(8,128)(2,1)S(1)} %fusion), channel_id=1, source_target_pairs={{0,4},{1,5},{2,6},{3,7},{4,0},{5,1},{6,2},{7,3},{8,12},{9,13},{10,... | collective-permute-start | bytes 786440 | tf_op jit(solution)/shard_map/ppermute | solution.py:504
  206.9 8.0 %collective-permute-start.15 = (bf16[8,128,128]{2,1,0:T(8,128)(2,1)S(1)}, bf16[8,128,128]{2,1,0:T(8,128)(2,1)S(1)}, u32[]{:S(2)}, u32[]{:S(2)}) collective-permute-start(bf16[8,128,128]{2,1,0:T(8,128)(2,1)S(1)} %all-to-all-done.2), channel_id=1, source_target_pairs={{0,24},{8,0},{16,8},{24,16},{1,25},{9,1},{17,9},{25,17},{2,26},{10... | collective-permute-start | bytes 786440 | tf_op jit(solution)/shard_map/ppermute | solution.py:468
where the time goes:
time: 217 us; the launch traced here: 216 us
  waiting for transfers between devices  99.2 us (46%)
  Pallas kernels  51.8 us (24%)
  starting transfers between devices  28.3 us (13%)
  blocking collectives  24.6 us (11%)
  other arithmetic  6.55 us (3%)
  local copies, waits for them, and re-layouts  5.14 us (2%)
    ppermute x2, waiting for transfers between devices, swap_panels(): return lax.ppermute(value, 'samp', [(i, i ^ bit) for i in range(panels)])  68.5 us
    ppermute x8, starting transfers between devices, send(): lax.ppermute(value, 'probe', [(2 * i + c, 2 * to + c) for i, to in pairs...  17 us
    pallas_call x1, Pallas kernels, own_tile(): pl.pallas_call(functools.partial(own_kernel, steps), grid_spec=pltpu.Pref...  15.9 us
    ppermute x8, waiting for transfers between devices, send(): lax.ppermute(value, 'probe', [(2 * i + c, 2 * to + c) for i, to in pairs...  15.6 us
    all_to_all x1, blocking collectives, body(): parts = lax.all_to_all(parts, 'probe', 0, 0)  14.7 us
    pallas_call x1, Pallas kernels, pair_tile(): pl.pallas_call(functools.partial(pair_kernel, steps), grid_spec=pltpu.Pre...  11.9 us
    all_to_all x1, waiting for transfers between devices, body(): lax.all_to_all(left.astype(BF16).reshape(shares, share, share), 'probe',...  11.9 us
    all_to_all x1, blocking collectives, body(): design = lax.all_to_all(copies, 'probe', 0, 0)  9.88 us
  transfers between devices with their start and end apart: 17, of which 8 were waited for; matrix products, arithmetic and copies ran while one was open for 3% of the time, Pallas kernels for 18%

commit v1 on v0

--- a/solution.py
+++ b/solution.py
@@ -40,7 +40,7 @@
     return jnp.concatenate([high, mid, low], axis=0)
 
 
-def project_kernel(core_ref, ids_ref, atlas_ref, methyl_ref, out_ref, panel_ref, same_ref, other_ref, gram_ref):
+def project_kernel(core_ref, ids_ref, atlas_ref, methyl_ref, out_ref, panel_ref, other_ref, gram_ref):
     kk = panel_ref.shape[0]
     blocks, _, share = out_ref.shape
     core = core_ref[0]
@@ -64,9 +64,7 @@
         out_ref[b, kk:, :] = jnp.zeros((kk, share), F32)
         out_ref[b, kk:, :kk] = gram_ref[...]
     for b in range(blocks // 2):
-        same = pl.multiple_of((2 * b + core) * share, share)
         other = pl.multiple_of((2 * b + 1 - core) * share, share)
-        same_ref[b * share : (b + 1) * share, :] = methyl_ref[pl.ds(same, share), :]
         other_ref[b * share : (b + 1) * share, :] = methyl_ref[pl.ds(other, share), :]
 
 
@@ -88,12 +86,10 @@
             pl.BlockSpec((chunk // share, 2 * K, share), lambda i: (i, 0, 0)),
             pl.BlockSpec((K, probes), lambda i: (0, 0)),
             half,
-            half,
         ),
         out_shape=(
             jax.ShapeDtypeStruct((shares, 2 * K, share), F32),
             jax.ShapeDtypeStruct((K, probes), BF16),
-            jax.ShapeDtypeStruct((rows // 2, probes), BF16),
             jax.ShapeDtypeStruct((rows // 2, probes), BF16),
         ),
         scratch_shapes=[pltpu.VMEM((K, K), F32)],
@@ -253,30 +249,28 @@
         store(at, width, (left * rate[:, cols]).astype(BF16))
 
 
-def put_tile(left, right, slots_ref, sends_ref, keep_ref):
+def put_tile(part, unused, sends, keep_ref):
     share = keep_ref.shape[1]
-    part = nt(left, right)
-    for p in range(right.shape[0] // share):
-        block = part[:, p * share : (p + 1) * share]
-        slot = slots_ref[p]
-
-        @pl.when(slot < 0)
-        def _():
-            keep_ref[...] = block
-
-        @pl.when(slot >= 0)
-        def _():
-            sends_ref[jnp.maximum(slot, 0)] = block.astype(BF16)
+    keep = None
+    for j, ref in enumerate(sends):
+        block = part[:, j * share : (j + 1) * share]
+        ref[...] = block.astype(BF16)
+        mine = jnp.where(unused == j, block, 0.0)
+        keep = mine if keep is None else keep + mine
+    keep_ref[...] = keep
 
 
 def own_kernel(
-    steps, slots_ref, core_ref, design_ref, mine_ref, theirs_ref, facts_ref, more_ref,
-    zscore_ref, sends_ref, keep_ref, z_ref, half_ref, terms_ref, moreterms_ref,
+    steps, line, slots_ref, at_ref, design_ref, mine_ref, theirs_ref, facts_ref, more_ref, *refs
 ):
+    (zscore_ref, *sends), (keep_ref, z_ref, half_ref, terms_ref, moreterms_ref) = (
+        refs[: line + 1],
+        refs[line + 1 :],
+    )
     step = pl.program_id(0)
     blocks, kk, share = design_ref.shape
     chunk, probes = mine_ref.shape
-    core = core_ref[0]
+    place, core = at_ref[0], at_ref[1]
 
     @pl.when(step == 0)
     def _():
@@ -298,16 +292,16 @@
         )
         for b in range(blocks // 2):
             here = pl.ds(pl.multiple_of((2 * b + core) * share, share), share)
-            there = pl.ds(pl.multiple_of(step * (chunk // 2) + b * share, share), share)
-            half_ref[there, :] = zscore_ref[here, :]
+            slot = slots_ref[step * (blocks // 2) + b]
+            half_ref[pl.ds(pl.multiple_of(slot * share, share), share), :] = zscore_ref[here, :]
 
     @pl.when(step >= steps)
     def _():
         rows = pl.ds(pl.multiple_of((step - steps) * chunk, chunk), chunk)
-        put_tile(z_ref[rows, :], half_ref[...], slots_ref, sends_ref, keep_ref)
-
-
-def own_tile(slots, core, rounds, design, mine, theirs, facts, more):
+        put_tile(nt(z_ref[rows, :], half_ref[...]), slots_ref[place], sends, keep_ref)
+
+
+def own_tile(slots, at, line, design, mine, theirs, facts, more):
     _, _, share = design.shape
     rows, probes = mine.shape
     chunk = row_chunk(share)
@@ -321,7 +315,7 @@
 
     whole = pl.BlockSpec((K + 8, probes), lambda i, *_: (0, 0))
     return pl.pallas_call(
-        functools.partial(own_kernel, steps),
+        functools.partial(own_kernel, steps, line),
         grid_spec=pltpu.PrefetchScalarGridSpec(
             num_scalar_prefetch=2,
             grid=(2 * steps,),
@@ -332,11 +326,8 @@
                 whole,
                 whole,
             ],
-            out_specs=[
-                pl.BlockSpec((chunk, 2 * probes), first),
-                pl.BlockSpec((rounds, chunk, share), lambda i, *_: (0, *second(i))),
-                pl.BlockSpec((chunk, share), second),
-            ],
+            out_specs=[pl.BlockSpec((chunk, 2 * probes), first)]
+            + [pl.BlockSpec((chunk, share), second)] * (line + 1),
             scratch_shapes=[
                 pltpu.VMEM((rows, 2 * probes), BF16),
                 pltpu.VMEM((rows // 2, 2 * probes), BF16),
@@ -344,54 +335,52 @@
                 pltpu.VMEM((3 * K, probes), BF16),
             ],
         ),
-        out_shape=(
-            jax.ShapeDtypeStruct((rows, 2 * probes), BF16),
-            jax.ShapeDtypeStruct((rounds, rows, share), BF16),
-            jax.ShapeDtypeStruct((rows, share), F32),
-        ),
+        out_shape=[jax.ShapeDtypeStruct((rows, 2 * probes), BF16)]
+        + [jax.ShapeDtypeStruct((rows, share), BF16)] * line
+        + [jax.ShapeDtypeStruct((rows, share), F32)],
         compiler_params=params("arbitrary"),
         cost_estimate=cost(2 * rows * rows * probes, 12 * rows * probes),
         name="own",
-    )(slots, core, design, mine, theirs, facts, more)
-
-
-def pair_kernel(
-    steps, slots_ref, design_ref, mine_ref, theirs_ref, facts_ref, more_ref, zscore_ref,
-    sends_ref, keep_ref, z_ref, terms_ref, moreterms_ref,
-):
+    )(slots, at, design, mine, theirs, facts, more)
+
+
+def pair_kernel(steps, last, slots_ref, at_ref, design_ref, raw_ref, facts_ref, zscore_ref, *refs):
+    refs, (z_ref, terms_ref) = refs[:-2], refs[-2:]
     step = pl.program_id(0)
-    blocks, kk, _ = design_ref.shape
-    chunk, probes = mine_ref.shape
+    blocks, kk, share = design_ref.shape
 
     @pl.when(step == 0)
     def _():
         terms_ref[...] = three_terms(facts_ref[:kk, :])
-        moreterms_ref[...] = three_terms(more_ref[:kk, :])
 
     @pl.when(step < steps)
     def _():
         design = jnp.concatenate([design_ref[b] for b in range(blocks)], axis=1)
-        rows = pl.ds(pl.multiple_of(step * chunk, chunk), chunk)
-
-        def store(base, at, width, value):
-            z_ref[rows, base + at : base + at + width] = value
-
-        standardise(design, mine_ref, terms_ref, facts_ref[kk : kk + 1, :], functools.partial(store, 0))
-        standardise(
-            design, theirs_ref, moreterms_ref, more_ref[kk : kk + 1, :], functools.partial(store, probes)
-        )
+
+        def store(at, width, value):
+            for b in range(blocks):
+                slot = slots_ref[step * blocks + b]
+                rows = pl.ds(pl.multiple_of(slot * share, share), share)
+                z_ref[rows, at : at + width] = value[b * share : (b + 1) * share, :]
+
+        standardise(design, raw_ref, terms_ref, facts_ref[kk : kk + 1, :], store)
 
     @pl.when(step >= steps)
     def _():
-        put_tile(zscore_ref[...], z_ref[...], slots_ref, sends_ref, keep_ref)
-
-
-def pair_tile(slots, rounds, design, mine, theirs, facts, more, zscore):
+        part = nt(zscore_ref[...], z_ref[...])
+        if last:
+            put_tile(part + refs[0][...], slots_ref[at_ref[0]], refs[1:-1], refs[-1])
+        else:
+            refs[0][...] = part
+
+
+def pair_tile(slots, at, line, design, raw, facts, zscore, which, partial):
     _, _, share = design.shape
-    half, probes = mine.shape
+    half, probes = raw.shape
     rows = zscore.shape[0]
     chunk = row_chunk(share)
     steps = half // chunk
+    last = partial is not None
 
     def first(i, *_):
         return (jnp.minimum(i, steps - 1), 0)
@@ -399,55 +388,126 @@
     def second(i, *_):
         return (jnp.maximum(i - steps, 0), 0)
 
-    whole = pl.BlockSpec((K + 8, probes), lambda i, *_: (0, 0))
-    return pl.pallas_call(
-        functools.partial(pair_kernel, steps),
+    total = pl.BlockSpec((chunk, half), second)
+    if last:
+        out_specs = [pl.BlockSpec((chunk, share), second)] * (line + 1)
+        out_shape = [jax.ShapeDtypeStruct((rows, share), BF16)] * line
+        out_shape += [jax.ShapeDtypeStruct((rows, share), F32)]
+    else:
+        out_specs = total
+        out_shape = jax.ShapeDtypeStruct((rows, half), F32)
+    return pl.pallas_call(
+        functools.partial(pair_kernel, steps, last),
         grid_spec=pltpu.PrefetchScalarGridSpec(
-            num_scalar_prefetch=1,
+            num_scalar_prefetch=2,
             grid=(steps + rows // chunk,),
             in_specs=[
                 pl.BlockSpec((chunk // share, K, share), lambda i, *_: (*first(i), 0)),
                 pl.BlockSpec((chunk, probes), first),
-                pl.BlockSpec((chunk, probes), first),
-                whole,
-                whole,
-                pl.BlockSpec((chunk, 2 * probes), second),
-            ],
-            out_specs=[
-                pl.BlockSpec((rounds, chunk, share), lambda i, *_: (0, *second(i))),
-                pl.BlockSpec((chunk, share), second),
-            ],
-            scratch_shapes=[
-                pltpu.VMEM((half, 2 * probes), BF16),
-                pltpu.VMEM((3 * K, probes), BF16),
-                pltpu.VMEM((3 * K, probes), BF16),
-            ],
+                pl.BlockSpec((K + 8, probes), lambda i, *_: (0, 0)),
+                pl.BlockSpec((chunk, probes), lambda i, *_: (second(i)[0], which)),
+            ]
+            + [total] * last,
+            out_specs=out_specs,
+            scratch_shapes=[pltpu.VMEM((half, probes), BF16), pltpu.VMEM((3 * K, probes), BF16)],
         ),
-        out_shape=(
-            jax.ShapeDtypeStruct((rounds, rows, share), BF16),
-            jax.ShapeDtypeStruct((rows, share), F32),
-        ),
+        out_shape=out_shape,
         compiler_params=params("arbitrary"),
-        cost_estimate=cost(2 * rows * rows * probes, 8 * rows * probes),
-        name="pair",
-    )(slots, design, mine, theirs, facts, more, zscore)
+        cost_estimate=cost(rows * rows * probes, 8 * rows * probes),
+        name="pair_last" if last else "pair_first",
+    )(slots, at, design, raw, facts, zscore, *([partial] * last))
+
+
+def fold_kernel(line, at_ref, keep_ref, *refs):
+    parts, (total_ref, same_ref, other_ref) = refs[:-3], refs[-3:]
+    place, core = at_ref[0], at_ref[1]
+    share = same_ref.shape[1]
+    total = keep_ref[...]
+    for ref in parts:
+        total = total + ref[...].astype(F32)
+    total_ref[...] = total
+    for j in range(line):
+        block = 2 * lax.rem(place + j, line)
+        same = pl.ds(pl.multiple_of((block + core) * share, share), share)
+        other = pl.ds(pl.multiple_of((block + 1 - core) * share, share), share)
+        same_ref[j] = total_ref[same, :].astype(BF16)
+        other_ref[j] = total_ref[other, :].astype(BF16)
+
+
+def fold(at, line, keep, parts):
+    rows, share = keep.shape
+    blocks = jax.ShapeDtypeStruct((line, share, share), BF16)
+    vmem = pl.BlockSpec(memory_space=pltpu.VMEM)
+    return pl.pallas_call(
+        functools.partial(fold_kernel, line),
+        in_specs=[pl.BlockSpec(memory_space=pltpu.SMEM)] + [vmem] * (1 + len(parts)),
+        out_shape=(jax.ShapeDtypeStruct((rows, share), F32), blocks, blocks),
+        compiler_params=params(),
+        cost_estimate=cost(rows * share * 8, rows * share * 16),
+        name="fold",
+    )(at, keep, *parts)
+
+
+def finish_kernel(line, probes, count, at_ref, keep_ref, *refs):
+    parts, left_ref, same_ref, other_ref, shifted, out_ref = (
+        refs[:count],
+        *refs[count : count + 3],
+        refs[count + 3 : -1],
+        refs[-1],
+    )
+    place, core = at_ref[0], at_ref[1]
+    share = keep_ref.shape[1]
+    total = keep_ref[...]
+    for ref in parts:
+        total = total + ref[...].astype(F32)
+    out_ref[0] = total * (1.0 / probes)
+    out_ref[1] = left_ref[...] * (1.0 / probes)
+    for j in range(line):
+        block = 2 * lax.rem(place - j + line, line)
+        for side in range(2):
+            if j == 0:
+                piece = (same_ref, other_ref)[side][0]
+            else:
+                piece = shifted[j - 1][side]
+            to = block + (core if side == 0 else 1 - core)
+            rows = pl.ds(pl.multiple_of(to * share, share), share)
+            out_ref[2, rows, :] = piece.astype(F32).T * (1.0 / probes)
+
+
+def finish(at, line, probes, keep, parts, left, same, other, shifted):
+    rows, share = keep.shape
+    vmem = pl.BlockSpec(memory_space=pltpu.VMEM)
+    return pl.pallas_call(
+        functools.partial(finish_kernel, line, probes, len(parts)),
+        in_specs=[pl.BlockSpec(memory_space=pltpu.SMEM)] + [vmem] * (4 + len(parts) + len(shifted)),
+        out_shape=jax.ShapeDtypeStruct((3, rows, share), F32),
+        compiler_params=params(),
+        cost_estimate=cost(rows * share * 16, rows * share * 30),
+        name="finish",
+    )(at, keep, *parts, left, same, other, *shifted)
 
 
 def line_rounds(line):
     far = line > 3
-    rounds = [[(0, 1), (line - 1, line - 2)] if far else []]
-    slots = [[-1] * line for _ in range(line)]
+    rounds, onward = [[]], []
+    slots = [[None] * line for _ in range(line)]
     for j in range(1, line):
         pairs = []
         for i in range(line):
             to = (i + j) % line
             if far and abs(to - i) == line - 1:
+                rounds[0].append((i, 1 if i == 0 else line - 2))
+                slots[i][to] = 0
+            elif far and (i, to) in ((1, line - 1), (line - 2, 0)):
+                onward.append((i, to))
                 slots[i][to] = 0
             else:
                 pairs.append((i, to))
                 slots[i][to] = j
         rounds.append(pairs)
-    return rounds, slots
+    for i in range(line):
+        slots[i][i] = next(j for j in range(line) if j not in slots[i])
+    return rounds, onward, slots
 
 
 def body(methyl, atlas, panel_ids):
@@ -459,13 +519,16 @@
     line = shares // 2
     position = lax.axis_index("probe")
     place, core = position // 2, position % 2
-    core_only = core[None]
+    at = jnp.stack([place, core]).astype(jnp.int32)
+
+    def along(value, axis, pairs):
+        return lax.ppermute(value, axis, pairs)
 
     def to_sibling(value):
-        return lax.ppermute(value, "probe", [(i, i ^ 1) for i in range(shares)])
+        return along(value, "probe", [(i, i ^ 1) for i in range(shares)])
 
     def to_panel(value, by):
-        return lax.ppermute(value, "samp", [(i, (i + by) % panels) for i in range(panels)])
+        return along(value, "samp", [(i, (i + by) % panels) for i in range(panels)])
 
     def to_panel_sibling(value, by):
         pairs = [
@@ -473,14 +536,18 @@
             for s in range(panels)
             for i in range(shares)
         ]
-        return lax.ppermute(value, ("samp", "probe"), pairs)
+        return along(value, ("samp", "probe"), pairs)
 
     def swap_panels(value, bit):
-        return lax.ppermute(value, "samp", [(i, i ^ bit) for i in range(panels)])
-
+        return along(value, "samp", [(i, i ^ bit) for i in range(panels)])
+
+    def on_line(value, pairs):
+        return along(value, "probe", [(2 * i + c, 2 * to + c) for i, to in pairs for c in (0, 1)])
+
+    same = lax.dynamic_index_in_dim(methyl.reshape(line, 2, share, -1), core, 1, False)
+    before_mine = to_panel(same.reshape(line * share, -1), 1)
     theirs = to_sibling(methyl)
-    parts, panel, same, other = project(core_only, panel_ids, atlas, methyl, shares)
-    before_mine = to_panel(same, 1)
+    parts, panel, other = project(core[None], panel_ids, atlas, methyl, shares)
     parts = lax.all_to_all(parts, "probe", 0, 0)
     scores, copies = descend(parts)
     design = lax.all_to_all(copies, "probe", 0, 0)
@@ -496,35 +563,35 @@
     facts = solve(part, peer, panel, 0.0001 * samples, samples)
     more = to_sibling(facts)
 
-    rounds, table = line_rounds(line)
+    rounds, onward, table = line_rounds(line)
     slots = jnp.take(jnp.array(table, jnp.int32), place, axis=0)
 
-    def reduced(sends, keep):
-        def send(value, pairs):
-            return lax.ppermute(
-                value, "probe", [(2 * i + c, 2 * to + c) for i, to in pairs for c in (0, 1)]
-            )
-
-        relay = send(sends[0], rounds[0]) if rounds[0] else None
-        total = keep
-        for j in [*range(1, 2), *range(line - 1, 1, -1)]:
-            value = sends[j]
-            if relay is not None and j in (2, line - 2):
-                at = (place == line - 2) & (j == 2) | (place == 1) & (j == line - 2)
-                value = jnp.where(at, value.astype(F32) + relay.astype(F32), value.astype(F32)).astype(BF16)
-            total = total + send(value, rounds[j]).astype(F32)
-        return total
-
-    zscore, sends, keep = own_tile(slots, core_only, line, design, methyl, theirs, facts, more)
-    own = reduced(sends, keep)
-    sends, keep = pair_tile(
-        slots, line, design_before, before_mine, before_theirs, facts, more, zscore
-    )
-    left = reduced(sends, keep)
-    blocks = lax.all_to_all(left.astype(BF16).reshape(shares, share, share), "probe", 0, 0)
-    blocks = to_panel(blocks, -1)
-    after = jnp.swapaxes(blocks.astype(F32), 1, 2).reshape(rows, share)
-    return jnp.stack([own, left, after]) / probes, scores
+    def arrivals(sends):
+        parts, relay = [], None
+        if onward:
+            relay = on_line(sends[0], rounds[0])
+        for j in range(1, line):
+            parts.append(on_line(sends[j], rounds[j]))
+        if onward:
+            joined = (sends[0].astype(F32) + relay.astype(F32)).astype(BF16)
+            parts.append(on_line(joined, onward))
+        return parts
+
+    zscore, *sends, own_keep = own_tile(slots, at, line, design, methyl, theirs, facts, more)
+    own_parts = arrivals(sends)
+    partial = pair_tile(slots, at, line, design_before, before_mine, facts, zscore, 0, None)
+    *sends, keep = pair_tile(slots, at, line, design_before, before_theirs, more, zscore, 1, partial)
+    left, same, other = fold(at, line, keep, arrivals(sends))
+    same, other = to_panel(same, -1), to_panel_sibling(other, -1)
+    shifted = [
+        on_line(jnp.stack([same[j], other[j]]), rounds_of_shift(line, j)) for j in range(1, line)
+    ]
+    total = finish(at, line, probes, own_keep, own_parts, left, same, other, shifted)
+    return total, scores
+
+
+def rounds_of_shift(line, by):
+    return [(i, (i + by) % line) for i in range(line)]
 
 
 def solution(mesh):

time: 217 us -> 218 us (level)
  starting transfers between devices: 28.3 us -> 46.6 us
  blocking collectives: 24.6 us -> 9.87 us
  waiting for transfers between devices: 99.2 us -> 84.8 us
  Pallas kernels: 51.8 us -> 62.8 us
  local copies, waits for them, and re-layouts: 5.14 us -> 8.09 us
  other arithmetic: 6.55 us -> 3.97 us
    ppermute x16 -> x22, starting transfers between devices: 24.9 us -> 41.7 us  [along(): return lax.ppermute(value, axis, pairs)]
    all_to_all x1 -> x0, blocking collectives: 14.7 us -> none  [body(): parts = lax.all_to_all(parts, 'probe', 0, 0)]
    pallas_call x2 -> x5, Pallas kernels: 27.8 us -> 39.4 us  [the longest x2 17.9 us: pair_tile(): pl.pallas_call(functools.partial(pair_kernel, steps, last), grid_spec=plt...]
    ppermute x16 -> x22, waiting for transfers between devices: 87.3 us -> 76.7 us  [along(): return lax.ppermute(value, axis, pairs)]
    all_to_all x1, waiting for transfers between devices: 11.9 us -> 8.11 us  [body(): parts = lax.all_to_all(parts, 'probe', 0, 0)]
    dynamic_slice x0 -> x1, local copies, waits for them, and re-layouts: none -> 3.18 us  [body(): lax.dynamic_index_in_dim(methyl.reshape(line, 2, share, -1), core, 1, False)]
    unnamed x18 -> x48, local copies, waits for them, and re-layouts: 2.81 us -> 4.89 us
  transfers between devices with their start and end apart: 17 -> 23, of which waited for: 8 -> 9; matrix products, arithmetic and copies ran while one was open for 3% -> 3% of each run, Pallas kernels for 18% -> 23%
where the time goes in v1:
time: 218 us; the launch traced here: 217 us
  waiting for transfers between devices  84.8 us (39%)
  Pallas kernels  62.8 us (29%)
  starting transfers between devices  46.6 us (21%)
  blocking collectives  9.87 us (5%)
  local copies, waits for them, and re-layouts  8.09 us (4%)
  other arithmetic  3.97 us (2%)
    ppermute x22, waiting for transfers between devices, along(): return lax.ppermute(value, axis, pairs)  76.7 us
    ppermute x22, starting transfers between devices, along(): return lax.ppermute(value, axis, pairs)  41.7 us
    pallas_call x2, Pallas kernels, pair_tile(): pl.pallas_call(functools.partial(pair_kernel, steps, last), grid_spec=plt...  17.9 us
    pallas_call x1, Pallas kernels, own_tile(): pl.pallas_call(functools.partial(own_kernel, steps, line), grid_spec=pltp...  15.8 us
    all_to_all x1, blocking collectives, body(): design = lax.all_to_all(copies, 'probe', 0, 0)  9.87 us
    all_to_all x1, waiting for transfers between devices, body(): parts = lax.all_to_all(parts, 'probe', 0, 0)  8.11 us
    pallas_call x1, Pallas kernels, descend(): pl.pallas_call(descend_kernel, out_shape=(jax.ShapeDtypeStruct((K, share)...  7.57 us
    pallas_call x1, Pallas kernels, solve(): pl.pallas_call(functools.partial(solve_kernel, ridge, samples), out_shape...  5.62 us
  transfers between devices with their start and end apart: 23, of which 9 were waited for; matrix products, arithmetic and copies ran while one was open for 3% of the time, Pallas kernels for 23%

profile of v1, /device:TPU:0, one launch (start us, length us, event | category | flops | bytes accessed | tf_op | source)
XLA Modules:
  0.0 217.1 jit_solution(2155840099757893660)
XLA Ops:
  1.2 3.2 %constant_dynamic-slice_fusion.1 = bf16[4,1,128,2048]{3,2,1,0:T(8,128)(2,1)} fusion(bf16[4,2,128,2048]{3,2,1,0:T(8,128)(2,1)} %bitcast.13, s32[]{:T(128)S(6)} %select_n.29), kind=kLoop, calls=%fused_computation.8 | loop fusion | bytes 4194308 | tf_op jit(solution)/shard_map/jit(dynamic_index_in_dim)/dynamic_slice | solution.py:547
  4.4 2.5 %collective-permute-start.11 = (bf16[512,2048]{1,0:T(8,128)(2,1)}, bf16[512,2048]{1,0:T(8,128)(2,1)S(1)}, u32[]{:S(2)}, u32[]{:S(2)}) collective-permute-start(bf16[512,2048]{1,0:T(8,128)(2,1)} %bitcast.6), channel_id=1, source_target_pairs={{0,8},{8,16},{16,24},{24,0},{1,9},{9,17},{17,25},{25,1},{2,10},{10... | collective-permute-start | bytes 6291464 | tf_op jit(solution)/shard_map/ppermute | solution.py:525
  6.9 5.3 %project.1 = (f32[8,64,128]{2,1,0:T(8,128)}, bf16[32,2048]{1,0:T(8,128)(2,1)}, bf16[512,2048]{1,0:T(8,128)(2,1)}) custom-call(s32[1]{0:T(128)} %bitcast.1.core_ref, s32[64]{0:T(128)} %ids_ref.1, bf16[64,2048]{1,0:T(8,128)(2,1)} %atlas_ref.1, bf16[1024,2048]{1,0:T(8,128)(2,1)} %mine_ref.1), custom_call_target="tpu_custom_call" | custom-call | flops 134217728 | bytes 8388608 | tf_op jit(solution)/shard_map/project/pallas_call | solution.py:76
  12.2 4.9 %all-to-all-start = ((f32[8,64,128]{2,1,0:T(8,128)}), f32[8,64,128]{2,1,0:T(8,128)S(1)}, u32[]{:S(2)}, u32[]{:S(2)}) async-start(f32[8,64,128]{2,1,0:T(8,128)} %get-tuple-element.21), calls=%async_computation | async-start | bytes 524288 | tf_op jit(solution)/shard_map/all_to_all | solution.py:551
  17.1 1.6 collective-permute-start.10
  18.7 8.1 %all-to-all-done.parts_ref = f32[8,64,128]{2,1,0:T(8,128)S(1)} async-done(((f32[8,64,128]{2,1,0:T(8,128)}), f32[8,64,128]{2,1,0:T(8,128)S(1)}, u32[]{:S(2)}, u32[]{:S(2)}) %all-to-all-start) | async-done | bytes 262176 | tf_op jit(solution)/shard_map/all_to_all | solution.py:551
  27.5 7.6 %descend.1 = (f32[32,128]{1,0:T(8,128)}, bf16[8,32,128]{2,1,0:T(8,128)(2,1)}) custom-call(f32[8,64,128]{2,1,0:T(8,128)} %copy-done.2), custom_call_target="tpu_custom_call" | custom-call | flops 33554432 | bytes 16384 | tf_op jit(solution)/shard_map/descend/pallas_call | solution.py:140
  35.1 9.9 %all_to_all.10.design_ref = bf16[8,32,128]{2,1,0:T(8,128)(2,1)} all-to-all(bf16[8,32,128]{2,1,0:T(8,128)(2,1)} %get-tuple-element.22), channel_id=1, replica_groups=mesh['samp'=4,'probe'=8] {'probe'}, dimensions={0} | all-to-all | bytes 131072 | tf_op jit(solution)/shard_map/all_to_all | solution.py:553
  45.0 4.9 %cross.1 = f32[32,2304]{1,0:T(8,128)} custom-call(bf16[8,32,128]{2,1,0:T(8,128)(2,1)} %all_to_all.10.design_ref, bf16[1024,2048]{1,0:T(8,128)(2,1)} %mine_ref.1, bf16[32,2048]{1,0:T(8,128)(2,1)} %get-tuple-element.23.panel_ref), custom_call_target="tpu_custom_call" | custom-call | flops 268435456 | bytes 4194304 | tf_op jit(solution)/shard_map/cross/pallas_call | solution.py:178
  49.8 1.5 collective-permute-start.1
  51.4 54.2 %collective-permute-done.1 = f32[32,2304]{1,0:T(8,128)S(1)} collective-permute-done((f32[32,2304]{1,0:T(8,128)}, f32[32,2304]{1,0:T(8,128)S(1)}, u32[]{:S(2)}, u32[]{:S(2)}) %collective-permute-start.1) | collective-permute-done | bytes 294944 | tf_op jit(solution)/shard_map/ppermute | solution.py:525
  106.7 8.9 %collective-permute-done.2.peer_ref = f32[32,2304]{1,0:T(8,128)S(1)} collective-permute-done((f32[32,2304]{1,0:T(8,128)S(1)}, f32[32,2304]{1,0:T(8,128)S(1)}, u32[]{:S(2)}, u32[]{:S(2)}) %collective-permute-start.2) | collective-permute-done | bytes 294944 | tf_op jit(solution)/shard_map/ppermute | solution.py:525
  116.3 5.6 %solve.1.facts_ref = f32[40,2048]{1,0:T(8,128)} custom-call(f32[32,2304]{1,0:T(8,128)} %copy-done.1, f32[32,2304]{1,0:T(8,128)} %copy-done.7, bf16[32,2048]{1,0:T(8,128)(2,1)} %get-tuple-element.23.panel_ref), custom_call_target="tpu_custom_call" | custom-call | flops 104857600 | bytes 1310720 | tf_op jit(solution)/shard_map/solve/pallas_call | solution.py:232
  124.8 15.8 %own.1 = (bf16[1024,4096]{1,0:T(8,128)(2,1)}, bf16[1024,128]{1,0:T(8,128)(2,1)}, bf16[1024,128]{1,0:T(8,128)(2,1)}, bf16[1024,128]{1,0:T(8,128)(2,1)}, bf16[1024,128]{1,0:T(8,128)(2,1)}, /*index=5*/f32[1024,128]{1,0:T(8,128)}) custom-call(s32[4]{0:T(128)} %fusion.slots_ref, s32[2]{0:T(128)} %pad_add_fusion.at_ref, ...), custom_call_target="tpu_custom_call" | custom-call | flops 4294967296 | bytes 25165824 | tf_op jit(solution)/shard_map/own/pallas_call | solution.py:317
  142.1 8.7 %pair_first.1.refs_0_ = f32[1024,512]{1,0:T(8,128)} custom-call(s32[4]{0:T(128)} %fusion.slots_ref, s32[2]{0:T(128)} %pad_add_fusion.at_ref, bf16[4,32,128]{2,1,0:T(8,128)(2,1)} %copy-done.17, bf16[512,2048]{1,0:T(8,128)(2,1)} %copy-done, f32[40,2048]{1,0:T(8,128)} %solve.1.facts_ref, bf16[1024,4096]{1,0:T(8,128)(2,1)} %get-tuple-element.30.zscore_ref), custom_call_target="tpu_custom_call" | custom-call | flops 2147483648 | bytes 16777216 | tf_op jit(solution)/shard_map/pair_first/pallas_call | solution.py:399
  150.8 9.2 %pair_last.1 = (bf16[1024,128]{1,0:T(8,128)(2,1)}, bf16[1024,128]{1,0:T(8,128)(2,1)}, bf16[1024,128]{1,0:T(8,128)(2,1)}, bf16[1024,128]{1,0:T(8,128)(2,1)}, f32[1024,128]{1,0:T(8,128)}) custom-call(s32[4]{0:T(128)} %fusion.slots_ref, s32[2]{0:T(128)} %pad_add_fusion.at_ref, bf16[4,32,128]{2,1,0:T(8,128)(2,1)} %copy-done.17, ...), custom_call_target="tpu_custom_call" | custom-call | flops 2147483648 | bytes 16777216 | tf_op jit(solution)/shard_map/pair_last/pallas_call | solution.py:399
  160.0 3.7 %collective-permute-start.15 = (bf16[1024,128]{1,0:T(8,128)(2,1)}, bf16[1024,128]{1,0:T(8,128)(2,1)S(1)}, u32[]{:S(2)}, u32[]{:S(2)}) collective-permute-start(bf16[1024,128]{1,0:T(8,128)(2,1)} %get-tuple-element.35), channel_id=1, source_target_pairs={{6,4},{7,5},{0,2},{1,3},{14,12},{15,13},{8,10},{9,11},{22,20},{23,... | collective-permute-start | bytes 786440 | tf_op jit(solution)/shard_map/ppermute | solution.py:525
  163.7 1.3 collective-permute-start.12
  165.1 5.6 %collective-permute-start.13 = (bf16[1024,128]{1,0:T(8,128)(2,1)}, bf16[1024,128]{1,0:T(8,128)(2,1)S(1)}, u32[]{:S(2)}, u32[]{:S(2)}) collective-permute-start(bf16[1024,128]{1,0:T(8,128)(2,1)} %get-tuple-element.33), channel_id=1, source_target_pairs={{0,4},{1,5},{6,2},{7,3},{8,12},{9,13},{14,10},{15,11},{16,20},{17,... | collective-permute-start | bytes 786440 | tf_op jit(solution)/shard_map/ppermute | solution.py:525
  174.3 4.6 %collective-permute-start.7 = (bf16[1024,128]{1,0:T(8,128)(2,1)S(1)}, bf16[1024,128]{1,0:T(8,128)(2,1)S(1)}, u32[]{:S(2)}, u32[]{:S(2)}) collective-permute-start(bf16[1024,128]{1,0:T(8,128)(2,1)S(1)} %copy-done.10), channel_id=1, source_target_pairs={{6,4},{7,5},{0,2},{1,3},{14,12},{15,13},{8,10},{9,11},{22,20},{23,... | collective-permute-start | bytes 786440 | tf_op jit(solution)/shard_map/ppermute | solution.py:525
  178.9 1.7 collective-permute-start.4
  180.6 1.4 collective-permute-done.13.refs_1_
  182.0 5.2 %collective-permute-start.5 = (bf16[1024,128]{1,0:T(8,128)(2,1)S(1)}, bf16[1024,128]{1,0:T(8,128)(2,1)S(1)}, u32[]{:S(2)}, u32[]{:S(2)}) collective-permute-start(bf16[1024,128]{1,0:T(8,128)(2,1)S(1)} %copy-done.22), channel_id=1, source_target_pairs={{0,4},{1,5},{6,2},{7,3},{8,12},{9,13},{14,10},{15,11},{16,20},{17,... | collective-permute-start | bytes 786440 | tf_op jit(solution)/shard_map/ppermute | solution.py:525
  188.5 2.0 collective-permute-done.16.refs_3_
  191.2 2.5 %fold.1 = (f32[1024,128]{1,0:T(8,128)}, bf16[4,128,128]{2,1,0:T(8,128)(2,1)}, bf16[4,128,128]{2,1,0:T(8,128)(2,1)}) custom-call(s32[2]{0:T(128)} %pad_add_fusion.at_ref, f32[1024,128]{1,0:T(8,128)} %get-tuple-element.31.keep_ref, bf16[1024,128]{1,0:T(8,128)(2,1)} %copy-done.13, bf16[1024,128]{1,0:T(8,128)(2,1)} %copy-done.14, bf16[1024,128]{1,0:T(8,128)(2,1)} %copy-done.15, ...), custom_call_target="tpu_custom_call" | custom-call | flops 1048576 | bytes 2097152 | tf_op jit(solution)/shard_map/fold/pallas_call | solution.py:441
  195.6 2.9 %collective-permute-done.18.refs_6_ = bf16[4,128,128]{2,1,0:T(8,128)(2,1)S(1)} collective-permute-done((bf16[4,128,128]{2,1,0:T(8,128)(2,1)}, bf16[4,128,128]{2,1,0:T(8,128)(2,1)S(1)}, u32[]{:S(2)}, u32[]{:S(2)}) %collective-permute-start.18) | collective-permute-done | bytes 131104 | tf_op jit(solution)/shard_map/ppermute | solution.py:525
  198.4 3.4 %collective-permute-start.17 = (bf16[4,128,128]{2,1,0:T(8,128)(2,1)}, bf16[4,128,128]{2,1,0:T(8,128)(2,1)S(1)}, u32[]{:S(2)}, u32[]{:S(2)}) collective-permute-start(bf16[4,128,128]{2,1,0:T(8,128)(2,1)} %get-tuple-element.37), channel_id=1, source_target_pairs={{0,24},{8,0},{16,8},{24,16},{1,25},{9,1},{17,9},{25,17},{2,26},{10... | collective-permute-start | bytes 393224 | tf_op jit(solution)/shard_map/ppermute | solution.py:525
  201.8 3.3 %collective-permute-done.17.refs_5_ = bf16[4,128,128]{2,1,0:T(8,128)(2,1)S(1)} collective-permute-done((bf16[4,128,128]{2,1,0:T(8,128)(2,1)}, bf16[4,128,128]{2,1,0:T(8,128)(2,1)S(1)}, u32[]{:S(2)}, u32[]{:S(2)}) %collective-permute-start.17) | collective-permute-done | bytes 131104 | tf_op jit(solution)/shard_map/ppermute | solution.py:525
  206.6 2.6 %collective-permute-start.21 = (bf16[2,128,128]{2,1,0:T(8,128)(2,1)S(1)}, bf16[2,128,128]{2,1,0:T(8,128)(2,1)S(1)}, u32[]{:S(2)}, u32[]{:S(2)}) collective-permute-start(bf16[2,128,128]{2,1,0:T(8,128)(2,1)S(1)} %pad_maximum_fusion.2), channel_id=1, source_target_pairs={{0,6},{1,7},{2,0},{3,1},{4,2},{5,3},{6,4},{7,5},{8,14},{9,15},{10,... | collective-permute-start | bytes 196616 | tf_op jit(solution)/shard_map/ppermute | solution.py:525
  209.2 2.1 collective-permute-done.19.refs_7_
  211.4 1.9 collective-permute-done.20.refs_8_
  214.0 3.1 %finish.1 = f32[3,1024,128]{2,1,0:T(8,128)} custom-call(s32[2]{0:T(128)} %pad_add_fusion.at_ref, f32[1024,128]{1,0:T(8,128)} %get-tuple-element.24.keep_ref, bf16[1024,128]{1,0:T(8,128)(2,1)} %copy-done.8, bf16[1024,128]{1,0:T(8,128)(2,1)} %copy-done.9, bf16[1024,128]{1,0:T(8,128)(2,1)} %copy-done.11, bf16[1024,128]{1,0:T(8,128)(2,1)} %copy-done.12, ...), custom_call_target="tpu_custom_call" | custom-call | flops 2097152 | bytes 3932160 | tf_op jit(solution)/shard_map/finish/pallas_call | solution.py:480
  (84 shorter events, 16.9 us)
Async XLA Ops:
  0.6 123.5 %collective-permute-start = (bf16[1024,2048]{1,0:T(8,128)(2,1)}, bf16[1024,2048]{1,0:T(8,128)(2,1)}, u32[]{:S(2)}, u32[]{:S(2)}) collective-permute-start(bf16[1024,2048]{1,0:T(8,128)(2,1)} %mine_ref.1), channel_id=1, source_target_pairs={{0,1},{1,0},{2,3},{3,2},{4,5},{5,4},{6,7},{7,6},{8,9},{9,8},{10,11... | collective-permute-start | bytes 12582920 | tf_op jit(solution)/shard_map/ppermute | solution.py:525
  4.4 136.3 %collective-permute-start.11 = (bf16[512,2048]{1,0:T(8,128)(2,1)}, bf16[512,2048]{1,0:T(8,128)(2,1)S(1)}, u32[]{:S(2)}, u32[]{:S(2)}) collective-permute-start(bf16[512,2048]{1,0:T(8,128)(2,1)} %bitcast.6), channel_id=1, source_target_pairs={{0,8},{8,16},{16,24},{24,0},{1,9},{9,17},{17,25},{25,1},{2,10},{10... | collective-permute-start | bytes 6291464 | tf_op jit(solution)/shard_map/ppermute | solution.py:525
  12.2 14.6 %all-to-all-start = ((f32[8,64,128]{2,1,0:T(8,128)}), f32[8,64,128]{2,1,0:T(8,128)S(1)}, u32[]{:S(2)}, u32[]{:S(2)}) async-start(f32[8,64,128]{2,1,0:T(8,128)} %get-tuple-element.21), calls=%async_computation | async-start | bytes 524288 | tf_op jit(solution)/shard_map/all_to_all | solution.py:551
  17.1 133.7 %collective-permute-start.10 = (bf16[512,2048]{1,0:T(8,128)(2,1)}, bf16[512,2048]{1,0:T(8,128)(2,1)}, u32[]{:S(2)}, u32[]{:S(2)}) collective-permute-start(bf16[512,2048]{1,0:T(8,128)(2,1)} %get-tuple-element.29), channel_id=1, source_target_pairs={{0,9},{1,8},{2,11},{3,10},{4,13},{5,12},{6,15},{7,14},{8,17},{9,16... | collective-permute-start | bytes 6291464 | tf_op jit(solution)/shard_map/ppermute | solution.py:525
  45.0 78.8 %copy-start.3 = (bf16[8,32,128]{2,1,0:T(8,128)(2,1)S(1)}, bf16[8,32,128]{2,1,0:T(8,128)(2,1)}, u32[]{:S(2)}) copy-start(bf16[8,32,128]{2,1,0:T(8,128)(2,1)} %all_to_all.10.design_ref) | copy-start | bytes 196612
  49.8 55.7 %collective-permute-start.1 = (f32[32,2304]{1,0:T(8,128)}, f32[32,2304]{1,0:T(8,128)S(1)}, u32[]{:S(2)}, u32[]{:S(2)}) collective-permute-start(f32[32,2304]{1,0:T(8,128)} %cross.1), channel_id=1, source_target_pairs={{0,16},{8,24},{16,0},{24,8},{1,17},{9,25},{17,1},{25,9},{2,18},{10... | collective-permute-start | bytes 884744 | tf_op jit(solution)/shard_map/ppermute | solution.py:525
  106.6 9.0 %copy-start.1 = (f32[32,2304]{1,0:T(8,128)}, f32[32,2304]{1,0:T(8,128)S(1)}, u32[]{:S(2)}) copy-start(f32[32,2304]{1,0:T(8,128)S(1)} %add.26.mine_ref) | copy-start | bytes 884740
  106.6 9.0 %collective-permute-start.2 = (f32[32,2304]{1,0:T(8,128)S(1)}, f32[32,2304]{1,0:T(8,128)S(1)}, u32[]{:S(2)}, u32[]{:S(2)}) collective-permute-start(f32[32,2304]{1,0:T(8,128)S(1)} %add.26.mine_ref), channel_id=1, source_target_pairs={{0,8},{8,0},{16,24},{24,16},{1,9},{9,1},{17,25},{25,17},{2,10},{10... | collective-permute-start | bytes 884744 | tf_op jit(solution)/shard_map/ppermute | solution.py:525
  121.9 2.2 collective-permute-start.3
  123.8 16.9 %collective-permute-start.9 = (bf16[4,32,128]{2,1,0:T(8,128)(2,1)S(1)}, bf16[4,32,128]{2,1,0:T(8,128)(2,1)S(1)}, u32[]{:S(2)}, u32[]{:S(2)}) collective-permute-start(bf16[4,32,128]{2,1,0:T(8,128)(2,1)S(1)} %dynamic-slice_bitcast_fusion), channel_id=1, source_target_pairs={{0,8},{8,16},{16,24},{24,0},{1,9},{9,17},{17,25},{25,1},{2,10},{10... | collective-permute-start | bytes 98312 | tf_op jit(solution)/shard_map/ppermute | solution.py:525
  150.8 23.4 %copy-start.10 = (bf16[1024,128]{1,0:T(8,128)(2,1)S(1)}, bf16[1024,128]{1,0:T(8,128)(2,1)}, u32[]{:S(2)}) copy-start(bf16[1024,128]{1,0:T(8,128)(2,1)} %get-tuple-element.28) | copy-start | bytes 786436
  150.8 28.1 %copy-start.23 = (bf16[1024,128]{1,0:T(8,128)(2,1)S(1)}, bf16[1024,128]{1,0:T(8,128)(2,1)}, u32[]{:S(2)}) copy-start(bf16[1024,128]{1,0:T(8,128)(2,1)} %get-tuple-element.25) | copy-start | bytes 786436
  150.8 31.2 %copy-start.22 = (bf16[1024,128]{1,0:T(8,128)(2,1)S(1)}, bf16[1024,128]{1,0:T(8,128)(2,1)}, u32[]{:S(2)}) copy-start(bf16[1024,128]{1,0:T(8,128)(2,1)} %get-tuple-element.26) | copy-start | bytes 786436
  150.8 36.4 %copy-start.21 = (bf16[1024,128]{1,0:T(8,128)(2,1)S(1)}, bf16[1024,128]{1,0:T(8,128)(2,1)}, u32[]{:S(2)}) copy-start(bf16[1024,128]{1,0:T(8,128)(2,1)} %get-tuple-element.27) | copy-start | bytes 786436
  160.0 11.9 %collective-permute-start.15 = (bf16[1024,128]{1,0:T(8,128)(2,1)}, bf16[1024,128]{1,0:T(8,128)(2,1)S(1)}, u32[]{:S(2)}, u32[]{:S(2)}) collective-permute-start(bf16[1024,128]{1,0:T(8,128)(2,1)} %get-tuple-element.35), channel_id=1, source_target_pairs={{6,4},{7,5},{0,2},{1,3},{14,12},{15,13},{8,10},{9,11},{22,20},{23,... | collective-permute-start | bytes 786440 | tf_op jit(solution)/shard_map/ppermute | solution.py:525
  163.7 15.1 %collective-permute-start.12 = (bf16[1024,128]{1,0:T(8,128)(2,1)}, bf16[1024,128]{1,0:T(8,128)(2,1)S(1)}, u32[]{:S(2)}, u32[]{:S(2)}) collective-permute-start(bf16[1024,128]{1,0:T(8,128)(2,1)} %get-tuple-element.32), channel_id=1, source_target_pairs={{0,2},{1,3},{2,4},{3,5},{4,6},{5,7},{8,10},{9,11},{10,12},{11,13},... | collective-permute-start | bytes 786440 | tf_op jit(solution)/shard_map/ppermute | solution.py:525
  165.1 16.9 %collective-permute-start.13 = (bf16[1024,128]{1,0:T(8,128)(2,1)}, bf16[1024,128]{1,0:T(8,128)(2,1)S(1)}, u32[]{:S(2)}, u32[]{:S(2)}) collective-permute-start(bf16[1024,128]{1,0:T(8,128)(2,1)} %get-tuple-element.33), channel_id=1, source_target_pairs={{0,4},{1,5},{6,2},{7,3},{8,12},{9,13},{14,10},{15,11},{16,20},{17,... | collective-permute-start | bytes 786440 | tf_op jit(solution)/shard_map/ppermute | solution.py:525
  170.6 16.6 %collective-permute-start.14 = (bf16[1024,128]{1,0:T(8,128)(2,1)}, bf16[1024,128]{1,0:T(8,128)(2,1)S(1)}, u32[]{:S(2)}, u32[]{:S(2)}) collective-permute-start(bf16[1024,128]{1,0:T(8,128)(2,1)} %get-tuple-element.34), channel_id=1, source_target_pairs={{2,0},{3,1},{4,2},{5,3},{6,4},{7,5},{10,8},{11,9},{12,10},{13,11},... | collective-permute-start | bytes 786440 | tf_op jit(solution)/shard_map/ppermute | solution.py:525
  173.0 17.5 %collective-permute-start.16 = (bf16[1024,128]{1,0:T(8,128)(2,1)S(1)}, bf16[1024,128]{1,0:T(8,128)(2,1)S(1)}, u32[]{:S(2)}, u32[]{:S(2)}) collective-permute-start(bf16[1024,128]{1,0:T(8,128)(2,1)S(1)} %add_convert_fusion), channel_id=1, source_target_pairs={{2,6},{3,7},{4,0},{5,1},{10,14},{11,15},{12,8},{13,9},{18,22},{19,... | collective-permute-start | bytes 786440 | tf_op jit(solution)/shard_map/ppermute | solution.py:525
  174.3 19.9 %collective-permute-start.7 = (bf16[1024,128]{1,0:T(8,128)(2,1)S(1)}, bf16[1024,128]{1,0:T(8,128)(2,1)S(1)}, u32[]{:S(2)}, u32[]{:S(2)}) collective-permute-start(bf16[1024,128]{1,0:T(8,128)(2,1)S(1)} %copy-done.10), channel_id=1, source_target_pairs={{6,4},{7,5},{0,2},{1,3},{14,12},{15,13},{8,10},{9,11},{22,20},{23,... | collective-permute-start | bytes 786440 | tf_op jit(solution)/shard_map/ppermute | solution.py:525
  178.9 11.6 %copy-start.13 = (bf16[1024,128]{1,0:T(8,128)(2,1)}, bf16[1024,128]{1,0:T(8,128)(2,1)S(1)}, u32[]{:S(2)}) copy-start(bf16[1024,128]{1,0:T(8,128)(2,1)S(1)} %collective-permute-done.12.refs_0_) | copy-start | bytes 786436
  178.9 27.3 %collective-permute-start.4 = (bf16[1024,128]{1,0:T(8,128)(2,1)S(1)}, bf16[1024,128]{1,0:T(8,128)(2,1)S(1)}, u32[]{:S(2)}, u32[]{:S(2)}) collective-permute-start(bf16[1024,128]{1,0:T(8,128)(2,1)S(1)} %copy-done.23), channel_id=1, source_target_pairs={{0,2},{1,3},{2,4},{3,5},{4,6},{5,7},{8,10},{9,11},{10,12},{11,13},... | collective-permute-start | bytes 786440 | tf_op jit(solution)/shard_map/ppermute | solution.py:525
  182.0 8.5 %copy-start.14 = (bf16[1024,128]{1,0:T(8,128)(2,1)}, bf16[1024,128]{1,0:T(8,128)(2,1)S(1)}, u32[]{:S(2)}) copy-start(bf16[1024,128]{1,0:T(8,128)(2,1)S(1)} %collective-permute-done.13.refs_1_) | copy-start | bytes 786436
  182.0 24.6 %collective-permute-start.5 = (bf16[1024,128]{1,0:T(8,128)(2,1)S(1)}, bf16[1024,128]{1,0:T(8,128)(2,1)S(1)}, u32[]{:S(2)}, u32[]{:S(2)}) collective-permute-start(bf16[1024,128]{1,0:T(8,128)(2,1)S(1)} %copy-done.22), channel_id=1, source_target_pairs={{0,4},{1,5},{6,2},{7,3},{8,12},{9,13},{14,10},{15,11},{16,20},{17,... | collective-permute-start | bytes 786440 | tf_op jit(solution)/shard_map/ppermute | solution.py:525
  187.2 22.0 %collective-permute-start.6 = (bf16[1024,128]{1,0:T(8,128)(2,1)S(1)}, bf16[1024,128]{1,0:T(8,128)(2,1)S(1)}, u32[]{:S(2)}, u32[]{:S(2)}) collective-permute-start(bf16[1024,128]{1,0:T(8,128)(2,1)S(1)} %copy-done.21), channel_id=1, source_target_pairs={{2,0},{3,1},{4,2},{5,3},{6,4},{7,5},{10,8},{11,9},{12,10},{13,11},... | collective-permute-start | bytes 786440 | tf_op jit(solution)/shard_map/ppermute | solution.py:525
  193.7 4.8 %collective-permute-start.18 = (bf16[4,128,128]{2,1,0:T(8,128)(2,1)}, bf16[4,128,128]{2,1,0:T(8,128)(2,1)S(1)}, u32[]{:S(2)}, u32[]{:S(2)}) collective-permute-start(bf16[4,128,128]{2,1,0:T(8,128)(2,1)} %get-tuple-element.38), channel_id=1, source_target_pairs={{0,25},{1,24},{2,27},{3,26},{4,29},{5,28},{6,31},{7,30},{8,1},{9,0... | collective-permute-start | bytes 393224 | tf_op jit(solution)/shard_map/ppermute | solution.py:525
  194.3 15.0 %collective-permute-start.8 = (bf16[1024,128]{1,0:T(8,128)(2,1)S(1)}, bf16[1024,128]{1,0:T(8,128)(2,1)S(1)}, u32[]{:S(2)}, u32[]{:S(2)}) collective-permute-start(bf16[1024,128]{1,0:T(8,128)(2,1)S(1)} %add_convert_fusion.1), channel_id=1, source_target_pairs={{2,6},{3,7},{4,0},{5,1},{10,14},{11,15},{12,8},{13,9},{18,22},{19,... | collective-permute-start | bytes 786440 | tf_op jit(solution)/shard_map/ppermute | solution.py:525
  198.4 14.9 %copy-start.4 = (bf16[4,128,128]{2,1,0:T(8,128)(2,1)}, bf16[4,128,128]{2,1,0:T(8,128)(2,1)S(1)}, u32[]{:S(2)}) copy-start(bf16[4,128,128]{2,1,0:T(8,128)(2,1)S(1)} %collective-permute-done.18.refs_6_) | copy-start | bytes 393220
  198.4 6.7 %collective-permute-start.17 = (bf16[4,128,128]{2,1,0:T(8,128)(2,1)}, bf16[4,128,128]{2,1,0:T(8,128)(2,1)S(1)}, u32[]{:S(2)}, u32[]{:S(2)}) collective-permute-start(bf16[4,128,128]{2,1,0:T(8,128)(2,1)} %get-tuple-element.37), channel_id=1, source_target_pairs={{0,24},{8,0},{16,8},{24,16},{1,25},{9,1},{17,9},{25,17},{2,26},{10... | collective-permute-start | bytes 393224 | tf_op jit(solution)/shard_map/ppermute | solution.py:525
  205.2 6.2 %collective-permute-start.19 = (bf16[2,128,128]{2,1,0:T(8,128)(2,1)S(1)}, bf16[2,128,128]{2,1,0:T(8,128)(2,1)S(1)}, u32[]{:S(2)}, u32[]{:S(2)}) collective-permute-start(bf16[2,128,128]{2,1,0:T(8,128)(2,1)S(1)} %pad_maximum_fusion), channel_id=1, source_target_pairs={{0,2},{1,3},{2,4},{3,5},{4,6},{5,7},{6,0},{7,1},{8,10},{9,11},{10,... | collective-permute-start | bytes 196616 | tf_op jit(solution)/shard_map/ppermute | solution.py:525
  206.2 7.1 %collective-permute-start.20 = (bf16[2,128,128]{2,1,0:T(8,128)(2,1)S(1)}, bf16[2,128,128]{2,1,0:T(8,128)(2,1)S(1)}, u32[]{:S(2)}, u32[]{:S(2)}) collective-permute-start(bf16[2,128,128]{2,1,0:T(8,128)(2,1)S(1)} %pad_maximum_fusion.1), channel_id=1, source_target_pairs={{0,4},{1,5},{2,6},{3,7},{4,0},{5,1},{6,2},{7,3},{8,12},{9,13},{10,... | collective-permute-start | bytes 196616 | tf_op jit(solution)/shard_map/ppermute | solution.py:525
  206.6 6.7 %collective-permute-start.21 = (bf16[2,128,128]{2,1,0:T(8,128)(2,1)S(1)}, bf16[2,128,128]{2,1,0:T(8,128)(2,1)S(1)}, u32[]{:S(2)}, u32[]{:S(2)}) collective-permute-start(bf16[2,128,128]{2,1,0:T(8,128)(2,1)S(1)} %pad_maximum_fusion.2), channel_id=1, source_target_pairs={{0,6},{1,7},{2,0},{3,1},{4,2},{5,3},{6,4},{7,5},{8,14},{9,15},{10,... | collective-permute-start | bytes 196616 | tf_op jit(solution)/shard_map/ppermute | solution.py:525
  (15 other events, 41.8 us)

commit v2 on v1

--- a/solution.py
+++ b/solution.py
@@ -249,28 +249,24 @@
         store(at, width, (left * rate[:, cols]).astype(BF16))
 
 
-def put_tile(part, unused, sends, keep_ref):
+def put_tile(part, sends, keep_ref):
     share = keep_ref.shape[1]
-    keep = None
-    for j, ref in enumerate(sends):
-        block = part[:, j * share : (j + 1) * share]
-        ref[...] = block.astype(BF16)
-        mine = jnp.where(unused == j, block, 0.0)
-        keep = mine if keep is None else keep + mine
-    keep_ref[...] = keep
+    keep_ref[...] = part[:, :share]
+    for j, ref in enumerate(sends, 1):
+        ref[...] = part[:, j * share : (j + 1) * share].astype(BF16)
 
 
 def own_kernel(
-    steps, line, slots_ref, at_ref, design_ref, mine_ref, theirs_ref, facts_ref, more_ref, *refs
+    steps, line, place_ref, core_ref, design_ref, mine_ref, theirs_ref, facts_ref, more_ref, *refs
 ):
     (zscore_ref, *sends), (keep_ref, z_ref, half_ref, terms_ref, moreterms_ref) = (
-        refs[: line + 1],
-        refs[line + 1 :],
+        refs[:line],
+        refs[line:],
     )
     step = pl.program_id(0)
     blocks, kk, share = design_ref.shape
     chunk, probes = mine_ref.shape
-    place, core = at_ref[0], at_ref[1]
+    place, core = place_ref[0], core_ref[0]
 
     @pl.when(step == 0)
     def _():
@@ -292,20 +288,21 @@
         )
         for b in range(blocks // 2):
             here = pl.ds(pl.multiple_of((2 * b + core) * share, share), share)
-            slot = slots_ref[step * (blocks // 2) + b]
+            slot = lax.rem(step * (blocks // 2) + b - place + line, line)
             half_ref[pl.ds(pl.multiple_of(slot * share, share), share), :] = zscore_ref[here, :]
 
     @pl.when(step >= steps)
     def _():
-        rows = pl.ds(pl.multiple_of((step - steps) * chunk, chunk), chunk)
-        put_tile(nt(z_ref[rows, :], half_ref[...]), slots_ref[place], sends, keep_ref)
-
-
-def own_tile(slots, at, line, design, mine, theirs, facts, more):
+        tall = keep_ref.shape[0]
+        rows = pl.ds(pl.multiple_of((step - steps) * tall, tall), tall)
+        put_tile(nt(z_ref[rows, :], half_ref[...]), sends, keep_ref)
+
+
+def own_tile(at, line, design, mine, theirs, facts, more):
     _, _, share = design.shape
     rows, probes = mine.shape
     chunk = row_chunk(share)
-    steps = rows // chunk
+    steps, tall = rows // chunk, 2 * chunk
 
     def first(i, *_):
         return (jnp.minimum(i, steps - 1), 0)
@@ -318,7 +315,7 @@
         functools.partial(own_kernel, steps, line),
         grid_spec=pltpu.PrefetchScalarGridSpec(
             num_scalar_prefetch=2,
-            grid=(2 * steps,),
+            grid=(steps + rows // tall,),
             in_specs=[
                 pl.BlockSpec((chunk // share, K, share), lambda i, *_: (*first(i), 0)),
                 pl.BlockSpec((chunk, probes), first),
@@ -327,7 +324,7 @@
                 whole,
             ],
             out_specs=[pl.BlockSpec((chunk, 2 * probes), first)]
-            + [pl.BlockSpec((chunk, share), second)] * (line + 1),
+            + [pl.BlockSpec((tall, share), second)] * line,
             scratch_shapes=[
                 pltpu.VMEM((rows, 2 * probes), BF16),
                 pltpu.VMEM((rows // 2, 2 * probes), BF16),
@@ -336,15 +333,15 @@
             ],
         ),
         out_shape=[jax.ShapeDtypeStruct((rows, 2 * probes), BF16)]
-        + [jax.ShapeDtypeStruct((rows, share), BF16)] * line
+        + [jax.ShapeDtypeStruct((rows, share), BF16)] * (line - 1)
         + [jax.ShapeDtypeStruct((rows, share), F32)],
         compiler_params=params("arbitrary"),
         cost_estimate=cost(2 * rows * rows * probes, 12 * rows * probes),
         name="own",
-    )(slots, at, design, mine, theirs, facts, more)
-
-
-def pair_kernel(steps, last, slots_ref, at_ref, design_ref, raw_ref, facts_ref, zscore_ref, *refs):
+    )(*at, design, mine, theirs, facts, more)
+
+
+def pair_kernel(steps, line, last, place_ref, design_ref, raw_ref, facts_ref, zscore_ref, *refs):
     refs, (z_ref, terms_ref) = refs[:-2], refs[-2:]
     step = pl.program_id(0)
     blocks, kk, share = design_ref.shape
@@ -359,7 +356,7 @@
 
         def store(at, width, value):
             for b in range(blocks):
-                slot = slots_ref[step * blocks + b]
+                slot = lax.rem(step * blocks + b - place_ref[0] + line, line)
                 rows = pl.ds(pl.multiple_of(slot * share, share), share)
                 z_ref[rows, at : at + width] = value[b * share : (b + 1) * share, :]
 
@@ -369,17 +366,17 @@
     def _():
         part = nt(zscore_ref[...], z_ref[...])
         if last:
-            put_tile(part + refs[0][...], slots_ref[at_ref[0]], refs[1:-1], refs[-1])
+            put_tile(part + refs[0][...], refs[1:-1], refs[-1])
         else:
             refs[0][...] = part
 
 
-def pair_tile(slots, at, line, design, raw, facts, zscore, which, partial):
+def pair_tile(at, line, design, raw, facts, zscore, which, partial):
     _, _, share = design.shape
     half, probes = raw.shape
     rows = zscore.shape[0]
     chunk = row_chunk(share)
-    steps = half // chunk
+    steps, tall = half // chunk, 2 * chunk
     last = partial is not None
 
     def first(i, *_):
@@ -388,24 +385,24 @@
     def second(i, *_):
         return (jnp.maximum(i - steps, 0), 0)
 
-    total = pl.BlockSpec((chunk, half), second)
+    total = pl.BlockSpec((tall, half), second)
     if last:
-        out_specs = [pl.BlockSpec((chunk, share), second)] * (line + 1)
-        out_shape = [jax.ShapeDtypeStruct((rows, share), BF16)] * line
+        out_specs = [pl.BlockSpec((tall, share), second)] * line
+        out_shape = [jax.ShapeDtypeStruct((rows, share), BF16)] * (line - 1)
         out_shape += [jax.ShapeDtypeStruct((rows, share), F32)]
     else:
         out_specs = total
         out_shape = jax.ShapeDtypeStruct((rows, half), F32)
     return pl.pallas_call(
-        functools.partial(pair_kernel, steps, last),
+        functools.partial(pair_kernel, steps, line, last),
         grid_spec=pltpu.PrefetchScalarGridSpec(
-            num_scalar_prefetch=2,
-            grid=(steps + rows // chunk,),
+            num_scalar_prefetch=1,
+            grid=(steps + rows // tall,),
             in_specs=[
                 pl.BlockSpec((chunk // share, K, share), lambda i, *_: (*first(i), 0)),
                 pl.BlockSpec((chunk, probes), first),
                 pl.BlockSpec((K + 8, probes), lambda i, *_: (0, 0)),
-                pl.BlockSpec((chunk, probes), lambda i, *_: (second(i)[0], which)),
+                pl.BlockSpec((tall, probes), lambda i, *_: (second(i)[0], which)),
             ]
             + [total] * last,
             out_specs=out_specs,
@@ -415,12 +412,12 @@
         compiler_params=params("arbitrary"),
         cost_estimate=cost(rows * rows * probes, 8 * rows * probes),
         name="pair_last" if last else "pair_first",
-    )(slots, at, design, raw, facts, zscore, *([partial] * last))
-
-
-def fold_kernel(line, at_ref, keep_ref, *refs):
+    )(at[0], design, raw, facts, zscore, *([partial] * last))
+
+
+def fold_kernel(line, place_ref, core_ref, keep_ref, *refs):
     parts, (total_ref, same_ref, other_ref) = refs[:-3], refs[-3:]
-    place, core = at_ref[0], at_ref[1]
+    place, core = place_ref[0], core_ref[0]
     share = same_ref.shape[1]
     total = keep_ref[...]
     for ref in parts:
@@ -440,74 +437,68 @@
     vmem = pl.BlockSpec(memory_space=pltpu.VMEM)
     return pl.pallas_call(
         functools.partial(fold_kernel, line),
-        in_specs=[pl.BlockSpec(memory_space=pltpu.SMEM)] + [vmem] * (1 + len(parts)),
+        in_specs=[pl.BlockSpec(memory_space=pltpu.SMEM)] * 2 + [vmem] * (1 + len(parts)),
         out_shape=(jax.ShapeDtypeStruct((rows, share), F32), blocks, blocks),
         compiler_params=params(),
         cost_estimate=cost(rows * share * 8, rows * share * 16),
         name="fold",
-    )(at, keep, *parts)
-
-
-def finish_kernel(line, probes, count, at_ref, keep_ref, *refs):
-    parts, left_ref, same_ref, other_ref, shifted, out_ref = (
-        refs[:count],
-        *refs[count : count + 3],
-        refs[count + 3 : -1],
-        refs[-1],
-    )
-    place, core = at_ref[0], at_ref[1]
-    share = keep_ref.shape[1]
-    total = keep_ref[...]
+    )(*at, keep, *parts)
+
+
+def scale_kernel(probes, own_ref, *refs):
+    parts, (left_ref, out_ref) = refs[:-2], refs[-2:]
+    total = own_ref[...]
     for ref in parts:
         total = total + ref[...].astype(F32)
     out_ref[0] = total * (1.0 / probes)
     out_ref[1] = left_ref[...] * (1.0 / probes)
+
+
+def scale(probes, keep, parts, left):
+    rows, share = keep.shape
+    vmem = pl.BlockSpec((rows, share), lambda i: (0, 0))
+    return pl.pallas_call(
+        functools.partial(scale_kernel, probes),
+        grid=(1,),
+        in_specs=[vmem] * (2 + len(parts)),
+        out_specs=pl.BlockSpec((2, rows, share), lambda i: (0, 0, 0)),
+        out_shape=jax.ShapeDtypeStruct((3, rows, share), F32),
+        compiler_params=params("arbitrary"),
+        cost_estimate=cost(rows * share * 16, rows * share * 30),
+        name="scale",
+    )(keep, *parts, left)
+
+
+def finish_kernel(line, probes, place_ref, core_ref, _, same_ref, other_ref, *refs):
+    shifted, out_ref = refs[:-1], refs[-1]
+    place, core = place_ref[0], core_ref[0]
+    share = same_ref.shape[1]
     for j in range(line):
         block = 2 * lax.rem(place - j + line, line)
         for side in range(2):
-            if j == 0:
-                piece = (same_ref, other_ref)[side][0]
-            else:
-                piece = shifted[j - 1][side]
+            piece = (same_ref, other_ref)[side][0] if j == 0 else shifted[j - 1][side]
             to = block + (core if side == 0 else 1 - core)
             rows = pl.ds(pl.multiple_of(to * share, share), share)
-            out_ref[2, rows, :] = piece.astype(F32).T * (1.0 / probes)
-
-
-def finish(at, line, probes, keep, parts, left, same, other, shifted):
-    rows, share = keep.shape
-    vmem = pl.BlockSpec(memory_space=pltpu.VMEM)
-    return pl.pallas_call(
-        functools.partial(finish_kernel, line, probes, len(parts)),
-        in_specs=[pl.BlockSpec(memory_space=pltpu.SMEM)] + [vmem] * (4 + len(parts) + len(shifted)),
-        out_shape=jax.ShapeDtypeStruct((3, rows, share), F32),
-        compiler_params=params(),
-        cost_estimate=cost(rows * share * 16, rows * share * 30),
+            out_ref[0, rows, :] = piece.astype(F32).T * (1.0 / probes)
+
+
+def finish(at, line, probes, tiles, same, other, shifted):
+    _, rows, share = tiles.shape
+    first = pl.BlockSpec((1, share, share), lambda i: (0, 0, 0))
+    pair = pl.BlockSpec((2, share, share), lambda i: (0, 0, 0))
+    return pl.pallas_call(
+        functools.partial(finish_kernel, line, probes),
+        grid=(1,),
+        in_specs=[pl.BlockSpec(memory_space=pltpu.SMEM)] * 2
+        + [pl.BlockSpec(memory_space=pl.ANY), first, first]
+        + [pair] * len(shifted),
+        out_specs=pl.BlockSpec((1, rows, share), lambda i: (2, 0, 0)),
+        out_shape=jax.ShapeDtypeStruct(tiles.shape, F32),
+        input_output_aliases={2: 0},
+        compiler_params=params("arbitrary"),
+        cost_estimate=cost(rows * share * 4, rows * share * 8),
         name="finish",
-    )(at, keep, *parts, left, same, other, *shifted)
-
-
-def line_rounds(line):
-    far = line > 3
-    rounds, onward = [[]], []
-    slots = [[None] * line for _ in range(line)]
-    for j in range(1, line):
-        pairs = []
-        for i in range(line):
-            to = (i + j) % line
-            if far and abs(to - i) == line - 1:
-                rounds[0].append((i, 1 if i == 0 else line - 2))
-                slots[i][to] = 0
-            elif far and (i, to) in ((1, line - 1), (line - 2, 0)):
-                onward.append((i, to))
-                slots[i][to] = 0
-            else:
-                pairs.append((i, to))
-                slots[i][to] = j
-        rounds.append(pairs)
-    for i in range(line):
-        slots[i][i] = next(j for j in range(line) if j not in slots[i])
-    return rounds, onward, slots
+    )(*at, tiles, same, other, *shifted)
 
 
 def body(methyl, atlas, panel_ids):
@@ -519,7 +510,7 @@
     line = shares // 2
     position = lax.axis_index("probe")
     place, core = position // 2, position % 2
-    at = jnp.stack([place, core]).astype(jnp.int32)
+    at = (place[None], core[None])
 
     def along(value, axis, pairs):
         return lax.ppermute(value, axis, pairs)
@@ -563,35 +554,21 @@
     facts = solve(part, peer, panel, 0.0001 * samples, samples)
     more = to_sibling(facts)
 
-    rounds, onward, table = line_rounds(line)
-    slots = jnp.take(jnp.array(table, jnp.int32), place, axis=0)
+    def round_of(by):
+        return [(i, (i + by) % line) for i in range(line)]
 
     def arrivals(sends):
-        parts, relay = [], None
-        if onward:
-            relay = on_line(sends[0], rounds[0])
-        for j in range(1, line):
-            parts.append(on_line(sends[j], rounds[j]))
-        if onward:
-            joined = (sends[0].astype(F32) + relay.astype(F32)).astype(BF16)
-            parts.append(on_line(joined, onward))
-        return parts
-
-    zscore, *sends, own_keep = own_tile(slots, at, line, design, methyl, theirs, facts, more)
+        return [on_line(value, round_of(j)) for j, value in enumerate(sends, 1)]
+
+    zscore, *sends, own_keep = own_tile(at, line, design, methyl, theirs, facts, more)
     own_parts = arrivals(sends)
-    partial = pair_tile(slots, at, line, design_before, before_mine, facts, zscore, 0, None)
-    *sends, keep = pair_tile(slots, at, line, design_before, before_theirs, more, zscore, 1, partial)
+    partial = pair_tile(at, line, design_before, before_mine, facts, zscore, 0, None)
+    *sends, keep = pair_tile(at, line, design_before, before_theirs, more, zscore, 1, partial)
     left, same, other = fold(at, line, keep, arrivals(sends))
     same, other = to_panel(same, -1), to_panel_sibling(other, -1)
-    shifted = [
-        on_line(jnp.stack([same[j], other[j]]), rounds_of_shift(line, j)) for j in range(1, line)
-    ]
-    total = finish(at, line, probes, own_keep, own_parts, left, same, other, shifted)
-    return total, scores
-
-
-def rounds_of_shift(line, by):
-    return [(i, (i + by) % line) for i in range(line)]
+    shifted = [on_line(jnp.stack([same[j], other[j]]), round_of(j)) for j in range(1, line)]
+    tiles = scale(probes, own_keep, own_parts, left)
+    return finish(at, line, probes, tiles, same, other, shifted), scores
 
 
 def solution(mesh):

time: 218 us -> 220 us (level)
  waiting for transfers between devices: 84.8 us -> 106 us
  starting transfers between devices: 46.6 us -> 32.3 us
  Pallas kernels: 62.8 us -> 59.7 us
  other arithmetic: 3.97 us -> 1.03 us
    ppermute x22 -> x18, waiting for transfers between devices: 76.7 us -> 98 us  [along(): return lax.ppermute(value, axis, pairs)]
    ppermute x22 -> x18, starting transfers between devices: 41.7 us -> 27.4 us  [along(): return lax.ppermute(value, axis, pairs)]
    pallas_call x3 -> x4, Pallas kernels: 21 us -> 19.4 us  [the longest x2 14.9 us: pair_tile(): pl.pallas_call(functools.partial(pair_kernel, steps, line, last), grid_sp...]
    unnamed x48 -> x42, local copies, waits for them, and re-layouts: 4.89 us -> 6.39 us
  transfers between devices with their start and end apart: 23 -> 19, of which waited for: 9 -> 9; matrix products, arithmetic and copies ran while one was open for 3% -> 2% of each run, Pallas kernels for 23% -> 22%
where the time goes in v2:
time: 220 us; the launch traced here: 219 us
  waiting for transfers between devices  106 us (48%)
  Pallas kernels  59.7 us (27%)
  starting transfers between devices  32.3 us (15%)
  blocking collectives  9.87 us (4%)
  local copies, waits for them, and re-layouts  9.58 us (4%)
    ppermute x18, waiting for transfers between devices, along(): return lax.ppermute(value, axis, pairs)  98 us
    ppermute x18, starting transfers between devices, along(): return lax.ppermute(value, axis, pairs)  27.4 us
    pallas_call x2, Pallas kernels, pair_tile(): pl.pallas_call(functools.partial(pair_kernel, steps, line, last), grid_sp...  14.9 us
    pallas_call x1, Pallas kernels, own_tile(): pl.pallas_call(functools.partial(own_kernel, steps, line), grid_spec=pltp...  14.6 us
    all_to_all x1, blocking collectives, body(): design = lax.all_to_all(copies, 'probe', 0, 0)  9.87 us
    all_to_all x1, waiting for transfers between devices, body(): parts = lax.all_to_all(parts, 'probe', 0, 0)  8.11 us
    pallas_call x1, Pallas kernels, descend(): pl.pallas_call(descend_kernel, out_shape=(jax.ShapeDtypeStruct((K, share)...  7.57 us
    unnamed x42, local copies, waits for them, and re-layouts  6.39 us
  transfers between devices with their start and end apart: 19, of which 9 were waited for; matrix products, arithmetic and copies ran while one was open for 2% of the time, Pallas kernels for 22%

profile of v2, /device:TPU:0, one launch (start us, length us, event | category | flops | bytes accessed | tf_op | source)
XLA Modules:
  0.0 219.3 jit_solution(7767559249766975602)
XLA Ops:
  1.2 3.2 %constant_dynamic-slice_fusion = bf16[4,1,128,2048]{3,2,1,0:T(8,128)(2,1)} fusion(bf16[4,2,128,2048]{3,2,1,0:T(8,128)(2,1)} %bitcast.11, s32[]{:T(128)S(6)} %select_n.19), kind=kLoop, calls=%fused_computation.4 | loop fusion | bytes 4194308 | tf_op jit(solution)/shard_map/jit(dynamic_index_in_dim)/dynamic_slice | solution.py:538
  4.4 2.5 %collective-permute-start.9 = (bf16[512,2048]{1,0:T(8,128)(2,1)}, bf16[512,2048]{1,0:T(8,128)(2,1)S(1)}, u32[]{:S(2)}, u32[]{:S(2)}) collective-permute-start(bf16[512,2048]{1,0:T(8,128)(2,1)} %bitcast.5), channel_id=1, source_target_pairs={{0,8},{8,16},{16,24},{24,0},{1,9},{9,17},{17,25},{25,1},{2,10},{10... | collective-permute-start | bytes 6291464 | tf_op jit(solution)/shard_map/ppermute | solution.py:516
  6.9 5.3 %project.1 = (f32[8,64,128]{2,1,0:T(8,128)}, bf16[32,2048]{1,0:T(8,128)(2,1)}, bf16[512,2048]{1,0:T(8,128)(2,1)}) custom-call(s32[1]{0:T(128)} %bitcast.1.core_ref, s32[64]{0:T(128)} %ids_ref.1, bf16[64,2048]{1,0:T(8,128)(2,1)} %atlas_ref.1, bf16[1024,2048]{1,0:T(8,128)(2,1)} %mine_ref.1), custom_call_target="tpu_custom_call" | custom-call | flops 134217728 | bytes 8388608 | tf_op jit(solution)/shard_map/project/pallas_call | solution.py:76
  12.2 4.9 %all-to-all-start = ((f32[8,64,128]{2,1,0:T(8,128)}), f32[8,64,128]{2,1,0:T(8,128)S(1)}, u32[]{:S(2)}, u32[]{:S(2)}) async-start(f32[8,64,128]{2,1,0:T(8,128)} %get-tuple-element.19), calls=%async_computation | async-start | bytes 524288 | tf_op jit(solution)/shard_map/all_to_all | solution.py:542
  17.1 1.6 collective-permute-start.8
  18.7 8.1 %all-to-all-done.parts_ref = f32[8,64,128]{2,1,0:T(8,128)S(1)} async-done(((f32[8,64,128]{2,1,0:T(8,128)}), f32[8,64,128]{2,1,0:T(8,128)S(1)}, u32[]{:S(2)}, u32[]{:S(2)}) %all-to-all-start) | async-done | bytes 262176 | tf_op jit(solution)/shard_map/all_to_all | solution.py:542
  27.5 7.6 %descend.1 = (f32[32,128]{1,0:T(8,128)}, bf16[8,32,128]{2,1,0:T(8,128)(2,1)}) custom-call(f32[8,64,128]{2,1,0:T(8,128)} %copy-done.2), custom_call_target="tpu_custom_call" | custom-call | flops 33554432 | bytes 16384 | tf_op jit(solution)/shard_map/descend/pallas_call | solution.py:140
  35.1 9.9 %all_to_all.10.design_ref = bf16[8,32,128]{2,1,0:T(8,128)(2,1)} all-to-all(bf16[8,32,128]{2,1,0:T(8,128)(2,1)} %get-tuple-element.20), channel_id=1, replica_groups=mesh['samp'=4,'probe'=8] {'probe'}, dimensions={0} | all-to-all | bytes 131072 | tf_op jit(solution)/shard_map/all_to_all | solution.py:544
  45.0 4.9 %cross.1 = f32[32,2304]{1,0:T(8,128)} custom-call(bf16[8,32,128]{2,1,0:T(8,128)(2,1)} %all_to_all.10.design_ref, bf16[1024,2048]{1,0:T(8,128)(2,1)} %mine_ref.1, bf16[32,2048]{1,0:T(8,128)(2,1)} %get-tuple-element.21.panel_ref), custom_call_target="tpu_custom_call" | custom-call | flops 268435456 | bytes 4194304 | tf_op jit(solution)/shard_map/cross/pallas_call | solution.py:178
  49.9 1.5 collective-permute-start.1
  51.4 54.2 %collective-permute-done.1 = f32[32,2304]{1,0:T(8,128)S(1)} collective-permute-done((f32[32,2304]{1,0:T(8,128)}, f32[32,2304]{1,0:T(8,128)S(1)}, u32[]{:S(2)}, u32[]{:S(2)}) %collective-permute-start.1) | collective-permute-done | bytes 294944 | tf_op jit(solution)/shard_map/ppermute | solution.py:516
  106.7 8.9 %collective-permute-done.2.peer_ref = f32[32,2304]{1,0:T(8,128)S(1)} collective-permute-done((f32[32,2304]{1,0:T(8,128)S(1)}, f32[32,2304]{1,0:T(8,128)S(1)}, u32[]{:S(2)}, u32[]{:S(2)}) %collective-permute-start.2) | collective-permute-done | bytes 294944 | tf_op jit(solution)/shard_map/ppermute | solution.py:516
  116.3 5.6 %solve.1.facts_ref = f32[40,2048]{1,0:T(8,128)} custom-call(f32[32,2304]{1,0:T(8,128)} %copy-done.1, f32[32,2304]{1,0:T(8,128)} %copy-done.7, bf16[32,2048]{1,0:T(8,128)(2,1)} %get-tuple-element.21.panel_ref), custom_call_target="tpu_custom_call" | custom-call | flops 104857600 | bytes 1310720 | tf_op jit(solution)/shard_map/solve/pallas_call | solution.py:232
  122.3 1.5 collective-permute-done.3.more_ref.facts_ref
  124.5 14.6 %own.1 = (bf16[1024,4096]{1,0:T(8,128)(2,1)}, bf16[1024,128]{1,0:T(8,128)(2,1)}, bf16[1024,128]{1,0:T(8,128)(2,1)}, bf16[1024,128]{1,0:T(8,128)(2,1)}, f32[1024,128]{1,0:T(8,128)}) custom-call(s32[1]{0:T(128)} %bitcast.place_ref, s32[1]{0:T(128)} %bitcast.1.core_ref, bf16[8,32,128]{2,1,0:T(8,128)(2,1)} %all_to_all.10.design_ref, ...), custom_call_target="tpu_custom_call" | custom-call | flops 4294967296 | bytes 25165824 | tf_op jit(solution)/shard_map/own/pallas_call | solution.py:314
  140.5 7.2 %pair_first.1.refs_0_ = f32[1024,512]{1,0:T(8,128)} custom-call(s32[1]{0:T(128)} %bitcast.place_ref, bf16[4,32,128]{2,1,0:T(8,128)(2,1)} %copy-done.14, bf16[512,2048]{1,0:T(8,128)(2,1)} %copy-done, f32[40,2048]{1,0:T(8,128)} %solve.1.facts_ref, bf16[1024,4096]{1,0:T(8,128)(2,1)} %get-tuple-element.27.zscore_ref), custom_call_target="tpu_custom_call" | custom-call | flops 2147483648 | bytes 16777216 | tf_op jit(solution)/shard_map/pair_first/pallas_call | solution.py:396
  147.7 7.7 %pair_last.1 = (bf16[1024,128]{1,0:T(8,128)(2,1)}, bf16[1024,128]{1,0:T(8,128)(2,1)}, bf16[1024,128]{1,0:T(8,128)(2,1)}, f32[1024,128]{1,0:T(8,128)}) custom-call(s32[1]{0:T(128)} %bitcast.place_ref, bf16[4,32,128]{2,1,0:T(8,128)(2,1)} %copy-done.14, bf16[512,2048]{1,0:T(8,128)(2,1)} %collective-permute-done.8.raw_ref, f32[40,2048]{1,0:T(8,128)} %copy-done.6, ...), custom_call_target="tpu_custom_call" | custom-call | flops 2147483648 | bytes 16777216 | tf_op jit(solution)/shard_map/pair_last/pallas_call | solution.py:396
  155.5 1.8 collective-permute-start.10
  157.3 2.6 %collective-permute-start.11 = (bf16[1024,128]{1,0:T(8,128)(2,1)}, bf16[1024,128]{1,0:T(8,128)(2,1)S(1)}, u32[]{:S(2)}, u32[]{:S(2)}) collective-permute-start(bf16[1024,128]{1,0:T(8,128)(2,1)} %get-tuple-element.30), channel_id=1, source_target_pairs={{0,4},{1,5},{2,6},{3,7},{4,0},{5,1},{6,2},{7,3},{8,12},{9,13},{10,... | collective-permute-start | bytes 786440 | tf_op jit(solution)/shard_map/ppermute | solution.py:516
  159.9 1.4 collective-permute-start.12
  161.2 5.6 %collective-permute-done.10.refs_0_ = bf16[1024,128]{1,0:T(8,128)(2,1)S(1)} collective-permute-done((bf16[1024,128]{1,0:T(8,128)(2,1)}, bf16[1024,128]{1,0:T(8,128)(2,1)S(1)}, u32[]{:S(2)}, u32[]{:S(2)}) %collective-permute-start.10) | collective-permute-done | bytes 262176 | tf_op jit(solution)/shard_map/ppermute | solution.py:516
  166.8 10.6 %collective-permute-done.11.refs_1_ = bf16[1024,128]{1,0:T(8,128)(2,1)S(1)} collective-permute-done((bf16[1024,128]{1,0:T(8,128)(2,1)}, bf16[1024,128]{1,0:T(8,128)(2,1)S(1)}, u32[]{:S(2)}, u32[]{:S(2)}) %collective-permute-start.11) | collective-permute-done | bytes 262176 | tf_op jit(solution)/shard_map/ppermute | solution.py:516
  178.3 2.3 %fold.1 = (f32[1024,128]{1,0:T(8,128)}, bf16[4,128,128]{2,1,0:T(8,128)(2,1)}, bf16[4,128,128]{2,1,0:T(8,128)(2,1)}) custom-call(s32[1]{0:T(128)} %bitcast.place_ref, s32[1]{0:T(128)} %bitcast.1.core_ref, f32[1024,128]{1,0:T(8,128)} %get-tuple-element.28.keep_ref, bf16[1024,128]{1,0:T(8,128)(2,1)} %copy-done.8, bf16[1024,128]{1,0:T(8,128)(2,1)} %copy-done.9, ...), custom_call_target="tpu_custom_call" | custom-call | flops 1048576 | bytes 2097152 | tf_op jit(solution)/shard_map/fold/pallas_call | solution.py:438
  181.3 6.1 %collective-permute-start.4 = (bf16[1024,128]{1,0:T(8,128)(2,1)S(1)}, bf16[1024,128]{1,0:T(8,128)(2,1)S(1)}, u32[]{:S(2)}, u32[]{:S(2)}) collective-permute-start(bf16[1024,128]{1,0:T(8,128)(2,1)S(1)} %copy-done.20), channel_id=1, source_target_pairs={{0,2},{1,3},{2,4},{3,5},{4,6},{5,7},{6,0},{7,1},{8,10},{9,11},{10,... | collective-permute-start | bytes 786440 | tf_op jit(solution)/shard_map/ppermute | solution.py:516
  188.4 1.5 collective-permute-start.6
  189.9 1.8 collective-permute-start.13
  191.6 3.8 %collective-permute-done.13.same_ref = bf16[4,128,128]{2,1,0:T(8,128)(2,1)S(1)} collective-permute-done((bf16[4,128,128]{2,1,0:T(8,128)(2,1)}, bf16[4,128,128]{2,1,0:T(8,128)(2,1)S(1)}, u32[]{:S(2)}, u32[]{:S(2)}) %collective-permute-start.13) | collective-permute-done | bytes 131104 | tf_op jit(solution)/shard_map/ppermute | solution.py:516
  197.8 1.7 collective-permute-start.17
  199.5 7.4 %collective-permute-done.5.refs_1_ = bf16[1024,128]{1,0:T(8,128)(2,1)S(1)} collective-permute-done((bf16[1024,128]{1,0:T(8,128)(2,1)S(1)}, bf16[1024,128]{1,0:T(8,128)(2,1)S(1)}, u32[]{:S(2)}, u32[]{:S(2)}) %collective-permute-start.5) | collective-permute-done | bytes 262176 | tf_op jit(solution)/shard_map/ppermute | solution.py:516
  207.7 2.6 %scale.1._ = f32[3,1024,128]{2,1,0:T(8,128)} custom-call(f32[1024,128]{1,0:T(8,128)} %get-tuple-element.22.own_ref, bf16[1024,128]{1,0:T(8,128)(2,1)} %copy-done.11, bf16[1024,128]{1,0:T(8,128)(2,1)} %copy-done.12, bf16[1024,128]{1,0:T(8,128)(2,1)} %copy-done.13, f32[1024,128]{1,0:T(8,128)} %get-tuple-element.32.refs_3_), custom_call_target="tpu_custom_call" | custom-call | flops 2097152 | bytes 3932160 | tf_op jit(solution)/shard_map/scale/pallas_call | solution.py:460
  210.3 5.9 %collective-permute-done.16.refs_1_ = bf16[2,128,128]{2,1,0:T(8,128)(2,1)S(1)} collective-permute-done((bf16[2,128,128]{2,1,0:T(8,128)(2,1)S(1)}, bf16[2,128,128]{2,1,0:T(8,128)(2,1)S(1)}, u32[]{:S(2)}, u32[]{:S(2)}) %collective-permute-start.16) | collective-permute-done | bytes 65568 | tf_op jit(solution)/shard_map/ppermute | solution.py:516
  217.5 1.9 finish.1
  (67 shorter events, 12.5 us)
Async XLA Ops:
  0.6 123.1 %collective-permute-start = (bf16[1024,2048]{1,0:T(8,128)(2,1)}, bf16[1024,2048]{1,0:T(8,128)(2,1)}, u32[]{:S(2)}, u32[]{:S(2)}) collective-permute-start(bf16[1024,2048]{1,0:T(8,128)(2,1)} %mine_ref.1), channel_id=1, source_target_pairs={{0,1},{1,0},{2,3},{3,2},{4,5},{5,4},{6,7},{7,6},{8,9},{9,8},{10,11... | collective-permute-start | bytes 12582920 | tf_op jit(solution)/shard_map/ppermute | solution.py:516
  4.4 134.8 %collective-permute-start.9 = (bf16[512,2048]{1,0:T(8,128)(2,1)}, bf16[512,2048]{1,0:T(8,128)(2,1)S(1)}, u32[]{:S(2)}, u32[]{:S(2)}) collective-permute-start(bf16[512,2048]{1,0:T(8,128)(2,1)} %bitcast.5), channel_id=1, source_target_pairs={{0,8},{8,16},{16,24},{24,0},{1,9},{9,17},{17,25},{25,1},{2,10},{10... | collective-permute-start | bytes 6291464 | tf_op jit(solution)/shard_map/ppermute | solution.py:516
  12.2 14.6 %all-to-all-start = ((f32[8,64,128]{2,1,0:T(8,128)}), f32[8,64,128]{2,1,0:T(8,128)S(1)}, u32[]{:S(2)}, u32[]{:S(2)}) async-start(f32[8,64,128]{2,1,0:T(8,128)} %get-tuple-element.19), calls=%async_computation | async-start | bytes 524288 | tf_op jit(solution)/shard_map/all_to_all | solution.py:542
  17.1 130.6 %collective-permute-start.8 = (bf16[512,2048]{1,0:T(8,128)(2,1)}, bf16[512,2048]{1,0:T(8,128)(2,1)}, u32[]{:S(2)}, u32[]{:S(2)}) collective-permute-start(bf16[512,2048]{1,0:T(8,128)(2,1)} %get-tuple-element.26), channel_id=1, source_target_pairs={{0,9},{1,8},{2,11},{3,10},{4,13},{5,12},{6,15},{7,14},{8,17},{9,16... | collective-permute-start | bytes 6291464 | tf_op jit(solution)/shard_map/ppermute | solution.py:516
  45.0 77.0 %copy-start.3 = (bf16[8,32,128]{2,1,0:T(8,128)(2,1)S(1)}, bf16[8,32,128]{2,1,0:T(8,128)(2,1)}, u32[]{:S(2)}) copy-start(bf16[8,32,128]{2,1,0:T(8,128)(2,1)} %all_to_all.10.design_ref) | copy-start | bytes 196612
  49.9 55.7 %collective-permute-start.1 = (f32[32,2304]{1,0:T(8,128)}, f32[32,2304]{1,0:T(8,128)S(1)}, u32[]{:S(2)}, u32[]{:S(2)}) collective-permute-start(f32[32,2304]{1,0:T(8,128)} %cross.1), channel_id=1, source_target_pairs={{0,16},{8,24},{16,0},{24,8},{1,17},{9,25},{17,1},{25,9},{2,18},{10... | collective-permute-start | bytes 884744 | tf_op jit(solution)/shard_map/ppermute | solution.py:516
  106.6 9.0 %copy-start.1 = (f32[32,2304]{1,0:T(8,128)}, f32[32,2304]{1,0:T(8,128)S(1)}, u32[]{:S(2)}) copy-start(f32[32,2304]{1,0:T(8,128)S(1)} %add.15.mine_ref) | copy-start | bytes 884740
  106.6 9.0 %collective-permute-start.2 = (f32[32,2304]{1,0:T(8,128)S(1)}, f32[32,2304]{1,0:T(8,128)S(1)}, u32[]{:S(2)}, u32[]{:S(2)}) collective-permute-start(f32[32,2304]{1,0:T(8,128)S(1)} %add.15.mine_ref), channel_id=1, source_target_pairs={{0,8},{8,0},{16,24},{24,16},{1,9},{9,1},{17,25},{25,17},{2,10},{10... | collective-permute-start | bytes 884744 | tf_op jit(solution)/shard_map/ppermute | solution.py:516
  121.9 1.8 collective-permute-start.3
  121.9 17.2 %collective-permute-start.7 = (bf16[4,32,128]{2,1,0:T(8,128)(2,1)S(1)}, bf16[4,32,128]{2,1,0:T(8,128)(2,1)S(1)}, u32[]{:S(2)}, u32[]{:S(2)}) collective-permute-start(bf16[4,32,128]{2,1,0:T(8,128)(2,1)S(1)} %dynamic-slice_bitcast_fusion), channel_id=1, source_target_pairs={{0,8},{8,16},{16,24},{24,0},{1,9},{9,17},{17,25},{25,1},{2,10},{10... | collective-permute-start | bytes 98312 | tf_op jit(solution)/shard_map/ppermute | solution.py:516
  139.1 1.4 copy-start
  147.7 33.6 %copy-start.20 = (bf16[1024,128]{1,0:T(8,128)(2,1)S(1)}, bf16[1024,128]{1,0:T(8,128)(2,1)}, u32[]{:S(2)}) copy-start(bf16[1024,128]{1,0:T(8,128)(2,1)} %get-tuple-element.23) | copy-start | bytes 786436
  147.7 39.7 %copy-start.19 = (bf16[1024,128]{1,0:T(8,128)(2,1)S(1)}, bf16[1024,128]{1,0:T(8,128)(2,1)}, u32[]{:S(2)}) copy-start(bf16[1024,128]{1,0:T(8,128)(2,1)} %get-tuple-element.24) | copy-start | bytes 786436
  147.7 40.7 %copy-start.18 = (bf16[1024,128]{1,0:T(8,128)(2,1)S(1)}, bf16[1024,128]{1,0:T(8,128)(2,1)}, u32[]{:S(2)}) copy-start(bf16[1024,128]{1,0:T(8,128)(2,1)} %get-tuple-element.25) | copy-start | bytes 786436
  155.5 11.3 %collective-permute-start.10 = (bf16[1024,128]{1,0:T(8,128)(2,1)}, bf16[1024,128]{1,0:T(8,128)(2,1)S(1)}, u32[]{:S(2)}, u32[]{:S(2)}) collective-permute-start(bf16[1024,128]{1,0:T(8,128)(2,1)} %get-tuple-element.29), channel_id=1, source_target_pairs={{0,2},{1,3},{2,4},{3,5},{4,6},{5,7},{6,0},{7,1},{8,10},{9,11},{10,... | collective-permute-start | bytes 786440 | tf_op jit(solution)/shard_map/ppermute | solution.py:516
  157.3 20.2 %collective-permute-start.11 = (bf16[1024,128]{1,0:T(8,128)(2,1)}, bf16[1024,128]{1,0:T(8,128)(2,1)S(1)}, u32[]{:S(2)}, u32[]{:S(2)}) collective-permute-start(bf16[1024,128]{1,0:T(8,128)(2,1)} %get-tuple-element.30), channel_id=1, source_target_pairs={{0,4},{1,5},{2,6},{3,7},{4,0},{5,1},{6,2},{7,3},{8,12},{9,13},{10,... | collective-permute-start | bytes 786440 | tf_op jit(solution)/shard_map/ppermute | solution.py:516
  159.9 17.6 %collective-permute-start.12 = (bf16[1024,128]{1,0:T(8,128)(2,1)}, bf16[1024,128]{1,0:T(8,128)(2,1)S(1)}, u32[]{:S(2)}, u32[]{:S(2)}) collective-permute-start(bf16[1024,128]{1,0:T(8,128)(2,1)} %get-tuple-element.31), channel_id=1, source_target_pairs={{0,6},{1,7},{2,0},{3,1},{4,2},{5,3},{6,4},{7,5},{8,14},{9,15},{10,... | collective-permute-start | bytes 786440 | tf_op jit(solution)/shard_map/ppermute | solution.py:516
  166.8 10.7 %copy-start.8 = (bf16[1024,128]{1,0:T(8,128)(2,1)}, bf16[1024,128]{1,0:T(8,128)(2,1)S(1)}, u32[]{:S(2)}) copy-start(bf16[1024,128]{1,0:T(8,128)(2,1)S(1)} %collective-permute-done.10.refs_0_) | copy-start | bytes 786436
  177.5 0.8 copy-start.10
  180.6 11.1 %collective-permute-start.14 = (bf16[4,128,128]{2,1,0:T(8,128)(2,1)}, bf16[4,128,128]{2,1,0:T(8,128)(2,1)S(1)}, u32[]{:S(2)}, u32[]{:S(2)}) collective-permute-start(bf16[4,128,128]{2,1,0:T(8,128)(2,1)} %get-tuple-element.34), channel_id=1, source_target_pairs={{0,25},{1,24},{2,27},{3,26},{4,29},{5,28},{6,31},{7,30},{8,1},{9,0... | collective-permute-start | bytes 393224 | tf_op jit(solution)/shard_map/ppermute | solution.py:516
  181.3 16.5 %collective-permute-start.4 = (bf16[1024,128]{1,0:T(8,128)(2,1)S(1)}, bf16[1024,128]{1,0:T(8,128)(2,1)S(1)}, u32[]{:S(2)}, u32[]{:S(2)}) collective-permute-start(bf16[1024,128]{1,0:T(8,128)(2,1)S(1)} %copy-done.20), channel_id=1, source_target_pairs={{0,2},{1,3},{2,4},{3,5},{4,6},{5,7},{6,0},{7,1},{8,10},{9,11},{10,... | collective-permute-start | bytes 786440 | tf_op jit(solution)/shard_map/ppermute | solution.py:516
  187.4 19.5 %collective-permute-start.5 = (bf16[1024,128]{1,0:T(8,128)(2,1)S(1)}, bf16[1024,128]{1,0:T(8,128)(2,1)S(1)}, u32[]{:S(2)}, u32[]{:S(2)}) collective-permute-start(bf16[1024,128]{1,0:T(8,128)(2,1)S(1)} %copy-done.19), channel_id=1, source_target_pairs={{0,4},{1,5},{2,6},{3,7},{4,0},{5,1},{6,2},{7,3},{8,12},{9,13},{10,... | collective-permute-start | bytes 786440 | tf_op jit(solution)/shard_map/ppermute | solution.py:516
  188.4 18.5 %collective-permute-start.6 = (bf16[1024,128]{1,0:T(8,128)(2,1)S(1)}, bf16[1024,128]{1,0:T(8,128)(2,1)S(1)}, u32[]{:S(2)}, u32[]{:S(2)}) collective-permute-start(bf16[1024,128]{1,0:T(8,128)(2,1)S(1)} %copy-done.18), channel_id=1, source_target_pairs={{0,6},{1,7},{2,0},{3,1},{4,2},{5,3},{6,4},{7,5},{8,14},{9,15},{10,... | collective-permute-start | bytes 786440 | tf_op jit(solution)/shard_map/ppermute | solution.py:516
  189.9 5.5 %collective-permute-start.13 = (bf16[4,128,128]{2,1,0:T(8,128)(2,1)}, bf16[4,128,128]{2,1,0:T(8,128)(2,1)S(1)}, u32[]{:S(2)}, u32[]{:S(2)}) collective-permute-start(bf16[4,128,128]{2,1,0:T(8,128)(2,1)} %get-tuple-element.33), channel_id=1, source_target_pairs={{0,24},{8,0},{16,8},{24,16},{1,25},{9,1},{17,9},{25,17},{2,26},{10... | collective-permute-start | bytes 393224 | tf_op jit(solution)/shard_map/ppermute | solution.py:516
  191.6 18.7 %copy-start.4 = (bf16[4,128,128]{2,1,0:T(8,128)(2,1)}, bf16[4,128,128]{2,1,0:T(8,128)(2,1)S(1)}, u32[]{:S(2)}) copy-start(bf16[4,128,128]{2,1,0:T(8,128)(2,1)S(1)} %collective-permute-done.14.other_ref) | copy-start | bytes 393220
  195.4 20.8 %copy-start.5 = (bf16[4,128,128]{2,1,0:T(8,128)(2,1)}, bf16[4,128,128]{2,1,0:T(8,128)(2,1)S(1)}, u32[]{:S(2)}) copy-start(bf16[4,128,128]{2,1,0:T(8,128)(2,1)S(1)} %collective-permute-done.13.same_ref) | copy-start | bytes 393220
  195.4 14.9 %collective-permute-start.15 = (bf16[2,128,128]{2,1,0:T(8,128)(2,1)S(1)}, bf16[2,128,128]{2,1,0:T(8,128)(2,1)S(1)}, u32[]{:S(2)}, u32[]{:S(2)}) collective-permute-start(bf16[2,128,128]{2,1,0:T(8,128)(2,1)S(1)} %pad_maximum_fusion), channel_id=1, source_target_pairs={{0,2},{1,3},{2,4},{3,5},{4,6},{5,7},{6,0},{7,1},{8,10},{9,11},{10,... | collective-permute-start | bytes 196616 | tf_op jit(solution)/shard_map/ppermute | solution.py:516
  196.5 19.7 %collective-permute-start.16 = (bf16[2,128,128]{2,1,0:T(8,128)(2,1)S(1)}, bf16[2,128,128]{2,1,0:T(8,128)(2,1)S(1)}, u32[]{:S(2)}, u32[]{:S(2)}) collective-permute-start(bf16[2,128,128]{2,1,0:T(8,128)(2,1)S(1)} %pad_maximum_fusion.1), channel_id=1, source_target_pairs={{0,4},{1,5},{2,6},{3,7},{4,0},{5,1},{6,2},{7,3},{8,12},{9,13},{10,... | collective-permute-start | bytes 196616 | tf_op jit(solution)/shard_map/ppermute | solution.py:516
  197.8 9.1 %copy-start.11 = (bf16[1024,128]{1,0:T(8,128)(2,1)}, bf16[1024,128]{1,0:T(8,128)(2,1)S(1)}, u32[]{:S(2)}) copy-start(bf16[1024,128]{1,0:T(8,128)(2,1)S(1)} %collective-permute-done.4.refs_0_) | copy-start | bytes 786436
  197.8 18.4 %collective-permute-start.17 = (bf16[2,128,128]{2,1,0:T(8,128)(2,1)S(1)}, bf16[2,128,128]{2,1,0:T(8,128)(2,1)S(1)}, u32[]{:S(2)}, u32[]{:S(2)}) collective-permute-start(bf16[2,128,128]{2,1,0:T(8,128)(2,1)S(1)} %pad_maximum_fusion.2), channel_id=1, source_target_pairs={{0,6},{1,7},{2,0},{3,1},{4,2},{5,3},{6,4},{7,5},{8,14},{9,15},{10,... | collective-permute-start | bytes 196616 | tf_op jit(solution)/shard_map/ppermute | solution.py:516
  206.9 0.8 copy-start.13
  210.3 5.9 %copy-start.15 = (bf16[2,128,128]{2,1,0:T(8,128)(2,1)}, bf16[2,128,128]{2,1,0:T(8,128)(2,1)S(1)}, u32[]{:S(2)}) copy-start(bf16[2,128,128]{2,1,0:T(8,128)(2,1)S(1)} %collective-permute-done.15.refs_0_) | copy-start | bytes 196612
  (8 other events, 5.4 us)

commit v3 on v2

--- a/solution.py
+++ b/solution.py
@@ -13,7 +13,7 @@
 F32, BF16 = jnp.float32, jnp.bfloat16
 HIGHEST = lax.Precision.HIGHEST
 LANES = 128
-VMEM_LIMIT = 60 * 1024 * 1024
+VMEM_LIMIT = 40 * 1024 * 1024
 
 
 def nt(a, b):
@@ -259,10 +259,7 @@
 def own_kernel(
     steps, line, place_ref, core_ref, design_ref, mine_ref, theirs_ref, facts_ref, more_ref, *refs
 ):
-    (zscore_ref, *sends), (keep_ref, z_ref, half_ref, terms_ref, moreterms_ref) = (
-        refs[:line],
-        refs[line:],
-    )
+    (z_ref, *sends), (keep_ref, half_ref, terms_ref, moreterms_ref) = refs[:line], refs[line:]
     step = pl.program_id(0)
     blocks, kk, share = design_ref.shape
     chunk, probes = mine_ref.shape
@@ -279,7 +276,6 @@
         rows = pl.ds(pl.multiple_of(step * chunk, chunk), chunk)
 
         def store(base, at, width, value):
-            zscore_ref[:, base + at : base + at + width] = value
             z_ref[rows, base + at : base + at + width] = value
 
         standardise(design, mine_ref, terms_ref, facts_ref[kk : kk + 1, :], functools.partial(store, 0))
@@ -287,9 +283,9 @@
             design, theirs_ref, moreterms_ref, more_ref[kk : kk + 1, :], functools.partial(store, probes)
         )
         for b in range(blocks // 2):
-            here = pl.ds(pl.multiple_of((2 * b + core) * share, share), share)
+            here = pl.ds(pl.multiple_of(step * chunk + (2 * b + core) * share, share), share)
             slot = lax.rem(step * (blocks // 2) + b - place + line, line)
-            half_ref[pl.ds(pl.multiple_of(slot * share, share), share), :] = zscore_ref[here, :]
+            half_ref[pl.ds(pl.multiple_of(slot * share, share), share), :] = z_ref[here, :]
 
     @pl.when(step >= steps)
     def _():
@@ -323,16 +319,15 @@
                 whole,
                 whole,
             ],
-            out_specs=[pl.BlockSpec((chunk, 2 * probes), first)]
+            out_specs=[pl.BlockSpec(memory_space=pltpu.VMEM)]
             + [pl.BlockSpec((tall, share), second)] * line,
             scratch_shapes=[
-                pltpu.VMEM((rows, 2 * probes), BF16),
                 pltpu.VMEM((rows // 2, 2 * probes), BF16),
                 pltpu.VMEM((3 * K, probes), BF16),
                 pltpu.VMEM((3 * K, probes), BF16),
             ],
         ),
-        out_shape=[jax.ShapeDtypeStruct((rows, 2 * probes), BF16)]
+        out_shape=[pltpu.VMEM((rows, 2 * probes), BF16)]
         + [jax.ShapeDtypeStruct((rows, share), BF16)] * (line - 1)
         + [jax.ShapeDtypeStruct((rows, share), F32)],
         compiler_params=params("arbitrary"),
@@ -341,10 +336,11 @@
     )(*at, design, mine, theirs, facts, more)
 
 
-def pair_kernel(steps, line, last, place_ref, design_ref, raw_ref, facts_ref, zscore_ref, *refs):
+def pair_kernel(steps, line, last, tall, which, place_ref, design_ref, raw_ref, facts_ref, zscore_ref, *refs):
     refs, (z_ref, terms_ref) = refs[:-2], refs[-2:]
     step = pl.program_id(0)
     blocks, kk, share = design_ref.shape
+    probes = raw_ref.shape[1]
 
     @pl.when(step == 0)
     def _():
@@ -364,7 +360,9 @@
 
     @pl.when(step >= steps)
     def _():
-        part = nt(zscore_ref[...], z_ref[...])
+        rows = pl.ds(pl.multiple_of((step - steps) * tall, tall), tall)
+        cols = slice(which * probes, (which + 1) * probes)
+        part = nt(zscore_ref[rows, cols], z_ref[...])
         if last:
             put_tile(part + refs[0][...], refs[1:-1], refs[-1])
         else:
@@ -394,7 +392,7 @@
         out_specs = total
         out_shape = jax.ShapeDtypeStruct((rows, half), F32)
     return pl.pallas_call(
-        functools.partial(pair_kernel, steps, line, last),
+        functools.partial(pair_kernel, steps, line, last, tall, which),
         grid_spec=pltpu.PrefetchScalarGridSpec(
             num_scalar_prefetch=1,
             grid=(steps + rows // tall,),
@@ -402,7 +400,7 @@
                 pl.BlockSpec((chunk // share, K, share), lambda i, *_: (*first(i), 0)),
                 pl.BlockSpec((chunk, probes), first),
                 pl.BlockSpec((K + 8, probes), lambda i, *_: (0, 0)),
-                pl.BlockSpec((tall, probes), lambda i, *_: (second(i)[0], which)),
+                pl.BlockSpec(memory_space=pltpu.VMEM),
             ]
             + [total] * last,
             out_specs=out_specs,
@@ -543,11 +541,12 @@
     scores, copies = descend(parts)
     design = lax.all_to_all(copies, "probe", 0, 0)
     part = cross_products(design, methyl, panel)
-    bit = panels // 2
-    while bit > 1:
-        part = part + swap_panels(part, bit)
-        bit //= 2
     peer = swap_panels(part, 1)
+    bit = 2
+    while bit < panels:
+        part = part + peer
+        peer = swap_panels(part, bit)
+        bit *= 2
     half = lax.dynamic_index_in_dim(design.reshape(line, 2, K, share), core, 1, False)
     design_before = to_panel(half, 1)
     before_theirs = to_panel_sibling(other, 1)
@@ -565,7 +564,8 @@
     partial = pair_tile(at, line, design_before, before_mine, facts, zscore, 0, None)
     *sends, keep = pair_tile(at, line, design_before, before_theirs, more, zscore, 1, partial)
     left, same, other = fold(at, line, keep, arrivals(sends))
-    same, other = to_panel(same, -1), to_panel_sibling(other, -1)
+    same = to_panel(same, -1)
+    other = to_panel_sibling(other, -1)
     shifted = [on_line(jnp.stack([same[j], other[j]]), round_of(j)) for j in range(1, line)]
     tiles = scale(probes, own_keep, own_parts, left)
     return finish(at, line, probes, tiles, same, other, shifted), scores

time: 220 us -> 198 us (0.900)
  Pallas kernels: 59.7 us -> 37.5 us
  waiting for transfers between devices: 106 us -> 112 us
    pallas_call x2, Pallas kernels: 14.9 us -> 8.54 us  [pair_tile(): pl.pallas_call(functools.partial(pair_kernel, steps, line, last, tall, wh...]
    ppermute x18, waiting for transfers between devices: 98 us -> 104 us  [along(): return lax.ppermute(value, axis, pairs)]
    pallas_call x1, Pallas kernels: 14.6 us -> 10.7 us  [own_tile(): pl.pallas_call(functools.partial(own_kernel, steps, line), grid_spec=pltp...]
    pallas_call x1, Pallas kernels: 4.88 us -> 2.08 us  [cross_products(): pl.pallas_call(cross_kernel, grid=(rows // chunk,), in_specs=[pl.BlockSpe...]
    unnamed x42 -> x10, local copies, waits for them, and re-layouts: 6.39 us -> 4.52 us
  transfers between devices with their start and end apart: 19 -> 19, of which waited for: 9 -> 9; matrix products, arithmetic and copies ran while one was open for 2% -> 2% of each run, Pallas kernels for 22% -> 16%
where the time goes in v3:
time: 198 us
  waiting for transfers between devices  112 us (57%)
  Pallas kernels  37.5 us (19%)
  starting transfers between devices  31.9 us (16%)
  blocking collectives  8.28 us (4%)
  local copies, waits for them, and re-layouts  7.91 us (4%)
    ppermute x18, waiting for transfers between devices, along(): return lax.ppermute(value, axis, pairs)  104 us
    ppermute x18, starting transfers between devices, along(): return lax.ppermute(value, axis, pairs)  27 us
    pallas_call x1, Pallas kernels, own_tile(): pl.pallas_call(functools.partial(own_kernel, steps, line), grid_spec=pltp...  10.7 us
    pallas_call x2, Pallas kernels, pair_tile(): pl.pallas_call(functools.partial(pair_kernel, steps, line, last, tall, wh...  8.54 us
    all_to_all x1, blocking collectives, body(): design = lax.all_to_all(copies, 'probe', 0, 0)  8.28 us
    all_to_all x1, waiting for transfers between devices, body(): parts = lax.all_to_all(parts, 'probe', 0, 0)  8.11 us
    pallas_call x1, Pallas kernels, descend(): pl.pallas_call(descend_kernel, out_shape=(jax.ShapeDtypeStruct((K, share)...  6.61 us
    all_to_all x1, starting transfers between devices, body(): parts = lax.all_to_all(parts, 'probe', 0, 0)  4.88 us
  transfers between devices with their start and end apart: 19, of which 9 were waited for; matrix products, arithmetic and copies ran while one was open for 2% of the time, Pallas kernels for 16%

profile of v3, /device:TPU:0, one launch (start us, length us, event | category | flops | bytes accessed | tf_op | source)
XLA Modules:
  0.0 198.1 jit_solution(16438694555766449787)
XLA Ops:
  1.2 3.4 %constant_dynamic-slice_fusion = bf16[4,1,128,2048]{3,2,1,0:T(8,128)(2,1)} fusion(bf16[4,2,128,2048]{3,2,1,0:T(8,128)(2,1)} %bitcast.11, s32[]{:T(128)S(6)} %select_n.19), kind=kLoop, calls=%fused_computation.4 | loop fusion | bytes 4194308 | tf_op jit(solution)/shard_map/jit(dynamic_index_in_dim)/dynamic_slice | solution.py:536
  4.6 2.5 %collective-permute-start.9 = (bf16[512,2048]{1,0:T(8,128)(2,1)}, bf16[512,2048]{1,0:T(8,128)(2,1)S(1)}, u32[]{:S(2)}, u32[]{:S(2)}) collective-permute-start(bf16[512,2048]{1,0:T(8,128)(2,1)} %bitcast.5), channel_id=1, source_target_pairs={{0,8},{8,16},{16,24},{24,0},{1,9},{9,17},{17,25},{25,1},{2,10},{10... | collective-permute-start | bytes 6291464 | tf_op jit(solution)/shard_map/ppermute | solution.py:514
  8.0 3.5 %project.1 = (f32[8,64,128]{2,1,0:T(8,128)}, bf16[32,2048]{1,0:T(8,128)(2,1)S(1)}, bf16[512,2048]{1,0:T(8,128)(2,1)S(1)}) custom-call(s32[1]{0:T(128)} %bitcast.1.core_ref, s32[64]{0:T(128)S(1)} %copy-done.3, bf16[64,2048]{1,0:T(8,128)(2,1)S(1)} %copy-done.2, bf16[1024,2048]{1,0:T(8,128)(2,1)S(1)} %copy-done), custom_call_target="tpu_custom_call" | custom-call | flops 134217728 | bytes 8388608 | tf_op jit(solution)/shard_map/project/pallas_call | solution.py:76
  11.6 1.4 copy-done.4
  12.9 4.9 %all-to-all-start = ((f32[8,64,128]{2,1,0:T(8,128)}), f32[8,64,128]{2,1,0:T(8,128)S(1)}, u32[]{:S(2)}, u32[]{:S(2)}) async-start(f32[8,64,128]{2,1,0:T(8,128)} %get-tuple-element.19), calls=%async_computation | async-start | bytes 524288 | tf_op jit(solution)/shard_map/all_to_all | solution.py:540
  17.8 1.6 collective-permute-start.8
  19.4 8.1 %all-to-all-done.parts_ref = f32[8,64,128]{2,1,0:T(8,128)S(1)} async-done(((f32[8,64,128]{2,1,0:T(8,128)}), f32[8,64,128]{2,1,0:T(8,128)S(1)}, u32[]{:S(2)}, u32[]{:S(2)}) %all-to-all-start) | async-done | bytes 262176 | tf_op jit(solution)/shard_map/all_to_all | solution.py:540
  27.5 6.6 %descend.1 = (f32[32,128]{1,0:T(8,128)}, bf16[8,32,128]{2,1,0:T(8,128)(2,1)S(1)}) custom-call(f32[8,64,128]{2,1,0:T(8,128)S(1)} %all-to-all-done.parts_ref), custom_call_target="tpu_custom_call" | custom-call | flops 33554432 | bytes 16384 | tf_op jit(solution)/shard_map/descend/pallas_call | solution.py:140
  34.1 8.3 %all_to_all.10.design_ref = bf16[8,32,128]{2,1,0:T(8,128)(2,1)S(1)} all-to-all(bf16[8,32,128]{2,1,0:T(8,128)(2,1)S(1)} %get-tuple-element.20), channel_id=1, replica_groups=mesh['samp'=4,'probe'=8] {'probe'}, dimensions={0} | all-to-all | bytes 131072 | tf_op jit(solution)/shard_map/all_to_all | solution.py:542
  42.4 2.2 %copy-done.1 = bf16[1024,2048]{1,0:T(8,128)(2,1)S(1)} copy-done((bf16[1024,2048]{1,0:T(8,128)(2,1)S(1)}, bf16[1024,2048]{1,0:T(8,128)(2,1)}, u32[]{:S(2)}) %copy-start.1) | copy-done | bytes 4194328
  44.6 2.1 %cross.1 = f32[32,2304]{1,0:T(8,128)S(1)} custom-call(bf16[8,32,128]{2,1,0:T(8,128)(2,1)S(1)} %all_to_all.10.design_ref, bf16[1024,2048]{1,0:T(8,128)(2,1)S(1)} %copy-done.1, bf16[32,2048]{1,0:T(8,128)(2,1)S(1)} %get-tuple-element.21.panel_ref), custom_call_target="tpu_custom_call" | custom-call | flops 268435456 | bytes 4194304 | tf_op jit(solution)/shard_map/cross/pallas_call | solution.py:178
  46.7 1.6 collective-permute-start.1
  48.2 57.8 %collective-permute-done.1 = f32[32,2304]{1,0:T(8,128)S(1)} collective-permute-done((f32[32,2304]{1,0:T(8,128)S(1)}, f32[32,2304]{1,0:T(8,128)S(1)}, u32[]{:S(2)}, u32[]{:S(2)}) %collective-permute-start.1) | collective-permute-done | bytes 294944 | tf_op jit(solution)/shard_map/ppermute | solution.py:514
  106.4 8.2 %collective-permute-done.2.peer_ref = f32[32,2304]{1,0:T(8,128)S(1)} collective-permute-done((f32[32,2304]{1,0:T(8,128)S(1)}, f32[32,2304]{1,0:T(8,128)S(1)}, u32[]{:S(2)}, u32[]{:S(2)}) %collective-permute-start.2) | collective-permute-done | bytes 294944 | tf_op jit(solution)/shard_map/ppermute | solution.py:514
  114.6 3.8 %solve.1.facts_ref = f32[40,2048]{1,0:T(8,128)S(1)} custom-call(f32[32,2304]{1,0:T(8,128)S(1)} %add.15.mine_ref, f32[32,2304]{1,0:T(8,128)S(1)} %collective-permute-done.2.peer_ref, bf16[32,2048]{1,0:T(8,128)(2,1)S(1)} %get-tuple-element.21.panel_ref), custom_call_target="tpu_custom_call" | custom-call | flops 104857600 | bytes 1310720 | tf_op jit(solution)/shard_map/solve/pallas_call | solution.py:232
  120.1 10.7 %own.1 = (bf16[1024,4096]{1,0:T(8,128)(2,1)S(1)}, bf16[1024,128]{1,0:T(8,128)(2,1)S(1)}, bf16[1024,128]{1,0:T(8,128)(2,1)S(1)}, bf16[1024,128]{1,0:T(8,128)(2,1)S(1)}, f32[1024,128]{1,0:T(8,128)S(1)}) custom-call(s32[1]{0:T(128)} %bitcast.place_ref, s32[1]{0:T(128)} %bitcast.1.core_ref, bf16[8,32,128]{2,1,0:T(8,128)(2,1)S(1)} %all_to_all.10.design_ref, ...), custom_call_target="tpu_custom_call" | custom-call | flops 4294967296 | bytes 25165824 | tf_op jit(solution)/shard_map/own/pallas_call | solution.py:310
  130.8 3.6 %pair_first.1.refs_0_ = f32[1024,512]{1,0:T(8,128)S(1)} custom-call(s32[1]{0:T(128)} %bitcast.place_ref, bf16[4,32,128]{2,1,0:T(8,128)(2,1)S(1)} %collective-permute-done.7.design_ref, bf16[512,2048]{1,0:T(8,128)(2,1)S(1)} %collective-permute-done.9.raw_ref, f32[40,2048]{1,0:T(8,128)S(1)} %solve.1.facts_ref, bf16[1024,4096]{1,0:T(8,128)(2,1)S(1)} %get-tuple-element.27.zscore_ref), custom_call_target="tpu_custom_call" | custom-call | flops 2147483648 | bytes 16777216 | tf_op jit(solution)/shard_map/pair_first/pallas_call | solution.py:394
  134.5 4.9 %pair_last.1 = (bf16[1024,128]{1,0:T(8,128)(2,1)S(1)}, bf16[1024,128]{1,0:T(8,128)(2,1)S(1)}, bf16[1024,128]{1,0:T(8,128)(2,1)S(1)}, f32[1024,128]{1,0:T(8,128)S(1)}) custom-call(s32[1]{0:T(128)} %bitcast.place_ref, bf16[4,32,128]{2,1,0:T(8,128)(2,1)S(1)} %collective-permute-done.7.design_ref, bf16[512,2048]{1,0:T(8,128)(2,1)} %collective-permute-done.8.raw_ref, ...), custom_call_target="tpu_custom_call" | custom-call | flops 2147483648 | bytes 16777216 | tf_op jit(solution)/shard_map/pair_last/pallas_call | solution.py:394
  139.4 1.6 collective-permute-start.10
  141.0 2.6 %collective-permute-start.11 = (bf16[1024,128]{1,0:T(8,128)(2,1)S(1)}, bf16[1024,128]{1,0:T(8,128)(2,1)S(1)}, u32[]{:S(2)}, u32[]{:S(2)}) collective-permute-start(bf16[1024,128]{1,0:T(8,128)(2,1)S(1)} %get-tuple-element.30), channel_id=1, source_target_pairs={{0,4},{1,5},{2,6},{3,7},{4,0},{5,1},{6,2},{7,3},{8,12},{9,13},{10,... | collective-permute-start | bytes 786440 | tf_op jit(solution)/shard_map/ppermute | solution.py:514
  143.6 1.3 collective-permute-start.12
  145.0 5.6 %collective-permute-done.10.refs_0_ = bf16[1024,128]{1,0:T(8,128)(2,1)S(1)} collective-permute-done((bf16[1024,128]{1,0:T(8,128)(2,1)S(1)}, bf16[1024,128]{1,0:T(8,128)(2,1)S(1)}, u32[]{:S(2)}, u32[]{:S(2)}) %collective-permute-start.10) | collective-permute-done | bytes 262176 | tf_op jit(solution)/shard_map/ppermute | solution.py:514
  150.6 10.5 %collective-permute-done.11.refs_1_ = bf16[1024,128]{1,0:T(8,128)(2,1)S(1)} collective-permute-done((bf16[1024,128]{1,0:T(8,128)(2,1)S(1)}, bf16[1024,128]{1,0:T(8,128)(2,1)S(1)}, u32[]{:S(2)}, u32[]{:S(2)}) %collective-permute-start.11) | collective-permute-done | bytes 262176 | tf_op jit(solution)/shard_map/ppermute | solution.py:514
  161.2 1.1 collective-permute-start.14
  162.3 6.2 %collective-permute-start.4 = (bf16[1024,128]{1,0:T(8,128)(2,1)S(1)}, bf16[1024,128]{1,0:T(8,128)(2,1)S(1)}, u32[]{:S(2)}, u32[]{:S(2)}) collective-permute-start(bf16[1024,128]{1,0:T(8,128)(2,1)S(1)} %get-tuple-element.23), channel_id=1, source_target_pairs={{0,2},{1,3},{2,4},{3,5},{4,6},{5,7},{6,0},{7,1},{8,10},{9,11},{10,... | collective-permute-start | bytes 786440 | tf_op jit(solution)/shard_map/ppermute | solution.py:514
  169.3 1.5 collective-permute-start.6
  171.4 4.8 %collective-permute-done.13.same_ref = bf16[4,128,128]{2,1,0:T(8,128)(2,1)S(1)} collective-permute-done((bf16[4,128,128]{2,1,0:T(8,128)(2,1)S(1)}, bf16[4,128,128]{2,1,0:T(8,128)(2,1)S(1)}, u32[]{:S(2)}, u32[]{:S(2)}) %collective-permute-start.13) | collective-permute-done | bytes 131104 | tf_op jit(solution)/shard_map/ppermute | solution.py:514
  177.2 1.4 collective-permute-start.16
  178.6 1.6 collective-permute-start.17
  180.2 7.6 %collective-permute-done.5.refs_1_ = bf16[1024,128]{1,0:T(8,128)(2,1)S(1)} collective-permute-done((bf16[1024,128]{1,0:T(8,128)(2,1)S(1)}, bf16[1024,128]{1,0:T(8,128)(2,1)S(1)}, u32[]{:S(2)}, u32[]{:S(2)}) %collective-permute-start.5) | collective-permute-done | bytes 262176 | tf_op jit(solution)/shard_map/ppermute | solution.py:514
  187.9 1.1 scale.1._
  189.0 8.2 %collective-permute-done.16.refs_1_ = bf16[2,128,128]{2,1,0:T(8,128)(2,1)S(1)} collective-permute-done((bf16[2,128,128]{2,1,0:T(8,128)(2,1)S(1)}, bf16[2,128,128]{2,1,0:T(8,128)(2,1)S(1)}, u32[]{:S(2)}, u32[]{:S(2)}) %collective-permute-start.16) | collective-permute-done | bytes 65568 | tf_op jit(solution)/shard_map/ppermute | solution.py:514
  (35 shorter events, 7.2 us)
Async XLA Ops:
  0.6 119.5 %collective-permute-start = (bf16[1024,2048]{1,0:T(8,128)(2,1)}, bf16[1024,2048]{1,0:T(8,128)(2,1)}, u32[]{:S(2)}, u32[]{:S(2)}) collective-permute-start(bf16[1024,2048]{1,0:T(8,128)(2,1)} %mine_ref.1), channel_id=1, source_target_pairs={{0,1},{1,0},{2,3},{3,2},{4,5},{5,4},{6,7},{7,6},{8,9},{9,8},{10,11... | collective-permute-start | bytes 12582920 | tf_op jit(solution)/shard_map/ppermute | solution.py:514
  1.2 5.9 %copy-start = (bf16[1024,2048]{1,0:T(8,128)(2,1)S(1)}, bf16[1024,2048]{1,0:T(8,128)(2,1)}, u32[]{:S(2)}) copy-start(bf16[1024,2048]{1,0:T(8,128)(2,1)} %mine_ref.1) | copy-start | bytes 12582916
  1.2 5.9 %copy-start.3 = (s32[64]{0:T(128)S(1)}, s32[64]{0:T(128)}, u32[]{:S(2)}) copy-start(s32[64]{0:T(128)} %ids_ref.1) | copy-start | bytes 772
  4.6 126.3 %collective-permute-start.9 = (bf16[512,2048]{1,0:T(8,128)(2,1)}, bf16[512,2048]{1,0:T(8,128)(2,1)S(1)}, u32[]{:S(2)}, u32[]{:S(2)}) collective-permute-start(bf16[512,2048]{1,0:T(8,128)(2,1)} %bitcast.5), channel_id=1, source_target_pairs={{0,8},{8,16},{16,24},{24,0},{1,9},{9,17},{17,25},{25,1},{2,10},{10... | collective-permute-start | bytes 6291464 | tf_op jit(solution)/shard_map/ppermute | solution.py:514
  7.1 1.0 copy-start.2
  11.6 1.4 copy-start.4
  12.9 14.6 %all-to-all-start = ((f32[8,64,128]{2,1,0:T(8,128)}), f32[8,64,128]{2,1,0:T(8,128)S(1)}, u32[]{:S(2)}, u32[]{:S(2)}) async-start(f32[8,64,128]{2,1,0:T(8,128)} %get-tuple-element.19), calls=%async_computation | async-start | bytes 524288 | tf_op jit(solution)/shard_map/all_to_all | solution.py:540
  17.8 116.7 %collective-permute-start.8 = (bf16[512,2048]{1,0:T(8,128)(2,1)}, bf16[512,2048]{1,0:T(8,128)(2,1)}, u32[]{:S(2)}, u32[]{:S(2)}) collective-permute-start(bf16[512,2048]{1,0:T(8,128)(2,1)} %copy-done.4), channel_id=1, source_target_pairs={{0,9},{1,8},{2,11},{3,10},{4,13},{5,12},{6,15},{7,14},{8,17},{9,16... | collective-permute-start | bytes 6291464 | tf_op jit(solution)/shard_map/ppermute | solution.py:514
  42.4 2.2 %copy-start.1 = (bf16[1024,2048]{1,0:T(8,128)(2,1)S(1)}, bf16[1024,2048]{1,0:T(8,128)(2,1)}, u32[]{:S(2)}) copy-start(bf16[1024,2048]{1,0:T(8,128)(2,1)} %mine_ref.1) | copy-start | bytes 12582916
  46.7 59.3 %collective-permute-start.1 = (f32[32,2304]{1,0:T(8,128)S(1)}, f32[32,2304]{1,0:T(8,128)S(1)}, u32[]{:S(2)}, u32[]{:S(2)}) collective-permute-start(f32[32,2304]{1,0:T(8,128)S(1)} %cross.1), channel_id=1, source_target_pairs={{0,8},{8,0},{16,24},{24,16},{1,9},{9,1},{17,25},{25,17},{2,10},{10... | collective-permute-start | bytes 884744 | tf_op jit(solution)/shard_map/ppermute | solution.py:514
  106.0 8.6 %collective-permute-start.2 = (f32[32,2304]{1,0:T(8,128)S(1)}, f32[32,2304]{1,0:T(8,128)S(1)}, u32[]{:S(2)}, u32[]{:S(2)}) collective-permute-start(f32[32,2304]{1,0:T(8,128)S(1)} %add.15.mine_ref), channel_id=1, source_target_pairs={{0,16},{8,24},{16,0},{24,8},{1,17},{9,25},{17,1},{25,9},{2,18},{10... | collective-permute-start | bytes 884744 | tf_op jit(solution)/shard_map/ppermute | solution.py:514
  118.4 1.7 collective-permute-start.3
  118.6 12.3 %collective-permute-start.7 = (bf16[4,32,128]{2,1,0:T(8,128)(2,1)S(1)}, bf16[4,32,128]{2,1,0:T(8,128)(2,1)S(1)}, u32[]{:S(2)}, u32[]{:S(2)}) collective-permute-start(bf16[4,32,128]{2,1,0:T(8,128)(2,1)S(1)} %dynamic-slice_bitcast_fusion), channel_id=1, source_target_pairs={{0,8},{8,16},{16,24},{24,0},{1,9},{9,17},{17,25},{25,1},{2,10},{10... | collective-permute-start | bytes 98312 | tf_op jit(solution)/shard_map/ppermute | solution.py:514
  139.4 11.2 %collective-permute-start.10 = (bf16[1024,128]{1,0:T(8,128)(2,1)S(1)}, bf16[1024,128]{1,0:T(8,128)(2,1)S(1)}, u32[]{:S(2)}, u32[]{:S(2)}) collective-permute-start(bf16[1024,128]{1,0:T(8,128)(2,1)S(1)} %get-tuple-element.29), channel_id=1, source_target_pairs={{0,2},{1,3},{2,4},{3,5},{4,6},{5,7},{6,0},{7,1},{8,10},{9,11},{10,... | collective-permute-start | bytes 786440 | tf_op jit(solution)/shard_map/ppermute | solution.py:514
  141.0 20.0 %collective-permute-start.11 = (bf16[1024,128]{1,0:T(8,128)(2,1)S(1)}, bf16[1024,128]{1,0:T(8,128)(2,1)S(1)}, u32[]{:S(2)}, u32[]{:S(2)}) collective-permute-start(bf16[1024,128]{1,0:T(8,128)(2,1)S(1)} %get-tuple-element.30), channel_id=1, source_target_pairs={{0,4},{1,5},{2,6},{3,7},{4,0},{5,1},{6,2},{7,3},{8,12},{9,13},{10,... | collective-permute-start | bytes 786440 | tf_op jit(solution)/shard_map/ppermute | solution.py:514
  143.6 17.4 %collective-permute-start.12 = (bf16[1024,128]{1,0:T(8,128)(2,1)S(1)}, bf16[1024,128]{1,0:T(8,128)(2,1)S(1)}, u32[]{:S(2)}, u32[]{:S(2)}) collective-permute-start(bf16[1024,128]{1,0:T(8,128)(2,1)S(1)} %get-tuple-element.31), channel_id=1, source_target_pairs={{0,6},{1,7},{2,0},{3,1},{4,2},{5,3},{6,4},{7,5},{8,14},{9,15},{10,... | collective-permute-start | bytes 786440 | tf_op jit(solution)/shard_map/ppermute | solution.py:514
  161.2 10.1 %collective-permute-start.14 = (bf16[4,128,128]{2,1,0:T(8,128)(2,1)S(1)}, bf16[4,128,128]{2,1,0:T(8,128)(2,1)S(1)}, u32[]{:S(2)}, u32[]{:S(2)}) collective-permute-start(bf16[4,128,128]{2,1,0:T(8,128)(2,1)S(1)} %get-tuple-element.34), channel_id=1, source_target_pairs={{0,25},{1,24},{2,27},{3,26},{4,29},{5,28},{6,31},{7,30},{8,1},{9,0... | collective-permute-start | bytes 393224 | tf_op jit(solution)/shard_map/ppermute | solution.py:514
  162.3 16.3 %collective-permute-start.4 = (bf16[1024,128]{1,0:T(8,128)(2,1)S(1)}, bf16[1024,128]{1,0:T(8,128)(2,1)S(1)}, u32[]{:S(2)}, u32[]{:S(2)}) collective-permute-start(bf16[1024,128]{1,0:T(8,128)(2,1)S(1)} %get-tuple-element.23), channel_id=1, source_target_pairs={{0,2},{1,3},{2,4},{3,5},{4,6},{5,7},{6,0},{7,1},{8,10},{9,11},{10,... | collective-permute-start | bytes 786440 | tf_op jit(solution)/shard_map/ppermute | solution.py:514
  168.5 19.4 %collective-permute-start.5 = (bf16[1024,128]{1,0:T(8,128)(2,1)S(1)}, bf16[1024,128]{1,0:T(8,128)(2,1)S(1)}, u32[]{:S(2)}, u32[]{:S(2)}) collective-permute-start(bf16[1024,128]{1,0:T(8,128)(2,1)S(1)} %get-tuple-element.24), channel_id=1, source_target_pairs={{0,4},{1,5},{2,6},{3,7},{4,0},{5,1},{6,2},{7,3},{8,12},{9,13},{10,... | collective-permute-start | bytes 786440 | tf_op jit(solution)/shard_map/ppermute | solution.py:514
  169.3 18.5 %collective-permute-start.6 = (bf16[1024,128]{1,0:T(8,128)(2,1)S(1)}, bf16[1024,128]{1,0:T(8,128)(2,1)S(1)}, u32[]{:S(2)}, u32[]{:S(2)}) collective-permute-start(bf16[1024,128]{1,0:T(8,128)(2,1)S(1)} %get-tuple-element.25), channel_id=1, source_target_pairs={{0,6},{1,7},{2,0},{3,1},{4,2},{5,3},{6,4},{7,5},{8,14},{9,15},{10,... | collective-permute-start | bytes 786440 | tf_op jit(solution)/shard_map/ppermute | solution.py:514
  170.8 5.3 %collective-permute-start.13 = (bf16[4,128,128]{2,1,0:T(8,128)(2,1)S(1)}, bf16[4,128,128]{2,1,0:T(8,128)(2,1)S(1)}, u32[]{:S(2)}, u32[]{:S(2)}) collective-permute-start(bf16[4,128,128]{2,1,0:T(8,128)(2,1)S(1)} %get-tuple-element.33), channel_id=1, source_target_pairs={{0,24},{8,0},{16,8},{24,16},{1,25},{9,1},{17,9},{25,17},{2,26},{10... | collective-permute-start | bytes 393224 | tf_op jit(solution)/shard_map/ppermute | solution.py:514
  176.2 12.8 %collective-permute-start.15 = (bf16[2,128,128]{2,1,0:T(8,128)(2,1)S(1)}, bf16[2,128,128]{2,1,0:T(8,128)(2,1)S(1)}, u32[]{:S(2)}, u32[]{:S(2)}) collective-permute-start(bf16[2,128,128]{2,1,0:T(8,128)(2,1)S(1)} %pad_maximum_fusion), channel_id=1, source_target_pairs={{0,2},{1,3},{2,4},{3,5},{4,6},{5,7},{6,0},{7,1},{8,10},{9,11},{10,... | collective-permute-start | bytes 196616 | tf_op jit(solution)/shard_map/ppermute | solution.py:514
  177.2 19.9 %collective-permute-start.16 = (bf16[2,128,128]{2,1,0:T(8,128)(2,1)S(1)}, bf16[2,128,128]{2,1,0:T(8,128)(2,1)S(1)}, u32[]{:S(2)}, u32[]{:S(2)}) collective-permute-start(bf16[2,128,128]{2,1,0:T(8,128)(2,1)S(1)} %pad_maximum_fusion.1), channel_id=1, source_target_pairs={{0,4},{1,5},{2,6},{3,7},{4,0},{5,1},{6,2},{7,3},{8,12},{9,13},{10,... | collective-permute-start | bytes 196616 | tf_op jit(solution)/shard_map/ppermute | solution.py:514
  178.6 18.5 %collective-permute-start.17 = (bf16[2,128,128]{2,1,0:T(8,128)(2,1)S(1)}, bf16[2,128,128]{2,1,0:T(8,128)(2,1)S(1)}, u32[]{:S(2)}, u32[]{:S(2)}) collective-permute-start(bf16[2,128,128]{2,1,0:T(8,128)(2,1)S(1)} %pad_maximum_fusion.2), channel_id=1, source_target_pairs={{0,6},{1,7},{2,0},{3,1},{4,2},{5,3},{6,4},{7,5},{8,14},{9,15},{10,... | collective-permute-start | bytes 196616 | tf_op jit(solution)/shard_map/ppermute | solution.py:514

commit v4 on v3

--- a/solution.py
+++ b/solution.py
@@ -40,7 +40,10 @@
     return jnp.concatenate([high, mid, low], axis=0)
 
 
-def project_kernel(core_ref, ids_ref, atlas_ref, methyl_ref, out_ref, panel_ref, other_ref, gram_ref):
+def project_kernel(
+    quarter, core_ref, ids_ref, atlas_ref, methyl_ref, out_ref, panel_ref, low_ref, high_ref, same_ref,
+    other_ref, gram_ref,
+):
     kk = panel_ref.shape[0]
     blocks, _, share = out_ref.shape
     core = core_ref[0]
@@ -63,19 +66,44 @@
         out_ref[b, :kk, :] = proj[:, b * share : (b + 1) * share]
         out_ref[b, kk:, :] = jnp.zeros((kk, share), F32)
         out_ref[b, kk:, :kk] = gram_ref[...]
-    for b in range(blocks // 2):
-        other = pl.multiple_of((2 * b + 1 - core) * share, share)
-        other_ref[b * share : (b + 1) * share, :] = methyl_ref[pl.ds(other, share), :]
+
+    def put(ref, side):
+        for b in range(blocks // 2):
+            start = pl.multiple_of((2 * b + side) * share, share)
+            ref[b * share : (b + 1) * share, :] = methyl_ref[pl.ds(start, share), :]
+
+    step, steps = pl.program_id(0), pl.num_programs(0)
+
+    @pl.when(step < quarter)
+    def _():
+        put(low_ref, 1 - core)
+
+    @pl.when(step >= steps - quarter)
+    def _():
+        put(high_ref, 1 - core)
+
+    @pl.when((step >= quarter) & (step < steps - quarter))
+    def _():
+        put(same_ref, core)
+        put(other_ref, 1 - core)
 
 
 def project(core, panel_ids, atlas, methyl, shares):
     rows, probes = methyl.shape
     share = rows // shares
     chunk = row_chunk(share)
-    half = pl.BlockSpec((chunk // 2, probes), lambda i: (i, 0))
-    return pl.pallas_call(
-        project_kernel,
-        grid=(rows // chunk,),
+    steps = rows // chunk
+    quarter = steps // 4
+
+    def half(first, count):
+        return pl.BlockSpec((chunk // 2, probes), lambda i: (jnp.clip(i - first, 0, count - 1), 0))
+
+    def rows_of(count):
+        return jax.ShapeDtypeStruct((count * chunk // 2, probes), BF16)
+
+    return pl.pallas_call(
+        functools.partial(project_kernel, quarter),
+        grid=(steps,),
         in_specs=[
             pl.BlockSpec(memory_space=pltpu.SMEM),
             pl.BlockSpec(memory_space=pltpu.SMEM),
@@ -85,12 +113,18 @@
         out_specs=(
             pl.BlockSpec((chunk // share, 2 * K, share), lambda i: (i, 0, 0)),
             pl.BlockSpec((K, probes), lambda i: (0, 0)),
-            half,
+            half(0, quarter),
+            half(steps - quarter, quarter),
+            half(quarter, steps - 2 * quarter),
+            half(quarter, steps - 2 * quarter),
         ),
         out_shape=(
             jax.ShapeDtypeStruct((shares, 2 * K, share), F32),
             jax.ShapeDtypeStruct((K, probes), BF16),
-            jax.ShapeDtypeStruct((rows // 2, probes), BF16),
+            rows_of(quarter),
+            rows_of(quarter),
+            rows_of(steps - 2 * quarter),
+            rows_of(steps - 2 * quarter),
         ),
         scratch_shapes=[pltpu.VMEM((K, K), F32)],
         compiler_params=params("arbitrary"),
@@ -336,85 +370,76 @@
     )(*at, design, mine, theirs, facts, more)
 
 
-def pair_kernel(steps, line, last, tall, which, place_ref, design_ref, raw_ref, facts_ref, zscore_ref, *refs):
-    refs, (z_ref, terms_ref) = refs[:-2], refs[-2:]
-    step = pl.program_id(0)
+def pair_kernel(index_of, line, count, place_ref, design_ref, facts_ref, more_ref, zscore_ref, *refs):
+    mine, theirs, refs = refs[: count[0]], refs[count[0] : sum(count)], refs[sum(count) :]
+    (*sends, keep_ref), (z_ref, terms_ref, moreterms_ref) = refs[:-3], refs[-3:]
     blocks, kk, share = design_ref.shape
-    probes = raw_ref.shape[1]
+    probes = facts_ref.shape[1]
+    tall = keep_ref.shape[0]
+    step, place = pl.program_id(0), place_ref[0]
 
     @pl.when(step == 0)
     def _():
         terms_ref[...] = three_terms(facts_ref[:kk, :])
-
-    @pl.when(step < steps)
-    def _():
+        moreterms_ref[...] = three_terms(more_ref[:kk, :])
         design = jnp.concatenate([design_ref[b] for b in range(blocks)], axis=1)
-
-        def store(at, width, value):
-            for b in range(blocks):
-                slot = lax.rem(step * blocks + b - place_ref[0] + line, line)
-                rows = pl.ds(pl.multiple_of(slot * share, share), share)
-                z_ref[rows, at : at + width] = value[b * share : (b + 1) * share, :]
-
-        standardise(design, raw_ref, terms_ref, facts_ref[kk : kk + 1, :], store)
-
-    @pl.when(step >= steps)
-    def _():
-        rows = pl.ds(pl.multiple_of((step - steps) * tall, tall), tall)
-        cols = slice(which * probes, (which + 1) * probes)
-        part = nt(zscore_ref[rows, cols], z_ref[...])
-        if last:
-            put_tile(part + refs[0][...], refs[1:-1], refs[-1])
-        else:
-            refs[0][...] = part
-
-
-def pair_tile(at, line, design, raw, facts, zscore, which, partial):
-    _, _, share = design.shape
-    half, probes = raw.shape
-    rows = zscore.shape[0]
-    chunk = row_chunk(share)
-    steps, tall = half // chunk, 2 * chunk
-    last = partial is not None
-
-    def first(i, *_):
-        return (jnp.minimum(i, steps - 1), 0)
-
-    def second(i, *_):
-        return (jnp.maximum(i - steps, 0), 0)
-
-    total = pl.BlockSpec((tall, half), second)
-    if last:
-        out_specs = [pl.BlockSpec((tall, share), second)] * line
-        out_shape = [jax.ShapeDtypeStruct((rows, share), BF16)] * (line - 1)
-        out_shape += [jax.ShapeDtypeStruct((rows, share), F32)]
-    else:
-        out_specs = total
-        out_shape = jax.ShapeDtypeStruct((rows, half), F32)
-    return pl.pallas_call(
-        functools.partial(pair_kernel, steps, line, last, tall, which),
+        for base, pieces, facts, terms in (
+            (0, mine, facts_ref, terms_ref),
+            (probes, theirs, more_ref, moreterms_ref),
+        ):
+            top = 0
+            for piece in pieces:
+                rows = slice(top, top + piece.shape[0])
+
+                def store(at, width, value):
+                    z_ref[rows, base + at : base + at + width] = value
+
+                standardise(design[:, rows], piece, terms, facts[kk : kk + 1, :], store)
+                top += piece.shape[0]
+
+    @pl.when(step > 0)
+    def _():
+        rows = pl.ds(pl.multiple_of((step - 1) * tall, tall), tall)
+        part = nt(zscore_ref[rows, :], z_ref[...])
+        for j, ref in enumerate([keep_ref, *sends]):
+            index, inside = index_of(lax.rem(place + j, line))
+            block = part[:, :share]
+            for b in range(1, blocks):
+                block = jnp.where(index == b, part[:, b * share : (b + 1) * share], block)
+            if j == 0:
+                block = jnp.where(inside, block, 0.0)
+            ref[...] = block.astype(ref.dtype)
+
+
+def pair_tile(index_of, at, line, design, mine, theirs, facts, more, zscore):
+    blocks, _, share = design.shape
+    rows, depth = zscore.shape
+    probes = depth // 2
+    tall = 2 * row_chunk(share)
+    vmem = pl.BlockSpec(memory_space=pltpu.VMEM)
+    column = pl.BlockSpec((tall, share), lambda i, *_: (jnp.maximum(i - 1, 0), 0))
+    return pl.pallas_call(
+        functools.partial(pair_kernel, index_of, line, (len(mine), len(theirs))),
         grid_spec=pltpu.PrefetchScalarGridSpec(
             num_scalar_prefetch=1,
-            grid=(steps + rows // tall,),
-            in_specs=[
-                pl.BlockSpec((chunk // share, K, share), lambda i, *_: (*first(i), 0)),
-                pl.BlockSpec((chunk, probes), first),
-                pl.BlockSpec((K + 8, probes), lambda i, *_: (0, 0)),
-                pl.BlockSpec(memory_space=pltpu.VMEM),
-            ]
-            + [total] * last,
-            out_specs=out_specs,
-            scratch_shapes=[pltpu.VMEM((half, probes), BF16), pltpu.VMEM((3 * K, probes), BF16)],
+            grid=(1 + rows // tall,),
+            in_specs=[vmem] * (4 + len(mine) + len(theirs)),
+            out_specs=[column] * line,
+            scratch_shapes=[
+                pltpu.VMEM((blocks * share, depth), BF16),
+                pltpu.VMEM((3 * K, probes), BF16),
+                pltpu.VMEM((3 * K, probes), BF16),
+            ],
         ),
-        out_shape=out_shape,
+        out_shape=[jax.ShapeDtypeStruct((rows, share), BF16)] * (line - 1)
+        + [jax.ShapeDtypeStruct((rows, share), F32)],
         compiler_params=params("arbitrary"),
-        cost_estimate=cost(rows * rows * probes, 8 * rows * probes),
-        name="pair_last" if last else "pair_first",
-    )(at[0], design, raw, facts, zscore, *([partial] * last))
-
-
-def fold_kernel(line, place_ref, core_ref, keep_ref, *refs):
-    parts, (total_ref, same_ref, other_ref) = refs[:-3], refs[-3:]
+        cost_estimate=cost(2 * rows * blocks * share * depth, 8 * rows * probes),
+    )(at[0], design, facts, more, zscore, *mine, *theirs)
+
+
+def fold_kernel(line, place_ref, core_ref, *refs):
+    (keep_ref, *parts), (total_ref, same_ref, other_ref) = refs[:-3], refs[-3:]
     place, core = place_ref[0], core_ref[0]
     share = same_ref.shape[1]
     total = keep_ref[...]
@@ -429,18 +454,18 @@
         other_ref[j] = total_ref[other, :].astype(BF16)
 
 
-def fold(at, line, keep, parts):
-    rows, share = keep.shape
+def fold(at, line, parts):
+    rows, share = parts[0].shape
     blocks = jax.ShapeDtypeStruct((line, share, share), BF16)
     vmem = pl.BlockSpec(memory_space=pltpu.VMEM)
     return pl.pallas_call(
         functools.partial(fold_kernel, line),
-        in_specs=[pl.BlockSpec(memory_space=pltpu.SMEM)] * 2 + [vmem] * (1 + len(parts)),
+        in_specs=[pl.BlockSpec(memory_space=pltpu.SMEM)] * 2 + [vmem] * len(parts),
         out_shape=(jax.ShapeDtypeStruct((rows, share), F32), blocks, blocks),
         compiler_params=params(),
         cost_estimate=cost(rows * share * 8, rows * share * 16),
         name="fold",
-    )(*at, keep, *parts)
+    )(*at, *parts)
 
 
 def scale_kernel(probes, own_ref, *refs):
@@ -533,10 +558,28 @@
     def on_line(value, pairs):
         return along(value, "probe", [(2 * i + c, 2 * to + c) for i, to in pairs for c in (0, 1)])
 
-    same = lax.dynamic_index_in_dim(methyl.reshape(line, 2, share, -1), core, 1, False)
-    before_mine = to_panel(same.reshape(line * share, -1), 1)
+    quarter = line // 4
+    ends = [*range(quarter), *range(line - quarter, line)]
+    inner = [*range(quarter, line - quarter)]
+
+    def among_ends(to):
+        high = to >= line - quarter
+        return jnp.where(high, to - (line - 2 * quarter), to), (to < quarter) | high
+
+    def among_inner(to):
+        return to - quarter, (to >= quarter) & (to < line - quarter)
+
+    halves = methyl.reshape(line, 2, share, -1)
+    first = jnp.concatenate(
+        [
+            lax.dynamic_index_in_dim(halves[:quarter], core, 1, False),
+            lax.dynamic_index_in_dim(halves[line - quarter :], core, 1, False),
+        ]
+    )
+    ends_mine = to_panel(first.reshape(len(ends) * share, -1), 1)
     theirs = to_sibling(methyl)
-    parts, panel, other = project(core[None], panel_ids, atlas, methyl, shares)
+    parts, panel, low, high, same, other = project(core[None], panel_ids, atlas, methyl, shares)
+    ends_low = to_panel_sibling(low, 1)
     parts = lax.all_to_all(parts, "probe", 0, 0)
     scores, copies = descend(parts)
     design = lax.all_to_all(copies, "probe", 0, 0)
@@ -549,21 +592,33 @@
         bit *= 2
     half = lax.dynamic_index_in_dim(design.reshape(line, 2, K, share), core, 1, False)
     design_before = to_panel(half, 1)
-    before_theirs = to_panel_sibling(other, 1)
+    ends_high = to_panel_sibling(high, 1)
+    inner_mine = to_panel(same, 1)
+    inner_theirs = to_panel_sibling(other, 1)
     facts = solve(part, peer, panel, 0.0001 * samples, samples)
     more = to_sibling(facts)
 
-    def round_of(by):
-        return [(i, (i + by) % line) for i in range(line)]
-
-    def arrivals(sends):
-        return [on_line(value, round_of(j)) for j, value in enumerate(sends, 1)]
+    def round_of(by, among=None):
+        pairs = [(i, (i + by) % line) for i in range(line)]
+        return pairs if among is None else [(i, to) for i, to in pairs if to in among]
+
+    def arrivals(sends, among=None):
+        return [on_line(value, round_of(j, among)) for j, value in enumerate(sends, 1)]
 
     zscore, *sends, own_keep = own_tile(at, line, design, methyl, theirs, facts, more)
     own_parts = arrivals(sends)
-    partial = pair_tile(at, line, design_before, before_mine, facts, zscore, 0, None)
-    *sends, keep = pair_tile(at, line, design_before, before_theirs, more, zscore, 1, partial)
-    left, same, other = fold(at, line, keep, arrivals(sends))
+    design_ends = jnp.concatenate([design_before[:quarter], design_before[line - quarter :]])
+    *sends, keep = pair_tile(
+        among_ends, at, line, design_ends, [ends_mine], [ends_low, ends_high],
+        facts, more, zscore,
+    )
+    pair_parts = [keep] + arrivals(sends, ends)
+    *sends, keep = pair_tile(
+        among_inner, at, line, design_before[quarter : line - quarter],
+        [inner_mine], [inner_theirs], facts, more, zscore,
+    )
+    pair_parts += [keep] + arrivals(sends, inner)
+    left, same, other = fold(at, line, pair_parts)
     same = to_panel(same, -1)
     other = to_panel_sibling(other, -1)
     shifted = [on_line(jnp.stack([same[j], other[j]]), round_of(j)) for j in range(1, line)]

time: 198 us -> 208 us (1.051)
  blocking collectives: 8.28 us -> 15.5 us
  waiting for transfers between devices: 112 us -> 106 us
  starting transfers between devices: 31.9 us -> 36.8 us
    all_to_all x1, blocking collectives: 8.28 us -> 15.5 us  [body(): parts = lax.all_to_all(parts, 'probe', 0, 0)]
    ppermute x18 -> x24, starting transfers between devices: 27 us -> 33.4 us  [along(): return lax.ppermute(value, axis, pairs)]
    all_to_all x1, waiting for transfers between devices: 8.11 us -> 3.14 us  [body(): design = lax.all_to_all(copies, 'probe', 0, 0)]
    dynamic_slice x1 -> x0, local copies, waits for them, and re-layouts: 3.36 us -> none  [body(): lax.dynamic_index_in_dim(methyl.reshape(line, 2, share, -1), core, 1, False)]
    unnamed x10 -> x12, local copies, waits for them, and re-layouts: 4.52 us -> 7 us
    ppermute x18 -> x24, waiting for transfers between devices: 104 us -> 103 us  [along(): return lax.ppermute(value, axis, pairs)]
  transfers between devices with their start and end apart: 19 -> 25, of which waited for: 9 -> 13; matrix products, arithmetic and copies ran while one was open for 2% -> 2% of each run, Pallas kernels for 16% -> 17%
where the time goes in v4:
time: 208 us
  waiting for transfers between devices  106 us (51%)
  Pallas kernels  37.6 us (18%)
  starting transfers between devices  36.8 us (18%)
  blocking collectives  15.5 us (7%)
  local copies, waits for them, and re-layouts  9.9 us (5%)
    ppermute x24, waiting for transfers between devices, along(): return lax.ppermute(value, axis, pairs)  103 us
    ppermute x24, starting transfers between devices, along(): return lax.ppermute(value, axis, pairs)  33.4 us
    all_to_all x1, blocking collectives, body(): parts = lax.all_to_all(parts, 'probe', 0, 0)  15.5 us
    pallas_call x1, Pallas kernels, own_tile(): pl.pallas_call(functools.partial(own_kernel, steps, line), grid_spec=pltp...  10.7 us
    pallas_call x2, Pallas kernels, pair_tile(): pl.pallas_call(functools.partial(pair_kernel, index_of, line, (len(mine),...  8.02 us
    unnamed x12, local copies, waits for them, and re-layouts  7 us
    pallas_call x1, Pallas kernels, descend(): pl.pallas_call(descend_kernel, out_shape=(jax.ShapeDtypeStruct((K, share)...  6.63 us
  transfers between devices with their start and end apart: 25, of which 13 were waited for; matrix products, arithmetic and copies ran while one was open for 2% of the time, Pallas kernels for 17%

profile of v4, /device:TPU:0, one launch (start us, length us, event | category | flops | bytes accessed | tf_op | source)
XLA Modules:
  0.0 207.7 jit_solution(17183881182694393518)
XLA Ops:
  1.2 2.2 %copy-done = bf16[1024,2048]{1,0:T(8,128)(2,1)S(1)} copy-done((bf16[1024,2048]{1,0:T(8,128)(2,1)S(1)}, bf16[1024,2048]{1,0:T(8,128)(2,1)}, u32[]{:S(2)}) %copy-start) | copy-done | bytes 4194328
  5.0 4.0 %project.1 = (f32[8,64,128]{2,1,0:T(8,128)S(1)}, bf16[32,2048]{1,0:T(8,128)(2,1)S(1)}, bf16[128,2048]{1,0:T(8,128)(2,1)S(1)}, bf16[128,2048]{1,0:T(8,128)(2,1)S(...) custom-call(s32[1]{0:T(128)} %bitcast.1.core_ref, s32[64]{0:T(128)S(1)} %copy-done.3, ...), custom_call_target="tpu_custom_call" | custom-call | flops 134217728 | bytes 8388608 | tf_op jit(solution)/shard_map/project/pallas_call | solution.py:104
  10.0 15.5 %all_to_all.10.parts_ref = f32[8,64,128]{2,1,0:T(8,128)S(1)} all-to-all(f32[8,64,128]{2,1,0:T(8,128)S(1)} %get-tuple-element.26), channel_id=1, replica_groups=mesh['samp'=4,'probe'=8] {'probe'}, dimensions={0} | all-to-all | bytes 524288 | tf_op jit(solution)/shard_map/all_to_all | solution.py:583
  25.4 6.6 %descend.1 = (f32[32,128]{1,0:T(8,128)}, bf16[8,32,128]{2,1,0:T(8,128)(2,1)}) custom-call(f32[8,64,128]{2,1,0:T(8,128)S(1)} %all_to_all.10.parts_ref), custom_call_target="tpu_custom_call" | custom-call | flops 33554432 | bytes 16384 | tf_op jit(solution)/shard_map/descend/pallas_call | solution.py:174
  32.1 3.3 %all-to-all-start.1 = ((bf16[8,32,128]{2,1,0:T(8,128)(2,1)}), bf16[8,32,128]{2,1,0:T(8,128)(2,1)S(1)}, u32[]{:S(2)}, u32[]{:S(2)}) async-start(bf16[8,32,128]{2,1,0:T(8,128)(2,1)} %get-tuple-element.27), calls=%async_computation.1 | async-start | bytes 131072 | tf_op jit(solution)/shard_map/all_to_all | solution.py:585
  38.1 3.1 %all-to-all-done.1.design_ref = bf16[8,32,128]{2,1,0:T(8,128)(2,1)S(1)} async-done(((bf16[8,32,128]{2,1,0:T(8,128)(2,1)}), bf16[8,32,128]{2,1,0:T(8,128)(2,1)S(1)}, u32[]{:S(2)}, u32[]{:S(2)}) %all-to-all-start.1) | async-done | bytes 65568 | tf_op jit(solution)/shard_map/all_to_all | solution.py:585
  41.3 2.2 %copy-done.1 = bf16[1024,2048]{1,0:T(8,128)(2,1)S(1)} copy-done((bf16[1024,2048]{1,0:T(8,128)(2,1)S(1)}, bf16[1024,2048]{1,0:T(8,128)(2,1)}, u32[]{:S(2)}) %copy-start.1) | copy-done | bytes 4194328
  43.5 2.1 %cross.1 = f32[32,2304]{1,0:T(8,128)S(1)} custom-call(bf16[8,32,128]{2,1,0:T(8,128)(2,1)S(1)} %all-to-all-done.1.design_ref, bf16[1024,2048]{1,0:T(8,128)(2,1)S(1)} %copy-done.1, bf16[32,2048]{1,0:T(8,128)(2,1)S(1)} %get-tuple-element.28.panel_ref), custom_call_target="tpu_custom_call" | custom-call | flops 268435456 | bytes 4194304 | tf_op jit(solution)/shard_map/cross/pallas_call | solution.py:212
  45.6 1.6 collective-permute-start.1
  47.1 1.6 fusion
  50.0 40.9 %collective-permute-done.1 = f32[32,2304]{1,0:T(8,128)S(1)} collective-permute-done((f32[32,2304]{1,0:T(8,128)S(1)}, f32[32,2304]{1,0:T(8,128)S(1)}, u32[]{:S(2)}, u32[]{:S(2)}) %collective-permute-start.1) | collective-permute-done | bytes 294944 | tf_op jit(solution)/shard_map/ppermute | solution.py:539
  94.1 6.0 %collective-permute-done.2.peer_ref = f32[32,2304]{1,0:T(8,128)S(1)} collective-permute-done((f32[32,2304]{1,0:T(8,128)S(1)}, f32[32,2304]{1,0:T(8,128)S(1)}, u32[]{:S(2)}, u32[]{:S(2)}) %collective-permute-start.2) | collective-permute-done | bytes 294944 | tf_op jit(solution)/shard_map/ppermute | solution.py:539
  100.1 3.8 %solve.1.facts_ref = f32[40,2048]{1,0:T(8,128)S(1)} custom-call(f32[32,2304]{1,0:T(8,128)S(1)} %add.16.mine_ref, f32[32,2304]{1,0:T(8,128)S(1)} %collective-permute-done.2.peer_ref, bf16[32,2048]{1,0:T(8,128)(2,1)S(1)} %get-tuple-element.28.panel_ref), custom_call_target="tpu_custom_call" | custom-call | flops 104857600 | bytes 1310720 | tf_op jit(solution)/shard_map/solve/pallas_call | solution.py:266
  104.0 1.6 collective-permute-done.3.more_ref
  105.6 1.7 collective-permute-start.10
  108.1 10.7 %own.1 = (bf16[1024,4096]{1,0:T(8,128)(2,1)S(1)}, bf16[1024,128]{1,0:T(8,128)(2,1)S(1)}, bf16[1024,128]{1,0:T(8,128)(2,1)S(1)}, bf16[1024,128]{1,0:T(8,128)(2,1)S(1)}, f32[1024,128]{1,0:T(8,128)S(1)}) custom-call(s32[1]{0:T(128)} %bitcast.place_ref, s32[1]{0:T(128)} %bitcast.1.core_ref, bf16[8,32,128]{2,1,0:T(8,128)(2,1)S(1)} %all-to-all-done.1.design_ref, ...), custom_call_target="tpu_custom_call" | custom-call | flops 4294967296 | bytes 25165824 | tf_op jit(solution)/shard_map/own/pallas_call | solution.py:344
  118.8 3.4 %shard_map.51 = (bf16[1024,128]{1,0:T(8,128)(2,1)S(1)}, bf16[1024,128]{1,0:T(8,128)(2,1)S(1)}, bf16[1024,128]{1,0:T(8,128)(2,1)S(1)}, f32[1024,128]{1,0:T(8,128)S(1)}) custom-call(s32[1]{0:T(128)} %bitcast.place_ref, bf16[2,32,128]{2,1,0:T(8,128)(2,1)S(1)} %slice.54.design_ref, f32[40,2048]{1,0:T(8,128)S(1)} %solve.1.facts_ref, ...), custom_call_target="tpu_custom_call" | custom-call | flops 2147483648 | bytes 16777216 | tf_op jit(solution)/shard_map/pallas_call | solution.py:421
  122.2 3.3 %collective-permute-start.16 = (bf16[1024,128]{1,0:T(8,128)(2,1)S(1)}, bf16[1024,128]{1,0:T(8,128)(2,1)S(1)}, u32[]{:S(2)}, u32[]{:S(2)}) collective-permute-start(bf16[1024,128]{1,0:T(8,128)(2,1)S(1)} %get-tuple-element.43), channel_id=1, source_target_pairs={{0,2},{1,3},{2,4},{3,5},{8,10},{9,11},{10,12},{11,13},{16,18},{17,... | collective-permute-start | bytes 786440 | tf_op jit(solution)/shard_map/ppermute | solution.py:539
  125.6 2.2 %collective-permute-start.17 = (bf16[1024,128]{1,0:T(8,128)(2,1)S(1)}, bf16[1024,128]{1,0:T(8,128)(2,1)S(1)}, u32[]{:S(2)}, u32[]{:S(2)}) collective-permute-start(bf16[1024,128]{1,0:T(8,128)(2,1)S(1)} %get-tuple-element.44), channel_id=1, source_target_pairs={{0,4},{1,5},{6,2},{7,3},{8,12},{9,13},{14,10},{15,11},{16,20},{17,... | collective-permute-start | bytes 786440 | tf_op jit(solution)/shard_map/ppermute | solution.py:539
  127.8 7.4 %collective-permute-done.10.refs_2_ = bf16[128,2048]{1,0:T(8,128)(2,1)S(1)} collective-permute-done((bf16[128,2048]{1,0:T(8,128)(2,1)}, bf16[128,2048]{1,0:T(8,128)(2,1)S(1)}, u32[]{:S(2)}, u32[]{:S(2)}) %collective-permute-start.10) | collective-permute-done | bytes 524320 | tf_op jit(solution)/shard_map/ppermute | solution.py:539
  135.8 9.7 %collective-permute-done.9.refs_1_ = bf16[128,2048]{1,0:T(8,128)(2,1)S(1)} collective-permute-done((bf16[128,2048]{1,0:T(8,128)(2,1)S(1)}, bf16[128,2048]{1,0:T(8,128)(2,1)S(1)}, u32[]{:S(2)}, u32[]{:S(2)}) %collective-permute-start.9) | collective-permute-done | bytes 524320 | tf_op jit(solution)/shard_map/ppermute | solution.py:539
  145.5 4.6 %shard_map.50 = (bf16[1024,128]{1,0:T(8,128)(2,1)S(1)}, bf16[1024,128]{1,0:T(8,128)(2,1)S(1)}, bf16[1024,128]{1,0:T(8,128)(2,1)S(1)}, f32[1024,128]{1,0:T(8,128)S(1)}) custom-call(s32[1]{0:T(128)} %bitcast.place_ref, bf16[2,32,128]{2,1,0:T(8,128)(2,1)S(1)} %pad_maximum_fusion.4.design_ref, f32[40,2048]{1,0:T(8,128)S(1)} %solve.1.facts_ref, ...), custom_call_target="tpu_custom_call" | custom-call | flops 2147483648 | bytes 16777216 | tf_op jit(solution)/shard_map/pallas_call | solution.py:421
  152.7 6.3 %collective-permute-start.13 = (bf16[1024,128]{1,0:T(8,128)(2,1)S(1)}, bf16[1024,128]{1,0:T(8,128)(2,1)S(1)}, u32[]{:S(2)}, u32[]{:S(2)}) collective-permute-start(bf16[1024,128]{1,0:T(8,128)(2,1)S(1)} %get-tuple-element.39), channel_id=1, source_target_pairs={{0,6},{1,7},{2,0},{3,1},{8,14},{9,15},{10,8},{11,9},{16,22},{17,23... | collective-permute-start | bytes 786440 | tf_op jit(solution)/shard_map/ppermute | solution.py:539
  159.1 3.1 %collective-permute-done.11.refs_1_ = bf16[1024,128]{1,0:T(8,128)(2,1)S(1)} collective-permute-done((bf16[1024,128]{1,0:T(8,128)(2,1)S(1)}, bf16[1024,128]{1,0:T(8,128)(2,1)S(1)}, u32[]{:S(2)}, u32[]{:S(2)}) %collective-permute-start.11) | collective-permute-done | bytes 262176 | tf_op jit(solution)/shard_map/ppermute | solution.py:539
  162.3 6.4 %collective-permute-done.12.refs_2_ = bf16[1024,128]{1,0:T(8,128)(2,1)S(1)} collective-permute-done((bf16[1024,128]{1,0:T(8,128)(2,1)S(1)}, bf16[1024,128]{1,0:T(8,128)(2,1)S(1)}, u32[]{:S(2)}, u32[]{:S(2)}) %collective-permute-start.12) | collective-permute-done | bytes 262176 | tf_op jit(solution)/shard_map/ppermute | solution.py:539
  168.6 5.6 %collective-permute-done.13.refs_3_ = bf16[1024,128]{1,0:T(8,128)(2,1)S(1)} collective-permute-done((bf16[1024,128]{1,0:T(8,128)(2,1)S(1)}, bf16[1024,128]{1,0:T(8,128)(2,1)S(1)}, u32[]{:S(2)}, u32[]{:S(2)}) %collective-permute-start.13) | collective-permute-done | bytes 262176 | tf_op jit(solution)/shard_map/ppermute | solution.py:539
  175.3 1.8 collective-permute-start.5
  177.1 2.0 collective-permute-start.6
  180.2 4.7 %collective-permute-done.20.other_ref = bf16[4,128,128]{2,1,0:T(8,128)(2,1)S(1)} collective-permute-done((bf16[4,128,128]{2,1,0:T(8,128)(2,1)S(1)}, bf16[4,128,128]{2,1,0:T(8,128)(2,1)S(1)}, u32[]{:S(2)}, u32[]{:S(2)}) %collective-permute-start.20) | collective-permute-done | bytes 131104 | tf_op jit(solution)/shard_map/ppermute | solution.py:539
  187.1 2.1 collective-permute-start.21
  189.1 7.3 %collective-permute-done.5.refs_1_ = bf16[1024,128]{1,0:T(8,128)(2,1)S(1)} collective-permute-done((bf16[1024,128]{1,0:T(8,128)(2,1)S(1)}, bf16[1024,128]{1,0:T(8,128)(2,1)S(1)}, u32[]{:S(2)}, u32[]{:S(2)}) %collective-permute-start.5) | collective-permute-done | bytes 262176 | tf_op jit(solution)/shard_map/ppermute | solution.py:539
  197.6 9.1 %collective-permute-done.22.refs_1_ = bf16[2,128,128]{2,1,0:T(8,128)(2,1)S(1)} collective-permute-done((bf16[2,128,128]{2,1,0:T(8,128)(2,1)S(1)}, bf16[2,128,128]{2,1,0:T(8,128)(2,1)S(1)}, u32[]{:S(2)}, u32[]{:S(2)}) %collective-permute-start.22) | collective-permute-done | bytes 65568 | tf_op jit(solution)/shard_map/ppermute | solution.py:539
  (54 shorter events, 21.0 us)
Async XLA Ops:
  0.6 106.7 %collective-permute-start = (bf16[1024,2048]{1,0:T(8,128)(2,1)}, bf16[1024,2048]{1,0:T(8,128)(2,1)}, u32[]{:S(2)}, u32[]{:S(2)}) collective-permute-start(bf16[1024,2048]{1,0:T(8,128)(2,1)} %mine_ref.1), channel_id=1, source_target_pairs={{0,1},{1,0},{2,3},{3,2},{4,5},{5,4},{6,7},{7,6},{8,9},{9,8},{10,11... | collective-permute-start | bytes 12582920 | tf_op jit(solution)/shard_map/ppermute | solution.py:539
  1.2 2.2 %copy-start = (bf16[1024,2048]{1,0:T(8,128)(2,1)S(1)}, bf16[1024,2048]{1,0:T(8,128)(2,1)}, u32[]{:S(2)}) copy-start(bf16[1024,2048]{1,0:T(8,128)(2,1)} %mine_ref.1) | copy-start | bytes 12582916
  3.4 0.9 copy-start.2
  4.3 0.7 copy-start.3
  9.0 1.0 copy-start.4
  10.0 22.1 %copy-start.5 = (bf16[128,2048]{1,0:T(8,128)(2,1)}, bf16[128,2048]{1,0:T(8,128)(2,1)S(1)}, u32[]{:S(2)}) copy-start(bf16[128,2048]{1,0:T(8,128)(2,1)S(1)} %get-tuple-element.35) | copy-start | bytes 1572868
  32.1 9.2 %all-to-all-start.1 = ((bf16[8,32,128]{2,1,0:T(8,128)(2,1)}), bf16[8,32,128]{2,1,0:T(8,128)(2,1)S(1)}, u32[]{:S(2)}, u32[]{:S(2)}) async-start(bf16[8,32,128]{2,1,0:T(8,128)(2,1)} %get-tuple-element.27), calls=%async_computation.1 | async-start | bytes 131072 | tf_op jit(solution)/shard_map/all_to_all | solution.py:585
  35.4 83.4 %collective-permute-start.14 = (bf16[256,2048]{1,0:T(8,128)(2,1)}, bf16[256,2048]{1,0:T(8,128)(2,1)S(1)}, u32[]{:S(2)}, u32[]{:S(2)}) collective-permute-start(bf16[256,2048]{1,0:T(8,128)(2,1)} %get-tuple-element.40), channel_id=1, source_target_pairs={{0,8},{8,16},{16,24},{24,0},{1,9},{9,17},{17,25},{25,1},{2,10},{10... | collective-permute-start | bytes 3145736 | tf_op jit(solution)/shard_map/ppermute | solution.py:539
  37.0 81.8 %collective-permute-start.15 = (bf16[256,2048]{1,0:T(8,128)(2,1)}, bf16[256,2048]{1,0:T(8,128)(2,1)S(1)}, u32[]{:S(2)}, u32[]{:S(2)}) collective-permute-start(bf16[256,2048]{1,0:T(8,128)(2,1)} %copy-done.4), channel_id=1, source_target_pairs={{0,9},{1,8},{2,11},{3,10},{4,13},{5,12},{6,15},{7,14},{8,17},{9,16... | collective-permute-start | bytes 3145736 | tf_op jit(solution)/shard_map/ppermute | solution.py:539
  41.3 2.2 %copy-start.1 = (bf16[1024,2048]{1,0:T(8,128)(2,1)S(1)}, bf16[1024,2048]{1,0:T(8,128)(2,1)}, u32[]{:S(2)}) copy-start(bf16[1024,2048]{1,0:T(8,128)(2,1)} %mine_ref.1) | copy-start | bytes 12582916
  45.6 45.3 %collective-permute-start.1 = (f32[32,2304]{1,0:T(8,128)S(1)}, f32[32,2304]{1,0:T(8,128)S(1)}, u32[]{:S(2)}, u32[]{:S(2)}) collective-permute-start(f32[32,2304]{1,0:T(8,128)S(1)} %cross.1), channel_id=1, source_target_pairs={{0,8},{8,0},{16,24},{24,16},{1,9},{9,1},{17,25},{25,17},{2,10},{10... | collective-permute-start | bytes 884744 | tf_op jit(solution)/shard_map/ppermute | solution.py:539
  90.9 9.2 %collective-permute-start.2 = (f32[32,2304]{1,0:T(8,128)S(1)}, f32[32,2304]{1,0:T(8,128)S(1)}, u32[]{:S(2)}, u32[]{:S(2)}) collective-permute-start(f32[32,2304]{1,0:T(8,128)S(1)} %add.16.mine_ref), channel_id=1, source_target_pairs={{0,16},{8,24},{16,0},{24,8},{1,17},{9,25},{17,1},{25,9},{2,18},{10... | collective-permute-start | bytes 884744 | tf_op jit(solution)/shard_map/ppermute | solution.py:539
  91.5 12.4 %collective-permute-start.7 = (bf16[4,32,128]{2,1,0:T(8,128)(2,1)S(1)}, bf16[4,32,128]{2,1,0:T(8,128)(2,1)S(1)}, u32[]{:S(2)}, u32[]{:S(2)}) collective-permute-start(bf16[4,32,128]{2,1,0:T(8,128)(2,1)S(1)} %dynamic-slice_bitcast_fusion.2), channel_id=1, source_target_pairs={{0,8},{8,16},{16,24},{24,0},{1,9},{9,17},{17,25},{25,1},{2,10},{10... | collective-permute-start | bytes 98312 | tf_op jit(solution)/shard_map/ppermute | solution.py:539
  100.1 45.4 %collective-permute-start.8 = (bf16[256,2048]{1,0:T(8,128)(2,1)}, bf16[256,2048]{1,0:T(8,128)(2,1)}, u32[]{:S(2)}, u32[]{:S(2)}) collective-permute-start(bf16[256,2048]{1,0:T(8,128)(2,1)} %bitcast.8), channel_id=1, source_target_pairs={{0,8},{8,16},{16,24},{24,0},{1,9},{9,17},{17,25},{25,1},{2,10},{10... | collective-permute-start | bytes 3145736 | tf_op jit(solution)/shard_map/ppermute | solution.py:539
  103.9 1.7 collective-permute-start.3
  105.6 29.6 %collective-permute-start.10 = (bf16[128,2048]{1,0:T(8,128)(2,1)}, bf16[128,2048]{1,0:T(8,128)(2,1)S(1)}, u32[]{:S(2)}, u32[]{:S(2)}) collective-permute-start(bf16[128,2048]{1,0:T(8,128)(2,1)} %copy-done.5), channel_id=1, source_target_pairs={{0,9},{1,8},{2,11},{3,10},{4,13},{5,12},{6,15},{7,14},{8,17},{9,16... | collective-permute-start | bytes 1572872 | tf_op jit(solution)/shard_map/ppermute | solution.py:539
  107.3 38.2 %collective-permute-start.9 = (bf16[128,2048]{1,0:T(8,128)(2,1)S(1)}, bf16[128,2048]{1,0:T(8,128)(2,1)S(1)}, u32[]{:S(2)}, u32[]{:S(2)}) collective-permute-start(bf16[128,2048]{1,0:T(8,128)(2,1)S(1)} %get-tuple-element.34), channel_id=1, source_target_pairs={{0,9},{1,8},{2,11},{3,10},{4,13},{5,12},{6,15},{7,14},{8,17},{9,16... | collective-permute-start | bytes 1572872 | tf_op jit(solution)/shard_map/ppermute | solution.py:539
  122.2 30.5 %collective-permute-start.16 = (bf16[1024,128]{1,0:T(8,128)(2,1)S(1)}, bf16[1024,128]{1,0:T(8,128)(2,1)S(1)}, u32[]{:S(2)}, u32[]{:S(2)}) collective-permute-start(bf16[1024,128]{1,0:T(8,128)(2,1)S(1)} %get-tuple-element.43), channel_id=1, source_target_pairs={{0,2},{1,3},{2,4},{3,5},{8,10},{9,11},{10,12},{11,13},{16,18},{17,... | collective-permute-start | bytes 786440 | tf_op jit(solution)/shard_map/ppermute | solution.py:539
  125.6 33.5 %collective-permute-start.17 = (bf16[1024,128]{1,0:T(8,128)(2,1)S(1)}, bf16[1024,128]{1,0:T(8,128)(2,1)S(1)}, u32[]{:S(2)}, u32[]{:S(2)}) collective-permute-start(bf16[1024,128]{1,0:T(8,128)(2,1)S(1)} %get-tuple-element.44), channel_id=1, source_target_pairs={{0,4},{1,5},{6,2},{7,3},{8,12},{9,13},{14,10},{15,11},{16,20},{17,... | collective-permute-start | bytes 786440 | tf_op jit(solution)/shard_map/ppermute | solution.py:539
  135.2 23.9 %collective-permute-start.18 = (bf16[1024,128]{1,0:T(8,128)(2,1)S(1)}, bf16[1024,128]{1,0:T(8,128)(2,1)S(1)}, u32[]{:S(2)}, u32[]{:S(2)}) collective-permute-start(bf16[1024,128]{1,0:T(8,128)(2,1)S(1)} %get-tuple-element.45), channel_id=1, source_target_pairs={{4,2},{5,3},{6,4},{7,5},{12,10},{13,11},{14,12},{15,13},{20,18},{2... | collective-permute-start | bytes 786440 | tf_op jit(solution)/shard_map/ppermute | solution.py:539
  150.1 12.1 %collective-permute-start.11 = (bf16[1024,128]{1,0:T(8,128)(2,1)S(1)}, bf16[1024,128]{1,0:T(8,128)(2,1)S(1)}, u32[]{:S(2)}, u32[]{:S(2)}) collective-permute-start(bf16[1024,128]{1,0:T(8,128)(2,1)S(1)} %get-tuple-element.37), channel_id=1, source_target_pairs={{4,6},{5,7},{6,0},{7,1},{12,14},{13,15},{14,8},{15,9},{20,22},{21,... | collective-permute-start | bytes 786440 | tf_op jit(solution)/shard_map/ppermute | solution.py:539
  151.4 17.2 %collective-permute-start.12 = (bf16[1024,128]{1,0:T(8,128)(2,1)S(1)}, bf16[1024,128]{1,0:T(8,128)(2,1)S(1)}, u32[]{:S(2)}, u32[]{:S(2)}) collective-permute-start(bf16[1024,128]{1,0:T(8,128)(2,1)S(1)} %get-tuple-element.38), channel_id=1, source_target_pairs={{2,6},{3,7},{4,0},{5,1},{10,14},{11,15},{12,8},{13,9},{18,22},{19,... | collective-permute-start | bytes 786440 | tf_op jit(solution)/shard_map/ppermute | solution.py:539
  152.7 21.4 %collective-permute-start.13 = (bf16[1024,128]{1,0:T(8,128)(2,1)S(1)}, bf16[1024,128]{1,0:T(8,128)(2,1)S(1)}, u32[]{:S(2)}, u32[]{:S(2)}) collective-permute-start(bf16[1024,128]{1,0:T(8,128)(2,1)S(1)} %get-tuple-element.39), channel_id=1, source_target_pairs={{0,6},{1,7},{2,0},{3,1},{8,14},{9,15},{10,8},{11,9},{16,22},{17,23... | collective-permute-start | bytes 786440 | tf_op jit(solution)/shard_map/ppermute | solution.py:539
  174.6 5.6 %collective-permute-start.19 = (bf16[4,128,128]{2,1,0:T(8,128)(2,1)S(1)}, bf16[4,128,128]{2,1,0:T(8,128)(2,1)S(1)}, u32[]{:S(2)}, u32[]{:S(2)}) collective-permute-start(bf16[4,128,128]{2,1,0:T(8,128)(2,1)S(1)} %get-tuple-element.47), channel_id=1, source_target_pairs={{0,24},{8,0},{16,8},{24,16},{1,25},{9,1},{17,9},{25,17},{2,26},{10... | collective-permute-start | bytes 393224 | tf_op jit(solution)/shard_map/ppermute | solution.py:539
  175.3 11.8 %collective-permute-start.4 = (bf16[1024,128]{1,0:T(8,128)(2,1)S(1)}, bf16[1024,128]{1,0:T(8,128)(2,1)S(1)}, u32[]{:S(2)}, u32[]{:S(2)}) collective-permute-start(bf16[1024,128]{1,0:T(8,128)(2,1)S(1)} %get-tuple-element.30), channel_id=1, source_target_pairs={{0,2},{1,3},{2,4},{3,5},{4,6},{5,7},{6,0},{7,1},{8,10},{9,11},{10,... | collective-permute-start | bytes 786440 | tf_op jit(solution)/shard_map/ppermute | solution.py:539
  175.3 21.2 %collective-permute-start.5 = (bf16[1024,128]{1,0:T(8,128)(2,1)S(1)}, bf16[1024,128]{1,0:T(8,128)(2,1)S(1)}, u32[]{:S(2)}, u32[]{:S(2)}) collective-permute-start(bf16[1024,128]{1,0:T(8,128)(2,1)S(1)} %get-tuple-element.31), channel_id=1, source_target_pairs={{0,4},{1,5},{2,6},{3,7},{4,0},{5,1},{6,2},{7,3},{8,12},{9,13},{10,... | collective-permute-start | bytes 786440 | tf_op jit(solution)/shard_map/ppermute | solution.py:539
  177.1 19.4 %collective-permute-start.6 = (bf16[1024,128]{1,0:T(8,128)(2,1)S(1)}, bf16[1024,128]{1,0:T(8,128)(2,1)S(1)}, u32[]{:S(2)}, u32[]{:S(2)}) collective-permute-start(bf16[1024,128]{1,0:T(8,128)(2,1)S(1)} %get-tuple-element.32), channel_id=1, source_target_pairs={{0,6},{1,7},{2,0},{3,1},{4,2},{5,3},{6,4},{7,5},{8,14},{9,15},{10,... | collective-permute-start | bytes 786440 | tf_op jit(solution)/shard_map/ppermute | solution.py:539
  179.1 5.7 %collective-permute-start.20 = (bf16[4,128,128]{2,1,0:T(8,128)(2,1)S(1)}, bf16[4,128,128]{2,1,0:T(8,128)(2,1)S(1)}, u32[]{:S(2)}, u32[]{:S(2)}) collective-permute-start(bf16[4,128,128]{2,1,0:T(8,128)(2,1)S(1)} %get-tuple-element.48), channel_id=1, source_target_pairs={{0,25},{1,24},{2,27},{3,26},{4,29},{5,28},{6,31},{7,30},{8,1},{9,0... | collective-permute-start | bytes 393224 | tf_op jit(solution)/shard_map/ppermute | solution.py:539
  184.9 12.7 %collective-permute-start.23 = (bf16[2,128,128]{2,1,0:T(8,128)(2,1)S(1)}, bf16[2,128,128]{2,1,0:T(8,128)(2,1)S(1)}, u32[]{:S(2)}, u32[]{:S(2)}) collective-permute-start(bf16[2,128,128]{2,1,0:T(8,128)(2,1)S(1)} %pad_maximum_fusion.3), channel_id=1, source_target_pairs={{0,6},{1,7},{2,0},{3,1},{4,2},{5,3},{6,4},{7,5},{8,14},{9,15},{10,... | collective-permute-start | bytes 196616 | tf_op jit(solution)/shard_map/ppermute | solution.py:539
  185.5 21.2 %collective-permute-start.22 = (bf16[2,128,128]{2,1,0:T(8,128)(2,1)S(1)}, bf16[2,128,128]{2,1,0:T(8,128)(2,1)S(1)}, u32[]{:S(2)}, u32[]{:S(2)}) collective-permute-start(bf16[2,128,128]{2,1,0:T(8,128)(2,1)S(1)} %pad_maximum_fusion.2), channel_id=1, source_target_pairs={{0,4},{1,5},{2,6},{3,7},{4,0},{5,1},{6,2},{7,3},{8,12},{9,13},{10,... | collective-permute-start | bytes 196616 | tf_op jit(solution)/shard_map/ppermute | solution.py:539
  187.1 19.6 %collective-permute-start.21 = (bf16[2,128,128]{2,1,0:T(8,128)(2,1)S(1)}, bf16[2,128,128]{2,1,0:T(8,128)(2,1)S(1)}, u32[]{:S(2)}, u32[]{:S(2)}) collective-permute-start(bf16[2,128,128]{2,1,0:T(8,128)(2,1)S(1)} %pad_maximum_fusion.1), channel_id=1, source_target_pairs={{0,2},{1,3},{2,4},{3,5},{4,6},{5,7},{6,0},{7,1},{8,10},{9,11},{10,... | collective-permute-start | bytes 196616 | tf_op jit(solution)/shard_map/ppermute | solution.py:539

commit v5 on v4

--- a/solution.py
+++ b/solution.py
@@ -41,8 +41,8 @@
 
 
 def project_kernel(
-    quarter, core_ref, ids_ref, atlas_ref, methyl_ref, out_ref, panel_ref, low_ref, high_ref, same_ref,
-    other_ref, gram_ref,
+    quarter, core_ref, ids_ref, atlas_ref, methyl_ref, out_ref, panel_ref, outer_ref, same_ref, other_ref,
+    gram_ref,
 ):
     kk = panel_ref.shape[0]
     blocks, _, share = out_ref.shape
@@ -74,13 +74,9 @@
 
     step, steps = pl.program_id(0), pl.num_programs(0)
 
-    @pl.when(step < quarter)
-    def _():
-        put(low_ref, 1 - core)
-
-    @pl.when(step >= steps - quarter)
-    def _():
-        put(high_ref, 1 - core)
+    @pl.when((step < quarter) | (step >= steps - quarter))
+    def _():
+        put(outer_ref, 1 - core)
 
     @pl.when((step >= quarter) & (step < steps - quarter))
     def _():
@@ -95,8 +91,11 @@
     steps = rows // chunk
     quarter = steps // 4
 
-    def half(first, count):
-        return pl.BlockSpec((chunk // 2, probes), lambda i: (jnp.clip(i - first, 0, count - 1), 0))
+    def outer(i):
+        return (jnp.where(i < steps - quarter, jnp.minimum(i, quarter - 1), i - steps + 2 * quarter), 0)
+
+    def inner(i):
+        return (jnp.clip(i - quarter, 0, steps - 2 * quarter - 1), 0)
 
     def rows_of(count):
         return jax.ShapeDtypeStruct((count * chunk // 2, probes), BF16)
@@ -113,16 +112,14 @@
         out_specs=(
             pl.BlockSpec((chunk // share, 2 * K, share), lambda i: (i, 0, 0)),
             pl.BlockSpec((K, probes), lambda i: (0, 0)),
-            half(0, quarter),
-            half(steps - quarter, quarter),
-            half(quarter, steps - 2 * quarter),
-            half(quarter, steps - 2 * quarter),
+            pl.BlockSpec((chunk // 2, probes), outer),
+            pl.BlockSpec((chunk // 2, probes), inner),
+            pl.BlockSpec((chunk // 2, probes), inner),
         ),
         out_shape=(
             jax.ShapeDtypeStruct((shares, 2 * K, share), F32),
             jax.ShapeDtypeStruct((K, probes), BF16),
-            rows_of(quarter),
-            rows_of(quarter),
+            rows_of(2 * quarter),
             rows_of(steps - 2 * quarter),
             rows_of(steps - 2 * quarter),
         ),
@@ -131,6 +128,32 @@
         cost_estimate=cost(2 * K * rows * probes, 4 * rows * probes),
         name="project",
     )(core, panel_ids, atlas, methyl)
+
+
+def copy_kernel(_, from_ref, to_ref):
+    to_ref[...] = from_ref[...]
+
+
+def pick_ends(core, methyl, line, share):
+    probes = methyl.shape[1]
+    quarter = line // 4
+
+    def block(i, core):
+        return (2 * jnp.where(i < quarter, i, i + line - 2 * quarter) + core[0], 0)
+
+    return pl.pallas_call(
+        copy_kernel,
+        grid_spec=pltpu.PrefetchScalarGridSpec(
+            num_scalar_prefetch=1,
+            grid=(2 * quarter,),
+            in_specs=[pl.BlockSpec((share, probes), block)],
+            out_specs=pl.BlockSpec((share, probes), lambda i, core: (i, 0)),
+        ),
+        out_shape=jax.ShapeDtypeStruct((2 * quarter * share, probes), BF16),
+        compiler_params=params("arbitrary"),
+        cost_estimate=cost(0, 8 * quarter * share * probes),
+        name="pick_ends",
+    )(core, methyl)
 
 
 def row_chunk(share):
@@ -569,30 +592,21 @@
     def among_inner(to):
         return to - quarter, (to >= quarter) & (to < line - quarter)
 
-    halves = methyl.reshape(line, 2, share, -1)
-    first = jnp.concatenate(
-        [
-            lax.dynamic_index_in_dim(halves[:quarter], core, 1, False),
-            lax.dynamic_index_in_dim(halves[line - quarter :], core, 1, False),
-        ]
-    )
-    ends_mine = to_panel(first.reshape(len(ends) * share, -1), 1)
+    ends_mine = to_panel(pick_ends(core[None], methyl, line, share), 1)
     theirs = to_sibling(methyl)
-    parts, panel, low, high, same, other = project(core[None], panel_ids, atlas, methyl, shares)
-    ends_low = to_panel_sibling(low, 1)
+    parts, panel, outer, same, other = project(core[None], panel_ids, atlas, methyl, shares)
+    ends_theirs = to_panel_sibling(outer, 1)
     parts = lax.all_to_all(parts, "probe", 0, 0)
     scores, copies = descend(parts)
     design = lax.all_to_all(copies, "probe", 0, 0)
     part = cross_products(design, methyl, panel)
+    bit = panels // 2
+    while bit > 1:
+        part = part + swap_panels(part, bit)
+        bit //= 2
     peer = swap_panels(part, 1)
-    bit = 2
-    while bit < panels:
-        part = part + peer
-        peer = swap_panels(part, bit)
-        bit *= 2
     half = lax.dynamic_index_in_dim(design.reshape(line, 2, K, share), core, 1, False)
     design_before = to_panel(half, 1)
-    ends_high = to_panel_sibling(high, 1)
     inner_mine = to_panel(same, 1)
     inner_theirs = to_panel_sibling(other, 1)
     facts = solve(part, peer, panel, 0.0001 * samples, samples)
@@ -602,14 +616,21 @@
         pairs = [(i, (i + by) % line) for i in range(line)]
         return pairs if among is None else [(i, to) for i, to in pairs if to in among]
 
-    def arrivals(sends, among=None):
-        return [on_line(value, round_of(j, among)) for j, value in enumerate(sends, 1)]
-
-    zscore, *sends, own_keep = own_tile(at, line, design, methyl, theirs, facts, more)
-    own_parts = arrivals(sends)
+    def arrivals(sends, among=None, rounds=None):
+        return [
+            on_line(value, round_of(j, among))
+            for j, value in enumerate(sends, 1)
+            if rounds is None or j in rounds
+        ]
+
+    early = {1, line - 1}
+    late = set(range(1, line)) - early
+
+    zscore, *own_sends, own_keep = own_tile(at, line, design, methyl, theirs, facts, more)
+    own_parts = arrivals(own_sends, rounds=early)
     design_ends = jnp.concatenate([design_before[:quarter], design_before[line - quarter :]])
     *sends, keep = pair_tile(
-        among_ends, at, line, design_ends, [ends_mine], [ends_low, ends_high],
+        among_ends, at, line, design_ends, [ends_mine], [ends_theirs],
         facts, more, zscore,
     )
     pair_parts = [keep] + arrivals(sends, ends)
@@ -618,6 +639,7 @@
         [inner_mine], [inner_theirs], facts, more, zscore,
     )
     pair_parts += [keep] + arrivals(sends, inner)
+    own_parts += arrivals(own_sends, rounds=late)
     left, same, other = fold(at, line, pair_parts)
     same = to_panel(same, -1)
     other = to_panel_sibling(other, -1)

time: 208 us -> 221 us (1.062)
  waiting for transfers between devices: 106 us -> 116 us
  blocking collectives: 15.5 us -> 23.8 us
  local copies, waits for them, and re-layouts: 9.9 us -> 6 us
  starting transfers between devices: 36.8 us -> 34.2 us
    ppermute x24 -> x23, waiting for transfers between devices: 103 us -> 116 us  [along(): return lax.ppermute(value, axis, pairs)]
    all_to_all x0 -> x1, blocking collectives: none -> 8.28 us  [body(): design = lax.all_to_all(copies, 'probe', 0, 0)]
    all_to_all x1 -> x0, starting transfers between devices: 3.35 us -> none  [body(): design = lax.all_to_all(copies, 'probe', 0, 0)]
    all_to_all x1 -> x0, waiting for transfers between devices: 3.14 us -> none  [body(): design = lax.all_to_all(copies, 'probe', 0, 0)]
    unnamed x12 -> x10, local copies, waits for them, and re-layouts: 7 us -> 5.98 us
    ppermute x24 -> x23, starting transfers between devices: 33.4 us -> 34.2 us  [along(): return lax.ppermute(value, axis, pairs)]
  transfers between devices with their start and end apart: 25 -> 23, of which waited for: 13 -> 12; matrix products, arithmetic and copies ran while one was open for 2% -> 0% of each run, Pallas kernels for 17% -> 17%
where the time goes in v5:
time: 221 us
  waiting for transfers between devices  116 us (52%)
  Pallas kernels  39.8 us (18%)
  starting transfers between devices  34.2 us (15%)
  blocking collectives  23.8 us (11%)
  local copies, waits for them, and re-layouts  6 us (3%)
    ppermute x23, waiting for transfers between devices, along(): return lax.ppermute(value, axis, pairs)  116 us
    ppermute x23, starting transfers between devices, along(): return lax.ppermute(value, axis, pairs)  34.2 us
    all_to_all x1, blocking collectives, body(): parts = lax.all_to_all(parts, 'probe', 0, 0)  15.5 us
    pallas_call x1, Pallas kernels, own_tile(): pl.pallas_call(functools.partial(own_kernel, steps, line), grid_spec=pltp...  10.7 us
    pallas_call x2, Pallas kernels, pair_tile(): pl.pallas_call(functools.partial(pair_kernel, index_of, line, (len(mine),...  9.56 us
    all_to_all x1, blocking collectives, body(): design = lax.all_to_all(copies, 'probe', 0, 0)  8.28 us
    pallas_call x1, Pallas kernels, descend(): pl.pallas_call(descend_kernel, out_shape=(jax.ShapeDtypeStruct((K, share)...  6.61 us
    unnamed x10, local copies, waits for them, and re-layouts  5.98 us
  transfers between devices with their start and end apart: 23, of which 12 were waited for; matrix products, arithmetic and copies ran while one was open for 0% of the time, Pallas kernels for 17%

profile of v5, /device:TPU:0, one launch (start us, length us, event | category | flops | bytes accessed | tf_op | source)
XLA Modules:
  0.0 220.6 jit_solution(14735293121743800975)
XLA Ops:
  1.2 2.2 copy-done
  5.0 4.5 %project.1 = (f32[8,64,128]{2,1,0:T(8,128)S(1)}, bf16[32,2048]{1,0:T(8,128)(2,1)S(1)}, bf16[256,2048]{1,0:T(8,128)(2,1)}, bf16[256,2048]{1,0:T(8,128)(2,1)}, bf16[256,2048]{1,0:T(8,128)(2,1)}) custom-call(s32[1]{0:T(128)} %bitcast.1.core_ref._, s32[64]{0:T(128)S(1)} %copy-done.4, bf16[64,2048]{1,0:T(8,128)(2,1)S(1)} %copy-done.3, bf16[1024,2048]{1,0:T(8,128)(2,1)S(1)} %copy-done), custom_call_target="tpu_custom_call" | custom-call | flops 134217728 | bytes 8388608 | tf_op jit(solution)/shard_map/project/pallas_call | solution.py:103
  9.5 15.5 %all_to_all.10.parts_ref = f32[8,64,128]{2,1,0:T(8,128)S(1)} all-to-all(f32[8,64,128]{2,1,0:T(8,128)S(1)} %get-tuple-element.25), channel_id=1, replica_groups=mesh['samp'=4,'probe'=8] {'probe'}, dimensions={0} | all-to-all | bytes 524288 | tf_op jit(solution)/shard_map/all_to_all | solution.py:599
  25.0 6.6 %descend.1 = (f32[32,128]{1,0:T(8,128)}, bf16[8,32,128]{2,1,0:T(8,128)(2,1)S(1)}) custom-call(f32[8,64,128]{2,1,0:T(8,128)S(1)} %all_to_all.10.parts_ref), custom_call_target="tpu_custom_call" | custom-call | flops 33554432 | bytes 16384 | tf_op jit(solution)/shard_map/descend/pallas_call | solution.py:197
  31.6 8.3 %all_to_all.11.design_ref = bf16[8,32,128]{2,1,0:T(8,128)(2,1)S(1)} all-to-all(bf16[8,32,128]{2,1,0:T(8,128)(2,1)S(1)} %get-tuple-element.26), channel_id=1, replica_groups=mesh['samp'=4,'probe'=8] {'probe'}, dimensions={0} | all-to-all | bytes 131072 | tf_op jit(solution)/shard_map/all_to_all | solution.py:601
  39.9 2.1 cross.1
  41.9 1.6 collective-permute-start.1
  43.5 7.0 %collective-permute-done.1 = f32[32,2304]{1,0:T(8,128)S(1)} collective-permute-done((f32[32,2304]{1,0:T(8,128)S(1)}, f32[32,2304]{1,0:T(8,128)S(1)}, u32[]{:S(2)}, u32[]{:S(2)}) %collective-permute-start.1) | collective-permute-done | bytes 294944 | tf_op jit(solution)/shard_map/ppermute | solution.py:562
  50.6 1.6 collective-permute-start.2
  52.2 6.2 %collective-permute-done.2.peer_ref = f32[32,2304]{1,0:T(8,128)S(1)} collective-permute-done((f32[32,2304]{1,0:T(8,128)S(1)}, f32[32,2304]{1,0:T(8,128)S(1)}, u32[]{:S(2)}, u32[]{:S(2)}) %collective-permute-start.2) | collective-permute-done | bytes 294944 | tf_op jit(solution)/shard_map/ppermute | solution.py:562
  58.4 3.8 %solve.1.facts_ref = f32[40,2048]{1,0:T(8,128)S(1)} custom-call(f32[32,2304]{1,0:T(8,128)S(1)} %add.13.mine_ref, f32[32,2304]{1,0:T(8,128)S(1)} %collective-permute-done.2.peer_ref, bf16[32,2048]{1,0:T(8,128)(2,1)S(1)} %get-tuple-element.27.panel_ref), custom_call_target="tpu_custom_call" | custom-call | flops 104857600 | bytes 1310720 | tf_op jit(solution)/shard_map/solve/pallas_call | solution.py:289
  62.3 1.5 collective-permute-start.13
  66.6 2.2 copy-done.2
  68.9 43.3 %collective-permute-done.7 = bf16[4,32,128]{2,1,0:T(8,128)(2,1)S(1)} collective-permute-done((bf16[4,32,128]{2,1,0:T(8,128)(2,1)S(1)}, bf16[4,32,128]{2,1,0:T(8,128)(2,1)S(1)}, u32[]{:S(2)}, u32[]{:S(2)}) %collective-permute-start.7) | collective-permute-done | bytes 32800 | tf_op jit(solution)/shard_map/ppermute | solution.py:562
  112.1 1.9 collective-permute-start.8
  114.0 10.7 %own.1 = (bf16[1024,4096]{1,0:T(8,128)(2,1)S(1)}, bf16[1024,128]{1,0:T(8,128)(2,1)S(1)}, bf16[1024,128]{1,0:T(8,128)(2,1)S(1)}, bf16[1024,128]{1,0:T(8,128)(2,1)S(1)}, f32[1024,128]{1,0:T(8,128)S(1)}) custom-call(s32[1]{0:T(128)} %bitcast.place_ref, s32[1]{0:T(128)} %bitcast.1.core_ref._, bf16[8,32,128]{2,1,0:T(8,128)(2,1)S(1)} %all_to_all.11.design_ref, ...), custom_call_target="tpu_custom_call" | custom-call | flops 4294967296 | bytes 25165824 | tf_op jit(solution)/shard_map/own/pallas_call | solution.py:367
  124.7 5.0 %shard_map.51 = (bf16[1024,128]{1,0:T(8,128)(2,1)S(1)}, bf16[1024,128]{1,0:T(8,128)(2,1)S(1)}, bf16[1024,128]{1,0:T(8,128)(2,1)S(1)}, f32[1024,128]{1,0:T(8,128)S(1)}) custom-call(s32[1]{0:T(128)} %bitcast.place_ref, bf16[2,32,128]{2,1,0:T(8,128)(2,1)S(1)} %slice.38.design_ref, f32[40,2048]{1,0:T(8,128)S(1)} %solve.1.facts_ref, ...), custom_call_target="tpu_custom_call" | custom-call | flops 2147483648 | bytes 16777216 | tf_op jit(solution)/shard_map/pallas_call | solution.py:444
  129.7 2.8 %collective-permute-start.15 = (bf16[1024,128]{1,0:T(8,128)(2,1)S(1)}, bf16[1024,128]{1,0:T(8,128)(2,1)S(1)}, u32[]{:S(2)}, u32[]{:S(2)}) collective-permute-start(bf16[1024,128]{1,0:T(8,128)(2,1)S(1)} %get-tuple-element.41), channel_id=1, source_target_pairs={{0,2},{1,3},{2,4},{3,5},{8,10},{9,11},{10,12},{11,13},{16,18},{17,... | collective-permute-start | bytes 786440 | tf_op jit(solution)/shard_map/ppermute | solution.py:562
  134.5 4.2 %collective-permute-done.9.refs_1_ = bf16[256,2048]{1,0:T(8,128)(2,1)S(1)} collective-permute-done((bf16[256,2048]{1,0:T(8,128)(2,1)}, bf16[256,2048]{1,0:T(8,128)(2,1)S(1)}, u32[]{:S(2)}, u32[]{:S(2)}) %collective-permute-start.9) | collective-permute-done | bytes 1048608 | tf_op jit(solution)/shard_map/ppermute | solution.py:562
  138.7 21.5 %collective-permute-done.8.refs_0_ = bf16[256,2048]{1,0:T(8,128)(2,1)} collective-permute-done((bf16[256,2048]{1,0:T(8,128)(2,1)S(1)}, bf16[256,2048]{1,0:T(8,128)(2,1)}, u32[]{:S(2)}, u32[]{:S(2)}) %collective-permute-start.8) | collective-permute-done | bytes 1048608 | tf_op jit(solution)/shard_map/ppermute | solution.py:562
  160.2 4.6 %shard_map.50 = (bf16[1024,128]{1,0:T(8,128)(2,1)S(1)}, bf16[1024,128]{1,0:T(8,128)(2,1)S(1)}, bf16[1024,128]{1,0:T(8,128)(2,1)S(1)}, f32[1024,128]{1,0:T(8,128)S(1)}) custom-call(s32[1]{0:T(128)} %bitcast.place_ref, bf16[2,32,128]{2,1,0:T(8,128)(2,1)S(1)} %pad_maximum_fusion.3.design_ref, f32[40,2048]{1,0:T(8,128)S(1)} %solve.1.facts_ref, ...), custom_call_target="tpu_custom_call" | custom-call | flops 2147483648 | bytes 16777216 | tf_op jit(solution)/shard_map/pallas_call | solution.py:444
  167.4 6.3 %collective-permute-start.12 = (bf16[1024,128]{1,0:T(8,128)(2,1)S(1)}, bf16[1024,128]{1,0:T(8,128)(2,1)S(1)}, u32[]{:S(2)}, u32[]{:S(2)}) collective-permute-start(bf16[1024,128]{1,0:T(8,128)(2,1)S(1)} %get-tuple-element.37), channel_id=1, source_target_pairs={{0,6},{1,7},{2,0},{3,1},{8,14},{9,15},{10,8},{11,9},{16,22},{17,23... | collective-permute-start | bytes 786440 | tf_op jit(solution)/shard_map/ppermute | solution.py:562
  173.8 3.5 %collective-permute-done.10.refs_1_ = bf16[1024,128]{1,0:T(8,128)(2,1)S(1)} collective-permute-done((bf16[1024,128]{1,0:T(8,128)(2,1)S(1)}, bf16[1024,128]{1,0:T(8,128)(2,1)S(1)}, u32[]{:S(2)}, u32[]{:S(2)}) %collective-permute-start.10) | collective-permute-done | bytes 262176 | tf_op jit(solution)/shard_map/ppermute | solution.py:562
  177.3 5.5 %collective-permute-done.11.refs_2_ = bf16[1024,128]{1,0:T(8,128)(2,1)S(1)} collective-permute-done((bf16[1024,128]{1,0:T(8,128)(2,1)S(1)}, bf16[1024,128]{1,0:T(8,128)(2,1)S(1)}, u32[]{:S(2)}, u32[]{:S(2)}) %collective-permute-start.11) | collective-permute-done | bytes 262176 | tf_op jit(solution)/shard_map/ppermute | solution.py:562
  182.8 5.5 %collective-permute-done.12.refs_3_ = bf16[1024,128]{1,0:T(8,128)(2,1)S(1)} collective-permute-done((bf16[1024,128]{1,0:T(8,128)(2,1)S(1)}, bf16[1024,128]{1,0:T(8,128)(2,1)S(1)}, u32[]{:S(2)}, u32[]{:S(2)}) %collective-permute-start.12) | collective-permute-done | bytes 262176 | tf_op jit(solution)/shard_map/ppermute | solution.py:562
  188.7 1.5 collective-permute-start.18
  190.2 3.8 %collective-permute-start.5 = (bf16[1024,128]{1,0:T(8,128)(2,1)S(1)}, bf16[1024,128]{1,0:T(8,128)(2,1)S(1)}, u32[]{:S(2)}, u32[]{:S(2)}) collective-permute-start(bf16[1024,128]{1,0:T(8,128)(2,1)S(1)} %get-tuple-element.30), channel_id=1, source_target_pairs={{0,6},{1,7},{2,0},{3,1},{4,2},{5,3},{6,4},{7,5},{8,14},{9,15},{10,... | collective-permute-start | bytes 786440 | tf_op jit(solution)/shard_map/ppermute | solution.py:562
  194.4 4.8 %collective-permute-done.19.other_ref = bf16[4,128,128]{2,1,0:T(8,128)(2,1)S(1)} collective-permute-done((bf16[4,128,128]{2,1,0:T(8,128)(2,1)S(1)}, bf16[4,128,128]{2,1,0:T(8,128)(2,1)S(1)}, u32[]{:S(2)}, u32[]{:S(2)}) %collective-permute-start.19) | collective-permute-done | bytes 131104 | tf_op jit(solution)/shard_map/ppermute | solution.py:562
  199.8 2.2 %collective-permute-start.21 = (bf16[2,128,128]{2,1,0:T(8,128)(2,1)S(1)}, bf16[2,128,128]{2,1,0:T(8,128)(2,1)S(1)}, u32[]{:S(2)}, u32[]{:S(2)}) collective-permute-start(bf16[2,128,128]{2,1,0:T(8,128)(2,1)S(1)} %pad_maximum_fusion.1), channel_id=1, source_target_pairs={{0,4},{1,5},{2,6},{3,7},{4,0},{5,1},{6,2},{7,3},{8,12},{9,13},{10,... | collective-permute-start | bytes 196616 | tf_op jit(solution)/shard_map/ppermute | solution.py:562
  202.1 2.1 collective-permute-start.20
  204.1 3.3 %collective-permute-done.5.refs_1_ = bf16[1024,128]{1,0:T(8,128)(2,1)S(1)} collective-permute-done((bf16[1024,128]{1,0:T(8,128)(2,1)S(1)}, bf16[1024,128]{1,0:T(8,128)(2,1)S(1)}, u32[]{:S(2)}, u32[]{:S(2)}) %collective-permute-start.5) | collective-permute-done | bytes 262176 | tf_op jit(solution)/shard_map/ppermute | solution.py:562
  207.4 10.6 %collective-permute-done.6.refs_2_ = bf16[1024,128]{1,0:T(8,128)(2,1)S(1)} collective-permute-done((bf16[1024,128]{1,0:T(8,128)(2,1)S(1)}, bf16[1024,128]{1,0:T(8,128)(2,1)S(1)}, u32[]{:S(2)}, u32[]{:S(2)}) %collective-permute-start.6) | collective-permute-done | bytes 262176 | tf_op jit(solution)/shard_map/ppermute | solution.py:562
  (47 shorter events, 13.7 us)
Async XLA Ops:
  0.6 113.4 %collective-permute-start = (bf16[1024,2048]{1,0:T(8,128)(2,1)}, bf16[1024,2048]{1,0:T(8,128)(2,1)}, u32[]{:S(2)}, u32[]{:S(2)}) collective-permute-start(bf16[1024,2048]{1,0:T(8,128)(2,1)} %from_ref.1), channel_id=1, source_target_pairs={{0,1},{1,0},{2,3},{3,2},{4,5},{5,4},{6,7},{7,6},{8,9},{9,8},{10,11... | collective-permute-start | bytes 12582920 | tf_op jit(solution)/shard_map/ppermute | solution.py:562
  1.2 2.2 copy-start
  3.4 0.9 copy-start.3
  4.3 0.7 copy-start.4
  5.0 34.9 %copy-start.1 = (bf16[1024,2048]{1,0:T(8,128)(2,1)S(1)}, bf16[1024,2048]{1,0:T(8,128)(2,1)}, u32[]{:S(2)}) copy-start(bf16[1024,2048]{1,0:T(8,128)(2,1)} %from_ref.1) | copy-start | bytes 12582916
  41.9 8.6 %collective-permute-start.1 = (f32[32,2304]{1,0:T(8,128)S(1)}, f32[32,2304]{1,0:T(8,128)S(1)}, u32[]{:S(2)}, u32[]{:S(2)}) collective-permute-start(f32[32,2304]{1,0:T(8,128)S(1)} %cross.1), channel_id=1, source_target_pairs={{0,16},{8,24},{16,0},{24,8},{1,17},{9,25},{17,1},{25,9},{2,18},{10... | collective-permute-start | bytes 884744 | tf_op jit(solution)/shard_map/ppermute | solution.py:562
  50.6 7.8 %collective-permute-start.2 = (f32[32,2304]{1,0:T(8,128)S(1)}, f32[32,2304]{1,0:T(8,128)S(1)}, u32[]{:S(2)}, u32[]{:S(2)}) collective-permute-start(f32[32,2304]{1,0:T(8,128)S(1)} %add.13.mine_ref), channel_id=1, source_target_pairs={{0,8},{8,0},{16,24},{24,16},{1,9},{9,1},{17,25},{25,17},{2,10},{10... | collective-permute-start | bytes 884744 | tf_op jit(solution)/shard_map/ppermute | solution.py:562
  62.2 49.9 %collective-permute-start.3 = (f32[40,2048]{1,0:T(8,128)S(1)}, f32[40,2048]{1,0:T(8,128)S(1)}, u32[]{:S(2)}, u32[]{:S(2)}) collective-permute-start(f32[40,2048]{1,0:T(8,128)S(1)} %solve.1.facts_ref), channel_id=1, source_target_pairs={{0,1},{1,0},{2,3},{3,2},{4,5},{5,4},{6,7},{7,6},{8,9},{9,8},{10,11... | collective-permute-start | bytes 983048 | tf_op jit(solution)/shard_map/ppermute | solution.py:562
  62.3 62.4 %collective-permute-start.13 = (bf16[256,2048]{1,0:T(8,128)(2,1)}, bf16[256,2048]{1,0:T(8,128)(2,1)}, u32[]{:S(2)}, u32[]{:S(2)}) collective-permute-start(bf16[256,2048]{1,0:T(8,128)(2,1)} %get-tuple-element.38), channel_id=1, source_target_pairs={{0,8},{8,16},{16,24},{24,0},{1,9},{9,17},{17,25},{25,1},{2,10},{10... | collective-permute-start | bytes 3145736 | tf_op jit(solution)/shard_map/ppermute | solution.py:562
  63.8 60.9 %collective-permute-start.14 = (bf16[256,2048]{1,0:T(8,128)(2,1)}, bf16[256,2048]{1,0:T(8,128)(2,1)}, u32[]{:S(2)}, u32[]{:S(2)}) collective-permute-start(bf16[256,2048]{1,0:T(8,128)(2,1)} %get-tuple-element.39), channel_id=1, source_target_pairs={{0,9},{1,8},{2,11},{3,10},{4,13},{5,12},{6,15},{7,14},{8,17},{9,16... | collective-permute-start | bytes 3145736 | tf_op jit(solution)/shard_map/ppermute | solution.py:562
  65.1 47.0 %collective-permute-start.7 = (bf16[4,32,128]{2,1,0:T(8,128)(2,1)S(1)}, bf16[4,32,128]{2,1,0:T(8,128)(2,1)S(1)}, u32[]{:S(2)}, u32[]{:S(2)}) collective-permute-start(bf16[4,32,128]{2,1,0:T(8,128)(2,1)S(1)} %dynamic-slice_bitcast_fusion), channel_id=1, source_target_pairs={{0,8},{8,16},{16,24},{24,0},{1,9},{9,17},{17,25},{25,1},{2,10},{10... | collective-permute-start | bytes 98312 | tf_op jit(solution)/shard_map/ppermute | solution.py:562
  66.6 2.2 copy-start.2
  112.1 26.6 %collective-permute-start.9 = (bf16[256,2048]{1,0:T(8,128)(2,1)}, bf16[256,2048]{1,0:T(8,128)(2,1)S(1)}, u32[]{:S(2)}, u32[]{:S(2)}) collective-permute-start(bf16[256,2048]{1,0:T(8,128)(2,1)} %get-tuple-element.33), channel_id=1, source_target_pairs={{0,9},{1,8},{2,11},{3,10},{4,13},{5,12},{6,15},{7,14},{8,17},{9,16... | collective-permute-start | bytes 3145736 | tf_op jit(solution)/shard_map/ppermute | solution.py:562
  112.1 48.1 %collective-permute-start.8 = (bf16[256,2048]{1,0:T(8,128)(2,1)S(1)}, bf16[256,2048]{1,0:T(8,128)(2,1)}, u32[]{:S(2)}, u32[]{:S(2)}) collective-permute-start(bf16[256,2048]{1,0:T(8,128)(2,1)S(1)} %pick_ends.1), channel_id=1, source_target_pairs={{0,8},{8,16},{16,24},{24,0},{1,9},{9,17},{17,25},{25,1},{2,10},{10... | collective-permute-start | bytes 3145736 | tf_op jit(solution)/shard_map/ppermute | solution.py:562
  129.7 37.7 %collective-permute-start.15 = (bf16[1024,128]{1,0:T(8,128)(2,1)S(1)}, bf16[1024,128]{1,0:T(8,128)(2,1)S(1)}, u32[]{:S(2)}, u32[]{:S(2)}) collective-permute-start(bf16[1024,128]{1,0:T(8,128)(2,1)S(1)} %get-tuple-element.41), channel_id=1, source_target_pairs={{0,2},{1,3},{2,4},{3,5},{8,10},{9,11},{10,12},{11,13},{16,18},{17,... | collective-permute-start | bytes 786440 | tf_op jit(solution)/shard_map/ppermute | solution.py:562
  132.5 41.3 %collective-permute-start.16 = (bf16[1024,128]{1,0:T(8,128)(2,1)S(1)}, bf16[1024,128]{1,0:T(8,128)(2,1)S(1)}, u32[]{:S(2)}, u32[]{:S(2)}) collective-permute-start(bf16[1024,128]{1,0:T(8,128)(2,1)S(1)} %get-tuple-element.42), channel_id=1, source_target_pairs={{0,4},{1,5},{6,2},{7,3},{8,12},{9,13},{14,10},{15,11},{16,20},{17,... | collective-permute-start | bytes 786440 | tf_op jit(solution)/shard_map/ppermute | solution.py:562
  133.8 40.0 %collective-permute-start.17 = (bf16[1024,128]{1,0:T(8,128)(2,1)S(1)}, bf16[1024,128]{1,0:T(8,128)(2,1)S(1)}, u32[]{:S(2)}, u32[]{:S(2)}) collective-permute-start(bf16[1024,128]{1,0:T(8,128)(2,1)S(1)} %get-tuple-element.43), channel_id=1, source_target_pairs={{4,2},{5,3},{6,4},{7,5},{12,10},{13,11},{14,12},{15,13},{20,18},{2... | collective-permute-start | bytes 786440 | tf_op jit(solution)/shard_map/ppermute | solution.py:562
  164.8 12.5 %collective-permute-start.10 = (bf16[1024,128]{1,0:T(8,128)(2,1)S(1)}, bf16[1024,128]{1,0:T(8,128)(2,1)S(1)}, u32[]{:S(2)}, u32[]{:S(2)}) collective-permute-start(bf16[1024,128]{1,0:T(8,128)(2,1)S(1)} %get-tuple-element.35), channel_id=1, source_target_pairs={{4,6},{5,7},{6,0},{7,1},{12,14},{13,15},{14,8},{15,9},{20,22},{21,... | collective-permute-start | bytes 786440 | tf_op jit(solution)/shard_map/ppermute | solution.py:562
  166.1 16.7 %collective-permute-start.11 = (bf16[1024,128]{1,0:T(8,128)(2,1)S(1)}, bf16[1024,128]{1,0:T(8,128)(2,1)S(1)}, u32[]{:S(2)}, u32[]{:S(2)}) collective-permute-start(bf16[1024,128]{1,0:T(8,128)(2,1)S(1)} %get-tuple-element.36), channel_id=1, source_target_pairs={{2,6},{3,7},{4,0},{5,1},{10,14},{11,15},{12,8},{13,9},{18,22},{19,... | collective-permute-start | bytes 786440 | tf_op jit(solution)/shard_map/ppermute | solution.py:562
  167.4 20.9 %collective-permute-start.12 = (bf16[1024,128]{1,0:T(8,128)(2,1)S(1)}, bf16[1024,128]{1,0:T(8,128)(2,1)S(1)}, u32[]{:S(2)}, u32[]{:S(2)}) collective-permute-start(bf16[1024,128]{1,0:T(8,128)(2,1)S(1)} %get-tuple-element.37), channel_id=1, source_target_pairs={{0,6},{1,7},{2,0},{3,1},{8,14},{9,15},{10,8},{11,9},{16,22},{17,23... | collective-permute-start | bytes 786440 | tf_op jit(solution)/shard_map/ppermute | solution.py:562
  188.7 5.7 %collective-permute-start.18 = (bf16[4,128,128]{2,1,0:T(8,128)(2,1)S(1)}, bf16[4,128,128]{2,1,0:T(8,128)(2,1)S(1)}, u32[]{:S(2)}, u32[]{:S(2)}) collective-permute-start(bf16[4,128,128]{2,1,0:T(8,128)(2,1)S(1)} %get-tuple-element.45), channel_id=1, source_target_pairs={{0,24},{8,0},{16,8},{24,16},{1,25},{9,1},{17,9},{25,17},{2,26},{10... | collective-permute-start | bytes 393224 | tf_op jit(solution)/shard_map/ppermute | solution.py:562
  190.2 11.9 %collective-permute-start.4 = (bf16[1024,128]{1,0:T(8,128)(2,1)S(1)}, bf16[1024,128]{1,0:T(8,128)(2,1)S(1)}, u32[]{:S(2)}, u32[]{:S(2)}) collective-permute-start(bf16[1024,128]{1,0:T(8,128)(2,1)S(1)} %get-tuple-element.29), channel_id=1, source_target_pairs={{0,2},{1,3},{2,4},{3,5},{4,6},{5,7},{6,0},{7,1},{8,10},{9,11},{10,... | collective-permute-start | bytes 786440 | tf_op jit(solution)/shard_map/ppermute | solution.py:562
  190.2 17.2 %collective-permute-start.5 = (bf16[1024,128]{1,0:T(8,128)(2,1)S(1)}, bf16[1024,128]{1,0:T(8,128)(2,1)S(1)}, u32[]{:S(2)}, u32[]{:S(2)}) collective-permute-start(bf16[1024,128]{1,0:T(8,128)(2,1)S(1)} %get-tuple-element.30), channel_id=1, source_target_pairs={{0,6},{1,7},{2,0},{3,1},{4,2},{5,3},{6,4},{7,5},{8,14},{9,15},{10,... | collective-permute-start | bytes 786440 | tf_op jit(solution)/shard_map/ppermute | solution.py:562
  194.0 24.0 %collective-permute-start.6 = (bf16[1024,128]{1,0:T(8,128)(2,1)S(1)}, bf16[1024,128]{1,0:T(8,128)(2,1)S(1)}, u32[]{:S(2)}, u32[]{:S(2)}) collective-permute-start(bf16[1024,128]{1,0:T(8,128)(2,1)S(1)} %get-tuple-element.31), channel_id=1, source_target_pairs={{0,4},{1,5},{2,6},{3,7},{4,0},{5,1},{6,2},{7,3},{8,12},{9,13},{10,... | collective-permute-start | bytes 786440 | tf_op jit(solution)/shard_map/ppermute | solution.py:562
  194.0 5.2 %collective-permute-start.19 = (bf16[4,128,128]{2,1,0:T(8,128)(2,1)S(1)}, bf16[4,128,128]{2,1,0:T(8,128)(2,1)S(1)}, u32[]{:S(2)}, u32[]{:S(2)}) collective-permute-start(bf16[4,128,128]{2,1,0:T(8,128)(2,1)S(1)} %get-tuple-element.46), channel_id=1, source_target_pairs={{0,25},{1,24},{2,27},{3,26},{4,29},{5,28},{6,31},{7,30},{8,1},{9,0... | collective-permute-start | bytes 393224 | tf_op jit(solution)/shard_map/ppermute | solution.py:562
  199.2 19.9 %collective-permute-start.22 = (bf16[2,128,128]{2,1,0:T(8,128)(2,1)S(1)}, bf16[2,128,128]{2,1,0:T(8,128)(2,1)S(1)}, u32[]{:S(2)}, u32[]{:S(2)}) collective-permute-start(bf16[2,128,128]{2,1,0:T(8,128)(2,1)S(1)} %pad_maximum_fusion.2), channel_id=1, source_target_pairs={{0,6},{1,7},{2,0},{3,1},{4,2},{5,3},{6,4},{7,5},{8,14},{9,15},{10,... | collective-permute-start | bytes 196616 | tf_op jit(solution)/shard_map/ppermute | solution.py:562
  199.8 19.8 %collective-permute-start.21 = (bf16[2,128,128]{2,1,0:T(8,128)(2,1)S(1)}, bf16[2,128,128]{2,1,0:T(8,128)(2,1)S(1)}, u32[]{:S(2)}, u32[]{:S(2)}) collective-permute-start(bf16[2,128,128]{2,1,0:T(8,128)(2,1)S(1)} %pad_maximum_fusion.1), channel_id=1, source_target_pairs={{0,4},{1,5},{2,6},{3,7},{4,0},{5,1},{6,2},{7,3},{8,12},{9,13},{10,... | collective-permute-start | bytes 196616 | tf_op jit(solution)/shard_map/ppermute | solution.py:562
  202.1 17.5 %collective-permute-start.20 = (bf16[2,128,128]{2,1,0:T(8,128)(2,1)S(1)}, bf16[2,128,128]{2,1,0:T(8,128)(2,1)S(1)}, u32[]{:S(2)}, u32[]{:S(2)}) collective-permute-start(bf16[2,128,128]{2,1,0:T(8,128)(2,1)S(1)} %pad_maximum_fusion), channel_id=1, source_target_pairs={{0,2},{1,3},{2,4},{3,5},{4,6},{5,7},{6,0},{7,1},{8,10},{9,11},{10,... | collective-permute-start | bytes 196616 | tf_op jit(solution)/shard_map/ppermute | solution.py:562

commit v6 on v5

--- a/solution.py
+++ b/solution.py
@@ -306,17 +306,10 @@
         store(at, width, (left * rate[:, cols]).astype(BF16))
 
 
-def put_tile(part, sends, keep_ref):
-    share = keep_ref.shape[1]
-    keep_ref[...] = part[:, :share]
-    for j, ref in enumerate(sends, 1):
-        ref[...] = part[:, j * share : (j + 1) * share].astype(BF16)
-
-
 def own_kernel(
     steps, line, place_ref, core_ref, design_ref, mine_ref, theirs_ref, facts_ref, more_ref, *refs
 ):
-    (z_ref, *sends), (keep_ref, half_ref, terms_ref, moreterms_ref) = refs[:line], refs[line:]
+    z_ref, swap_ref, keep_ref, half_ref, terms_ref, moreterms_ref = refs
     step = pl.program_id(0)
     blocks, kk, share = design_ref.shape
     chunk, probes = mine_ref.shape
@@ -341,14 +334,17 @@
         )
         for b in range(blocks // 2):
             here = pl.ds(pl.multiple_of(step * chunk + (2 * b + core) * share, share), share)
-            slot = lax.rem(step * (blocks // 2) + b - place + line, line)
+            slot = jnp.bitwise_xor(step * (blocks // 2) + b, place)
             half_ref[pl.ds(pl.multiple_of(slot * share, share), share), :] = z_ref[here, :]
 
     @pl.when(step >= steps)
     def _():
-        tall = keep_ref.shape[0]
+        tall = keep_ref.shape[1]
         rows = pl.ds(pl.multiple_of((step - steps) * tall, tall), tall)
-        put_tile(nt(z_ref[rows, :], half_ref[...]), sends, keep_ref)
+        part = nt(z_ref[rows, :], half_ref[...])
+        for slot in range(0, line, 2):
+            keep_ref[slot // 2] = part[:, slot * share : (slot + 1) * share]
+            swap_ref[slot // 2] = part[:, (slot + 1) * share : (slot + 2) * share].astype(BF16)
 
 
 def own_tile(at, line, design, mine, theirs, facts, more):
@@ -377,7 +373,7 @@
                 whole,
             ],
             out_specs=[pl.BlockSpec(memory_space=pltpu.VMEM)]
-            + [pl.BlockSpec((tall, share), second)] * line,
+            + [pl.BlockSpec((line // 2, tall, share), lambda i, *_: (0, *second(i)))] * 2,
             scratch_shapes=[
                 pltpu.VMEM((rows // 2, 2 * probes), BF16),
                 pltpu.VMEM((3 * K, probes), BF16),
@@ -385,45 +381,43 @@
             ],
         ),
         out_shape=[pltpu.VMEM((rows, 2 * probes), BF16)]
-        + [jax.ShapeDtypeStruct((rows, share), BF16)] * (line - 1)
-        + [jax.ShapeDtypeStruct((rows, share), F32)],
+        + [jax.ShapeDtypeStruct((line // 2, rows, share), dtype) for dtype in (BF16, F32)],
         compiler_params=params("arbitrary"),
         cost_estimate=cost(2 * rows * rows * probes, 12 * rows * probes),
         name="own",
     )(*at, design, mine, theirs, facts, more)
 
 
-def pair_kernel(index_of, line, count, place_ref, design_ref, facts_ref, more_ref, zscore_ref, *refs):
-    mine, theirs, refs = refs[: count[0]], refs[count[0] : sum(count)], refs[sum(count) :]
-    (*sends, keep_ref), (z_ref, terms_ref, moreterms_ref) = refs[:-3], refs[-3:]
+def pair_kernel(index_of, line, first, sides, given, last, place_ref, design_ref, zscore_ref, *refs):
+    facts, raws, refs = refs[:sides], refs[sides : 2 * sides], refs[2 * sides :]
+    given_ref, refs = (refs[0], refs[1:]) if given else (None, refs)
+    outs, (z_ref, *terms) = refs[: -1 - sides], refs[-1 - sides :]
     blocks, kk, share = design_ref.shape
-    probes = facts_ref.shape[1]
-    tall = keep_ref.shape[0]
+    probes = facts[0].shape[1]
+    tall = outs[0].shape[0]
     step, place = pl.program_id(0), place_ref[0]
 
     @pl.when(step == 0)
     def _():
-        terms_ref[...] = three_terms(facts_ref[:kk, :])
-        moreterms_ref[...] = three_terms(more_ref[:kk, :])
         design = jnp.concatenate([design_ref[b] for b in range(blocks)], axis=1)
-        for base, pieces, facts, terms in (
-            (0, mine, facts_ref, terms_ref),
-            (probes, theirs, more_ref, moreterms_ref),
-        ):
-            top = 0
-            for piece in pieces:
-                rows = slice(top, top + piece.shape[0])
-
-                def store(at, width, value):
-                    z_ref[rows, base + at : base + at + width] = value
-
-                standardise(design[:, rows], piece, terms, facts[kk : kk + 1, :], store)
-                top += piece.shape[0]
+        for side in range(sides):
+            terms[side][...] = three_terms(facts[side][:kk, :])
+
+            def store(at, width, value):
+                z_ref[:, side * probes + at : side * probes + at + width] = value
+
+            standardise(design, raws[side], terms[side], facts[side][kk : kk + 1, :], store)
 
     @pl.when(step > 0)
     def _():
         rows = pl.ds(pl.multiple_of((step - 1) * tall, tall), tall)
-        part = nt(zscore_ref[rows, :], z_ref[...])
+        part = nt(zscore_ref[rows, first * probes : (first + sides) * probes], z_ref[...])
+        if given:
+            part = part + given_ref[rows, :]
+        if not last:
+            outs[0][...] = part
+            return
+        *sends, keep_ref = outs
         for j, ref in enumerate([keep_ref, *sends]):
             index, inside = index_of(lax.rem(place + j, line))
             block = part[:, :share]
@@ -434,31 +428,30 @@
             ref[...] = block.astype(ref.dtype)
 
 
-def pair_tile(index_of, at, line, design, mine, theirs, facts, more, zscore):
+def pair_tile(index_of, at, line, design, zscore, first, facts, raws, given=None, last=True):
     blocks, _, share = design.shape
     rows, depth = zscore.shape
-    probes = depth // 2
+    probes, sides = depth // 2, len(facts)
     tall = 2 * row_chunk(share)
-    vmem = pl.BlockSpec(memory_space=pltpu.VMEM)
-    column = pl.BlockSpec((tall, share), lambda i, *_: (jnp.maximum(i - 1, 0), 0))
-    return pl.pallas_call(
-        functools.partial(pair_kernel, index_of, line, (len(mine), len(theirs))),
+    given = [] if given is None else [given]
+    width = share if last else blocks * share
+    column = pl.BlockSpec((tall, width), lambda i, *_: (jnp.maximum(i - 1, 0), 0))
+    whole = jax.ShapeDtypeStruct((rows, width), F32)
+    sends = [jax.ShapeDtypeStruct((rows, share), BF16)] * (line - 1)
+    return pl.pallas_call(
+        functools.partial(pair_kernel, index_of, line, first, sides, bool(given), last),
         grid_spec=pltpu.PrefetchScalarGridSpec(
             num_scalar_prefetch=1,
             grid=(1 + rows // tall,),
-            in_specs=[vmem] * (4 + len(mine) + len(theirs)),
-            out_specs=[column] * line,
-            scratch_shapes=[
-                pltpu.VMEM((blocks * share, depth), BF16),
-                pltpu.VMEM((3 * K, probes), BF16),
-                pltpu.VMEM((3 * K, probes), BF16),
-            ],
+            in_specs=[pl.BlockSpec(memory_space=pltpu.VMEM)] * (2 + 2 * sides + len(given)),
+            out_specs=[column] * line if last else [column],
+            scratch_shapes=[pltpu.VMEM((blocks * share, sides * probes), BF16)]
+            + [pltpu.VMEM((3 * K, probes), BF16)] * sides,
         ),
-        out_shape=[jax.ShapeDtypeStruct((rows, share), BF16)] * (line - 1)
-        + [jax.ShapeDtypeStruct((rows, share), F32)],
+        out_shape=sends + [whole] if last else [whole],
         compiler_params=params("arbitrary"),
-        cost_estimate=cost(2 * rows * blocks * share * depth, 8 * rows * probes),
-    )(at[0], design, facts, more, zscore, *mine, *theirs)
+        cost_estimate=cost(2 * rows * blocks * share * sides * probes, 4 * rows * probes),
+    )(at[0], design, zscore, *facts, *raws, *given)
 
 
 def fold_kernel(line, place_ref, core_ref, *refs):
@@ -616,30 +609,36 @@
         pairs = [(i, (i + by) % line) for i in range(line)]
         return pairs if among is None else [(i, to) for i, to in pairs if to in among]
 
-    def arrivals(sends, among=None, rounds=None):
-        return [
-            on_line(value, round_of(j, among))
-            for j, value in enumerate(sends, 1)
-            if rounds is None or j in rounds
-        ]
-
-    early = {1, line - 1}
-    late = set(range(1, line)) - early
-
-    zscore, *own_sends, own_keep = own_tile(at, line, design, methyl, theirs, facts, more)
-    own_parts = arrivals(own_sends, rounds=early)
+    def arrivals(sends, among):
+        return [on_line(value, round_of(j, among)) for j, value in enumerate(sends, 1)]
+
+
+    zscore, swap, keep = own_tile(at, line, design, methyl, theirs, facts, more)
+    given = on_line(swap, [(i, i ^ 1) for i in range(line)])
     design_ends = jnp.concatenate([design_before[:quarter], design_before[line - quarter :]])
-    *sends, keep = pair_tile(
-        among_ends, at, line, design_ends, [ends_mine], [ends_theirs],
-        facts, more, zscore,
+    *sends, pair_keep = pair_tile(
+        among_ends, at, line, design_ends, zscore, 0, [facts, more],
+        [ends_mine, ends_theirs],
     )
-    pair_parts = [keep] + arrivals(sends, ends)
-    *sends, keep = pair_tile(
-        among_inner, at, line, design_before[quarter : line - quarter],
-        [inner_mine], [inner_theirs], facts, more, zscore,
+    pair_parts = [pair_keep] + arrivals(sends, ends)
+    bit = 2
+    while bit < line:
+        swap = keep[1::2] + given[1::2].astype(F32)
+        keep = keep[::2] + given[::2].astype(F32)
+        given = on_line(swap.astype(BF16), [(i, i ^ bit) for i in range(line)])
+        bit *= 2
+    own_keep, own_parts = keep[0], [given[0]]
+    design_inner = design_before[quarter : line - quarter]
+    (partial,) = pair_tile(
+        among_inner, at, line, design_inner, zscore, 0, [facts], [inner_mine],
+        last=False,
     )
-    pair_parts += [keep] + arrivals(sends, inner)
-    own_parts += arrivals(own_sends, rounds=late)
+    *sends, pair_keep = pair_tile(
+        among_inner, at, line, design_inner, zscore, 1, [more], [inner_theirs],
+        given=partial,
+    )
+    pair_parts.append(pair_keep)
+    pair_parts += arrivals(sends, inner)
     left, same, other = fold(at, line, pair_parts)
     same = to_panel(same, -1)
     other = to_panel_sibling(other, -1)

time: 221 us -> 222 us (level)
  starting transfers between devices: 34.2 us -> 27.2 us
  waiting for transfers between devices: 116 us -> 122 us
    ppermute x23 -> x22, starting transfers between devices: 34.2 us -> 27.2 us  [along(): return lax.ppermute(value, axis, pairs)]
    ppermute x23 -> x22, waiting for transfers between devices: 116 us -> 122 us  [along(): return lax.ppermute(value, axis, pairs)]
    pallas_call x2 -> x3, Pallas kernels: 9.56 us -> 11.1 us  [pair_tile(): pl.pallas_call(functools.partial(pair_kernel, index_of, line, first, side...]
  transfers between devices with their start and end apart: 23 -> 22, of which waited for: 12 -> 12; matrix products, arithmetic and copies ran while one was open for 0% -> 0% of each run, Pallas kernels for 17% -> 18%
where the time goes in v6:
time: 222 us
  waiting for transfers between devices  122 us (55%)
  Pallas kernels  41.4 us (19%)
  starting transfers between devices  27.2 us (12%)
  blocking collectives  23.8 us (11%)
  local copies, waits for them, and re-layouts  6 us (3%)
    ppermute x22, waiting for transfers between devices, along(): return lax.ppermute(value, axis, pairs)  122 us
    ppermute x22, starting transfers between devices, along(): return lax.ppermute(value, axis, pairs)  27.2 us
    all_to_all x1, blocking collectives, body(): parts = lax.all_to_all(parts, 'probe', 0, 0)  15.5 us
    pallas_call x3, Pallas kernels, pair_tile(): pl.pallas_call(functools.partial(pair_kernel, index_of, line, first, side...  11.1 us
    pallas_call x1, Pallas kernels, own_tile(): pl.pallas_call(functools.partial(own_kernel, steps, line), grid_spec=pltp...  10.8 us
    all_to_all x1, blocking collectives, body(): design = lax.all_to_all(copies, 'probe', 0, 0)  8.28 us
    pallas_call x1, Pallas kernels, descend(): pl.pallas_call(descend_kernel, out_shape=(jax.ShapeDtypeStruct((K, share)...  6.61 us
    unnamed x10, local copies, waits for them, and re-layouts  5.98 us
  transfers between devices with their start and end apart: 22, of which 12 were waited for; matrix products, arithmetic and copies ran while one was open for 0% of the time, Pallas kernels for 18%

profile of v6, /device:TPU:0, one launch (start us, length us, event | category | flops | bytes accessed | tf_op | source)
XLA Modules:
  0.0 221.8 jit_solution(10226972152722284465)
XLA Ops:
  1.2 2.2 copy-done
  5.0 4.5 %project.1 = (f32[8,64,128]{2,1,0:T(8,128)S(1)}, bf16[32,2048]{1,0:T(8,128)(2,1)S(1)}, bf16[256,2048]{1,0:T(8,128)(2,1)}, bf16[256,2048]{1,0:T(8,128)(2,1)}, bf16[256,2048]{1,0:T(8,128)(2,1)}) custom-call(s32[1]{0:T(128)} %bitcast.1.core_ref._, s32[64]{0:T(128)S(1)} %copy-done.4, bf16[64,2048]{1,0:T(8,128)(2,1)S(1)} %copy-done.3, bf16[1024,2048]{1,0:T(8,128)(2,1)S(1)} %copy-done), custom_call_target="tpu_custom_call" | custom-call | flops 134217728 | bytes 8388608 | tf_op jit(solution)/shard_map/project/pallas_call | solution.py:103
  9.5 15.5 %all_to_all.10.parts_ref = f32[8,64,128]{2,1,0:T(8,128)S(1)} all-to-all(f32[8,64,128]{2,1,0:T(8,128)S(1)} %get-tuple-element.23), channel_id=1, replica_groups=mesh['samp'=4,'probe'=8] {'probe'}, dimensions={0} | all-to-all | bytes 524288 | tf_op jit(solution)/shard_map/all_to_all | solution.py:592
  25.0 6.6 %descend.1 = (f32[32,128]{1,0:T(8,128)}, bf16[8,32,128]{2,1,0:T(8,128)(2,1)S(1)}) custom-call(f32[8,64,128]{2,1,0:T(8,128)S(1)} %all_to_all.10.parts_ref), custom_call_target="tpu_custom_call" | custom-call | flops 33554432 | bytes 16384 | tf_op jit(solution)/shard_map/descend/pallas_call | solution.py:197
  31.6 8.3 %all_to_all.11.design_ref = bf16[8,32,128]{2,1,0:T(8,128)(2,1)S(1)} all-to-all(bf16[8,32,128]{2,1,0:T(8,128)(2,1)S(1)} %get-tuple-element.24), channel_id=1, replica_groups=mesh['samp'=4,'probe'=8] {'probe'}, dimensions={0} | all-to-all | bytes 131072 | tf_op jit(solution)/shard_map/all_to_all | solution.py:594
  39.9 2.1 cross.1
  41.9 1.6 collective-permute-start.1
  43.5 7.0 %collective-permute-done.1 = f32[32,2304]{1,0:T(8,128)S(1)} collective-permute-done((f32[32,2304]{1,0:T(8,128)S(1)}, f32[32,2304]{1,0:T(8,128)S(1)}, u32[]{:S(2)}, u32[]{:S(2)}) %collective-permute-start.1) | collective-permute-done | bytes 294944 | tf_op jit(solution)/shard_map/ppermute | solution.py:555
  50.6 1.6 collective-permute-start.2
  52.2 6.2 %collective-permute-done.2.peer_ref = f32[32,2304]{1,0:T(8,128)S(1)} collective-permute-done((f32[32,2304]{1,0:T(8,128)S(1)}, f32[32,2304]{1,0:T(8,128)S(1)}, u32[]{:S(2)}, u32[]{:S(2)}) %collective-permute-start.2) | collective-permute-done | bytes 294944 | tf_op jit(solution)/shard_map/ppermute | solution.py:555
  58.4 3.8 %solve.1.facts_ref.refs_0_ = f32[40,2048]{1,0:T(8,128)S(1)} custom-call(f32[32,2304]{1,0:T(8,128)S(1)} %add.19.mine_ref, f32[32,2304]{1,0:T(8,128)S(1)} %collective-permute-done.2.peer_ref, bf16[32,2048]{1,0:T(8,128)(2,1)S(1)} %get-tuple-element.25.panel_ref), custom_call_target="tpu_custom_call" | custom-call | flops 104857600 | bytes 1310720 | tf_op jit(solution)/shard_map/solve/pallas_call | solution.py:289
  62.3 1.6 collective-permute-start.13
  65.1 1.5 collective-permute-start.6
  66.6 2.2 copy-done.2
  68.8 43.3 %collective-permute-done.6 = bf16[4,32,128]{2,1,0:T(8,128)(2,1)S(1)} collective-permute-done((bf16[4,32,128]{2,1,0:T(8,128)(2,1)S(1)}, bf16[4,32,128]{2,1,0:T(8,128)(2,1)S(1)}, u32[]{:S(2)}, u32[]{:S(2)}) %collective-permute-start.6) | collective-permute-done | bytes 32800 | tf_op jit(solution)/shard_map/ppermute | solution.py:555
  112.1 1.9 collective-permute-start.7
  114.0 10.8 %own.1 = (bf16[1024,4096]{1,0:T(8,128)(2,1)S(1)}, bf16[2,1024,128]{2,1,0:T(8,128)(2,1)S(1)}, f32[2,1024,128]{2,1,0:T(8,128)S(1)}) custom-call(s32[1]{0:T(128)} %bitcast.place_ref, s32[1]{0:T(128)} %bitcast.1.core_ref._, bf16[8,32,128]{2,1,0:T(8,128)(2,1)S(1)} %all_to_all.11.design_ref, bf16[1024,2048]{1,0:T(8,128)(2,1)} %from_ref.1, ...), custom_call_target="tpu_custom_call" | custom-call | flops 4294967296 | bytes 25165824 | tf_op jit(solution)/shard_map/own/pallas_call | solution.py:363
  124.9 3.2 %shard_map.51.refs_2_ = f32[1024,256]{1,0:T(8,128)S(1)} custom-call(s32[1]{0:T(128)} %bitcast.place_ref, bf16[2,32,128]{2,1,0:T(8,128)(2,1)S(1)} %slice.60.design_ref, bf16[1024,4096]{1,0:T(8,128)(2,1)S(1)} %get-tuple-element.28.zscore_ref, f32[40,2048]{1,0:T(8,128)S(1)} %solve.1.facts_ref.refs_0_, bf16[256,2048]{1,0:T(8,128)(2,1)} %collective-permute-done.13.refs_1_), custom_call_target="tpu_custom_call" | custom-call | flops 1073741824 | bytes 8388608 | tf_op jit(solution)/shard_map/pallas_call | solution.py:441
  128.1 3.2 %shard_map.52 = (bf16[1024,128]{1,0:T(8,128)(2,1)S(1)}, bf16[1024,128]{1,0:T(8,128)(2,1)S(1)}, bf16[1024,128]{1,0:T(8,128)(2,1)S(1)}, f32[1024,128]{1,0:T(8,128)S(1)}) custom-call(s32[1]{0:T(128)} %bitcast.place_ref, bf16[2,32,128]{2,1,0:T(8,128)(2,1)S(1)} %slice.60.design_ref, bf16[1024,4096]{1,0:T(8,128)(2,1)S(1)} %get-tuple-element.28.zscore_ref, ...), custom_call_target="tpu_custom_call" | custom-call | flops 1073741824 | bytes 8388608 | tf_op jit(solution)/shard_map/pallas_call | solution.py:441
  131.4 2.8 %collective-permute-start.14 = (bf16[1024,128]{1,0:T(8,128)(2,1)S(1)}, bf16[1024,128]{1,0:T(8,128)(2,1)S(1)}, u32[]{:S(2)}, u32[]{:S(2)}) collective-permute-start(bf16[1024,128]{1,0:T(8,128)(2,1)S(1)} %get-tuple-element.37), channel_id=1, source_target_pairs={{0,2},{1,3},{2,4},{3,5},{8,10},{9,11},{10,12},{11,13},{16,18},{17,... | collective-permute-start | bytes 786440 | tf_op jit(solution)/shard_map/ppermute | solution.py:555
  134.2 1.3 collective-permute-start.15
  136.2 2.4 %collective-permute-done.8.refs_3_ = bf16[256,2048]{1,0:T(8,128)(2,1)S(1)} collective-permute-done((bf16[256,2048]{1,0:T(8,128)(2,1)}, bf16[256,2048]{1,0:T(8,128)(2,1)S(1)}, u32[]{:S(2)}, u32[]{:S(2)}) %collective-permute-start.8) | collective-permute-done | bytes 1048608 | tf_op jit(solution)/shard_map/ppermute | solution.py:555
  138.7 21.5 %collective-permute-done.7.refs_2_ = bf16[256,2048]{1,0:T(8,128)(2,1)} collective-permute-done((bf16[256,2048]{1,0:T(8,128)(2,1)S(1)}, bf16[256,2048]{1,0:T(8,128)(2,1)}, u32[]{:S(2)}, u32[]{:S(2)}) %collective-permute-start.7) | collective-permute-done | bytes 1048608 | tf_op jit(solution)/shard_map/ppermute | solution.py:555
  160.2 4.6 %shard_map.50 = (bf16[1024,128]{1,0:T(8,128)(2,1)S(1)}, bf16[1024,128]{1,0:T(8,128)(2,1)S(1)}, bf16[1024,128]{1,0:T(8,128)(2,1)S(1)}, f32[1024,128]{1,0:T(8,128)S(1)}) custom-call(s32[1]{0:T(128)} %bitcast.place_ref, bf16[2,32,128]{2,1,0:T(8,128)(2,1)S(1)} %pad_maximum_fusion.3.design_ref, bf16[1024,4096]{1,0:T(8,128)(2,1)S(1)} %get-tuple-element.28.zscore_ref, ...), custom_call_target="tpu_custom_call" | custom-call | flops 2147483648 | bytes 8388608 | tf_op jit(solution)/shard_map/pallas_call | solution.py:441
  166.1 3.0 %collective-permute-start.11 = (bf16[1024,128]{1,0:T(8,128)(2,1)S(1)}, bf16[1024,128]{1,0:T(8,128)(2,1)S(1)}, u32[]{:S(2)}, u32[]{:S(2)}) collective-permute-start(bf16[1024,128]{1,0:T(8,128)(2,1)S(1)} %get-tuple-element.33), channel_id=1, source_target_pairs={{0,6},{1,7},{2,0},{3,1},{8,14},{9,15},{10,8},{11,9},{16,22},{17,23... | collective-permute-start | bytes 786440 | tf_op jit(solution)/shard_map/ppermute | solution.py:555
  170.4 11.5 %collective-permute-done.10.refs_2_ = bf16[1024,128]{1,0:T(8,128)(2,1)S(1)} collective-permute-done((bf16[1024,128]{1,0:T(8,128)(2,1)S(1)}, bf16[1024,128]{1,0:T(8,128)(2,1)S(1)}, u32[]{:S(2)}, u32[]{:S(2)}) %collective-permute-start.10) | collective-permute-done | bytes 262176 | tf_op jit(solution)/shard_map/ppermute | solution.py:555
  181.9 5.5 %collective-permute-done.11.refs_3_ = bf16[1024,128]{1,0:T(8,128)(2,1)S(1)} collective-permute-done((bf16[1024,128]{1,0:T(8,128)(2,1)S(1)}, bf16[1024,128]{1,0:T(8,128)(2,1)S(1)}, u32[]{:S(2)}, u32[]{:S(2)}) %collective-permute-start.11) | collective-permute-done | bytes 262176 | tf_op jit(solution)/shard_map/ppermute | solution.py:555
  187.8 1.5 collective-permute-start.17
  190.2 4.0 %collective-permute-done.17.same_ref = bf16[4,128,128]{2,1,0:T(8,128)(2,1)S(1)} collective-permute-done((bf16[4,128,128]{2,1,0:T(8,128)(2,1)S(1)}, bf16[4,128,128]{2,1,0:T(8,128)(2,1)S(1)}, u32[]{:S(2)}, u32[]{:S(2)}) %collective-permute-start.17) | collective-permute-done | bytes 131104 | tf_op jit(solution)/shard_map/ppermute | solution.py:555
  196.3 7.3 %collective-permute-done.4 = bf16[2,1024,128]{2,1,0:T(8,128)(2,1)S(1)} collective-permute-done((bf16[2,1024,128]{2,1,0:T(8,128)(2,1)S(1)}, bf16[2,1024,128]{2,1,0:T(8,128)(2,1)S(1)}, u32[]{:S(2)}, u32[]{:S(2)}) %collective-permute-start.4) | collective-permute-done | bytes 524320 | tf_op jit(solution)/shard_map/ppermute | solution.py:555
  203.8 3.0 %collective-permute-start.20 = (bf16[2,128,128]{2,1,0:T(8,128)(2,1)S(1)}, bf16[2,128,128]{2,1,0:T(8,128)(2,1)S(1)}, u32[]{:S(2)}, u32[]{:S(2)}) collective-permute-start(bf16[2,128,128]{2,1,0:T(8,128)(2,1)S(1)} %pad_maximum_fusion.1), channel_id=1, source_target_pairs={{0,4},{1,5},{2,6},{3,7},{4,0},{5,1},{6,2},{7,3},{8,12},{9,13},{10,... | collective-permute-start | bytes 196616 | tf_op jit(solution)/shard_map/ppermute | solution.py:555
  207.1 12.5 %collective-permute-done.5 = bf16[1,1024,128]{2,1,0:T(8,128)(2,1)S(1)} collective-permute-done((bf16[1,1024,128]{2,1,0:T(8,128)(2,1)S(1)}, bf16[1,1024,128]{2,1,0:T(8,128)(2,1)S(1)}, u32[]{:S(2)}, u32[]{:S(2)}) %collective-permute-start.5) | collective-permute-done | bytes 262176 | tf_op jit(solution)/shard_map/ppermute | solution.py:555
  (47 shorter events, 13.1 us)
Async XLA Ops:
  0.6 113.4 %collective-permute-start = (bf16[1024,2048]{1,0:T(8,128)(2,1)}, bf16[1024,2048]{1,0:T(8,128)(2,1)}, u32[]{:S(2)}, u32[]{:S(2)}) collective-permute-start(bf16[1024,2048]{1,0:T(8,128)(2,1)} %from_ref.1), channel_id=1, source_target_pairs={{0,1},{1,0},{2,3},{3,2},{4,5},{5,4},{6,7},{7,6},{8,9},{9,8},{10,11... | collective-permute-start | bytes 12582920 | tf_op jit(solution)/shard_map/ppermute | solution.py:555
  1.2 2.2 copy-start
  3.4 0.9 copy-start.3
  4.3 0.7 copy-start.4
  5.0 34.9 %copy-start.1 = (bf16[1024,2048]{1,0:T(8,128)(2,1)S(1)}, bf16[1024,2048]{1,0:T(8,128)(2,1)}, u32[]{:S(2)}) copy-start(bf16[1024,2048]{1,0:T(8,128)(2,1)} %from_ref.1) | copy-start | bytes 12582916
  41.9 8.6 %collective-permute-start.1 = (f32[32,2304]{1,0:T(8,128)S(1)}, f32[32,2304]{1,0:T(8,128)S(1)}, u32[]{:S(2)}, u32[]{:S(2)}) collective-permute-start(f32[32,2304]{1,0:T(8,128)S(1)} %cross.1), channel_id=1, source_target_pairs={{0,16},{8,24},{16,0},{24,8},{1,17},{9,25},{17,1},{25,9},{2,18},{10... | collective-permute-start | bytes 884744 | tf_op jit(solution)/shard_map/ppermute | solution.py:555
  50.6 7.8 %collective-permute-start.2 = (f32[32,2304]{1,0:T(8,128)S(1)}, f32[32,2304]{1,0:T(8,128)S(1)}, u32[]{:S(2)}, u32[]{:S(2)}) collective-permute-start(f32[32,2304]{1,0:T(8,128)S(1)} %add.19.mine_ref), channel_id=1, source_target_pairs={{0,8},{8,0},{16,24},{24,16},{1,9},{9,1},{17,25},{25,17},{2,10},{10... | collective-permute-start | bytes 884744 | tf_op jit(solution)/shard_map/ppermute | solution.py:555
  62.2 49.9 %collective-permute-start.3 = (f32[40,2048]{1,0:T(8,128)S(1)}, f32[40,2048]{1,0:T(8,128)S(1)}, u32[]{:S(2)}, u32[]{:S(2)}) collective-permute-start(f32[40,2048]{1,0:T(8,128)S(1)} %solve.1.facts_ref.refs_0_), channel_id=1, source_target_pairs={{0,1},{1,0},{2,3},{3,2},{4,5},{5,4},{6,7},{7,6},{8,9},{9,8},{10,11... | collective-permute-start | bytes 983048 | tf_op jit(solution)/shard_map/ppermute | solution.py:555
  62.3 62.6 %collective-permute-start.13 = (bf16[256,2048]{1,0:T(8,128)(2,1)}, bf16[256,2048]{1,0:T(8,128)(2,1)}, u32[]{:S(2)}, u32[]{:S(2)}) collective-permute-start(bf16[256,2048]{1,0:T(8,128)(2,1)} %get-tuple-element.35), channel_id=1, source_target_pairs={{0,8},{8,16},{16,24},{24,0},{1,9},{9,17},{17,25},{25,1},{2,10},{10... | collective-permute-start | bytes 3145736 | tf_op jit(solution)/shard_map/ppermute | solution.py:555
  63.8 64.3 %collective-permute-start.12 = (bf16[256,2048]{1,0:T(8,128)(2,1)}, bf16[256,2048]{1,0:T(8,128)(2,1)}, u32[]{:S(2)}, u32[]{:S(2)}) collective-permute-start(bf16[256,2048]{1,0:T(8,128)(2,1)} %get-tuple-element.34), channel_id=1, source_target_pairs={{0,9},{1,8},{2,11},{3,10},{4,13},{5,12},{6,15},{7,14},{8,17},{9,16... | collective-permute-start | bytes 3145736 | tf_op jit(solution)/shard_map/ppermute | solution.py:555
  65.1 47.0 %collective-permute-start.6 = (bf16[4,32,128]{2,1,0:T(8,128)(2,1)S(1)}, bf16[4,32,128]{2,1,0:T(8,128)(2,1)S(1)}, u32[]{:S(2)}, u32[]{:S(2)}) collective-permute-start(bf16[4,32,128]{2,1,0:T(8,128)(2,1)S(1)} %dynamic-slice_bitcast_fusion), channel_id=1, source_target_pairs={{0,8},{8,16},{16,24},{24,0},{1,9},{9,17},{17,25},{25,1},{2,10},{10... | collective-permute-start | bytes 98312 | tf_op jit(solution)/shard_map/ppermute | solution.py:555
  66.6 2.2 copy-start.2
  112.1 26.6 %collective-permute-start.8 = (bf16[256,2048]{1,0:T(8,128)(2,1)}, bf16[256,2048]{1,0:T(8,128)(2,1)S(1)}, u32[]{:S(2)}, u32[]{:S(2)}) collective-permute-start(bf16[256,2048]{1,0:T(8,128)(2,1)} %get-tuple-element.29), channel_id=1, source_target_pairs={{0,9},{1,8},{2,11},{3,10},{4,13},{5,12},{6,15},{7,14},{8,17},{9,16... | collective-permute-start | bytes 3145736 | tf_op jit(solution)/shard_map/ppermute | solution.py:555
  112.1 48.1 %collective-permute-start.7 = (bf16[256,2048]{1,0:T(8,128)(2,1)S(1)}, bf16[256,2048]{1,0:T(8,128)(2,1)}, u32[]{:S(2)}, u32[]{:S(2)}) collective-permute-start(bf16[256,2048]{1,0:T(8,128)(2,1)S(1)} %pick_ends.1), channel_id=1, source_target_pairs={{0,8},{8,16},{16,24},{24,0},{1,9},{9,17},{17,25},{25,1},{2,10},{10... | collective-permute-start | bytes 3145736 | tf_op jit(solution)/shard_map/ppermute | solution.py:555
  131.4 37.7 %collective-permute-start.14 = (bf16[1024,128]{1,0:T(8,128)(2,1)S(1)}, bf16[1024,128]{1,0:T(8,128)(2,1)S(1)}, u32[]{:S(2)}, u32[]{:S(2)}) collective-permute-start(bf16[1024,128]{1,0:T(8,128)(2,1)S(1)} %get-tuple-element.37), channel_id=1, source_target_pairs={{0,2},{1,3},{2,4},{3,5},{8,10},{9,11},{10,12},{11,13},{16,18},{17,... | collective-permute-start | bytes 786440 | tf_op jit(solution)/shard_map/ppermute | solution.py:555
  134.2 36.2 %collective-permute-start.15 = (bf16[1024,128]{1,0:T(8,128)(2,1)S(1)}, bf16[1024,128]{1,0:T(8,128)(2,1)S(1)}, u32[]{:S(2)}, u32[]{:S(2)}) collective-permute-start(bf16[1024,128]{1,0:T(8,128)(2,1)S(1)} %get-tuple-element.38), channel_id=1, source_target_pairs={{0,4},{1,5},{6,2},{7,3},{8,12},{9,13},{14,10},{15,11},{16,20},{17,... | collective-permute-start | bytes 786440 | tf_op jit(solution)/shard_map/ppermute | solution.py:555
  135.5 34.8 %collective-permute-start.16 = (bf16[1024,128]{1,0:T(8,128)(2,1)S(1)}, bf16[1024,128]{1,0:T(8,128)(2,1)S(1)}, u32[]{:S(2)}, u32[]{:S(2)}) collective-permute-start(bf16[1024,128]{1,0:T(8,128)(2,1)S(1)} %get-tuple-element.39), channel_id=1, source_target_pairs={{4,2},{5,3},{6,4},{7,5},{12,10},{13,11},{14,12},{15,13},{20,18},{2... | collective-permute-start | bytes 786440 | tf_op jit(solution)/shard_map/ppermute | solution.py:555
  164.8 17.1 %collective-permute-start.10 = (bf16[1024,128]{1,0:T(8,128)(2,1)S(1)}, bf16[1024,128]{1,0:T(8,128)(2,1)S(1)}, u32[]{:S(2)}, u32[]{:S(2)}) collective-permute-start(bf16[1024,128]{1,0:T(8,128)(2,1)S(1)} %get-tuple-element.32), channel_id=1, source_target_pairs={{2,6},{3,7},{4,0},{5,1},{10,14},{11,15},{12,8},{13,9},{18,22},{19,... | collective-permute-start | bytes 786440 | tf_op jit(solution)/shard_map/ppermute | solution.py:555
  166.1 21.3 %collective-permute-start.11 = (bf16[1024,128]{1,0:T(8,128)(2,1)S(1)}, bf16[1024,128]{1,0:T(8,128)(2,1)S(1)}, u32[]{:S(2)}, u32[]{:S(2)}) collective-permute-start(bf16[1024,128]{1,0:T(8,128)(2,1)S(1)} %get-tuple-element.33), channel_id=1, source_target_pairs={{0,6},{1,7},{2,0},{3,1},{8,14},{9,15},{10,8},{11,9},{16,22},{17,23... | collective-permute-start | bytes 786440 | tf_op jit(solution)/shard_map/ppermute | solution.py:555
  169.1 18.3 %collective-permute-start.9 = (bf16[1024,128]{1,0:T(8,128)(2,1)S(1)}, bf16[1024,128]{1,0:T(8,128)(2,1)S(1)}, u32[]{:S(2)}, u32[]{:S(2)}) collective-permute-start(bf16[1024,128]{1,0:T(8,128)(2,1)S(1)} %get-tuple-element.31), channel_id=1, source_target_pairs={{4,6},{5,7},{6,0},{7,1},{12,14},{13,15},{14,8},{15,9},{20,22},{21,... | collective-permute-start | bytes 786440 | tf_op jit(solution)/shard_map/ppermute | solution.py:555
  187.8 6.4 %collective-permute-start.17 = (bf16[4,128,128]{2,1,0:T(8,128)(2,1)S(1)}, bf16[4,128,128]{2,1,0:T(8,128)(2,1)S(1)}, u32[]{:S(2)}, u32[]{:S(2)}) collective-permute-start(bf16[4,128,128]{2,1,0:T(8,128)(2,1)S(1)} %get-tuple-element.41), channel_id=1, source_target_pairs={{0,24},{8,0},{16,8},{24,16},{1,25},{9,1},{17,9},{25,17},{2,26},{10... | collective-permute-start | bytes 393224 | tf_op jit(solution)/shard_map/ppermute | solution.py:555
  189.3 14.3 %collective-permute-start.4 = (bf16[2,1024,128]{2,1,0:T(8,128)(2,1)S(1)}, bf16[2,1024,128]{2,1,0:T(8,128)(2,1)S(1)}, u32[]{:S(2)}, u32[]{:S(2)}) collective-permute-start(bf16[2,1024,128]{2,1,0:T(8,128)(2,1)S(1)} %get-tuple-element.27), channel_id=1, source_target_pairs={{0,2},{1,3},{2,0},{3,1},{4,6},{5,7},{6,4},{7,5},{8,10},{9,11},{10,... | collective-permute-start | bytes 1572872 | tf_op jit(solution)/shard_map/ppermute | solution.py:555
  189.3 5.9 %collective-permute-start.18 = (bf16[4,128,128]{2,1,0:T(8,128)(2,1)S(1)}, bf16[4,128,128]{2,1,0:T(8,128)(2,1)S(1)}, u32[]{:S(2)}, u32[]{:S(2)}) collective-permute-start(bf16[4,128,128]{2,1,0:T(8,128)(2,1)S(1)} %get-tuple-element.42), channel_id=1, source_target_pairs={{0,25},{1,24},{2,27},{3,26},{4,29},{5,28},{6,31},{7,30},{8,1},{9,0... | collective-permute-start | bytes 393224 | tf_op jit(solution)/shard_map/ppermute | solution.py:555
  195.2 25.4 %collective-permute-start.21 = (bf16[2,128,128]{2,1,0:T(8,128)(2,1)S(1)}, bf16[2,128,128]{2,1,0:T(8,128)(2,1)S(1)}, u32[]{:S(2)}, u32[]{:S(2)}) collective-permute-start(bf16[2,128,128]{2,1,0:T(8,128)(2,1)S(1)} %pad_maximum_fusion.2), channel_id=1, source_target_pairs={{0,6},{1,7},{2,0},{3,1},{4,2},{5,3},{6,4},{7,5},{8,14},{9,15},{10,... | collective-permute-start | bytes 196616 | tf_op jit(solution)/shard_map/ppermute | solution.py:555
  203.7 15.9 %collective-permute-start.5 = (bf16[1,1024,128]{2,1,0:T(8,128)(2,1)S(1)}, bf16[1,1024,128]{2,1,0:T(8,128)(2,1)S(1)}, u32[]{:S(2)}, u32[]{:S(2)}) collective-permute-start(bf16[1,1024,128]{2,1,0:T(8,128)(2,1)S(1)} %get-tuple-element.44), channel_id=1, source_target_pairs={{0,4},{1,5},{2,6},{3,7},{4,0},{5,1},{6,2},{7,3},{8,12},{9,13},{10,... | collective-permute-start | bytes 786440 | tf_op jit(solution)/shard_map/ppermute | solution.py:555
  203.8 17.1 %collective-permute-start.20 = (bf16[2,128,128]{2,1,0:T(8,128)(2,1)S(1)}, bf16[2,128,128]{2,1,0:T(8,128)(2,1)S(1)}, u32[]{:S(2)}, u32[]{:S(2)}) collective-permute-start(bf16[2,128,128]{2,1,0:T(8,128)(2,1)S(1)} %pad_maximum_fusion.1), channel_id=1, source_target_pairs={{0,4},{1,5},{2,6},{3,7},{4,0},{5,1},{6,2},{7,3},{8,12},{9,13},{10,... | collective-permute-start | bytes 196616 | tf_op jit(solution)/shard_map/ppermute | solution.py:555
  206.8 14.1 %collective-permute-start.19 = (bf16[2,128,128]{2,1,0:T(8,128)(2,1)S(1)}, bf16[2,128,128]{2,1,0:T(8,128)(2,1)S(1)}, u32[]{:S(2)}, u32[]{:S(2)}) collective-permute-start(bf16[2,128,128]{2,1,0:T(8,128)(2,1)S(1)} %pad_maximum_fusion), channel_id=1, source_target_pairs={{0,2},{1,3},{2,4},{3,5},{4,6},{5,7},{6,0},{7,1},{8,10},{9,11},{10,... | collective-permute-start | bytes 196616 | tf_op jit(solution)/shard_map/ppermute | solution.py:555

commit v7 on v6

--- a/solution.py
+++ b/solution.py
@@ -306,10 +306,29 @@
         store(at, width, (left * rate[:, cols]).astype(BF16))
 
 
+def relayed(place, line):
+    far = jnp.where(place <= 1, line - 1, 0)
+    return jnp.where((place <= 1) | (place >= line - 2), lax.rem(far - place + line, line), 0)
+
+
+def put_tile(part, own, sends, keep_ref):
+    share = keep_ref.shape[1]
+    keep = None
+    for j, ref in enumerate(sends):
+        block = part[:, j * share : (j + 1) * share]
+        ref[...] = block.astype(BF16)
+        mine = jnp.where(own == j, block, 0.0)
+        keep = mine if keep is None else keep + mine
+    keep_ref[...] = keep
+
+
 def own_kernel(
     steps, line, place_ref, core_ref, design_ref, mine_ref, theirs_ref, facts_ref, more_ref, *refs
 ):
-    z_ref, swap_ref, keep_ref, half_ref, terms_ref, moreterms_ref = refs
+    (z_ref, *sends), (keep_ref, half_ref, terms_ref, moreterms_ref) = (
+        refs[: line + 1],
+        refs[line + 1 :],
+    )
     step = pl.program_id(0)
     blocks, kk, share = design_ref.shape
     chunk, probes = mine_ref.shape
@@ -334,17 +353,16 @@
         )
         for b in range(blocks // 2):
             here = pl.ds(pl.multiple_of(step * chunk + (2 * b + core) * share, share), share)
-            slot = jnp.bitwise_xor(step * (blocks // 2) + b, place)
+            away = lax.rem(step * (blocks // 2) + b - place + line, line)
+            skipped = relayed(place, line)
+            slot = jnp.where(away == 0, skipped, jnp.where(away == skipped, 0, away))
             half_ref[pl.ds(pl.multiple_of(slot * share, share), share), :] = z_ref[here, :]
 
     @pl.when(step >= steps)
     def _():
-        tall = keep_ref.shape[1]
+        tall = keep_ref.shape[0]
         rows = pl.ds(pl.multiple_of((step - steps) * tall, tall), tall)
-        part = nt(z_ref[rows, :], half_ref[...])
-        for slot in range(0, line, 2):
-            keep_ref[slot // 2] = part[:, slot * share : (slot + 1) * share]
-            swap_ref[slot // 2] = part[:, (slot + 1) * share : (slot + 2) * share].astype(BF16)
+        put_tile(nt(z_ref[rows, :], half_ref[...]), relayed(place, line), sends, keep_ref)
 
 
 def own_tile(at, line, design, mine, theirs, facts, more):
@@ -373,7 +391,7 @@
                 whole,
             ],
             out_specs=[pl.BlockSpec(memory_space=pltpu.VMEM)]
-            + [pl.BlockSpec((line // 2, tall, share), lambda i, *_: (0, *second(i)))] * 2,
+            + [pl.BlockSpec((tall, share), second)] * (line + 1),
             scratch_shapes=[
                 pltpu.VMEM((rows // 2, 2 * probes), BF16),
                 pltpu.VMEM((3 * K, probes), BF16),
@@ -381,7 +399,8 @@
             ],
         ),
         out_shape=[pltpu.VMEM((rows, 2 * probes), BF16)]
-        + [jax.ShapeDtypeStruct((line // 2, rows, share), dtype) for dtype in (BF16, F32)],
+        + [jax.ShapeDtypeStruct((rows, share), BF16)] * line
+        + [jax.ShapeDtypeStruct((rows, share), F32)],
         compiler_params=params("arbitrary"),
         cost_estimate=cost(2 * rows * rows * probes, 12 * rows * probes),
         name="own",
@@ -394,7 +413,7 @@
     outs, (z_ref, *terms) = refs[: -1 - sides], refs[-1 - sides :]
     blocks, kk, share = design_ref.shape
     probes = facts[0].shape[1]
-    tall = outs[0].shape[0]
+    tall = outs[0].shape[-2]
     step, place = pl.program_id(0), place_ref[0]
 
     @pl.when(step == 0)
@@ -416,6 +435,15 @@
             part = part + given_ref[rows, :]
         if not last:
             outs[0][...] = part
+            return
+        if index_of is None:
+            swap_ref, keep_ref = outs
+            odd = lax.rem(place, 2) == 1
+            for k in range(blocks // 2):
+                low = part[:, 2 * k * share : (2 * k + 1) * share]
+                high = part[:, (2 * k + 1) * share : (2 * k + 2) * share]
+                swap_ref[k] = jnp.where(odd, low, high).astype(BF16)
+                keep_ref[k] = jnp.where(odd, high, low)
             return
         *sends, keep_ref = outs
         for j, ref in enumerate([keep_ref, *sends]):
@@ -438,17 +466,23 @@
     column = pl.BlockSpec((tall, width), lambda i, *_: (jnp.maximum(i - 1, 0), 0))
     whole = jax.ShapeDtypeStruct((rows, width), F32)
     sends = [jax.ShapeDtypeStruct((rows, share), BF16)] * (line - 1)
+    out_specs = [column] * line if last else [column]
+    out_shape = sends + [whole] if last else [whole]
+    if last and index_of is None:
+        halves = (blocks // 2, tall, share)
+        out_specs = [pl.BlockSpec(halves, lambda i, *_: (0, jnp.maximum(i - 1, 0), 0))] * 2
+        out_shape = [jax.ShapeDtypeStruct((blocks // 2, rows, share), t) for t in (BF16, F32)]
     return pl.pallas_call(
         functools.partial(pair_kernel, index_of, line, first, sides, bool(given), last),
         grid_spec=pltpu.PrefetchScalarGridSpec(
             num_scalar_prefetch=1,
             grid=(1 + rows // tall,),
             in_specs=[pl.BlockSpec(memory_space=pltpu.VMEM)] * (2 + 2 * sides + len(given)),
-            out_specs=[column] * line if last else [column],
+            out_specs=out_specs,
             scratch_shapes=[pltpu.VMEM((blocks * share, sides * probes), BF16)]
             + [pltpu.VMEM((3 * K, probes), BF16)] * sides,
         ),
-        out_shape=sends + [whole] if last else [whole],
+        out_shape=out_shape,
         compiler_params=params("arbitrary"),
         cost_estimate=cost(2 * rows * blocks * share * sides * probes, 4 * rows * probes),
     )(at[0], design, zscore, *facts, *raws, *given)
@@ -577,10 +611,6 @@
     quarter = line // 4
     ends = [*range(quarter), *range(line - quarter, line)]
     inner = [*range(quarter, line - quarter)]
-
-    def among_ends(to):
-        high = to >= line - quarter
-        return jnp.where(high, to - (line - 2 * quarter), to), (to < quarter) | high
 
     def among_inner(to):
         return to - quarter, (to >= quarter) & (to < line - quarter)
@@ -612,33 +642,46 @@
     def arrivals(sends, among):
         return [on_line(value, round_of(j, among)) for j, value in enumerate(sends, 1)]
 
-
-    zscore, swap, keep = own_tile(at, line, design, methyl, theirs, facts, more)
-    given = on_line(swap, [(i, i ^ 1) for i in range(line)])
+    def near_round(by):
+        return [(i, to) for i, to in round_of(by) if line <= 3 or abs(to - i) < line - 1]
+
+    zscore, *own_sends, own_keep = own_tile(at, line, design, methyl, theirs, facts, more)
+    relay = on_line(own_sends[0], [(0, 1), (line - 1, line - 2)])
+    late = sorted({2, line - 2})
+    own_parts = [
+        on_line(own_sends[j], near_round(j)) for j in range(1, line) if j not in late
+    ]
     design_ends = jnp.concatenate([design_before[:quarter], design_before[line - quarter :]])
-    *sends, pair_keep = pair_tile(
-        among_ends, at, line, design_ends, zscore, 0, [facts, more],
+    swap, keep = pair_tile(
+        None, at, line, design_ends, zscore, 0, [facts, more],
         [ends_mine, ends_theirs],
     )
-    pair_parts = [pair_keep] + arrivals(sends, ends)
-    bit = 2
-    while bit < line:
-        swap = keep[1::2] + given[1::2].astype(F32)
-        keep = keep[::2] + given[::2].astype(F32)
-        given = on_line(swap.astype(BF16), [(i, i ^ bit) for i in range(line)])
-        bit *= 2
-    own_keep, own_parts = keep[0], [given[0]]
+    given = on_line(swap, [(i, i ^ 1) for i in range(line)])
+    for j in late:
+        passing = ((place == 1) & (j == line - 2)) | ((place == line - 2) & (j == 2))
+        joined = (own_sends[0].astype(F32) + relay.astype(F32)).astype(BF16)
+        own_parts.append(on_line(jnp.where(passing, joined, own_sends[j]), near_round(j)))
     design_inner = design_before[quarter : line - quarter]
     (partial,) = pair_tile(
         among_inner, at, line, design_inner, zscore, 0, [facts], [inner_mine],
         last=False,
     )
+    keep = keep + given.astype(F32)
+
+    def sum_for(to):
+        if quarter == 1:
+            return keep[0]
+        which = jnp.where(to >= line - quarter, to - line + 2 * quarter, to) // 2
+        return lax.dynamic_index_in_dim(keep, jnp.clip(which, 0, quarter - 1), 0, False)
+
+    pair_parts = [jnp.where((place < quarter) | (place >= line - quarter), sum_for(place), 0.0)]
+    for j in range(2, line, 2):
+        pair_parts.append(on_line(sum_for((place + j) % line).astype(BF16), round_of(j, ends)))
     *sends, pair_keep = pair_tile(
         among_inner, at, line, design_inner, zscore, 1, [more], [inner_theirs],
         given=partial,
     )
-    pair_parts.append(pair_keep)
-    pair_parts += arrivals(sends, inner)
+    pair_parts += [pair_keep] + arrivals(sends, inner)
     left, same, other = fold(at, line, pair_parts)
     same = to_panel(same, -1)
     other = to_panel_sibling(other, -1)

time: 222 us -> 212 us (0.955)
  waiting for transfers between devices: 122 us -> 93.9 us
  starting transfers between devices: 27.2 us -> 35.5 us
  local copies, waits for them, and re-layouts: 6 us -> 11.7 us
  other arithmetic: 0.15 us -> 2.84 us
    ppermute x22 -> x23, waiting for transfers between devices: 122 us -> 93.9 us  [along(): return lax.ppermute(value, axis, pairs)]
    ppermute x22 -> x23, starting transfers between devices: 27.2 us -> 35.5 us  [along(): return lax.ppermute(value, axis, pairs)]
    unnamed x10 -> x34, local copies, waits for them, and re-layouts: 5.98 us -> 11.7 us
  transfers between devices with their start and end apart: 22 -> 23, of which waited for: 12 -> 10; matrix products, arithmetic and copies ran while one was open for 0% -> 1% of each run, Pallas kernels for 18% -> 20%
where the time goes in v7:
time: 212 us
  waiting for transfers between devices  93.9 us (44%)
  Pallas kernels  42.9 us (20%)
  starting transfers between devices  35.5 us (17%)
  blocking collectives  23.8 us (11%)
  local copies, waits for them, and re-layouts  11.7 us (6%)
  other arithmetic  2.84 us (1%)
    ppermute x23, waiting for transfers between devices, along(): return lax.ppermute(value, axis, pairs)  93.9 us
    ppermute x23, starting transfers between devices, along(): return lax.ppermute(value, axis, pairs)  35.5 us
    all_to_all x1, blocking collectives, body(): parts = lax.all_to_all(parts, 'probe', 0, 0)  15.5 us
    pallas_call x3, Pallas kernels, pair_tile(): pl.pallas_call(functools.partial(pair_kernel, index_of, line, first, side...  12.6 us
    unnamed x34, local copies, waits for them, and re-layouts  11.7 us
    pallas_call x1, Pallas kernels, own_tile(): pl.pallas_call(functools.partial(own_kernel, steps, line), grid_spec=pltp...  10.7 us
    all_to_all x1, blocking collectives, body(): design = lax.all_to_all(copies, 'probe', 0, 0)  8.28 us
    pallas_call x1, Pallas kernels, descend(): pl.pallas_call(descend_kernel, out_shape=(jax.ShapeDtypeStruct((K, share)...  6.61 us
  transfers between devices with their start and end apart: 23, of which 10 were waited for; matrix products, arithmetic and copies ran while one was open for 1% of the time, Pallas kernels for 20%

profile of v7, /device:TPU:0, one launch (start us, length us, event | category | flops | bytes accessed | tf_op | source)
XLA Modules:
  0.0 211.6 jit_solution(3296684314723672983)
XLA Ops:
  1.2 2.2 %copy-done.2 = bf16[1024,2048]{1,0:T(8,128)(2,1)S(1)} copy-done((bf16[1024,2048]{1,0:T(8,128)(2,1)S(1)}, bf16[1024,2048]{1,0:T(8,128)(2,1)}, u32[]{:S(2)}) %copy-start.2) | copy-done | bytes 4194328
  5.0 3.7 %project.1 = (f32[8,64,128]{2,1,0:T(8,128)S(1)}, bf16[32,2048]{1,0:T(8,128)(2,1)S(1)}, bf16[256,2048]{1,0:T(8,128)(2,1)}, bf16[256,2048]{1,0:T(8,128)(2,1)S(1)}, bf16[256,2048]{1,0:T(8,128)(2,1)S(1)}) custom-call(s32[1]{0:T(128)} %bitcast.1.core_ref._, s32[64]{0:T(128)S(1)} %copy-done.11, bf16[64,2048]{1,0:T(8,128)(2,1)S(1)} %copy-done.4, ...), custom_call_target="tpu_custom_call" | custom-call | flops 134217728 | bytes 8388608 | tf_op jit(solution)/shard_map/project/pallas_call | solution.py:103
  8.7 15.5 %all_to_all.10.parts_ref = f32[8,64,128]{2,1,0:T(8,128)S(1)} all-to-all(f32[8,64,128]{2,1,0:T(8,128)S(1)} %get-tuple-element.24), channel_id=1, replica_groups=mesh['samp'=4,'probe'=8] {'probe'}, dimensions={0} | all-to-all | bytes 524288 | tf_op jit(solution)/shard_map/all_to_all | solution.py:622
  24.2 6.6 %descend.1 = (f32[32,128]{1,0:T(8,128)}, bf16[8,32,128]{2,1,0:T(8,128)(2,1)S(1)}) custom-call(f32[8,64,128]{2,1,0:T(8,128)S(1)} %all_to_all.10.parts_ref), custom_call_target="tpu_custom_call" | custom-call | flops 33554432 | bytes 16384 | tf_op jit(solution)/shard_map/descend/pallas_call | solution.py:197
  30.8 8.3 %all_to_all.11.design_ref = bf16[8,32,128]{2,1,0:T(8,128)(2,1)S(1)} all-to-all(bf16[8,32,128]{2,1,0:T(8,128)(2,1)S(1)} %get-tuple-element.25), channel_id=1, replica_groups=mesh['samp'=4,'probe'=8] {'probe'}, dimensions={0} | all-to-all | bytes 131072 | tf_op jit(solution)/shard_map/all_to_all | solution.py:624
  39.1 2.1 cross.1
  41.2 1.6 collective-permute-start.1
  42.8 7.0 %collective-permute-done.1 = f32[32,2304]{1,0:T(8,128)S(1)} collective-permute-done((f32[32,2304]{1,0:T(8,128)S(1)}, f32[32,2304]{1,0:T(8,128)S(1)}, u32[]{:S(2)}, u32[]{:S(2)}) %collective-permute-start.1) | collective-permute-done | bytes 294944 | tf_op jit(solution)/shard_map/ppermute | solution.py:589
  49.8 1.6 collective-permute-start.2
  51.4 6.2 %collective-permute-done.2.peer_ref = f32[32,2304]{1,0:T(8,128)S(1)} collective-permute-done((f32[32,2304]{1,0:T(8,128)S(1)}, f32[32,2304]{1,0:T(8,128)S(1)}, u32[]{:S(2)}, u32[]{:S(2)}) %collective-permute-start.2) | collective-permute-done | bytes 294944 | tf_op jit(solution)/shard_map/ppermute | solution.py:589
  57.6 3.8 %solve.1.facts_ref.refs_0_ = f32[40,2048]{1,0:T(8,128)S(1)} custom-call(f32[32,2304]{1,0:T(8,128)S(1)} %add.19.mine_ref, f32[32,2304]{1,0:T(8,128)S(1)} %collective-permute-done.2.peer_ref, bf16[32,2048]{1,0:T(8,128)(2,1)S(1)} %get-tuple-element.26.panel_ref), custom_call_target="tpu_custom_call" | custom-call | flops 104857600 | bytes 1310720 | tf_op jit(solution)/shard_map/solve/pallas_call | solution.py:289
  61.5 1.6 collective-permute-start.10
  63.2 1.5 collective-permute-start.9
  66.2 45.0 %collective-permute-done.8 = bf16[4,32,128]{2,1,0:T(8,128)(2,1)S(1)} collective-permute-done((bf16[4,32,128]{2,1,0:T(8,128)(2,1)S(1)}, bf16[4,32,128]{2,1,0:T(8,128)(2,1)S(1)}, u32[]{:S(2)}, u32[]{:S(2)}) %collective-permute-start.8) | collective-permute-done | bytes 32800 | tf_op jit(solution)/shard_map/ppermute | solution.py:589
  113.2 10.7 %own.1 = (bf16[1024,4096]{1,0:T(8,128)(2,1)S(1)}, bf16[1024,128]{1,0:T(8,128)(2,1)S(1)}, bf16[1024,128]{1,0:T(8,128)(2,1)S(1)}, bf16[1024,128]{1,0:T(8,128)(2,1)...) custom-call(s32[1]{0:T(128)} %bitcast.place_ref, s32[1]{0:T(128)} %bitcast.1.core_ref._, ...), custom_call_target="tpu_custom_call" | custom-call | flops 4294967296 | bytes 25165824 | tf_op jit(solution)/shard_map/own/pallas_call | solution.py:381
  126.0 5.4 %shard_map.50 = (bf16[1,1024,128]{2,1,0:T(8,128)(2,1)S(1)}, f32[1,1024,128]{2,1,0:T(8,128)S(1)}) custom-call(s32[1]{0:T(128)} %bitcast.place_ref, bf16[2,32,128]{2,1,0:T(8,128)(2,1)S(1)} %pad_maximum_fusion.3.design_ref, bf16[1024,4096]{1,0:T(8,128)(2,1)S(1)} %get-tuple-element.32.zscore_ref, f32[40,2048]{1,0:T(8,128)S(1)} %solve.1.facts_ref.refs_0_, ...), custom_call_target="tpu_custom_call" | custom-call | flops 2147483648 | bytes 8388608 | tf_op jit(solution)/shard_map/pallas_call | solution.py:475
  132.5 6.1 %collective-permute-done.14.refs_1_ = bf16[256,2048]{1,0:T(8,128)(2,1)} collective-permute-done((bf16[256,2048]{1,0:T(8,128)(2,1)}, bf16[256,2048]{1,0:T(8,128)(2,1)}, u32[]{:S(2)}, u32[]{:S(2)}) %collective-permute-start.14) | collective-permute-done | bytes 1048608 | tf_op jit(solution)/shard_map/ppermute | solution.py:589
  138.5 3.4 %copy-done.1 = bf16[1024,4096]{1,0:T(8,128)(2,1)S(1)} copy-done((bf16[1024,4096]{1,0:T(8,128)(2,1)S(1)}, bf16[1024,4096]{1,0:T(8,128)(2,1)}, u32[]{:S(2)}) %copy-start.1) | copy-done | bytes 8388632
  141.9 3.2 %shard_map.51.refs_2_ = f32[1024,256]{1,0:T(8,128)S(1)} custom-call(s32[1]{0:T(128)} %bitcast.place_ref, bf16[2,32,128]{2,1,0:T(8,128)(2,1)S(1)} %slice.38.design_ref, bf16[1024,4096]{1,0:T(8,128)(2,1)S(1)} %copy-done.1, f32[40,2048]{1,0:T(8,128)S(1)} %solve.1.facts_ref.refs_0_, bf16[256,2048]{1,0:T(8,128)(2,1)} %collective-permute-done.14.refs_1_), custom_call_target="tpu_custom_call" | custom-call | flops 1073741824 | bytes 8388608 | tf_op jit(solution)/shard_map/pallas_call | solution.py:475
  145.2 13.1 %collective-permute-done.13.refs_1_ = bf16[256,2048]{1,0:T(8,128)(2,1)} collective-permute-done((bf16[256,2048]{1,0:T(8,128)(2,1)}, bf16[256,2048]{1,0:T(8,128)(2,1)}, u32[]{:S(2)}, u32[]{:S(2)}) %collective-permute-start.13) | collective-permute-done | bytes 1048608 | tf_op jit(solution)/shard_map/ppermute | solution.py:589
  158.2 4.0 %shard_map.52 = (bf16[1024,128]{1,0:T(8,128)(2,1)}, bf16[1024,128]{1,0:T(8,128)(2,1)}, bf16[1024,128]{1,0:T(8,128)(2,1)}, f32[1024,128]{1,0:T(8,128)S(1)}) custom-call(s32[1]{0:T(128)} %bitcast.place_ref, bf16[2,32,128]{2,1,0:T(8,128)(2,1)S(1)} %slice.38.design_ref, bf16[1024,4096]{1,0:T(8,128)(2,1)S(1)} %copy-done.1, ...), custom_call_target="tpu_custom_call" | custom-call | flops 1073741824 | bytes 8388608 | tf_op jit(solution)/shard_map/pallas_call | solution.py:475
  162.2 2.8 %collective-permute-start.15 = (bf16[1024,128]{1,0:T(8,128)(2,1)}, bf16[1024,128]{1,0:T(8,128)(2,1)S(1)}, u32[]{:S(2)}, u32[]{:S(2)}) collective-permute-start(bf16[1024,128]{1,0:T(8,128)(2,1)} %get-tuple-element.39), channel_id=1, source_target_pairs={{0,2},{1,3},{2,4},{3,5},{8,10},{9,11},{10,12},{11,13},{16,18},{17,... | collective-permute-start | bytes 786440 | tf_op jit(solution)/shard_map/ppermute | solution.py:589
  168.4 1.7 fusion.1
  171.5 7.5 %collective-permute-start.6 = (bf16[1024,128]{1,0:T(8,128)(2,1)S(1)}, bf16[1024,128]{1,0:T(8,128)(2,1)}, u32[]{:S(2)}, u32[]{:S(2)}) collective-permute-start(bf16[1024,128]{1,0:T(8,128)(2,1)S(1)} %copy-done.6), channel_id=1, source_target_pairs={{0,2},{1,3},{6,4},{7,5},{8,10},{9,11},{14,12},{15,13},{16,18},{17,... | collective-permute-start | bytes 786440 | tf_op jit(solution)/shard_map/ppermute | solution.py:589
  182.3 5.8 %collective-permute-done.12.refs_1_ = bf16[1024,128]{1,0:T(8,128)(2,1)S(1)} collective-permute-done((bf16[1024,128]{1,0:T(8,128)(2,1)}, bf16[1024,128]{1,0:T(8,128)(2,1)S(1)}, u32[]{:S(2)}, u32[]{:S(2)}) %collective-permute-start.12) | collective-permute-done | bytes 262176 | tf_op jit(solution)/shard_map/ppermute | solution.py:589
  192.3 1.7 collective-permute-start.19
  193.9 2.4 %collective-permute-done.18.same_ref = bf16[4,128,128]{2,1,0:T(8,128)(2,1)S(1)} collective-permute-done((bf16[4,128,128]{2,1,0:T(8,128)(2,1)S(1)}, bf16[4,128,128]{2,1,0:T(8,128)(2,1)S(1)}, u32[]{:S(2)}, u32[]{:S(2)}) %collective-permute-start.18) | collective-permute-done | bytes 131104 | tf_op jit(solution)/shard_map/ppermute | solution.py:589
  196.4 1.8 collective-permute-done.19.other_ref
  198.2 2.7 %collective-permute-start.21 = (bf16[2,128,128]{2,1,0:T(8,128)(2,1)S(1)}, bf16[2,128,128]{2,1,0:T(8,128)(2,1)S(1)}, u32[]{:S(2)}, u32[]{:S(2)}) collective-permute-start(bf16[2,128,128]{2,1,0:T(8,128)(2,1)S(1)} %pad_maximum_fusion.1), channel_id=1, source_target_pairs={{0,4},{1,5},{2,6},{3,7},{4,0},{5,1},{6,2},{7,3},{8,12},{9,13},{10,... | collective-permute-start | bytes 196616 | tf_op jit(solution)/shard_map/ppermute | solution.py:589
  201.0 2.1 collective-permute-start.20
  203.1 4.8 %collective-permute-done.7.refs_2_ = bf16[1024,128]{1,0:T(8,128)(2,1)S(1)} collective-permute-done((bf16[1024,128]{1,0:T(8,128)(2,1)S(1)}, bf16[1024,128]{1,0:T(8,128)(2,1)S(1)}, u32[]{:S(2)}, u32[]{:S(2)}) %collective-permute-start.7) | collective-permute-done | bytes 262176 | tf_op jit(solution)/shard_map/ppermute | solution.py:589
  209.0 1.6 collective-permute-done.21.refs_1_
  (74 shorter events, 23.2 us)
Async XLA Ops:
  0.6 112.6 %collective-permute-start = (bf16[1024,2048]{1,0:T(8,128)(2,1)}, bf16[1024,2048]{1,0:T(8,128)(2,1)}, u32[]{:S(2)}, u32[]{:S(2)}) collective-permute-start(bf16[1024,2048]{1,0:T(8,128)(2,1)} %from_ref.1), channel_id=1, source_target_pairs={{0,1},{1,0},{2,3},{3,2},{4,5},{5,4},{6,7},{7,6},{8,9},{9,8},{10,11... | collective-permute-start | bytes 12582920 | tf_op jit(solution)/shard_map/ppermute | solution.py:589
  1.2 2.2 %copy-start.2 = (bf16[1024,2048]{1,0:T(8,128)(2,1)S(1)}, bf16[1024,2048]{1,0:T(8,128)(2,1)}, u32[]{:S(2)}) copy-start(bf16[1024,2048]{1,0:T(8,128)(2,1)} %from_ref.1) | copy-start | bytes 12582916
  5.0 34.1 %copy-start.3 = (bf16[1024,2048]{1,0:T(8,128)(2,1)S(1)}, bf16[1024,2048]{1,0:T(8,128)(2,1)}, u32[]{:S(2)}) copy-start(bf16[1024,2048]{1,0:T(8,128)(2,1)} %from_ref.1) | copy-start | bytes 12582916
  8.7 54.5 %copy-start.12 = (bf16[256,2048]{1,0:T(8,128)(2,1)}, bf16[256,2048]{1,0:T(8,128)(2,1)S(1)}, u32[]{:S(2)}) copy-start(bf16[256,2048]{1,0:T(8,128)(2,1)S(1)} %get-tuple-element.36) | copy-start | bytes 3145732
  8.7 54.5 %copy-start.13 = (bf16[256,2048]{1,0:T(8,128)(2,1)}, bf16[256,2048]{1,0:T(8,128)(2,1)S(1)}, u32[]{:S(2)}) copy-start(bf16[256,2048]{1,0:T(8,128)(2,1)S(1)} %get-tuple-element.37) | copy-start | bytes 3145732
  41.2 8.6 %collective-permute-start.1 = (f32[32,2304]{1,0:T(8,128)S(1)}, f32[32,2304]{1,0:T(8,128)S(1)}, u32[]{:S(2)}, u32[]{:S(2)}) collective-permute-start(f32[32,2304]{1,0:T(8,128)S(1)} %cross.1), channel_id=1, source_target_pairs={{0,16},{8,24},{16,0},{24,8},{1,17},{9,25},{17,1},{25,9},{2,18},{10... | collective-permute-start | bytes 884744 | tf_op jit(solution)/shard_map/ppermute | solution.py:589
  49.8 7.8 %collective-permute-start.2 = (f32[32,2304]{1,0:T(8,128)S(1)}, f32[32,2304]{1,0:T(8,128)S(1)}, u32[]{:S(2)}, u32[]{:S(2)}) collective-permute-start(f32[32,2304]{1,0:T(8,128)S(1)} %add.19.mine_ref), channel_id=1, source_target_pairs={{0,8},{8,0},{16,24},{24,16},{1,9},{9,1},{17,25},{25,17},{2,10},{10... | collective-permute-start | bytes 884744 | tf_op jit(solution)/shard_map/ppermute | solution.py:589
  61.4 50.5 %collective-permute-start.3 = (f32[40,2048]{1,0:T(8,128)S(1)}, f32[40,2048]{1,0:T(8,128)S(1)}, u32[]{:S(2)}, u32[]{:S(2)}) collective-permute-start(f32[40,2048]{1,0:T(8,128)S(1)} %solve.1.facts_ref.refs_0_), channel_id=1, source_target_pairs={{0,1},{1,0},{2,3},{3,2},{4,5},{5,4},{6,7},{7,6},{8,9},{9,8},{10,11... | collective-permute-start | bytes 983048 | tf_op jit(solution)/shard_map/ppermute | solution.py:589
  61.5 64.5 %collective-permute-start.10 = (bf16[256,2048]{1,0:T(8,128)(2,1)}, bf16[256,2048]{1,0:T(8,128)(2,1)S(1)}, u32[]{:S(2)}, u32[]{:S(2)}) collective-permute-start(bf16[256,2048]{1,0:T(8,128)(2,1)} %get-tuple-element.33), channel_id=1, source_target_pairs={{0,9},{1,8},{2,11},{3,10},{4,13},{5,12},{6,15},{7,14},{8,17},{9,16... | collective-permute-start | bytes 3145736 | tf_op jit(solution)/shard_map/ppermute | solution.py:589
  63.2 62.8 %collective-permute-start.9 = (bf16[256,2048]{1,0:T(8,128)(2,1)S(1)}, bf16[256,2048]{1,0:T(8,128)(2,1)}, u32[]{:S(2)}, u32[]{:S(2)}) collective-permute-start(bf16[256,2048]{1,0:T(8,128)(2,1)S(1)} %pick_ends.1), channel_id=1, source_target_pairs={{0,8},{8,16},{16,24},{24,0},{1,9},{9,17},{17,25},{25,1},{2,10},{10... | collective-permute-start | bytes 3145736 | tf_op jit(solution)/shard_map/ppermute | solution.py:589
  64.7 46.5 %collective-permute-start.8 = (bf16[4,32,128]{2,1,0:T(8,128)(2,1)S(1)}, bf16[4,32,128]{2,1,0:T(8,128)(2,1)S(1)}, u32[]{:S(2)}, u32[]{:S(2)}) collective-permute-start(bf16[4,32,128]{2,1,0:T(8,128)(2,1)S(1)} %dynamic-slice_bitcast_fusion), channel_id=1, source_target_pairs={{0,8},{8,16},{16,24},{24,0},{1,9},{9,17},{17,25},{25,1},{2,10},{10... | collective-permute-start | bytes 98312 | tf_op jit(solution)/shard_map/ppermute | solution.py:589
  111.3 27.2 %collective-permute-start.14 = (bf16[256,2048]{1,0:T(8,128)(2,1)}, bf16[256,2048]{1,0:T(8,128)(2,1)}, u32[]{:S(2)}, u32[]{:S(2)}) collective-permute-start(bf16[256,2048]{1,0:T(8,128)(2,1)} %copy-done.13), channel_id=1, source_target_pairs={{0,8},{8,16},{16,24},{24,0},{1,9},{9,17},{17,25},{25,1},{2,10},{10... | collective-permute-start | bytes 3145736 | tf_op jit(solution)/shard_map/ppermute | solution.py:589
  111.9 46.4 %collective-permute-start.13 = (bf16[256,2048]{1,0:T(8,128)(2,1)}, bf16[256,2048]{1,0:T(8,128)(2,1)}, u32[]{:S(2)}, u32[]{:S(2)}) collective-permute-start(bf16[256,2048]{1,0:T(8,128)(2,1)} %copy-done.12), channel_id=1, source_target_pairs={{0,9},{1,8},{2,11},{3,10},{4,13},{5,12},{6,15},{7,14},{8,17},{9,16... | collective-permute-start | bytes 3145736 | tf_op jit(solution)/shard_map/ppermute | solution.py:589
  126.0 5.4 %copy-start = (bf16[1024,4096]{1,0:T(8,128)(2,1)}, bf16[1024,4096]{1,0:T(8,128)(2,1)S(1)}, u32[]{:S(2)}) copy-start(bf16[1024,4096]{1,0:T(8,128)(2,1)S(1)} %get-tuple-element.32.zscore_ref) | copy-start | bytes 25165828
  126.0 5.4 %copy-start.5 = (bf16[1024,128]{1,0:T(8,128)(2,1)}, bf16[1024,128]{1,0:T(8,128)(2,1)S(1)}, u32[]{:S(2)}) copy-start(bf16[1024,128]{1,0:T(8,128)(2,1)S(1)} %get-tuple-element.30) | copy-start | bytes 786436
  131.5 36.3 %collective-permute-start.11 = (bf16[1,1024,128]{2,1,0:T(8,128)(2,1)S(1)}, bf16[1,1024,128]{2,1,0:T(8,128)(2,1)S(1)}, u32[]{:S(2)}, u32[]{:S(2)}) collective-permute-start(bf16[1,1024,128]{2,1,0:T(8,128)(2,1)S(1)} %get-tuple-element.35), channel_id=1, source_target_pairs={{0,2},{1,3},{2,0},{3,1},{4,6},{5,7},{6,4},{7,5},{8,10},{9,11},{10,... | collective-permute-start | bytes 786440 | tf_op jit(solution)/shard_map/ppermute | solution.py:589
  138.5 3.4 %copy-start.1 = (bf16[1024,4096]{1,0:T(8,128)(2,1)S(1)}, bf16[1024,4096]{1,0:T(8,128)(2,1)}, u32[]{:S(2)}) copy-start(bf16[1024,4096]{1,0:T(8,128)(2,1)} %copy-done) | copy-start | bytes 25165828
  145.1 26.3 %copy-start.6 = (bf16[1024,128]{1,0:T(8,128)(2,1)S(1)}, bf16[1024,128]{1,0:T(8,128)(2,1)}, u32[]{:S(2)}) copy-start(bf16[1024,128]{1,0:T(8,128)(2,1)} %copy-done.5) | copy-start | bytes 786436
  145.1 46.0 %copy-start.8 = (bf16[1024,128]{1,0:T(8,128)(2,1)S(1)}, bf16[1024,128]{1,0:T(8,128)(2,1)}, u32[]{:S(2)}) copy-start(bf16[1024,128]{1,0:T(8,128)(2,1)} %copy-done.7) | copy-start | bytes 786436
  162.2 16.8 %collective-permute-start.15 = (bf16[1024,128]{1,0:T(8,128)(2,1)}, bf16[1024,128]{1,0:T(8,128)(2,1)S(1)}, u32[]{:S(2)}, u32[]{:S(2)}) collective-permute-start(bf16[1024,128]{1,0:T(8,128)(2,1)} %get-tuple-element.39), channel_id=1, source_target_pairs={{0,2},{1,3},{2,4},{3,5},{8,10},{9,11},{10,12},{11,13},{16,18},{17,... | collective-permute-start | bytes 786440 | tf_op jit(solution)/shard_map/ppermute | solution.py:589
  165.1 15.2 %collective-permute-start.16 = (bf16[1024,128]{1,0:T(8,128)(2,1)}, bf16[1024,128]{1,0:T(8,128)(2,1)S(1)}, u32[]{:S(2)}, u32[]{:S(2)}) collective-permute-start(bf16[1024,128]{1,0:T(8,128)(2,1)} %get-tuple-element.40), channel_id=1, source_target_pairs={{0,4},{1,5},{6,2},{7,3},{8,12},{9,13},{14,10},{15,11},{16,20},{17,... | collective-permute-start | bytes 786440 | tf_op jit(solution)/shard_map/ppermute | solution.py:589
  166.4 15.9 %collective-permute-start.17 = (bf16[1024,128]{1,0:T(8,128)(2,1)}, bf16[1024,128]{1,0:T(8,128)(2,1)}, u32[]{:S(2)}, u32[]{:S(2)}) collective-permute-start(bf16[1024,128]{1,0:T(8,128)(2,1)} %get-tuple-element.41), channel_id=1, source_target_pairs={{4,2},{5,3},{6,4},{7,5},{12,10},{13,11},{14,12},{15,13},{20,18},{2... | collective-permute-start | bytes 786440 | tf_op jit(solution)/shard_map/ppermute | solution.py:589
  170.2 18.0 %collective-permute-start.12 = (bf16[1024,128]{1,0:T(8,128)(2,1)}, bf16[1024,128]{1,0:T(8,128)(2,1)S(1)}, u32[]{:S(2)}, u32[]{:S(2)}) collective-permute-start(bf16[1024,128]{1,0:T(8,128)(2,1)} %get-tuple-element.46), channel_id=1, source_target_pairs={{2,6},{3,7},{4,0},{5,1},{10,14},{11,15},{12,8},{13,9},{18,22},{19,... | collective-permute-start | bytes 786440 | tf_op jit(solution)/shard_map/ppermute | solution.py:589
  171.5 19.7 %collective-permute-start.6 = (bf16[1024,128]{1,0:T(8,128)(2,1)S(1)}, bf16[1024,128]{1,0:T(8,128)(2,1)}, u32[]{:S(2)}, u32[]{:S(2)}) collective-permute-start(bf16[1024,128]{1,0:T(8,128)(2,1)S(1)} %copy-done.6), channel_id=1, source_target_pairs={{0,2},{1,3},{6,4},{7,5},{8,10},{9,11},{14,12},{15,13},{16,18},{17,... | collective-permute-start | bytes 786440 | tf_op jit(solution)/shard_map/ppermute | solution.py:589
  179.0 22.0 %collective-permute-start.4 = (bf16[1024,128]{1,0:T(8,128)(2,1)}, bf16[1024,128]{1,0:T(8,128)(2,1)S(1)}, u32[]{:S(2)}, u32[]{:S(2)}) collective-permute-start(bf16[1024,128]{1,0:T(8,128)(2,1)} %copy-done.15), channel_id=1, source_target_pairs={{0,2},{1,3},{2,4},{3,5},{4,6},{5,7},{8,10},{9,11},{10,12},{11,13},... | collective-permute-start | bytes 786440 | tf_op jit(solution)/shard_map/ppermute | solution.py:589
  181.0 22.0 %collective-permute-start.5 = (bf16[1024,128]{1,0:T(8,128)(2,1)}, bf16[1024,128]{1,0:T(8,128)(2,1)S(1)}, u32[]{:S(2)}, u32[]{:S(2)}) collective-permute-start(bf16[1024,128]{1,0:T(8,128)(2,1)} %copy-done.14), channel_id=1, source_target_pairs={{2,0},{3,1},{4,2},{5,3},{6,4},{7,5},{10,8},{11,9},{12,10},{13,11},... | collective-permute-start | bytes 786440 | tf_op jit(solution)/shard_map/ppermute | solution.py:589
  190.3 6.0 %collective-permute-start.18 = (bf16[4,128,128]{2,1,0:T(8,128)(2,1)S(1)}, bf16[4,128,128]{2,1,0:T(8,128)(2,1)S(1)}, u32[]{:S(2)}, u32[]{:S(2)}) collective-permute-start(bf16[4,128,128]{2,1,0:T(8,128)(2,1)S(1)} %get-tuple-element.43), channel_id=1, source_target_pairs={{0,24},{8,0},{16,8},{24,16},{1,25},{9,1},{17,9},{25,17},{2,26},{10... | collective-permute-start | bytes 393224 | tf_op jit(solution)/shard_map/ppermute | solution.py:589
  192.2 15.7 %collective-permute-start.7 = (bf16[1024,128]{1,0:T(8,128)(2,1)S(1)}, bf16[1024,128]{1,0:T(8,128)(2,1)S(1)}, u32[]{:S(2)}, u32[]{:S(2)}) collective-permute-start(bf16[1024,128]{1,0:T(8,128)(2,1)S(1)} %fusion.2), channel_id=1, source_target_pairs={{0,4},{1,5},{2,6},{3,7},{4,0},{5,1},{6,2},{7,3},{8,12},{9,13},{10,... | collective-permute-start | bytes 786440 | tf_op jit(solution)/shard_map/ppermute | solution.py:589
  192.3 5.8 %collective-permute-start.19 = (bf16[4,128,128]{2,1,0:T(8,128)(2,1)S(1)}, bf16[4,128,128]{2,1,0:T(8,128)(2,1)S(1)}, u32[]{:S(2)}, u32[]{:S(2)}) collective-permute-start(bf16[4,128,128]{2,1,0:T(8,128)(2,1)S(1)} %get-tuple-element.44), channel_id=1, source_target_pairs={{0,25},{1,24},{2,27},{3,26},{4,29},{5,28},{6,31},{7,30},{8,1},{9,0... | collective-permute-start | bytes 393224 | tf_op jit(solution)/shard_map/ppermute | solution.py:589
  198.2 10.8 %collective-permute-start.22 = (bf16[2,128,128]{2,1,0:T(8,128)(2,1)S(1)}, bf16[2,128,128]{2,1,0:T(8,128)(2,1)S(1)}, u32[]{:S(2)}, u32[]{:S(2)}) collective-permute-start(bf16[2,128,128]{2,1,0:T(8,128)(2,1)S(1)} %pad_maximum_fusion.2), channel_id=1, source_target_pairs={{0,6},{1,7},{2,0},{3,1},{4,2},{5,3},{6,4},{7,5},{8,14},{9,15},{10,... | collective-permute-start | bytes 196616 | tf_op jit(solution)/shard_map/ppermute | solution.py:589
  198.2 12.4 %collective-permute-start.21 = (bf16[2,128,128]{2,1,0:T(8,128)(2,1)S(1)}, bf16[2,128,128]{2,1,0:T(8,128)(2,1)S(1)}, u32[]{:S(2)}, u32[]{:S(2)}) collective-permute-start(bf16[2,128,128]{2,1,0:T(8,128)(2,1)S(1)} %pad_maximum_fusion.1), channel_id=1, source_target_pairs={{0,4},{1,5},{2,6},{3,7},{4,0},{5,1},{6,2},{7,3},{8,12},{9,13},{10,... | collective-permute-start | bytes 196616 | tf_op jit(solution)/shard_map/ppermute | solution.py:589
  201.0 9.6 %collective-permute-start.20 = (bf16[2,128,128]{2,1,0:T(8,128)(2,1)S(1)}, bf16[2,128,128]{2,1,0:T(8,128)(2,1)S(1)}, u32[]{:S(2)}, u32[]{:S(2)}) collective-permute-start(bf16[2,128,128]{2,1,0:T(8,128)(2,1)S(1)} %pad_maximum_fusion), channel_id=1, source_target_pairs={{0,2},{1,3},{2,4},{3,5},{4,6},{5,7},{6,0},{7,1},{8,10},{9,11},{10,... | collective-permute-start | bytes 196616 | tf_op jit(solution)/shard_map/ppermute | solution.py:589
  (8 other events, 6.1 us)

commit v8 on v6

--- a/solution.py
+++ b/solution.py
@@ -306,10 +306,17 @@
         store(at, width, (left * rate[:, cols]).astype(BF16))
 
 
+def put_tile(part, sends, keep_ref):
+    share = keep_ref.shape[1]
+    keep_ref[...] = part[:, :share]
+    for j, ref in enumerate(sends, 1):
+        ref[...] = part[:, j * share : (j + 1) * share].astype(BF16)
+
+
 def own_kernel(
     steps, line, place_ref, core_ref, design_ref, mine_ref, theirs_ref, facts_ref, more_ref, *refs
 ):
-    z_ref, swap_ref, keep_ref, half_ref, terms_ref, moreterms_ref = refs
+    (z_ref, *sends), (keep_ref, half_ref, terms_ref, moreterms_ref) = refs[:line], refs[line:]
     step = pl.program_id(0)
     blocks, kk, share = design_ref.shape
     chunk, probes = mine_ref.shape
@@ -334,17 +341,14 @@
         )
         for b in range(blocks // 2):
             here = pl.ds(pl.multiple_of(step * chunk + (2 * b + core) * share, share), share)
-            slot = jnp.bitwise_xor(step * (blocks // 2) + b, place)
+            slot = lax.rem(step * (blocks // 2) + b - place + line, line)
             half_ref[pl.ds(pl.multiple_of(slot * share, share), share), :] = z_ref[here, :]
 
     @pl.when(step >= steps)
     def _():
-        tall = keep_ref.shape[1]
+        tall = keep_ref.shape[0]
         rows = pl.ds(pl.multiple_of((step - steps) * tall, tall), tall)
-        part = nt(z_ref[rows, :], half_ref[...])
-        for slot in range(0, line, 2):
-            keep_ref[slot // 2] = part[:, slot * share : (slot + 1) * share]
-            swap_ref[slot // 2] = part[:, (slot + 1) * share : (slot + 2) * share].astype(BF16)
+        put_tile(nt(z_ref[rows, :], half_ref[...]), sends, keep_ref)
 
 
 def own_tile(at, line, design, mine, theirs, facts, more):
@@ -373,7 +377,7 @@
                 whole,
             ],
             out_specs=[pl.BlockSpec(memory_space=pltpu.VMEM)]
-            + [pl.BlockSpec((line // 2, tall, share), lambda i, *_: (0, *second(i)))] * 2,
+            + [pl.BlockSpec((tall, share), second)] * line,
             scratch_shapes=[
                 pltpu.VMEM((rows // 2, 2 * probes), BF16),
                 pltpu.VMEM((3 * K, probes), BF16),
@@ -381,7 +385,8 @@
             ],
         ),
         out_shape=[pltpu.VMEM((rows, 2 * probes), BF16)]
-        + [jax.ShapeDtypeStruct((line // 2, rows, share), dtype) for dtype in (BF16, F32)],
+        + [jax.ShapeDtypeStruct((rows, share), BF16)] * (line - 1)
+        + [jax.ShapeDtypeStruct((rows, share), F32)],
         compiler_params=params("arbitrary"),
         cost_estimate=cost(2 * rows * rows * probes, 12 * rows * probes),
         name="own",
@@ -609,36 +614,37 @@
         pairs = [(i, (i + by) % line) for i in range(line)]
         return pairs if among is None else [(i, to) for i, to in pairs if to in among]
 
-    def arrivals(sends, among):
-        return [on_line(value, round_of(j, among)) for j, value in enumerate(sends, 1)]
-
-
-    zscore, swap, keep = own_tile(at, line, design, methyl, theirs, facts, more)
-    given = on_line(swap, [(i, i ^ 1) for i in range(line)])
+    def arrivals(sends, among=None, rounds=None):
+        return [
+            on_line(value, round_of(j, among))
+            for j, value in enumerate(sends, 1)
+            if rounds is None or j in rounds
+        ]
+
+    early = {1, line - 1}
+    late = set(range(1, line)) - early
+
+    zscore, *own_sends, own_keep = own_tile(at, line, design, methyl, theirs, facts, more)
+    own_parts = arrivals(own_sends, rounds=early)
     design_ends = jnp.concatenate([design_before[:quarter], design_before[line - quarter :]])
-    *sends, pair_keep = pair_tile(
+    *sends, keep = pair_tile(
         among_ends, at, line, design_ends, zscore, 0, [facts, more],
         [ends_mine, ends_theirs],
     )
-    pair_parts = [pair_keep] + arrivals(sends, ends)
-    bit = 2
-    while bit < line:
-        swap = keep[1::2] + given[1::2].astype(F32)
-        keep = keep[::2] + given[::2].astype(F32)
-        given = on_line(swap.astype(BF16), [(i, i ^ bit) for i in range(line)])
-        bit *= 2
-    own_keep, own_parts = keep[0], [given[0]]
+    pair_parts = [keep] + arrivals(sends, ends)
     design_inner = design_before[quarter : line - quarter]
     (partial,) = pair_tile(
         among_inner, at, line, design_inner, zscore, 0, [facts], [inner_mine],
         last=False,
     )
-    *sends, pair_keep = pair_tile(
+    *sends, keep = pair_tile(
         among_inner, at, line, design_inner, zscore, 1, [more], [inner_theirs],
         given=partial,
     )
-    pair_parts.append(pair_keep)
-    pair_parts += arrivals(sends, inner)
+    pair_parts.append(keep)
+    pair_parts += arrivals(sends, inner, late)
+    pair_parts += arrivals(sends, inner, early)
+    own_parts += arrivals(own_sends, rounds=late)
     left, same, other = fold(at, line, pair_parts)
     same = to_panel(same, -1)
     other = to_panel_sibling(other, -1)

time: 222 us -> 221 us (level)
  waiting for transfers between devices: 122 us -> 114 us
  starting transfers between devices: 27.2 us -> 34.2 us
    ppermute x22 -> x23, waiting for transfers between devices: 122 us -> 114 us  [along(): return lax.ppermute(value, axis, pairs)]
    ppermute x22 -> x23, starting transfers between devices: 27.2 us -> 34.2 us  [along(): return lax.ppermute(value, axis, pairs)]
  transfers between devices with their start and end apart: 22 -> 23, of which waited for: 12 -> 12; matrix products, arithmetic and copies ran while one was open for 0% -> 0% of each run, Pallas kernels for 18% -> 18%
where the time goes in v8:
time: 221 us
  waiting for transfers between devices  114 us (52%)
  Pallas kernels  41.3 us (19%)
  starting transfers between devices  34.2 us (15%)
  blocking collectives  23.8 us (11%)
  local copies, waits for them, and re-layouts  6 us (3%)
    ppermute x23, waiting for transfers between devices, along(): return lax.ppermute(value, axis, pairs)  114 us
    ppermute x23, starting transfers between devices, along(): return lax.ppermute(value, axis, pairs)  34.2 us
    all_to_all x1, blocking collectives, body(): parts = lax.all_to_all(parts, 'probe', 0, 0)  15.5 us
    pallas_call x3, Pallas kernels, pair_tile(): pl.pallas_call(functools.partial(pair_kernel, index_of, line, first, side...  11.1 us
    pallas_call x1, Pallas kernels, own_tile(): pl.pallas_call(functools.partial(own_kernel, steps, line), grid_spec=pltp...  10.7 us
    all_to_all x1, blocking collectives, body(): design = lax.all_to_all(copies, 'probe', 0, 0)  8.28 us
    pallas_call x1, Pallas kernels, descend(): pl.pallas_call(descend_kernel, out_shape=(jax.ShapeDtypeStruct((K, share)...  6.61 us
    unnamed x10, local copies, waits for them, and re-layouts  5.98 us
  transfers between devices with their start and end apart: 23, of which 12 were waited for; matrix products, arithmetic and copies ran while one was open for 0% of the time, Pallas kernels for 18%

profile of v8, /device:TPU:0, one launch (start us, length us, event | category | flops | bytes accessed | tf_op | source)
XLA Modules:
  0.0 220.6 jit_solution(11274167836705304041)
XLA Ops:
  1.2 2.2 copy-done
  5.0 4.5 %project.1 = (f32[8,64,128]{2,1,0:T(8,128)S(1)}, bf16[32,2048]{1,0:T(8,128)(2,1)S(1)}, bf16[256,2048]{1,0:T(8,128)(2,1)}, bf16[256,2048]{1,0:T(8,128)(2,1)}, bf16[256,2048]{1,0:T(8,128)(2,1)}) custom-call(s32[1]{0:T(128)} %bitcast.1.core_ref._, s32[64]{0:T(128)S(1)} %copy-done.4, bf16[64,2048]{1,0:T(8,128)(2,1)S(1)} %copy-done.3, bf16[1024,2048]{1,0:T(8,128)(2,1)S(1)} %copy-done), custom_call_target="tpu_custom_call" | custom-call | flops 134217728 | bytes 8388608 | tf_op jit(solution)/shard_map/project/pallas_call | solution.py:103
  9.5 15.5 %all_to_all.10.parts_ref = f32[8,64,128]{2,1,0:T(8,128)S(1)} all-to-all(f32[8,64,128]{2,1,0:T(8,128)S(1)} %get-tuple-element.25), channel_id=1, replica_groups=mesh['samp'=4,'probe'=8] {'probe'}, dimensions={0} | all-to-all | bytes 524288 | tf_op jit(solution)/shard_map/all_to_all | solution.py:597
  25.0 6.6 %descend.1 = (f32[32,128]{1,0:T(8,128)}, bf16[8,32,128]{2,1,0:T(8,128)(2,1)S(1)}) custom-call(f32[8,64,128]{2,1,0:T(8,128)S(1)} %all_to_all.10.parts_ref), custom_call_target="tpu_custom_call" | custom-call | flops 33554432 | bytes 16384 | tf_op jit(solution)/shard_map/descend/pallas_call | solution.py:197
  31.6 8.3 %all_to_all.11.design_ref = bf16[8,32,128]{2,1,0:T(8,128)(2,1)S(1)} all-to-all(bf16[8,32,128]{2,1,0:T(8,128)(2,1)S(1)} %get-tuple-element.26), channel_id=1, replica_groups=mesh['samp'=4,'probe'=8] {'probe'}, dimensions={0} | all-to-all | bytes 131072 | tf_op jit(solution)/shard_map/all_to_all | solution.py:599
  39.9 2.1 cross.1
  41.9 1.6 collective-permute-start.1
  43.5 7.0 %collective-permute-done.1 = f32[32,2304]{1,0:T(8,128)S(1)} collective-permute-done((f32[32,2304]{1,0:T(8,128)S(1)}, f32[32,2304]{1,0:T(8,128)S(1)}, u32[]{:S(2)}, u32[]{:S(2)}) %collective-permute-start.1) | collective-permute-done | bytes 294944 | tf_op jit(solution)/shard_map/ppermute | solution.py:560
  50.6 1.6 collective-permute-start.2
  52.2 6.2 %collective-permute-done.2.peer_ref = f32[32,2304]{1,0:T(8,128)S(1)} collective-permute-done((f32[32,2304]{1,0:T(8,128)S(1)}, f32[32,2304]{1,0:T(8,128)S(1)}, u32[]{:S(2)}, u32[]{:S(2)}) %collective-permute-start.2) | collective-permute-done | bytes 294944 | tf_op jit(solution)/shard_map/ppermute | solution.py:560
  58.4 3.8 %solve.1.facts_ref.refs_0_ = f32[40,2048]{1,0:T(8,128)S(1)} custom-call(f32[32,2304]{1,0:T(8,128)S(1)} %add.13.mine_ref, f32[32,2304]{1,0:T(8,128)S(1)} %collective-permute-done.2.peer_ref, bf16[32,2048]{1,0:T(8,128)(2,1)S(1)} %get-tuple-element.27.panel_ref), custom_call_target="tpu_custom_call" | custom-call | flops 104857600 | bytes 1310720 | tf_op jit(solution)/shard_map/solve/pallas_call | solution.py:289
  66.6 2.2 copy-done.2
  68.8 43.3 %collective-permute-done.7 = bf16[4,32,128]{2,1,0:T(8,128)(2,1)S(1)} collective-permute-done((bf16[4,32,128]{2,1,0:T(8,128)(2,1)S(1)}, bf16[4,32,128]{2,1,0:T(8,128)(2,1)S(1)}, u32[]{:S(2)}, u32[]{:S(2)}) %collective-permute-start.7) | collective-permute-done | bytes 32800 | tf_op jit(solution)/shard_map/ppermute | solution.py:560
  112.1 1.9 collective-permute-start.8
  114.0 10.7 %own.1 = (bf16[1024,4096]{1,0:T(8,128)(2,1)S(1)}, bf16[1024,128]{1,0:T(8,128)(2,1)S(1)}, bf16[1024,128]{1,0:T(8,128)(2,1)S(1)}, bf16[1024,128]{1,0:T(8,128)(2,1)S(1)}, f32[1024,128]{1,0:T(8,128)S(1)}) custom-call(s32[1]{0:T(128)} %bitcast.place_ref, s32[1]{0:T(128)} %bitcast.1.core_ref._, bf16[8,32,128]{2,1,0:T(8,128)(2,1)S(1)} %all_to_all.11.design_ref, ...), custom_call_target="tpu_custom_call" | custom-call | flops 4294967296 | bytes 25165824 | tf_op jit(solution)/shard_map/own/pallas_call | solution.py:367
  124.7 3.2 %shard_map.51.refs_2_ = f32[1024,256]{1,0:T(8,128)S(1)} custom-call(s32[1]{0:T(128)} %bitcast.place_ref, bf16[2,32,128]{2,1,0:T(8,128)(2,1)S(1)} %slice.38.design_ref, bf16[1024,4096]{1,0:T(8,128)(2,1)S(1)} %get-tuple-element.32.zscore_ref, f32[40,2048]{1,0:T(8,128)S(1)} %solve.1.facts_ref.refs_0_, bf16[256,2048]{1,0:T(8,128)(2,1)} %collective-permute-done.14.refs_1_), custom_call_target="tpu_custom_call" | custom-call | flops 1073741824 | bytes 8388608 | tf_op jit(solution)/shard_map/pallas_call | solution.py:446
  127.9 3.2 %shard_map.52 = (bf16[1024,128]{1,0:T(8,128)(2,1)S(1)}, bf16[1024,128]{1,0:T(8,128)(2,1)S(1)}, bf16[1024,128]{1,0:T(8,128)(2,1)S(1)}, f32[1024,128]{1,0:T(8,128)S(1)}) custom-call(s32[1]{0:T(128)} %bitcast.place_ref, bf16[2,32,128]{2,1,0:T(8,128)(2,1)S(1)} %slice.38.design_ref, bf16[1024,4096]{1,0:T(8,128)(2,1)S(1)} %get-tuple-element.32.zscore_ref, ...), custom_call_target="tpu_custom_call" | custom-call | flops 1073741824 | bytes 8388608 | tf_op jit(solution)/shard_map/pallas_call | solution.py:446
  131.2 2.4 %collective-permute-start.15 = (bf16[1024,128]{1,0:T(8,128)(2,1)S(1)}, bf16[1024,128]{1,0:T(8,128)(2,1)S(1)}, u32[]{:S(2)}, u32[]{:S(2)}) collective-permute-start(bf16[1024,128]{1,0:T(8,128)(2,1)S(1)} %get-tuple-element.41), channel_id=1, source_target_pairs={{0,4},{1,5},{6,2},{7,3},{8,12},{9,13},{14,10},{15,11},{16,20},{17,... | collective-permute-start | bytes 786440 | tf_op jit(solution)/shard_map/ppermute | solution.py:560
  133.6 1.7 collective-permute-start.16
  136.0 2.6 %collective-permute-done.9.refs_3_ = bf16[256,2048]{1,0:T(8,128)(2,1)S(1)} collective-permute-done((bf16[256,2048]{1,0:T(8,128)(2,1)}, bf16[256,2048]{1,0:T(8,128)(2,1)S(1)}, u32[]{:S(2)}, u32[]{:S(2)}) %collective-permute-start.9) | collective-permute-done | bytes 1048608 | tf_op jit(solution)/shard_map/ppermute | solution.py:560
  138.7 21.5 %collective-permute-done.8.refs_2_ = bf16[256,2048]{1,0:T(8,128)(2,1)} collective-permute-done((bf16[256,2048]{1,0:T(8,128)(2,1)S(1)}, bf16[256,2048]{1,0:T(8,128)(2,1)}, u32[]{:S(2)}, u32[]{:S(2)}) %collective-permute-start.8) | collective-permute-done | bytes 1048608 | tf_op jit(solution)/shard_map/ppermute | solution.py:560
  160.2 4.6 %shard_map.50 = (bf16[1024,128]{1,0:T(8,128)(2,1)S(1)}, bf16[1024,128]{1,0:T(8,128)(2,1)S(1)}, bf16[1024,128]{1,0:T(8,128)(2,1)S(1)}, f32[1024,128]{1,0:T(8,128)S(1)}) custom-call(s32[1]{0:T(128)} %bitcast.place_ref, bf16[2,32,128]{2,1,0:T(8,128)(2,1)S(1)} %pad_maximum_fusion.3.design_ref, bf16[1024,4096]{1,0:T(8,128)(2,1)S(1)} %get-tuple-element.32.zscore_ref, ...), custom_call_target="tpu_custom_call" | custom-call | flops 2147483648 | bytes 8388608 | tf_op jit(solution)/shard_map/pallas_call | solution.py:446
  167.4 6.3 %collective-permute-start.12 = (bf16[1024,128]{1,0:T(8,128)(2,1)S(1)}, bf16[1024,128]{1,0:T(8,128)(2,1)S(1)}, u32[]{:S(2)}, u32[]{:S(2)}) collective-permute-start(bf16[1024,128]{1,0:T(8,128)(2,1)S(1)} %get-tuple-element.37), channel_id=1, source_target_pairs={{0,6},{1,7},{2,0},{3,1},{8,14},{9,15},{10,8},{11,9},{16,22},{17,23... | collective-permute-start | bytes 786440 | tf_op jit(solution)/shard_map/ppermute | solution.py:560
  173.8 3.5 %collective-permute-done.10.refs_1_ = bf16[1024,128]{1,0:T(8,128)(2,1)S(1)} collective-permute-done((bf16[1024,128]{1,0:T(8,128)(2,1)S(1)}, bf16[1024,128]{1,0:T(8,128)(2,1)S(1)}, u32[]{:S(2)}, u32[]{:S(2)}) %collective-permute-start.10) | collective-permute-done | bytes 262176 | tf_op jit(solution)/shard_map/ppermute | solution.py:560
  177.2 5.5 %collective-permute-done.11.refs_2_ = bf16[1024,128]{1,0:T(8,128)(2,1)S(1)} collective-permute-done((bf16[1024,128]{1,0:T(8,128)(2,1)S(1)}, bf16[1024,128]{1,0:T(8,128)(2,1)S(1)}, u32[]{:S(2)}, u32[]{:S(2)}) %collective-permute-start.11) | collective-permute-done | bytes 262176 | tf_op jit(solution)/shard_map/ppermute | solution.py:560
  182.8 5.5 %collective-permute-done.12.refs_3_ = bf16[1024,128]{1,0:T(8,128)(2,1)S(1)} collective-permute-done((bf16[1024,128]{1,0:T(8,128)(2,1)S(1)}, bf16[1024,128]{1,0:T(8,128)(2,1)S(1)}, u32[]{:S(2)}, u32[]{:S(2)}) %collective-permute-start.12) | collective-permute-done | bytes 262176 | tf_op jit(solution)/shard_map/ppermute | solution.py:560
  190.2 3.8 %collective-permute-start.5 = (bf16[1024,128]{1,0:T(8,128)(2,1)S(1)}, bf16[1024,128]{1,0:T(8,128)(2,1)S(1)}, u32[]{:S(2)}, u32[]{:S(2)}) collective-permute-start(bf16[1024,128]{1,0:T(8,128)(2,1)S(1)} %get-tuple-element.30), channel_id=1, source_target_pairs={{0,6},{1,7},{2,0},{3,1},{4,2},{5,3},{6,4},{7,5},{8,14},{9,15},{10,... | collective-permute-start | bytes 786440 | tf_op jit(solution)/shard_map/ppermute | solution.py:560
  194.4 4.8 %collective-permute-done.19.other_ref = bf16[4,128,128]{2,1,0:T(8,128)(2,1)S(1)} collective-permute-done((bf16[4,128,128]{2,1,0:T(8,128)(2,1)S(1)}, bf16[4,128,128]{2,1,0:T(8,128)(2,1)S(1)}, u32[]{:S(2)}, u32[]{:S(2)}) %collective-permute-start.19) | collective-permute-done | bytes 131104 | tf_op jit(solution)/shard_map/ppermute | solution.py:560
  199.8 2.2 %collective-permute-start.21 = (bf16[2,128,128]{2,1,0:T(8,128)(2,1)S(1)}, bf16[2,128,128]{2,1,0:T(8,128)(2,1)S(1)}, u32[]{:S(2)}, u32[]{:S(2)}) collective-permute-start(bf16[2,128,128]{2,1,0:T(8,128)(2,1)S(1)} %pad_maximum_fusion.1), channel_id=1, source_target_pairs={{0,4},{1,5},{2,6},{3,7},{4,0},{5,1},{6,2},{7,3},{8,12},{9,13},{10,... | collective-permute-start | bytes 196616 | tf_op jit(solution)/shard_map/ppermute | solution.py:560
  202.1 2.1 collective-permute-start.20
  204.1 3.3 %collective-permute-done.5.refs_1_ = bf16[1024,128]{1,0:T(8,128)(2,1)S(1)} collective-permute-done((bf16[1024,128]{1,0:T(8,128)(2,1)S(1)}, bf16[1024,128]{1,0:T(8,128)(2,1)S(1)}, u32[]{:S(2)}, u32[]{:S(2)}) %collective-permute-start.5) | collective-permute-done | bytes 262176 | tf_op jit(solution)/shard_map/ppermute | solution.py:560
  207.4 10.6 %collective-permute-done.6.refs_2_ = bf16[1024,128]{1,0:T(8,128)(2,1)S(1)} collective-permute-done((bf16[1024,128]{1,0:T(8,128)(2,1)S(1)}, bf16[1024,128]{1,0:T(8,128)(2,1)S(1)}, u32[]{:S(2)}, u32[]{:S(2)}) %collective-permute-start.6) | collective-permute-done | bytes 262176 | tf_op jit(solution)/shard_map/ppermute | solution.py:560
  (48 shorter events, 15.4 us)
Async XLA Ops:
  0.6 113.4 %collective-permute-start = (bf16[1024,2048]{1,0:T(8,128)(2,1)}, bf16[1024,2048]{1,0:T(8,128)(2,1)}, u32[]{:S(2)}, u32[]{:S(2)}) collective-permute-start(bf16[1024,2048]{1,0:T(8,128)(2,1)} %from_ref.1), channel_id=1, source_target_pairs={{0,1},{1,0},{2,3},{3,2},{4,5},{5,4},{6,7},{7,6},{8,9},{9,8},{10,11... | collective-permute-start | bytes 12582920 | tf_op jit(solution)/shard_map/ppermute | solution.py:560
  1.2 2.2 copy-start
  3.4 0.9 copy-start.3
  4.3 0.7 copy-start.4
  5.0 34.9 %copy-start.1 = (bf16[1024,2048]{1,0:T(8,128)(2,1)S(1)}, bf16[1024,2048]{1,0:T(8,128)(2,1)}, u32[]{:S(2)}) copy-start(bf16[1024,2048]{1,0:T(8,128)(2,1)} %from_ref.1) | copy-start | bytes 12582916
  41.9 8.6 %collective-permute-start.1 = (f32[32,2304]{1,0:T(8,128)S(1)}, f32[32,2304]{1,0:T(8,128)S(1)}, u32[]{:S(2)}, u32[]{:S(2)}) collective-permute-start(f32[32,2304]{1,0:T(8,128)S(1)} %cross.1), channel_id=1, source_target_pairs={{0,16},{8,24},{16,0},{24,8},{1,17},{9,25},{17,1},{25,9},{2,18},{10... | collective-permute-start | bytes 884744 | tf_op jit(solution)/shard_map/ppermute | solution.py:560
  50.6 7.8 %collective-permute-start.2 = (f32[32,2304]{1,0:T(8,128)S(1)}, f32[32,2304]{1,0:T(8,128)S(1)}, u32[]{:S(2)}, u32[]{:S(2)}) collective-permute-start(f32[32,2304]{1,0:T(8,128)S(1)} %add.13.mine_ref), channel_id=1, source_target_pairs={{0,8},{8,0},{16,24},{24,16},{1,9},{9,1},{17,25},{25,17},{2,10},{10... | collective-permute-start | bytes 884744 | tf_op jit(solution)/shard_map/ppermute | solution.py:560
  62.2 49.9 %collective-permute-start.3 = (f32[40,2048]{1,0:T(8,128)S(1)}, f32[40,2048]{1,0:T(8,128)S(1)}, u32[]{:S(2)}, u32[]{:S(2)}) collective-permute-start(f32[40,2048]{1,0:T(8,128)S(1)} %solve.1.facts_ref.refs_0_), channel_id=1, source_target_pairs={{0,1},{1,0},{2,3},{3,2},{4,5},{5,4},{6,7},{7,6},{8,9},{9,8},{10,11... | collective-permute-start | bytes 983048 | tf_op jit(solution)/shard_map/ppermute | solution.py:560
  62.3 62.4 %collective-permute-start.14 = (bf16[256,2048]{1,0:T(8,128)(2,1)}, bf16[256,2048]{1,0:T(8,128)(2,1)}, u32[]{:S(2)}, u32[]{:S(2)}) collective-permute-start(bf16[256,2048]{1,0:T(8,128)(2,1)} %get-tuple-element.39), channel_id=1, source_target_pairs={{0,8},{8,16},{16,24},{24,0},{1,9},{9,17},{17,25},{25,1},{2,10},{10... | collective-permute-start | bytes 3145736 | tf_op jit(solution)/shard_map/ppermute | solution.py:560
  63.8 64.1 %collective-permute-start.13 = (bf16[256,2048]{1,0:T(8,128)(2,1)}, bf16[256,2048]{1,0:T(8,128)(2,1)}, u32[]{:S(2)}, u32[]{:S(2)}) collective-permute-start(bf16[256,2048]{1,0:T(8,128)(2,1)} %get-tuple-element.38), channel_id=1, source_target_pairs={{0,9},{1,8},{2,11},{3,10},{4,13},{5,12},{6,15},{7,14},{8,17},{9,16... | collective-permute-start | bytes 3145736 | tf_op jit(solution)/shard_map/ppermute | solution.py:560
  65.1 47.0 %collective-permute-start.7 = (bf16[4,32,128]{2,1,0:T(8,128)(2,1)S(1)}, bf16[4,32,128]{2,1,0:T(8,128)(2,1)S(1)}, u32[]{:S(2)}, u32[]{:S(2)}) collective-permute-start(bf16[4,32,128]{2,1,0:T(8,128)(2,1)S(1)} %dynamic-slice_bitcast_fusion), channel_id=1, source_target_pairs={{0,8},{8,16},{16,24},{24,0},{1,9},{9,17},{17,25},{25,1},{2,10},{10... | collective-permute-start | bytes 98312 | tf_op jit(solution)/shard_map/ppermute | solution.py:560
  66.6 2.2 copy-start.2
  112.1 26.6 %collective-permute-start.9 = (bf16[256,2048]{1,0:T(8,128)(2,1)}, bf16[256,2048]{1,0:T(8,128)(2,1)S(1)}, u32[]{:S(2)}, u32[]{:S(2)}) collective-permute-start(bf16[256,2048]{1,0:T(8,128)(2,1)} %get-tuple-element.33), channel_id=1, source_target_pairs={{0,9},{1,8},{2,11},{3,10},{4,13},{5,12},{6,15},{7,14},{8,17},{9,16... | collective-permute-start | bytes 3145736 | tf_op jit(solution)/shard_map/ppermute | solution.py:560
  112.1 48.1 %collective-permute-start.8 = (bf16[256,2048]{1,0:T(8,128)(2,1)S(1)}, bf16[256,2048]{1,0:T(8,128)(2,1)}, u32[]{:S(2)}, u32[]{:S(2)}) collective-permute-start(bf16[256,2048]{1,0:T(8,128)(2,1)S(1)} %pick_ends.1), channel_id=1, source_target_pairs={{0,8},{8,16},{16,24},{24,0},{1,9},{9,17},{17,25},{25,1},{2,10},{10... | collective-permute-start | bytes 3145736 | tf_op jit(solution)/shard_map/ppermute | solution.py:560
  131.2 36.2 %collective-permute-start.15 = (bf16[1024,128]{1,0:T(8,128)(2,1)S(1)}, bf16[1024,128]{1,0:T(8,128)(2,1)S(1)}, u32[]{:S(2)}, u32[]{:S(2)}) collective-permute-start(bf16[1024,128]{1,0:T(8,128)(2,1)S(1)} %get-tuple-element.41), channel_id=1, source_target_pairs={{0,4},{1,5},{6,2},{7,3},{8,12},{9,13},{14,10},{15,11},{16,20},{17,... | collective-permute-start | bytes 786440 | tf_op jit(solution)/shard_map/ppermute | solution.py:560
  133.6 40.1 %collective-permute-start.16 = (bf16[1024,128]{1,0:T(8,128)(2,1)S(1)}, bf16[1024,128]{1,0:T(8,128)(2,1)S(1)}, u32[]{:S(2)}, u32[]{:S(2)}) collective-permute-start(bf16[1024,128]{1,0:T(8,128)(2,1)S(1)} %get-tuple-element.42), channel_id=1, source_target_pairs={{0,2},{1,3},{2,4},{3,5},{8,10},{9,11},{10,12},{11,13},{16,18},{17,... | collective-permute-start | bytes 786440 | tf_op jit(solution)/shard_map/ppermute | solution.py:560
  135.4 38.4 %collective-permute-start.17 = (bf16[1024,128]{1,0:T(8,128)(2,1)S(1)}, bf16[1024,128]{1,0:T(8,128)(2,1)S(1)}, u32[]{:S(2)}, u32[]{:S(2)}) collective-permute-start(bf16[1024,128]{1,0:T(8,128)(2,1)S(1)} %get-tuple-element.43), channel_id=1, source_target_pairs={{4,2},{5,3},{6,4},{7,5},{12,10},{13,11},{14,12},{15,13},{20,18},{2... | collective-permute-start | bytes 786440 | tf_op jit(solution)/shard_map/ppermute | solution.py:560
  164.8 12.4 %collective-permute-start.10 = (bf16[1024,128]{1,0:T(8,128)(2,1)S(1)}, bf16[1024,128]{1,0:T(8,128)(2,1)S(1)}, u32[]{:S(2)}, u32[]{:S(2)}) collective-permute-start(bf16[1024,128]{1,0:T(8,128)(2,1)S(1)} %get-tuple-element.35), channel_id=1, source_target_pairs={{4,6},{5,7},{6,0},{7,1},{12,14},{13,15},{14,8},{15,9},{20,22},{21,... | collective-permute-start | bytes 786440 | tf_op jit(solution)/shard_map/ppermute | solution.py:560
  166.1 16.7 %collective-permute-start.11 = (bf16[1024,128]{1,0:T(8,128)(2,1)S(1)}, bf16[1024,128]{1,0:T(8,128)(2,1)S(1)}, u32[]{:S(2)}, u32[]{:S(2)}) collective-permute-start(bf16[1024,128]{1,0:T(8,128)(2,1)S(1)} %get-tuple-element.36), channel_id=1, source_target_pairs={{2,6},{3,7},{4,0},{5,1},{10,14},{11,15},{12,8},{13,9},{18,22},{19,... | collective-permute-start | bytes 786440 | tf_op jit(solution)/shard_map/ppermute | solution.py:560
  167.4 20.9 %collective-permute-start.12 = (bf16[1024,128]{1,0:T(8,128)(2,1)S(1)}, bf16[1024,128]{1,0:T(8,128)(2,1)S(1)}, u32[]{:S(2)}, u32[]{:S(2)}) collective-permute-start(bf16[1024,128]{1,0:T(8,128)(2,1)S(1)} %get-tuple-element.37), channel_id=1, source_target_pairs={{0,6},{1,7},{2,0},{3,1},{8,14},{9,15},{10,8},{11,9},{16,22},{17,23... | collective-permute-start | bytes 786440 | tf_op jit(solution)/shard_map/ppermute | solution.py:560
  188.7 5.7 %collective-permute-start.18 = (bf16[4,128,128]{2,1,0:T(8,128)(2,1)S(1)}, bf16[4,128,128]{2,1,0:T(8,128)(2,1)S(1)}, u32[]{:S(2)}, u32[]{:S(2)}) collective-permute-start(bf16[4,128,128]{2,1,0:T(8,128)(2,1)S(1)} %get-tuple-element.45), channel_id=1, source_target_pairs={{0,24},{8,0},{16,8},{24,16},{1,25},{9,1},{17,9},{25,17},{2,26},{10... | collective-permute-start | bytes 393224 | tf_op jit(solution)/shard_map/ppermute | solution.py:560
  190.2 11.9 %collective-permute-start.4 = (bf16[1024,128]{1,0:T(8,128)(2,1)S(1)}, bf16[1024,128]{1,0:T(8,128)(2,1)S(1)}, u32[]{:S(2)}, u32[]{:S(2)}) collective-permute-start(bf16[1024,128]{1,0:T(8,128)(2,1)S(1)} %get-tuple-element.29), channel_id=1, source_target_pairs={{0,2},{1,3},{2,4},{3,5},{4,6},{5,7},{6,0},{7,1},{8,10},{9,11},{10,... | collective-permute-start | bytes 786440 | tf_op jit(solution)/shard_map/ppermute | solution.py:560
  190.2 17.2 %collective-permute-start.5 = (bf16[1024,128]{1,0:T(8,128)(2,1)S(1)}, bf16[1024,128]{1,0:T(8,128)(2,1)S(1)}, u32[]{:S(2)}, u32[]{:S(2)}) collective-permute-start(bf16[1024,128]{1,0:T(8,128)(2,1)S(1)} %get-tuple-element.30), channel_id=1, source_target_pairs={{0,6},{1,7},{2,0},{3,1},{4,2},{5,3},{6,4},{7,5},{8,14},{9,15},{10,... | collective-permute-start | bytes 786440 | tf_op jit(solution)/shard_map/ppermute | solution.py:560
  194.0 24.0 %collective-permute-start.6 = (bf16[1024,128]{1,0:T(8,128)(2,1)S(1)}, bf16[1024,128]{1,0:T(8,128)(2,1)S(1)}, u32[]{:S(2)}, u32[]{:S(2)}) collective-permute-start(bf16[1024,128]{1,0:T(8,128)(2,1)S(1)} %get-tuple-element.31), channel_id=1, source_target_pairs={{0,4},{1,5},{2,6},{3,7},{4,0},{5,1},{6,2},{7,3},{8,12},{9,13},{10,... | collective-permute-start | bytes 786440 | tf_op jit(solution)/shard_map/ppermute | solution.py:560
  194.0 5.2 %collective-permute-start.19 = (bf16[4,128,128]{2,1,0:T(8,128)(2,1)S(1)}, bf16[4,128,128]{2,1,0:T(8,128)(2,1)S(1)}, u32[]{:S(2)}, u32[]{:S(2)}) collective-permute-start(bf16[4,128,128]{2,1,0:T(8,128)(2,1)S(1)} %get-tuple-element.46), channel_id=1, source_target_pairs={{0,25},{1,24},{2,27},{3,26},{4,29},{5,28},{6,31},{7,30},{8,1},{9,0... | collective-permute-start | bytes 393224 | tf_op jit(solution)/shard_map/ppermute | solution.py:560
  199.2 19.9 %collective-permute-start.22 = (bf16[2,128,128]{2,1,0:T(8,128)(2,1)S(1)}, bf16[2,128,128]{2,1,0:T(8,128)(2,1)S(1)}, u32[]{:S(2)}, u32[]{:S(2)}) collective-permute-start(bf16[2,128,128]{2,1,0:T(8,128)(2,1)S(1)} %pad_maximum_fusion.2), channel_id=1, source_target_pairs={{0,6},{1,7},{2,0},{3,1},{4,2},{5,3},{6,4},{7,5},{8,14},{9,15},{10,... | collective-permute-start | bytes 196616 | tf_op jit(solution)/shard_map/ppermute | solution.py:560
  199.8 19.8 %collective-permute-start.21 = (bf16[2,128,128]{2,1,0:T(8,128)(2,1)S(1)}, bf16[2,128,128]{2,1,0:T(8,128)(2,1)S(1)}, u32[]{:S(2)}, u32[]{:S(2)}) collective-permute-start(bf16[2,128,128]{2,1,0:T(8,128)(2,1)S(1)} %pad_maximum_fusion.1), channel_id=1, source_target_pairs={{0,4},{1,5},{2,6},{3,7},{4,0},{5,1},{6,2},{7,3},{8,12},{9,13},{10,... | collective-permute-start | bytes 196616 | tf_op jit(solution)/shard_map/ppermute | solution.py:560
  202.1 17.5 %collective-permute-start.20 = (bf16[2,128,128]{2,1,0:T(8,128)(2,1)S(1)}, bf16[2,128,128]{2,1,0:T(8,128)(2,1)S(1)}, u32[]{:S(2)}, u32[]{:S(2)}) collective-permute-start(bf16[2,128,128]{2,1,0:T(8,128)(2,1)S(1)} %pad_maximum_fusion), channel_id=1, source_target_pairs={{0,2},{1,3},{2,4},{3,5},{4,6},{5,7},{6,0},{7,1},{8,10},{9,11},{10,... | collective-permute-start | bytes 196616 | tf_op jit(solution)/shard_map/ppermute | solution.py:560

commit v9 on v8

--- a/solution.py
+++ b/solution.py
@@ -261,9 +261,12 @@
     return work[:, kk:]
 
 
-def solve_kernel(ridge, samples, mine_ref, peer_ref, panel_ref, out_ref):
+def solve_kernel(ridge, samples, *refs):
+    parts, panel_ref, out_ref = refs[:-2], refs[-2], refs[-1]
     kk, probes = panel_ref.shape
-    total = mine_ref[...] + peer_ref[...]
+    total = parts[0][...]
+    for ref in parts[1:]:
+        total = total + ref[...]
     cross = total[:, :probes]
     wgram = total[:, probes : probes + kk]
     start = jnp.concatenate(
@@ -284,7 +287,7 @@
     out_ref[kk:, :] = jnp.broadcast_to(rate, (out_ref.shape[0] - kk, probes))
 
 
-def solve(mine, peer, panel, ridge, samples):
+def solve(parts, panel, ridge, samples):
     probes = panel.shape[1]
     return pl.pallas_call(
         functools.partial(solve_kernel, ridge, samples),
@@ -292,7 +295,7 @@
         compiler_params=params(),
         cost_estimate=cost(50 * K * K * probes, 20 * K * probes),
         name="solve",
-    )(mine, peer, panel)
+    )(*parts, panel)
 
 
 def standardise(design, methyl_ref, terms_ref, rate, store):
@@ -489,28 +492,31 @@
     )(*at, *parts)
 
 
-def scale_kernel(probes, own_ref, *refs):
-    parts, (left_ref, out_ref) = refs[:-2], refs[-2:]
+def scale_kernel(probes, wholes, own_ref, *refs):
+    parts, halves, (left_ref, out_ref) = refs[:wholes], refs[wholes:-2], refs[-2:]
     total = own_ref[...]
     for ref in parts:
         total = total + ref[...].astype(F32)
+    for top, bottom in zip(halves[: len(halves) // 2], halves[len(halves) // 2 :]):
+        total = total + jnp.concatenate([top[...], bottom[...]], axis=0).astype(F32)
     out_ref[0] = total * (1.0 / probes)
     out_ref[1] = left_ref[...] * (1.0 / probes)
 
 
-def scale(probes, keep, parts, left):
+def scale(probes, keep, parts, tops, bottoms, left):
     rows, share = keep.shape
-    vmem = pl.BlockSpec((rows, share), lambda i: (0, 0))
-    return pl.pallas_call(
-        functools.partial(scale_kernel, probes),
+    whole = pl.BlockSpec((rows, share), lambda i: (0, 0))
+    half = pl.BlockSpec((rows // 2, share), lambda i: (0, 0))
+    return pl.pallas_call(
+        functools.partial(scale_kernel, probes, len(parts)),
         grid=(1,),
-        in_specs=[vmem] * (2 + len(parts)),
+        in_specs=[whole] * (1 + len(parts)) + [half] * (2 * len(tops)) + [whole],
         out_specs=pl.BlockSpec((2, rows, share), lambda i: (0, 0, 0)),
         out_shape=jax.ShapeDtypeStruct((3, rows, share), F32),
         compiler_params=params("arbitrary"),
         cost_estimate=cost(rows * share * 16, rows * share * 30),
         name="scale",
-    )(keep, *parts, left)
+    )(keep, *parts, *tops, *bottoms, left)
 
 
 def finish_kernel(line, probes, place_ref, core_ref, _, same_ref, other_ref, *refs):
@@ -598,16 +604,12 @@
     scores, copies = descend(parts)
     design = lax.all_to_all(copies, "probe", 0, 0)
     part = cross_products(design, methyl, panel)
-    bit = panels // 2
-    while bit > 1:
-        part = part + swap_panels(part, bit)
-        bit //= 2
-    peer = swap_panels(part, 1)
+    peers = [swap_panels(part, mask) for mask in range(1, panels)]
     half = lax.dynamic_index_in_dim(design.reshape(line, 2, K, share), core, 1, False)
     design_before = to_panel(half, 1)
     inner_mine = to_panel(same, 1)
     inner_theirs = to_panel_sibling(other, 1)
-    facts = solve(part, peer, panel, 0.0001 * samples, samples)
+    facts = solve([part, *peers], panel, 0.0001 * samples, samples)
     more = to_sibling(facts)
 
     def round_of(by, among=None):
@@ -621,11 +623,11 @@
             if rounds is None or j in rounds
         ]
 
+    zscore, *own_sends, own_keep = own_tile(at, line, design, methyl, theirs, facts, more)
     early = {1, line - 1}
     late = set(range(1, line)) - early
-
-    zscore, *own_sends, own_keep = own_tile(at, line, design, methyl, theirs, facts, more)
     own_parts = arrivals(own_sends, rounds=early)
+    tops = arrivals([value[: rows // 2] for value in own_sends], rounds=late)
     design_ends = jnp.concatenate([design_before[:quarter], design_before[line - quarter :]])
     *sends, keep = pair_tile(
         among_ends, at, line, design_ends, zscore, 0, [facts, more],
@@ -644,12 +646,12 @@
     pair_parts.append(keep)
     pair_parts += arrivals(sends, inner, late)
     pair_parts += arrivals(sends, inner, early)
-    own_parts += arrivals(own_sends, rounds=late)
+    bottoms = arrivals([value[rows // 2 :] for value in own_sends], rounds=late)
     left, same, other = fold(at, line, pair_parts)
     same = to_panel(same, -1)
     other = to_panel_sibling(other, -1)
     shifted = [on_line(jnp.stack([same[j], other[j]]), round_of(j)) for j in range(1, line)]
-    tiles = scale(probes, own_keep, own_parts, left)
+    tiles = scale(probes, own_keep, own_parts, tops, bottoms, left)
     return finish(at, line, probes, tiles, same, other, shifted), scores
 
 

time: 221 us -> 221 us (level)
  starting transfers between devices: 34.2 us -> 31.2 us
  waiting for transfers between devices: 114 us -> 117 us
    ppermute x23 -> x25, starting transfers between devices: 34.2 us -> 31.2 us  [along(): return lax.ppermute(value, axis, pairs)]
    ppermute x23 -> x25, waiting for transfers between devices: 114 us -> 117 us  [along(): return lax.ppermute(value, axis, pairs)]
  transfers between devices with their start and end apart: 23 -> 25, of which waited for: 12 -> 13; matrix products, arithmetic and copies ran while one was open for 0% -> 0% of each run, Pallas kernels for 18% -> 18%
where the time goes in v9:
time: 221 us; the launch traced here: 220 us
  waiting for transfers between devices  117 us (53%)
  Pallas kernels  41.3 us (19%)
  starting transfers between devices  31.2 us (14%)
  blocking collectives  23.8 us (11%)
  local copies, waits for them, and re-layouts  6.02 us (3%)
    ppermute x25, waiting for transfers between devices, along(): return lax.ppermute(value, axis, pairs)  117 us
    ppermute x25, starting transfers between devices, along(): return lax.ppermute(value, axis, pairs)  31.2 us
    all_to_all x1, blocking collectives, body(): parts = lax.all_to_all(parts, 'probe', 0, 0)  15.5 us
    pallas_call x3, Pallas kernels, pair_tile(): pl.pallas_call(functools.partial(pair_kernel, index_of, line, first, side...  11.1 us
    pallas_call x1, Pallas kernels, own_tile(): pl.pallas_call(functools.partial(own_kernel, steps, line), grid_spec=pltp...  10.7 us
    all_to_all x1, blocking collectives, body(): design = lax.all_to_all(copies, 'probe', 0, 0)  8.28 us
    pallas_call x1, Pallas kernels, descend(): pl.pallas_call(descend_kernel, out_shape=(jax.ShapeDtypeStruct((K, share)...  6.61 us
    unnamed x10, local copies, waits for them, and re-layouts  5.98 us
  transfers between devices with their start and end apart: 25, of which 13 were waited for; matrix products, arithmetic and copies ran while one was open for 0% of the time, Pallas kernels for 18%

profile of v9, /device:TPU:0, one launch (start us, length us, event | category | flops | bytes accessed | tf_op | source)
XLA Modules:
  0.0 220.2 jit_solution(18017272423585833855)
XLA Ops:
  1.2 2.2 copy-done
  5.0 4.5 %project.1 = (f32[8,64,128]{2,1,0:T(8,128)S(1)}, bf16[32,2048]{1,0:T(8,128)(2,1)S(1)}, bf16[256,2048]{1,0:T(8,128)(2,1)}, bf16[256,2048]{1,0:T(8,128)(2,1)}, bf16[256,2048]{1,0:T(8,128)(2,1)}) custom-call(s32[1]{0:T(128)} %bitcast.1.core_ref._, s32[64]{0:T(128)S(1)} %copy-done.4, bf16[64,2048]{1,0:T(8,128)(2,1)S(1)} %copy-done.3, bf16[1024,2048]{1,0:T(8,128)(2,1)S(1)} %copy-done), custom_call_target="tpu_custom_call" | custom-call | flops 134217728 | bytes 8388608 | tf_op jit(solution)/shard_map/project/pallas_call | solution.py:103
  9.5 15.5 %all_to_all.10.parts_ref = f32[8,64,128]{2,1,0:T(8,128)S(1)} all-to-all(f32[8,64,128]{2,1,0:T(8,128)S(1)} %get-tuple-element.25), channel_id=1, replica_groups=mesh['samp'=4,'probe'=8] {'probe'}, dimensions={0} | all-to-all | bytes 524288 | tf_op jit(solution)/shard_map/all_to_all | solution.py:603
  24.9 6.6 %descend.1 = (f32[32,128]{1,0:T(8,128)}, bf16[8,32,128]{2,1,0:T(8,128)(2,1)S(1)}) custom-call(f32[8,64,128]{2,1,0:T(8,128)S(1)} %all_to_all.10.parts_ref), custom_call_target="tpu_custom_call" | custom-call | flops 33554432 | bytes 16384 | tf_op jit(solution)/shard_map/descend/pallas_call | solution.py:197
  31.5 8.3 %all_to_all.11.design_ref = bf16[8,32,128]{2,1,0:T(8,128)(2,1)S(1)} all-to-all(bf16[8,32,128]{2,1,0:T(8,128)(2,1)S(1)} %get-tuple-element.26), channel_id=1, replica_groups=mesh['samp'=4,'probe'=8] {'probe'}, dimensions={0} | all-to-all | bytes 131072 | tf_op jit(solution)/shard_map/all_to_all | solution.py:605
  39.8 2.1 cross.1.refs_0_
  41.9 1.6 collective-permute-start.1
  45.5 6.4 %collective-permute-done.1.refs_1_ = f32[32,2304]{1,0:T(8,128)S(1)} collective-permute-done((f32[32,2304]{1,0:T(8,128)S(1)}, f32[32,2304]{1,0:T(8,128)S(1)}, u32[]{:S(2)}, u32[]{:S(2)}) %collective-permute-start.1) | collective-permute-done | bytes 294944 | tf_op jit(solution)/shard_map/ppermute | solution.py:566
  51.9 6.2 %collective-permute-done.2.refs_2_ = f32[32,2304]{1,0:T(8,128)S(1)} collective-permute-done((f32[32,2304]{1,0:T(8,128)S(1)}, f32[32,2304]{1,0:T(8,128)S(1)}, u32[]{:S(2)}, u32[]{:S(2)}) %collective-permute-start.2) | collective-permute-done | bytes 294944 | tf_op jit(solution)/shard_map/ppermute | solution.py:566
  58.1 3.8 %solve.1.facts_ref.refs_0_ = f32[40,2048]{1,0:T(8,128)S(1)} custom-call(f32[32,2304]{1,0:T(8,128)S(1)} %cross.1.refs_0_, f32[32,2304]{1,0:T(8,128)S(1)} %collective-permute-done.1.refs_1_, f32[32,2304]{1,0:T(8,128)S(1)} %collective-permute-done.2.refs_2_, f32[32,2304]{1,0:T(8,128)S(1)} %collective-permute-done.3.refs_3_, ...), custom_call_target="tpu_custom_call" | custom-call | flops 104857600 | bytes 1310720 | tf_op jit(solution)/shard_map/solve/pallas_call | solution.py:292
  65.3 2.2 copy-done.2
  67.6 44.2 %collective-permute-done.9 = bf16[4,32,128]{2,1,0:T(8,128)(2,1)S(1)} collective-permute-done((bf16[4,32,128]{2,1,0:T(8,128)(2,1)S(1)}, bf16[4,32,128]{2,1,0:T(8,128)(2,1)S(1)}, u32[]{:S(2)}, u32[]{:S(2)}) %collective-permute-start.9) | collective-permute-done | bytes 32800 | tf_op jit(solution)/shard_map/ppermute | solution.py:566
  111.8 1.9 collective-permute-start.10
  113.7 10.7 %own.1 = (bf16[1024,4096]{1,0:T(8,128)(2,1)S(1)}, bf16[1024,128]{1,0:T(8,128)(2,1)S(1)}, bf16[1024,128]{1,0:T(8,128)(2,1)S(1)}, bf16[1024,128]{1,0:T(8,128)(2,1)S(1)}, f32[1024,128]{1,0:T(8,128)S(1)}) custom-call(s32[1]{0:T(128)} %bitcast.place_ref, s32[1]{0:T(128)} %bitcast.1.core_ref._, bf16[8,32,128]{2,1,0:T(8,128)(2,1)S(1)} %all_to_all.11.design_ref, ...), custom_call_target="tpu_custom_call" | custom-call | flops 4294967296 | bytes 25165824 | tf_op jit(solution)/shard_map/own/pallas_call | solution.py:370
  124.4 3.2 %shard_map.51.refs_2_ = f32[1024,256]{1,0:T(8,128)S(1)} custom-call(s32[1]{0:T(128)} %bitcast.place_ref, bf16[2,32,128]{2,1,0:T(8,128)(2,1)S(1)} %slice.46.design_ref, bf16[1024,4096]{1,0:T(8,128)(2,1)S(1)} %get-tuple-element.32.zscore_ref, f32[40,2048]{1,0:T(8,128)S(1)} %solve.1.facts_ref.refs_0_, bf16[256,2048]{1,0:T(8,128)(2,1)} %collective-permute-done.16.refs_1_), custom_call_target="tpu_custom_call" | custom-call | flops 1073741824 | bytes 8388608 | tf_op jit(solution)/shard_map/pallas_call | solution.py:449
  127.7 3.2 %shard_map.52 = (bf16[1024,128]{1,0:T(8,128)(2,1)S(1)}, bf16[1024,128]{1,0:T(8,128)(2,1)S(1)}, bf16[1024,128]{1,0:T(8,128)(2,1)S(1)}, f32[1024,128]{1,0:T(8,128)S(1)}) custom-call(s32[1]{0:T(128)} %bitcast.place_ref, bf16[2,32,128]{2,1,0:T(8,128)(2,1)S(1)} %slice.46.design_ref, bf16[1024,4096]{1,0:T(8,128)(2,1)S(1)} %get-tuple-element.32.zscore_ref, ...), custom_call_target="tpu_custom_call" | custom-call | flops 1073741824 | bytes 8388608 | tf_op jit(solution)/shard_map/pallas_call | solution.py:449
  130.9 2.4 %collective-permute-start.17 = (bf16[1024,128]{1,0:T(8,128)(2,1)S(1)}, bf16[1024,128]{1,0:T(8,128)(2,1)S(1)}, u32[]{:S(2)}, u32[]{:S(2)}) collective-permute-start(bf16[1024,128]{1,0:T(8,128)(2,1)S(1)} %get-tuple-element.41), channel_id=1, source_target_pairs={{0,4},{1,5},{6,2},{7,3},{8,12},{9,13},{14,10},{15,11},{16,20},{17,... | collective-permute-start | bytes 786440 | tf_op jit(solution)/shard_map/ppermute | solution.py:566
  133.3 1.6 collective-permute-start.18
  135.7 2.7 %collective-permute-done.11.refs_3_ = bf16[256,2048]{1,0:T(8,128)(2,1)S(1)} collective-permute-done((bf16[256,2048]{1,0:T(8,128)(2,1)}, bf16[256,2048]{1,0:T(8,128)(2,1)S(1)}, u32[]{:S(2)}, u32[]{:S(2)}) %collective-permute-start.11) | collective-permute-done | bytes 1048608 | tf_op jit(solution)/shard_map/ppermute | solution.py:566
  138.4 21.5 %collective-permute-done.10.refs_2_ = bf16[256,2048]{1,0:T(8,128)(2,1)} collective-permute-done((bf16[256,2048]{1,0:T(8,128)(2,1)S(1)}, bf16[256,2048]{1,0:T(8,128)(2,1)}, u32[]{:S(2)}, u32[]{:S(2)}) %collective-permute-start.10) | collective-permute-done | bytes 1048608 | tf_op jit(solution)/shard_map/ppermute | solution.py:566
  159.9 4.6 %shard_map.50 = (bf16[1024,128]{1,0:T(8,128)(2,1)S(1)}, bf16[1024,128]{1,0:T(8,128)(2,1)S(1)}, bf16[1024,128]{1,0:T(8,128)(2,1)S(1)}, f32[1024,128]{1,0:T(8,128)S(1)}) custom-call(s32[1]{0:T(128)} %bitcast.place_ref, bf16[2,32,128]{2,1,0:T(8,128)(2,1)S(1)} %pad_maximum_fusion.3.design_ref, bf16[1024,4096]{1,0:T(8,128)(2,1)S(1)} %get-tuple-element.32.zscore_ref, ...), custom_call_target="tpu_custom_call" | custom-call | flops 2147483648 | bytes 8388608 | tf_op jit(solution)/shard_map/pallas_call | solution.py:449
  167.1 6.3 %collective-permute-start.14 = (bf16[1024,128]{1,0:T(8,128)(2,1)S(1)}, bf16[1024,128]{1,0:T(8,128)(2,1)S(1)}, u32[]{:S(2)}, u32[]{:S(2)}) collective-permute-start(bf16[1024,128]{1,0:T(8,128)(2,1)S(1)} %get-tuple-element.37), channel_id=1, source_target_pairs={{0,6},{1,7},{2,0},{3,1},{8,14},{9,15},{10,8},{11,9},{16,22},{17,23... | collective-permute-start | bytes 786440 | tf_op jit(solution)/shard_map/ppermute | solution.py:566
  173.5 3.5 %collective-permute-done.12.refs_1_ = bf16[1024,128]{1,0:T(8,128)(2,1)S(1)} collective-permute-done((bf16[1024,128]{1,0:T(8,128)(2,1)S(1)}, bf16[1024,128]{1,0:T(8,128)(2,1)S(1)}, u32[]{:S(2)}, u32[]{:S(2)}) %collective-permute-start.12) | collective-permute-done | bytes 262176 | tf_op jit(solution)/shard_map/ppermute | solution.py:566
  177.0 5.5 %collective-permute-done.13.refs_2_ = bf16[1024,128]{1,0:T(8,128)(2,1)S(1)} collective-permute-done((bf16[1024,128]{1,0:T(8,128)(2,1)S(1)}, bf16[1024,128]{1,0:T(8,128)(2,1)S(1)}, u32[]{:S(2)}, u32[]{:S(2)}) %collective-permute-start.13) | collective-permute-done | bytes 262176 | tf_op jit(solution)/shard_map/ppermute | solution.py:566
  182.5 5.5 %collective-permute-done.14.refs_3_ = bf16[1024,128]{1,0:T(8,128)(2,1)S(1)} collective-permute-done((bf16[1024,128]{1,0:T(8,128)(2,1)S(1)}, bf16[1024,128]{1,0:T(8,128)(2,1)S(1)}, u32[]{:S(2)}, u32[]{:S(2)}) %collective-permute-start.14) | collective-permute-done | bytes 262176 | tf_op jit(solution)/shard_map/ppermute | solution.py:566
  188.6 2.9 %collective-permute-start.8 = (bf16[512,128]{1,0:T(8,128)(2,1)S(1)}, bf16[512,128]{1,0:T(8,128)(2,1)S(1)}, u32[]{:S(2)}, u32[]{:S(2)}) collective-permute-start(bf16[512,128]{1,0:T(8,128)(2,1)S(1)} %get-tuple-element.48), channel_id=1, source_target_pairs={{0,4},{1,5},{2,6},{3,7},{4,0},{5,1},{6,2},{7,3},{8,12},{9,13},{10,... | collective-permute-start | bytes 393224 | tf_op jit(solution)/shard_map/ppermute | solution.py:566
  191.5 3.8 %collective-permute-start.6 = (bf16[1024,128]{1,0:T(8,128)(2,1)S(1)}, bf16[1024,128]{1,0:T(8,128)(2,1)S(1)}, u32[]{:S(2)}, u32[]{:S(2)}) collective-permute-start(bf16[1024,128]{1,0:T(8,128)(2,1)S(1)} %get-tuple-element.30), channel_id=1, source_target_pairs={{0,6},{1,7},{2,0},{3,1},{4,2},{5,3},{6,4},{7,5},{8,14},{9,15},{10,... | collective-permute-start | bytes 786440 | tf_op jit(solution)/shard_map/ppermute | solution.py:566
  196.5 4.0 %collective-permute-done.21.other_ref = bf16[4,128,128]{2,1,0:T(8,128)(2,1)S(1)} collective-permute-done((bf16[4,128,128]{2,1,0:T(8,128)(2,1)S(1)}, bf16[4,128,128]{2,1,0:T(8,128)(2,1)S(1)}, u32[]{:S(2)}, u32[]{:S(2)}) %collective-permute-start.21) | collective-permute-done | bytes 131104 | tf_op jit(solution)/shard_map/ppermute | solution.py:566
  200.7 4.6 %collective-permute-done.7.refs_2_ = bf16[512,128]{1,0:T(8,128)(2,1)S(1)} collective-permute-done((bf16[512,128]{1,0:T(8,128)(2,1)S(1)}, bf16[512,128]{1,0:T(8,128)(2,1)S(1)}, u32[]{:S(2)}, u32[]{:S(2)}) %collective-permute-start.7) | collective-permute-done | bytes 131104 | tf_op jit(solution)/shard_map/ppermute | solution.py:566
  205.3 2.8 %collective-permute-done.8.refs_3_ = bf16[512,128]{1,0:T(8,128)(2,1)S(1)} collective-permute-done((bf16[512,128]{1,0:T(8,128)(2,1)S(1)}, bf16[512,128]{1,0:T(8,128)(2,1)S(1)}, u32[]{:S(2)}, u32[]{:S(2)}) %collective-permute-start.8) | collective-permute-done | bytes 131104 | tf_op jit(solution)/shard_map/ppermute | solution.py:566
  208.1 3.0 %collective-permute-done.6.refs_1_ = bf16[1024,128]{1,0:T(8,128)(2,1)S(1)} collective-permute-done((bf16[1024,128]{1,0:T(8,128)(2,1)S(1)}, bf16[1024,128]{1,0:T(8,128)(2,1)S(1)}, u32[]{:S(2)}, u32[]{:S(2)}) %collective-permute-start.6) | collective-permute-done | bytes 262176 | tf_op jit(solution)/shard_map/ppermute | solution.py:566
  212.1 7.1 %collective-permute-done.23.refs_1_ = bf16[2,128,128]{2,1,0:T(8,128)(2,1)S(1)} collective-permute-done((bf16[2,128,128]{2,1,0:T(8,128)(2,1)S(1)}, bf16[2,128,128]{2,1,0:T(8,128)(2,1)S(1)}, u32[]{:S(2)}, u32[]{:S(2)}) %collective-permute-start.23) | collective-permute-done | bytes 65568 | tf_op jit(solution)/shard_map/ppermute | solution.py:566
  (52 shorter events, 14.9 us)
Async XLA Ops:
  0.6 113.1 %collective-permute-start = (bf16[1024,2048]{1,0:T(8,128)(2,1)}, bf16[1024,2048]{1,0:T(8,128)(2,1)}, u32[]{:S(2)}, u32[]{:S(2)}) collective-permute-start(bf16[1024,2048]{1,0:T(8,128)(2,1)} %from_ref.1), channel_id=1, source_target_pairs={{0,1},{1,0},{2,3},{3,2},{4,5},{5,4},{6,7},{7,6},{8,9},{9,8},{10,11... | collective-permute-start | bytes 12582920 | tf_op jit(solution)/shard_map/ppermute | solution.py:566
  1.2 2.2 copy-start
  3.4 0.9 copy-start.3
  4.3 0.7 copy-start.4
  5.0 34.9 %copy-start.1 = (bf16[1024,2048]{1,0:T(8,128)(2,1)S(1)}, bf16[1024,2048]{1,0:T(8,128)(2,1)}, u32[]{:S(2)}) copy-start(bf16[1024,2048]{1,0:T(8,128)(2,1)} %from_ref.1) | copy-start | bytes 12582916
  41.9 9.9 %collective-permute-start.1 = (f32[32,2304]{1,0:T(8,128)S(1)}, f32[32,2304]{1,0:T(8,128)S(1)}, u32[]{:S(2)}, u32[]{:S(2)}) collective-permute-start(f32[32,2304]{1,0:T(8,128)S(1)} %cross.1.refs_0_), channel_id=1, source_target_pairs={{0,8},{8,0},{16,24},{24,16},{1,9},{9,1},{17,25},{25,17},{2,10},{10... | collective-permute-start | bytes 884744 | tf_op jit(solution)/shard_map/ppermute | solution.py:566
  43.5 14.6 %collective-permute-start.2 = (f32[32,2304]{1,0:T(8,128)S(1)}, f32[32,2304]{1,0:T(8,128)S(1)}, u32[]{:S(2)}, u32[]{:S(2)}) collective-permute-start(f32[32,2304]{1,0:T(8,128)S(1)} %cross.1.refs_0_), channel_id=1, source_target_pairs={{0,16},{8,24},{16,0},{24,8},{1,17},{9,25},{17,1},{25,9},{2,18},{10... | collective-permute-start | bytes 884744 | tf_op jit(solution)/shard_map/ppermute | solution.py:566
  45.0 13.1 %collective-permute-start.3 = (f32[32,2304]{1,0:T(8,128)S(1)}, f32[32,2304]{1,0:T(8,128)S(1)}, u32[]{:S(2)}, u32[]{:S(2)}) collective-permute-start(f32[32,2304]{1,0:T(8,128)S(1)} %cross.1.refs_0_), channel_id=1, source_target_pairs={{0,24},{8,16},{16,8},{24,0},{1,25},{9,17},{17,9},{25,1},{2,26},{10... | collective-permute-start | bytes 884744 | tf_op jit(solution)/shard_map/ppermute | solution.py:566
  61.9 49.9 %collective-permute-start.4 = (f32[40,2048]{1,0:T(8,128)S(1)}, f32[40,2048]{1,0:T(8,128)S(1)}, u32[]{:S(2)}, u32[]{:S(2)}) collective-permute-start(f32[40,2048]{1,0:T(8,128)S(1)} %solve.1.facts_ref.refs_0_), channel_id=1, source_target_pairs={{0,1},{1,0},{2,3},{3,2},{4,5},{5,4},{6,7},{7,6},{8,9},{9,8},{10,11... | collective-permute-start | bytes 983048 | tf_op jit(solution)/shard_map/ppermute | solution.py:566
  62.0 62.4 %collective-permute-start.16 = (bf16[256,2048]{1,0:T(8,128)(2,1)}, bf16[256,2048]{1,0:T(8,128)(2,1)}, u32[]{:S(2)}, u32[]{:S(2)}) collective-permute-start(bf16[256,2048]{1,0:T(8,128)(2,1)} %get-tuple-element.39), channel_id=1, source_target_pairs={{0,8},{8,16},{16,24},{24,0},{1,9},{9,17},{17,25},{25,1},{2,10},{10... | collective-permute-start | bytes 3145736 | tf_op jit(solution)/shard_map/ppermute | solution.py:566
  63.2 64.4 %collective-permute-start.15 = (bf16[256,2048]{1,0:T(8,128)(2,1)}, bf16[256,2048]{1,0:T(8,128)(2,1)}, u32[]{:S(2)}, u32[]{:S(2)}) collective-permute-start(bf16[256,2048]{1,0:T(8,128)(2,1)} %get-tuple-element.38), channel_id=1, source_target_pairs={{0,9},{1,8},{2,11},{3,10},{4,13},{5,12},{6,15},{7,14},{8,17},{9,16... | collective-permute-start | bytes 3145736 | tf_op jit(solution)/shard_map/ppermute | solution.py:566
  64.8 47.0 %collective-permute-start.9 = (bf16[4,32,128]{2,1,0:T(8,128)(2,1)S(1)}, bf16[4,32,128]{2,1,0:T(8,128)(2,1)S(1)}, u32[]{:S(2)}, u32[]{:S(2)}) collective-permute-start(bf16[4,32,128]{2,1,0:T(8,128)(2,1)S(1)} %dynamic-slice_bitcast_fusion), channel_id=1, source_target_pairs={{0,8},{8,16},{16,24},{24,0},{1,9},{9,17},{17,25},{25,1},{2,10},{10... | collective-permute-start | bytes 98312 | tf_op jit(solution)/shard_map/ppermute | solution.py:566
  65.3 2.2 copy-start.2
  111.8 26.6 %collective-permute-start.11 = (bf16[256,2048]{1,0:T(8,128)(2,1)}, bf16[256,2048]{1,0:T(8,128)(2,1)S(1)}, u32[]{:S(2)}, u32[]{:S(2)}) collective-permute-start(bf16[256,2048]{1,0:T(8,128)(2,1)} %get-tuple-element.33), channel_id=1, source_target_pairs={{0,9},{1,8},{2,11},{3,10},{4,13},{5,12},{6,15},{7,14},{8,17},{9,16... | collective-permute-start | bytes 3145736 | tf_op jit(solution)/shard_map/ppermute | solution.py:566
  111.8 48.1 %collective-permute-start.10 = (bf16[256,2048]{1,0:T(8,128)(2,1)S(1)}, bf16[256,2048]{1,0:T(8,128)(2,1)}, u32[]{:S(2)}, u32[]{:S(2)}) collective-permute-start(bf16[256,2048]{1,0:T(8,128)(2,1)S(1)} %pick_ends.1), channel_id=1, source_target_pairs={{0,8},{8,16},{16,24},{24,0},{1,9},{9,17},{17,25},{25,1},{2,10},{10... | collective-permute-start | bytes 3145736 | tf_op jit(solution)/shard_map/ppermute | solution.py:566
  130.9 36.2 %collective-permute-start.17 = (bf16[1024,128]{1,0:T(8,128)(2,1)S(1)}, bf16[1024,128]{1,0:T(8,128)(2,1)S(1)}, u32[]{:S(2)}, u32[]{:S(2)}) collective-permute-start(bf16[1024,128]{1,0:T(8,128)(2,1)S(1)} %get-tuple-element.41), channel_id=1, source_target_pairs={{0,4},{1,5},{6,2},{7,3},{8,12},{9,13},{14,10},{15,11},{16,20},{17,... | collective-permute-start | bytes 786440 | tf_op jit(solution)/shard_map/ppermute | solution.py:566
  133.3 40.2 %collective-permute-start.18 = (bf16[1024,128]{1,0:T(8,128)(2,1)S(1)}, bf16[1024,128]{1,0:T(8,128)(2,1)S(1)}, u32[]{:S(2)}, u32[]{:S(2)}) collective-permute-start(bf16[1024,128]{1,0:T(8,128)(2,1)S(1)} %get-tuple-element.42), channel_id=1, source_target_pairs={{0,2},{1,3},{2,4},{3,5},{8,10},{9,11},{10,12},{11,13},{16,18},{17,... | collective-permute-start | bytes 786440 | tf_op jit(solution)/shard_map/ppermute | solution.py:566
  135.0 38.5 %collective-permute-start.19 = (bf16[1024,128]{1,0:T(8,128)(2,1)S(1)}, bf16[1024,128]{1,0:T(8,128)(2,1)S(1)}, u32[]{:S(2)}, u32[]{:S(2)}) collective-permute-start(bf16[1024,128]{1,0:T(8,128)(2,1)S(1)} %get-tuple-element.43), channel_id=1, source_target_pairs={{4,2},{5,3},{6,4},{7,5},{12,10},{13,11},{14,12},{15,13},{20,18},{2... | collective-permute-start | bytes 786440 | tf_op jit(solution)/shard_map/ppermute | solution.py:566
  164.5 12.4 %collective-permute-start.12 = (bf16[1024,128]{1,0:T(8,128)(2,1)S(1)}, bf16[1024,128]{1,0:T(8,128)(2,1)S(1)}, u32[]{:S(2)}, u32[]{:S(2)}) collective-permute-start(bf16[1024,128]{1,0:T(8,128)(2,1)S(1)} %get-tuple-element.35), channel_id=1, source_target_pairs={{4,6},{5,7},{6,0},{7,1},{12,14},{13,15},{14,8},{15,9},{20,22},{21,... | collective-permute-start | bytes 786440 | tf_op jit(solution)/shard_map/ppermute | solution.py:566
  165.8 16.7 %collective-permute-start.13 = (bf16[1024,128]{1,0:T(8,128)(2,1)S(1)}, bf16[1024,128]{1,0:T(8,128)(2,1)S(1)}, u32[]{:S(2)}, u32[]{:S(2)}) collective-permute-start(bf16[1024,128]{1,0:T(8,128)(2,1)S(1)} %get-tuple-element.36), channel_id=1, source_target_pairs={{2,6},{3,7},{4,0},{5,1},{10,14},{11,15},{12,8},{13,9},{18,22},{19,... | collective-permute-start | bytes 786440 | tf_op jit(solution)/shard_map/ppermute | solution.py:566
  167.1 20.9 %collective-permute-start.14 = (bf16[1024,128]{1,0:T(8,128)(2,1)S(1)}, bf16[1024,128]{1,0:T(8,128)(2,1)S(1)}, u32[]{:S(2)}, u32[]{:S(2)}) collective-permute-start(bf16[1024,128]{1,0:T(8,128)(2,1)S(1)} %get-tuple-element.37), channel_id=1, source_target_pairs={{0,6},{1,7},{2,0},{3,1},{8,14},{9,15},{10,8},{11,9},{16,22},{17,23... | collective-permute-start | bytes 786440 | tf_op jit(solution)/shard_map/ppermute | solution.py:566
  188.4 6.9 %collective-permute-start.20 = (bf16[4,128,128]{2,1,0:T(8,128)(2,1)S(1)}, bf16[4,128,128]{2,1,0:T(8,128)(2,1)S(1)}, u32[]{:S(2)}, u32[]{:S(2)}) collective-permute-start(bf16[4,128,128]{2,1,0:T(8,128)(2,1)S(1)} %get-tuple-element.45), channel_id=1, source_target_pairs={{0,24},{8,0},{16,8},{24,16},{1,25},{9,1},{17,9},{25,17},{2,26},{10... | collective-permute-start | bytes 393224 | tf_op jit(solution)/shard_map/ppermute | solution.py:566
  188.5 16.8 %collective-permute-start.7 = (bf16[512,128]{1,0:T(8,128)(2,1)S(1)}, bf16[512,128]{1,0:T(8,128)(2,1)S(1)}, u32[]{:S(2)}, u32[]{:S(2)}) collective-permute-start(bf16[512,128]{1,0:T(8,128)(2,1)S(1)} %get-tuple-element.49), channel_id=1, source_target_pairs={{0,4},{1,5},{2,6},{3,7},{4,0},{5,1},{6,2},{7,3},{8,12},{9,13},{10,... | collective-permute-start | bytes 393224 | tf_op jit(solution)/shard_map/ppermute | solution.py:566
  188.6 19.5 %collective-permute-start.8 = (bf16[512,128]{1,0:T(8,128)(2,1)S(1)}, bf16[512,128]{1,0:T(8,128)(2,1)S(1)}, u32[]{:S(2)}, u32[]{:S(2)}) collective-permute-start(bf16[512,128]{1,0:T(8,128)(2,1)S(1)} %get-tuple-element.48), channel_id=1, source_target_pairs={{0,4},{1,5},{2,6},{3,7},{4,0},{5,1},{6,2},{7,3},{8,12},{9,13},{10,... | collective-permute-start | bytes 393224 | tf_op jit(solution)/shard_map/ppermute | solution.py:566
  191.5 16.6 %collective-permute-start.5 = (bf16[1024,128]{1,0:T(8,128)(2,1)S(1)}, bf16[1024,128]{1,0:T(8,128)(2,1)S(1)}, u32[]{:S(2)}, u32[]{:S(2)}) collective-permute-start(bf16[1024,128]{1,0:T(8,128)(2,1)S(1)} %get-tuple-element.29), channel_id=1, source_target_pairs={{0,2},{1,3},{2,4},{3,5},{4,6},{5,7},{6,0},{7,1},{8,10},{9,11},{10,... | collective-permute-start | bytes 786440 | tf_op jit(solution)/shard_map/ppermute | solution.py:566
  191.5 19.5 %collective-permute-start.6 = (bf16[1024,128]{1,0:T(8,128)(2,1)S(1)}, bf16[1024,128]{1,0:T(8,128)(2,1)S(1)}, u32[]{:S(2)}, u32[]{:S(2)}) collective-permute-start(bf16[1024,128]{1,0:T(8,128)(2,1)S(1)} %get-tuple-element.30), channel_id=1, source_target_pairs={{0,6},{1,7},{2,0},{3,1},{4,2},{5,3},{6,4},{7,5},{8,14},{9,15},{10,... | collective-permute-start | bytes 786440 | tf_op jit(solution)/shard_map/ppermute | solution.py:566
  195.3 5.2 %collective-permute-start.21 = (bf16[4,128,128]{2,1,0:T(8,128)(2,1)S(1)}, bf16[4,128,128]{2,1,0:T(8,128)(2,1)S(1)}, u32[]{:S(2)}, u32[]{:S(2)}) collective-permute-start(bf16[4,128,128]{2,1,0:T(8,128)(2,1)S(1)} %get-tuple-element.46), channel_id=1, source_target_pairs={{0,25},{1,24},{2,27},{3,26},{4,29},{5,28},{6,31},{7,30},{8,1},{9,0... | collective-permute-start | bytes 393224 | tf_op jit(solution)/shard_map/ppermute | solution.py:566
  200.6 11.6 %collective-permute-start.24 = (bf16[2,128,128]{2,1,0:T(8,128)(2,1)S(1)}, bf16[2,128,128]{2,1,0:T(8,128)(2,1)S(1)}, u32[]{:S(2)}, u32[]{:S(2)}) collective-permute-start(bf16[2,128,128]{2,1,0:T(8,128)(2,1)S(1)} %pad_maximum_fusion.2), channel_id=1, source_target_pairs={{0,6},{1,7},{2,0},{3,1},{4,2},{5,3},{6,4},{7,5},{8,14},{9,15},{10,... | collective-permute-start | bytes 196616 | tf_op jit(solution)/shard_map/ppermute | solution.py:566
  205.3 13.9 %collective-permute-start.23 = (bf16[2,128,128]{2,1,0:T(8,128)(2,1)S(1)}, bf16[2,128,128]{2,1,0:T(8,128)(2,1)S(1)}, u32[]{:S(2)}, u32[]{:S(2)}) collective-permute-start(bf16[2,128,128]{2,1,0:T(8,128)(2,1)S(1)} %pad_maximum_fusion.1), channel_id=1, source_target_pairs={{0,4},{1,5},{2,6},{3,7},{4,0},{5,1},{6,2},{7,3},{8,12},{9,13},{10,... | collective-permute-start | bytes 196616 | tf_op jit(solution)/shard_map/ppermute | solution.py:566
  208.1 11.1 %collective-permute-start.22 = (bf16[2,128,128]{2,1,0:T(8,128)(2,1)S(1)}, bf16[2,128,128]{2,1,0:T(8,128)(2,1)S(1)}, u32[]{:S(2)}, u32[]{:S(2)}) collective-permute-start(bf16[2,128,128]{2,1,0:T(8,128)(2,1)S(1)} %pad_maximum_fusion), channel_id=1, source_target_pairs={{0,2},{1,3},{2,4},{3,5},{4,6},{5,7},{6,0},{7,1},{8,10},{9,11},{10,... | collective-permute-start | bytes 196616 | tf_op jit(solution)/shard_map/ppermute | solution.py:566

commit v10 on v9

--- a/solution.py
+++ b/solution.py
@@ -13,6 +13,7 @@
 F32, BF16 = jnp.float32, jnp.bfloat16
 HIGHEST = lax.Precision.HIGHEST
 LANES = 128
+HALF = LANES // 2
 VMEM_LIMIT = 40 * 1024 * 1024
 
 
@@ -223,9 +224,9 @@
         out_ref[:, cols] += jnp.dot(design, methyl_ref[:, cols], preferred_element_type=F32)
         left = methyl_ref[:, cols].astype(F32) - tn(design, panel_ref[:, cols])
         squares = jnp.sum(left * left, axis=0, keepdims=True)
-        for b in range(0, width, LANES):
-            row = (at + b) // LANES
-            out_ref[row : row + 1, probes + LANES :] += squares[:, b : b + LANES]
+        for b in range(0, width, HALF):
+            row = (at + b) // HALF
+            out_ref[row : row + 1, probes + HALF :] += squares[:, b : b + HALF]
 
 
 def cross_products(design, methyl, panel):
@@ -240,8 +241,8 @@
             pl.BlockSpec((chunk, probes), lambda i: (i, 0)),
             pl.BlockSpec((K, probes), lambda i: (0, 0)),
         ],
-        out_specs=pl.BlockSpec((K, probes + 2 * LANES), lambda i: (0, 0)),
-        out_shape=jax.ShapeDtypeStruct((K, probes + 2 * LANES), F32),
+        out_specs=pl.BlockSpec((K, probes + LANES), lambda i: (0, 0)),
+        out_shape=jax.ShapeDtypeStruct((K, probes + LANES), F32),
         compiler_params=params("arbitrary"),
         cost_estimate=cost(4 * K * rows * probes, 2 * rows * probes),
         name="cross",
@@ -270,7 +271,7 @@
     cross = total[:, :probes]
     wgram = total[:, probes : probes + kk]
     start = jnp.concatenate(
-        [total[r : r + 1, probes + LANES :] for r in range(probes // LANES)], axis=1
+        [total[r : r + 1, probes + HALF :] for r in range(probes // HALF)], axis=1
     )
     row = lax.broadcasted_iota(jnp.int32, (kk, kk), 0)
     col = lax.broadcasted_iota(jnp.int32, (kk, kk), 1)
@@ -646,11 +647,13 @@
     pair_parts.append(keep)
     pair_parts += arrivals(sends, inner, late)
     pair_parts += arrivals(sends, inner, early)
-    bottoms = arrivals([value[rows // 2 :] for value in own_sends], rounds=late)
     left, same, other = fold(at, line, pair_parts)
     same = to_panel(same, -1)
     other = to_panel_sibling(other, -1)
-    shifted = [on_line(jnp.stack([same[j], other[j]]), round_of(j)) for j in range(1, line)]
+    bottoms = arrivals([value[rows // 2 :] for value in own_sends], rounds=late)
+    shifted = []
+    for j in range(1, line):
+        shifted.append(on_line(jnp.stack([same[j], other[j]]), round_of(j)))
     tiles = scale(probes, own_keep, own_parts, tops, bottoms, left)
     return finish(at, line, probes, tiles, same, other, shifted), scores
 

time: 221 us -> 220 us (level)
  no operation moved by 1% of the time
where the time goes in v10:
time: 220 us
  waiting for transfers between devices  116 us (53%)
  Pallas kernels  41.5 us (19%)
  starting transfers between devices  31.2 us (14%)
  blocking collectives  23.8 us (11%)
  local copies, waits for them, and re-layouts  6.02 us (3%)
    ppermute x25, waiting for transfers between devices, along(): return lax.ppermute(value, axis, pairs)  116 us
    ppermute x25, starting transfers between devices, along(): return lax.ppermute(value, axis, pairs)  31.2 us
    all_to_all x1, blocking collectives, body(): parts = lax.all_to_all(parts, 'probe', 0, 0)  15.5 us
    pallas_call x3, Pallas kernels, pair_tile(): pl.pallas_call(functools.partial(pair_kernel, index_of, line, first, side...  11.1 us
    pallas_call x1, Pallas kernels, own_tile(): pl.pallas_call(functools.partial(own_kernel, steps, line), grid_spec=pltp...  10.7 us
    all_to_all x1, blocking collectives, body(): design = lax.all_to_all(copies, 'probe', 0, 0)  8.28 us
    pallas_call x1, Pallas kernels, descend(): pl.pallas_call(descend_kernel, out_shape=(jax.ShapeDtypeStruct((K, share)...  6.61 us
    unnamed x10, local copies, waits for them, and re-layouts  5.98 us
  transfers between devices with their start and end apart: 25, of which 13 were waited for; matrix products, arithmetic and copies ran while one was open for 0% of the time, Pallas kernels for 18%

profile of v10, /device:TPU:0, one launch (start us, length us, event | category | flops | bytes accessed | tf_op | source)
XLA Modules:
  0.0 219.6 jit_solution(18167062296789319467)
XLA Ops:
  1.2 2.2 copy-done
  5.0 4.5 %project.1 = (f32[8,64,128]{2,1,0:T(8,128)S(1)}, bf16[32,2048]{1,0:T(8,128)(2,1)S(1)}, bf16[256,2048]{1,0:T(8,128)(2,1)}, bf16[256,2048]{1,0:T(8,128)(2,1)}, bf16[256,2048]{1,0:T(8,128)(2,1)}) custom-call(s32[1]{0:T(128)} %bitcast.1.core_ref._, s32[64]{0:T(128)S(1)} %copy-done.4, bf16[64,2048]{1,0:T(8,128)(2,1)S(1)} %copy-done.3, bf16[1024,2048]{1,0:T(8,128)(2,1)S(1)} %copy-done), custom_call_target="tpu_custom_call" | custom-call | flops 134217728 | bytes 8388608 | tf_op jit(solution)/shard_map/project/pallas_call | solution.py:104
  9.5 15.5 %all_to_all.10.parts_ref = f32[8,64,128]{2,1,0:T(8,128)S(1)} all-to-all(f32[8,64,128]{2,1,0:T(8,128)S(1)} %get-tuple-element.25), channel_id=1, replica_groups=mesh['samp'=4,'probe'=8] {'probe'}, dimensions={0} | all-to-all | bytes 524288 | tf_op jit(solution)/shard_map/all_to_all | solution.py:604
  24.9 6.6 %descend.1 = (f32[32,128]{1,0:T(8,128)}, bf16[8,32,128]{2,1,0:T(8,128)(2,1)S(1)}) custom-call(f32[8,64,128]{2,1,0:T(8,128)S(1)} %all_to_all.10.parts_ref), custom_call_target="tpu_custom_call" | custom-call | flops 33554432 | bytes 16384 | tf_op jit(solution)/shard_map/descend/pallas_call | solution.py:198
  31.5 8.3 %all_to_all.11.design_ref = bf16[8,32,128]{2,1,0:T(8,128)(2,1)S(1)} all-to-all(bf16[8,32,128]{2,1,0:T(8,128)(2,1)S(1)} %get-tuple-element.26), channel_id=1, replica_groups=mesh['samp'=4,'probe'=8] {'probe'}, dimensions={0} | all-to-all | bytes 131072 | tf_op jit(solution)/shard_map/all_to_all | solution.py:606
  39.8 2.3 %cross.1.refs_0_ = f32[32,2176]{1,0:T(8,128)S(1)} custom-call(bf16[8,32,128]{2,1,0:T(8,128)(2,1)S(1)} %all_to_all.11.design_ref, bf16[1024,2048]{1,0:T(8,128)(2,1)S(1)} %copy-done.1, bf16[32,2048]{1,0:T(8,128)(2,1)S(1)} %get-tuple-element.27.panel_ref.refs_4_), custom_call_target="tpu_custom_call" | custom-call | flops 268435456 | bytes 4194304 | tf_op jit(solution)/shard_map/cross/pallas_call | solution.py:236
  43.6 1.5 collective-permute-start.2
  45.7 6.0 %collective-permute-done.1.refs_1_ = f32[32,2176]{1,0:T(8,128)S(1)} collective-permute-done((f32[32,2176]{1,0:T(8,128)S(1)}, f32[32,2176]{1,0:T(8,128)S(1)}, u32[]{:S(2)}, u32[]{:S(2)}) %collective-permute-start.1) | collective-permute-done | bytes 278560 | tf_op jit(solution)/shard_map/ppermute | solution.py:567
  51.7 5.8 %collective-permute-done.2.refs_2_ = f32[32,2176]{1,0:T(8,128)S(1)} collective-permute-done((f32[32,2176]{1,0:T(8,128)S(1)}, f32[32,2176]{1,0:T(8,128)S(1)}, u32[]{:S(2)}, u32[]{:S(2)}) %collective-permute-start.2) | collective-permute-done | bytes 278560 | tf_op jit(solution)/shard_map/ppermute | solution.py:567
  57.5 3.8 %solve.1.facts_ref.refs_0_ = f32[40,2048]{1,0:T(8,128)S(1)} custom-call(f32[32,2176]{1,0:T(8,128)S(1)} %cross.1.refs_0_, f32[32,2176]{1,0:T(8,128)S(1)} %collective-permute-done.1.refs_1_, f32[32,2176]{1,0:T(8,128)S(1)} %collective-permute-done.2.refs_2_, f32[32,2176]{1,0:T(8,128)S(1)} %collective-permute-done.3.refs_3_, ...), custom_call_target="tpu_custom_call" | custom-call | flops 104857600 | bytes 1310720 | tf_op jit(solution)/shard_map/solve/pallas_call | solution.py:293
  64.8 2.2 copy-done.2
  67.1 44.2 %collective-permute-done.9 = bf16[4,32,128]{2,1,0:T(8,128)(2,1)S(1)} collective-permute-done((bf16[4,32,128]{2,1,0:T(8,128)(2,1)S(1)}, bf16[4,32,128]{2,1,0:T(8,128)(2,1)S(1)}, u32[]{:S(2)}, u32[]{:S(2)}) %collective-permute-start.9) | collective-permute-done | bytes 32800 | tf_op jit(solution)/shard_map/ppermute | solution.py:567
  111.3 1.9 collective-permute-start.10
  113.2 10.7 %own.1 = (bf16[1024,4096]{1,0:T(8,128)(2,1)S(1)}, bf16[1024,128]{1,0:T(8,128)(2,1)S(1)}, bf16[1024,128]{1,0:T(8,128)(2,1)S(1)}, bf16[1024,128]{1,0:T(8,128)(2,1)S(1)}, f32[1024,128]{1,0:T(8,128)S(1)}) custom-call(s32[1]{0:T(128)} %bitcast.place_ref, s32[1]{0:T(128)} %bitcast.1.core_ref._, bf16[8,32,128]{2,1,0:T(8,128)(2,1)S(1)} %all_to_all.11.design_ref, ...), custom_call_target="tpu_custom_call" | custom-call | flops 4294967296 | bytes 25165824 | tf_op jit(solution)/shard_map/own/pallas_call | solution.py:371
  123.9 3.2 %shard_map.51.refs_2_ = f32[1024,256]{1,0:T(8,128)S(1)} custom-call(s32[1]{0:T(128)} %bitcast.place_ref, bf16[2,32,128]{2,1,0:T(8,128)(2,1)S(1)} %slice.46.design_ref, bf16[1024,4096]{1,0:T(8,128)(2,1)S(1)} %get-tuple-element.32.zscore_ref, f32[40,2048]{1,0:T(8,128)S(1)} %solve.1.facts_ref.refs_0_, bf16[256,2048]{1,0:T(8,128)(2,1)} %collective-permute-done.16.refs_1_), custom_call_target="tpu_custom_call" | custom-call | flops 1073741824 | bytes 8388608 | tf_op jit(solution)/shard_map/pallas_call | solution.py:450
  127.1 3.2 %shard_map.52 = (bf16[1024,128]{1,0:T(8,128)(2,1)S(1)}, bf16[1024,128]{1,0:T(8,128)(2,1)S(1)}, bf16[1024,128]{1,0:T(8,128)(2,1)S(1)}, f32[1024,128]{1,0:T(8,128)S(1)}) custom-call(s32[1]{0:T(128)} %bitcast.place_ref, bf16[2,32,128]{2,1,0:T(8,128)(2,1)S(1)} %slice.46.design_ref, bf16[1024,4096]{1,0:T(8,128)(2,1)S(1)} %get-tuple-element.32.zscore_ref, ...), custom_call_target="tpu_custom_call" | custom-call | flops 1073741824 | bytes 8388608 | tf_op jit(solution)/shard_map/pallas_call | solution.py:450
  130.4 2.4 %collective-permute-start.17 = (bf16[1024,128]{1,0:T(8,128)(2,1)S(1)}, bf16[1024,128]{1,0:T(8,128)(2,1)S(1)}, u32[]{:S(2)}, u32[]{:S(2)}) collective-permute-start(bf16[1024,128]{1,0:T(8,128)(2,1)S(1)} %get-tuple-element.41), channel_id=1, source_target_pairs={{0,4},{1,5},{6,2},{7,3},{8,12},{9,13},{14,10},{15,11},{16,20},{17,... | collective-permute-start | bytes 786440 | tf_op jit(solution)/shard_map/ppermute | solution.py:567
  132.8 1.7 collective-permute-start.18
  135.1 2.7 %collective-permute-done.11.refs_3_ = bf16[256,2048]{1,0:T(8,128)(2,1)S(1)} collective-permute-done((bf16[256,2048]{1,0:T(8,128)(2,1)}, bf16[256,2048]{1,0:T(8,128)(2,1)S(1)}, u32[]{:S(2)}, u32[]{:S(2)}) %collective-permute-start.11) | collective-permute-done | bytes 1048608 | tf_op jit(solution)/shard_map/ppermute | solution.py:567
  137.9 21.5 %collective-permute-done.10.refs_2_ = bf16[256,2048]{1,0:T(8,128)(2,1)} collective-permute-done((bf16[256,2048]{1,0:T(8,128)(2,1)S(1)}, bf16[256,2048]{1,0:T(8,128)(2,1)}, u32[]{:S(2)}, u32[]{:S(2)}) %collective-permute-start.10) | collective-permute-done | bytes 1048608 | tf_op jit(solution)/shard_map/ppermute | solution.py:567
  159.4 4.6 %shard_map.50 = (bf16[1024,128]{1,0:T(8,128)(2,1)S(1)}, bf16[1024,128]{1,0:T(8,128)(2,1)S(1)}, bf16[1024,128]{1,0:T(8,128)(2,1)S(1)}, f32[1024,128]{1,0:T(8,128)S(1)}) custom-call(s32[1]{0:T(128)} %bitcast.place_ref, bf16[2,32,128]{2,1,0:T(8,128)(2,1)S(1)} %pad_maximum_fusion.3.design_ref, bf16[1024,4096]{1,0:T(8,128)(2,1)S(1)} %get-tuple-element.32.zscore_ref, ...), custom_call_target="tpu_custom_call" | custom-call | flops 2147483648 | bytes 8388608 | tf_op jit(solution)/shard_map/pallas_call | solution.py:450
  166.6 6.3 %collective-permute-start.14 = (bf16[1024,128]{1,0:T(8,128)(2,1)S(1)}, bf16[1024,128]{1,0:T(8,128)(2,1)S(1)}, u32[]{:S(2)}, u32[]{:S(2)}) collective-permute-start(bf16[1024,128]{1,0:T(8,128)(2,1)S(1)} %get-tuple-element.37), channel_id=1, source_target_pairs={{0,6},{1,7},{2,0},{3,1},{8,14},{9,15},{10,8},{11,9},{16,22},{17,23... | collective-permute-start | bytes 786440 | tf_op jit(solution)/shard_map/ppermute | solution.py:567
  173.0 3.5 %collective-permute-done.12.refs_1_ = bf16[1024,128]{1,0:T(8,128)(2,1)S(1)} collective-permute-done((bf16[1024,128]{1,0:T(8,128)(2,1)S(1)}, bf16[1024,128]{1,0:T(8,128)(2,1)S(1)}, u32[]{:S(2)}, u32[]{:S(2)}) %collective-permute-start.12) | collective-permute-done | bytes 262176 | tf_op jit(solution)/shard_map/ppermute | solution.py:567
  176.4 5.5 %collective-permute-done.13.refs_2_ = bf16[1024,128]{1,0:T(8,128)(2,1)S(1)} collective-permute-done((bf16[1024,128]{1,0:T(8,128)(2,1)S(1)}, bf16[1024,128]{1,0:T(8,128)(2,1)S(1)}, u32[]{:S(2)}, u32[]{:S(2)}) %collective-permute-start.13) | collective-permute-done | bytes 262176 | tf_op jit(solution)/shard_map/ppermute | solution.py:567
  181.9 5.5 %collective-permute-done.14.refs_3_ = bf16[1024,128]{1,0:T(8,128)(2,1)S(1)} collective-permute-done((bf16[1024,128]{1,0:T(8,128)(2,1)S(1)}, bf16[1024,128]{1,0:T(8,128)(2,1)S(1)}, u32[]{:S(2)}, u32[]{:S(2)}) %collective-permute-start.14) | collective-permute-done | bytes 262176 | tf_op jit(solution)/shard_map/ppermute | solution.py:567
  188.1 2.9 %collective-permute-start.8 = (bf16[512,128]{1,0:T(8,128)(2,1)S(1)}, bf16[512,128]{1,0:T(8,128)(2,1)S(1)}, u32[]{:S(2)}, u32[]{:S(2)}) collective-permute-start(bf16[512,128]{1,0:T(8,128)(2,1)S(1)} %get-tuple-element.48), channel_id=1, source_target_pairs={{0,4},{1,5},{2,6},{3,7},{4,0},{5,1},{6,2},{7,3},{8,12},{9,13},{10,... | collective-permute-start | bytes 393224 | tf_op jit(solution)/shard_map/ppermute | solution.py:567
  191.0 3.8 %collective-permute-start.6 = (bf16[1024,128]{1,0:T(8,128)(2,1)S(1)}, bf16[1024,128]{1,0:T(8,128)(2,1)S(1)}, u32[]{:S(2)}, u32[]{:S(2)}) collective-permute-start(bf16[1024,128]{1,0:T(8,128)(2,1)S(1)} %get-tuple-element.30), channel_id=1, source_target_pairs={{0,6},{1,7},{2,0},{3,1},{4,2},{5,3},{6,4},{7,5},{8,14},{9,15},{10,... | collective-permute-start | bytes 786440 | tf_op jit(solution)/shard_map/ppermute | solution.py:567
  196.0 4.0 %collective-permute-done.21.other_ref = bf16[4,128,128]{2,1,0:T(8,128)(2,1)S(1)} collective-permute-done((bf16[4,128,128]{2,1,0:T(8,128)(2,1)S(1)}, bf16[4,128,128]{2,1,0:T(8,128)(2,1)S(1)}, u32[]{:S(2)}, u32[]{:S(2)}) %collective-permute-start.21) | collective-permute-done | bytes 131104 | tf_op jit(solution)/shard_map/ppermute | solution.py:567
  200.2 4.6 %collective-permute-done.7.refs_2_ = bf16[512,128]{1,0:T(8,128)(2,1)S(1)} collective-permute-done((bf16[512,128]{1,0:T(8,128)(2,1)S(1)}, bf16[512,128]{1,0:T(8,128)(2,1)S(1)}, u32[]{:S(2)}, u32[]{:S(2)}) %collective-permute-start.7) | collective-permute-done | bytes 131104 | tf_op jit(solution)/shard_map/ppermute | solution.py:567
  204.8 2.8 %collective-permute-done.8.refs_3_ = bf16[512,128]{1,0:T(8,128)(2,1)S(1)} collective-permute-done((bf16[512,128]{1,0:T(8,128)(2,1)S(1)}, bf16[512,128]{1,0:T(8,128)(2,1)S(1)}, u32[]{:S(2)}, u32[]{:S(2)}) %collective-permute-start.8) | collective-permute-done | bytes 131104 | tf_op jit(solution)/shard_map/ppermute | solution.py:567
  207.5 3.0 %collective-permute-done.6.refs_1_ = bf16[1024,128]{1,0:T(8,128)(2,1)S(1)} collective-permute-done((bf16[1024,128]{1,0:T(8,128)(2,1)S(1)}, bf16[1024,128]{1,0:T(8,128)(2,1)S(1)}, u32[]{:S(2)}, u32[]{:S(2)}) %collective-permute-start.6) | collective-permute-done | bytes 262176 | tf_op jit(solution)/shard_map/ppermute | solution.py:567
  211.6 7.1 %collective-permute-done.23.refs_1_ = bf16[2,128,128]{2,1,0:T(8,128)(2,1)S(1)} collective-permute-done((bf16[2,128,128]{2,1,0:T(8,128)(2,1)S(1)}, bf16[2,128,128]{2,1,0:T(8,128)(2,1)S(1)}, u32[]{:S(2)}, u32[]{:S(2)}) %collective-permute-start.23) | collective-permute-done | bytes 65568 | tf_op jit(solution)/shard_map/ppermute | solution.py:567
  (52 shorter events, 14.9 us)
Async XLA Ops:
  0.6 112.6 %collective-permute-start = (bf16[1024,2048]{1,0:T(8,128)(2,1)}, bf16[1024,2048]{1,0:T(8,128)(2,1)}, u32[]{:S(2)}, u32[]{:S(2)}) collective-permute-start(bf16[1024,2048]{1,0:T(8,128)(2,1)} %from_ref.1), channel_id=1, source_target_pairs={{0,1},{1,0},{2,3},{3,2},{4,5},{5,4},{6,7},{7,6},{8,9},{9,8},{10,11... | collective-permute-start | bytes 12582920 | tf_op jit(solution)/shard_map/ppermute | solution.py:567
  1.2 2.2 copy-start
  3.4 0.9 copy-start.3
  4.3 0.7 copy-start.4
  5.0 34.9 %copy-start.1 = (bf16[1024,2048]{1,0:T(8,128)(2,1)S(1)}, bf16[1024,2048]{1,0:T(8,128)(2,1)}, u32[]{:S(2)}) copy-start(bf16[1024,2048]{1,0:T(8,128)(2,1)} %from_ref.1) | copy-start | bytes 12582916
  42.1 9.6 %collective-permute-start.1 = (f32[32,2176]{1,0:T(8,128)S(1)}, f32[32,2176]{1,0:T(8,128)S(1)}, u32[]{:S(2)}, u32[]{:S(2)}) collective-permute-start(f32[32,2176]{1,0:T(8,128)S(1)} %cross.1.refs_0_), channel_id=1, source_target_pairs={{0,8},{8,0},{16,24},{24,16},{1,9},{9,1},{17,25},{25,17},{2,10},{10... | collective-permute-start | bytes 835592 | tf_op jit(solution)/shard_map/ppermute | solution.py:567
  43.6 13.9 %collective-permute-start.2 = (f32[32,2176]{1,0:T(8,128)S(1)}, f32[32,2176]{1,0:T(8,128)S(1)}, u32[]{:S(2)}, u32[]{:S(2)}) collective-permute-start(f32[32,2176]{1,0:T(8,128)S(1)} %cross.1.refs_0_), channel_id=1, source_target_pairs={{0,16},{8,24},{16,0},{24,8},{1,17},{9,25},{17,1},{25,9},{2,18},{10... | collective-permute-start | bytes 835592 | tf_op jit(solution)/shard_map/ppermute | solution.py:567
  45.2 12.4 %collective-permute-start.3 = (f32[32,2176]{1,0:T(8,128)S(1)}, f32[32,2176]{1,0:T(8,128)S(1)}, u32[]{:S(2)}, u32[]{:S(2)}) collective-permute-start(f32[32,2176]{1,0:T(8,128)S(1)} %cross.1.refs_0_), channel_id=1, source_target_pairs={{0,24},{8,16},{16,8},{24,0},{1,25},{9,17},{17,9},{25,1},{2,26},{10... | collective-permute-start | bytes 835592 | tf_op jit(solution)/shard_map/ppermute | solution.py:567
  61.4 49.9 %collective-permute-start.4 = (f32[40,2048]{1,0:T(8,128)S(1)}, f32[40,2048]{1,0:T(8,128)S(1)}, u32[]{:S(2)}, u32[]{:S(2)}) collective-permute-start(f32[40,2048]{1,0:T(8,128)S(1)} %solve.1.facts_ref.refs_0_), channel_id=1, source_target_pairs={{0,1},{1,0},{2,3},{3,2},{4,5},{5,4},{6,7},{7,6},{8,9},{9,8},{10,11... | collective-permute-start | bytes 983048 | tf_op jit(solution)/shard_map/ppermute | solution.py:567
  61.4 62.4 %collective-permute-start.16 = (bf16[256,2048]{1,0:T(8,128)(2,1)}, bf16[256,2048]{1,0:T(8,128)(2,1)}, u32[]{:S(2)}, u32[]{:S(2)}) collective-permute-start(bf16[256,2048]{1,0:T(8,128)(2,1)} %get-tuple-element.39), channel_id=1, source_target_pairs={{0,8},{8,16},{16,24},{24,0},{1,9},{9,17},{17,25},{25,1},{2,10},{10... | collective-permute-start | bytes 3145736 | tf_op jit(solution)/shard_map/ppermute | solution.py:567
  62.7 64.4 %collective-permute-start.15 = (bf16[256,2048]{1,0:T(8,128)(2,1)}, bf16[256,2048]{1,0:T(8,128)(2,1)}, u32[]{:S(2)}, u32[]{:S(2)}) collective-permute-start(bf16[256,2048]{1,0:T(8,128)(2,1)} %get-tuple-element.38), channel_id=1, source_target_pairs={{0,9},{1,8},{2,11},{3,10},{4,13},{5,12},{6,15},{7,14},{8,17},{9,16... | collective-permute-start | bytes 3145736 | tf_op jit(solution)/shard_map/ppermute | solution.py:567
  64.3 47.0 %collective-permute-start.9 = (bf16[4,32,128]{2,1,0:T(8,128)(2,1)S(1)}, bf16[4,32,128]{2,1,0:T(8,128)(2,1)S(1)}, u32[]{:S(2)}, u32[]{:S(2)}) collective-permute-start(bf16[4,32,128]{2,1,0:T(8,128)(2,1)S(1)} %dynamic-slice_bitcast_fusion), channel_id=1, source_target_pairs={{0,8},{8,16},{16,24},{24,0},{1,9},{9,17},{17,25},{25,1},{2,10},{10... | collective-permute-start | bytes 98312 | tf_op jit(solution)/shard_map/ppermute | solution.py:567
  64.8 2.2 copy-start.2
  111.3 26.6 %collective-permute-start.11 = (bf16[256,2048]{1,0:T(8,128)(2,1)}, bf16[256,2048]{1,0:T(8,128)(2,1)S(1)}, u32[]{:S(2)}, u32[]{:S(2)}) collective-permute-start(bf16[256,2048]{1,0:T(8,128)(2,1)} %get-tuple-element.33), channel_id=1, source_target_pairs={{0,9},{1,8},{2,11},{3,10},{4,13},{5,12},{6,15},{7,14},{8,17},{9,16... | collective-permute-start | bytes 3145736 | tf_op jit(solution)/shard_map/ppermute | solution.py:567
  111.3 48.1 %collective-permute-start.10 = (bf16[256,2048]{1,0:T(8,128)(2,1)S(1)}, bf16[256,2048]{1,0:T(8,128)(2,1)}, u32[]{:S(2)}, u32[]{:S(2)}) collective-permute-start(bf16[256,2048]{1,0:T(8,128)(2,1)S(1)} %pick_ends.1), channel_id=1, source_target_pairs={{0,8},{8,16},{16,24},{24,0},{1,9},{9,17},{17,25},{25,1},{2,10},{10... | collective-permute-start | bytes 3145736 | tf_op jit(solution)/shard_map/ppermute | solution.py:567
  130.4 36.2 %collective-permute-start.17 = (bf16[1024,128]{1,0:T(8,128)(2,1)S(1)}, bf16[1024,128]{1,0:T(8,128)(2,1)S(1)}, u32[]{:S(2)}, u32[]{:S(2)}) collective-permute-start(bf16[1024,128]{1,0:T(8,128)(2,1)S(1)} %get-tuple-element.41), channel_id=1, source_target_pairs={{0,4},{1,5},{6,2},{7,3},{8,12},{9,13},{14,10},{15,11},{16,20},{17,... | collective-permute-start | bytes 786440 | tf_op jit(solution)/shard_map/ppermute | solution.py:567
  132.8 40.2 %collective-permute-start.18 = (bf16[1024,128]{1,0:T(8,128)(2,1)S(1)}, bf16[1024,128]{1,0:T(8,128)(2,1)S(1)}, u32[]{:S(2)}, u32[]{:S(2)}) collective-permute-start(bf16[1024,128]{1,0:T(8,128)(2,1)S(1)} %get-tuple-element.42), channel_id=1, source_target_pairs={{0,2},{1,3},{2,4},{3,5},{8,10},{9,11},{10,12},{11,13},{16,18},{17,... | collective-permute-start | bytes 786440 | tf_op jit(solution)/shard_map/ppermute | solution.py:567
  134.4 38.5 %collective-permute-start.19 = (bf16[1024,128]{1,0:T(8,128)(2,1)S(1)}, bf16[1024,128]{1,0:T(8,128)(2,1)S(1)}, u32[]{:S(2)}, u32[]{:S(2)}) collective-permute-start(bf16[1024,128]{1,0:T(8,128)(2,1)S(1)} %get-tuple-element.43), channel_id=1, source_target_pairs={{4,2},{5,3},{6,4},{7,5},{12,10},{13,11},{14,12},{15,13},{20,18},{2... | collective-permute-start | bytes 786440 | tf_op jit(solution)/shard_map/ppermute | solution.py:567
  164.0 12.4 %collective-permute-start.12 = (bf16[1024,128]{1,0:T(8,128)(2,1)S(1)}, bf16[1024,128]{1,0:T(8,128)(2,1)S(1)}, u32[]{:S(2)}, u32[]{:S(2)}) collective-permute-start(bf16[1024,128]{1,0:T(8,128)(2,1)S(1)} %get-tuple-element.35), channel_id=1, source_target_pairs={{4,6},{5,7},{6,0},{7,1},{12,14},{13,15},{14,8},{15,9},{20,22},{21,... | collective-permute-start | bytes 786440 | tf_op jit(solution)/shard_map/ppermute | solution.py:567
  165.3 16.7 %collective-permute-start.13 = (bf16[1024,128]{1,0:T(8,128)(2,1)S(1)}, bf16[1024,128]{1,0:T(8,128)(2,1)S(1)}, u32[]{:S(2)}, u32[]{:S(2)}) collective-permute-start(bf16[1024,128]{1,0:T(8,128)(2,1)S(1)} %get-tuple-element.36), channel_id=1, source_target_pairs={{2,6},{3,7},{4,0},{5,1},{10,14},{11,15},{12,8},{13,9},{18,22},{19,... | collective-permute-start | bytes 786440 | tf_op jit(solution)/shard_map/ppermute | solution.py:567
  166.6 20.9 %collective-permute-start.14 = (bf16[1024,128]{1,0:T(8,128)(2,1)S(1)}, bf16[1024,128]{1,0:T(8,128)(2,1)S(1)}, u32[]{:S(2)}, u32[]{:S(2)}) collective-permute-start(bf16[1024,128]{1,0:T(8,128)(2,1)S(1)} %get-tuple-element.37), channel_id=1, source_target_pairs={{0,6},{1,7},{2,0},{3,1},{8,14},{9,15},{10,8},{11,9},{16,22},{17,23... | collective-permute-start | bytes 786440 | tf_op jit(solution)/shard_map/ppermute | solution.py:567
  187.9 6.9 %collective-permute-start.20 = (bf16[4,128,128]{2,1,0:T(8,128)(2,1)S(1)}, bf16[4,128,128]{2,1,0:T(8,128)(2,1)S(1)}, u32[]{:S(2)}, u32[]{:S(2)}) collective-permute-start(bf16[4,128,128]{2,1,0:T(8,128)(2,1)S(1)} %get-tuple-element.45), channel_id=1, source_target_pairs={{0,24},{8,0},{16,8},{24,16},{1,25},{9,1},{17,9},{25,17},{2,26},{10... | collective-permute-start | bytes 393224 | tf_op jit(solution)/shard_map/ppermute | solution.py:567
  188.0 16.8 %collective-permute-start.7 = (bf16[512,128]{1,0:T(8,128)(2,1)S(1)}, bf16[512,128]{1,0:T(8,128)(2,1)S(1)}, u32[]{:S(2)}, u32[]{:S(2)}) collective-permute-start(bf16[512,128]{1,0:T(8,128)(2,1)S(1)} %get-tuple-element.49), channel_id=1, source_target_pairs={{0,4},{1,5},{2,6},{3,7},{4,0},{5,1},{6,2},{7,3},{8,12},{9,13},{10,... | collective-permute-start | bytes 393224 | tf_op jit(solution)/shard_map/ppermute | solution.py:567
  188.1 19.5 %collective-permute-start.8 = (bf16[512,128]{1,0:T(8,128)(2,1)S(1)}, bf16[512,128]{1,0:T(8,128)(2,1)S(1)}, u32[]{:S(2)}, u32[]{:S(2)}) collective-permute-start(bf16[512,128]{1,0:T(8,128)(2,1)S(1)} %get-tuple-element.48), channel_id=1, source_target_pairs={{0,4},{1,5},{2,6},{3,7},{4,0},{5,1},{6,2},{7,3},{8,12},{9,13},{10,... | collective-permute-start | bytes 393224 | tf_op jit(solution)/shard_map/ppermute | solution.py:567
  191.0 16.6 %collective-permute-start.5 = (bf16[1024,128]{1,0:T(8,128)(2,1)S(1)}, bf16[1024,128]{1,0:T(8,128)(2,1)S(1)}, u32[]{:S(2)}, u32[]{:S(2)}) collective-permute-start(bf16[1024,128]{1,0:T(8,128)(2,1)S(1)} %get-tuple-element.29), channel_id=1, source_target_pairs={{0,2},{1,3},{2,4},{3,5},{4,6},{5,7},{6,0},{7,1},{8,10},{9,11},{10,... | collective-permute-start | bytes 786440 | tf_op jit(solution)/shard_map/ppermute | solution.py:567
  191.0 19.5 %collective-permute-start.6 = (bf16[1024,128]{1,0:T(8,128)(2,1)S(1)}, bf16[1024,128]{1,0:T(8,128)(2,1)S(1)}, u32[]{:S(2)}, u32[]{:S(2)}) collective-permute-start(bf16[1024,128]{1,0:T(8,128)(2,1)S(1)} %get-tuple-element.30), channel_id=1, source_target_pairs={{0,6},{1,7},{2,0},{3,1},{4,2},{5,3},{6,4},{7,5},{8,14},{9,15},{10,... | collective-permute-start | bytes 786440 | tf_op jit(solution)/shard_map/ppermute | solution.py:567
  194.8 5.2 %collective-permute-start.21 = (bf16[4,128,128]{2,1,0:T(8,128)(2,1)S(1)}, bf16[4,128,128]{2,1,0:T(8,128)(2,1)S(1)}, u32[]{:S(2)}, u32[]{:S(2)}) collective-permute-start(bf16[4,128,128]{2,1,0:T(8,128)(2,1)S(1)} %get-tuple-element.46), channel_id=1, source_target_pairs={{0,25},{1,24},{2,27},{3,26},{4,29},{5,28},{6,31},{7,30},{8,1},{9,0... | collective-permute-start | bytes 393224 | tf_op jit(solution)/shard_map/ppermute | solution.py:567
  200.1 11.6 %collective-permute-start.24 = (bf16[2,128,128]{2,1,0:T(8,128)(2,1)S(1)}, bf16[2,128,128]{2,1,0:T(8,128)(2,1)S(1)}, u32[]{:S(2)}, u32[]{:S(2)}) collective-permute-start(bf16[2,128,128]{2,1,0:T(8,128)(2,1)S(1)} %pad_maximum_fusion.2), channel_id=1, source_target_pairs={{0,6},{1,7},{2,0},{3,1},{4,2},{5,3},{6,4},{7,5},{8,14},{9,15},{10,... | collective-permute-start | bytes 196616 | tf_op jit(solution)/shard_map/ppermute | solution.py:567
  204.8 13.9 %collective-permute-start.23 = (bf16[2,128,128]{2,1,0:T(8,128)(2,1)S(1)}, bf16[2,128,128]{2,1,0:T(8,128)(2,1)S(1)}, u32[]{:S(2)}, u32[]{:S(2)}) collective-permute-start(bf16[2,128,128]{2,1,0:T(8,128)(2,1)S(1)} %pad_maximum_fusion.1), channel_id=1, source_target_pairs={{0,4},{1,5},{2,6},{3,7},{4,0},{5,1},{6,2},{7,3},{8,12},{9,13},{10,... | collective-permute-start | bytes 196616 | tf_op jit(solution)/shard_map/ppermute | solution.py:567
  207.5 11.1 %collective-permute-start.22 = (bf16[2,128,128]{2,1,0:T(8,128)(2,1)S(1)}, bf16[2,128,128]{2,1,0:T(8,128)(2,1)S(1)}, u32[]{:S(2)}, u32[]{:S(2)}) collective-permute-start(bf16[2,128,128]{2,1,0:T(8,128)(2,1)S(1)} %pad_maximum_fusion), channel_id=1, source_target_pairs={{0,2},{1,3},{2,4},{3,5},{4,6},{5,7},{6,0},{7,1},{8,10},{9,11},{10,... | collective-permute-start | bytes 196616 | tf_op jit(solution)/shard_map/ppermute | solution.py:567

commit v11 on v10

--- a/solution.py
+++ b/solution.py
@@ -310,17 +310,29 @@
         store(at, width, (left * rate[:, cols]).astype(BF16))
 
 
-def put_tile(part, sends, keep_ref):
+def relayed(place, line):
+    far = jnp.where(place <= 1, line - 1, 0)
+    return jnp.where((place <= 1) | (place >= line - 2), lax.rem(far - place + line, line), 0)
+
+
+def put_tile(part, own, sends, keep_ref):
     share = keep_ref.shape[1]
-    keep_ref[...] = part[:, :share]
-    for j, ref in enumerate(sends, 1):
-        ref[...] = part[:, j * share : (j + 1) * share].astype(BF16)
+    keep = None
+    for j, ref in enumerate(sends):
+        block = part[:, j * share : (j + 1) * share]
+        ref[...] = block.astype(BF16)
+        mine = jnp.where(own == j, block, 0.0)
+        keep = mine if keep is None else keep + mine
+    keep_ref[...] = keep
 
 
 def own_kernel(
     steps, line, place_ref, core_ref, design_ref, mine_ref, theirs_ref, facts_ref, more_ref, *refs
 ):
-    (z_ref, *sends), (keep_ref, half_ref, terms_ref, moreterms_ref) = refs[:line], refs[line:]
+    (z_ref, *sends), (keep_ref, half_ref, terms_ref, moreterms_ref) = (
+        refs[: line + 1],
+        refs[line + 1 :],
+    )
     step = pl.program_id(0)
     blocks, kk, share = design_ref.shape
     chunk, probes = mine_ref.shape
@@ -345,14 +357,16 @@
         )
         for b in range(blocks // 2):
             here = pl.ds(pl.multiple_of(step * chunk + (2 * b + core) * share, share), share)
-            slot = lax.rem(step * (blocks // 2) + b - place + line, line)
+            away = lax.rem(step * (blocks // 2) + b - place + line, line)
+            skipped = relayed(place, line)
+            slot = jnp.where(away == 0, skipped, jnp.where(away == skipped, 0, away))
             half_ref[pl.ds(pl.multiple_of(slot * share, share), share), :] = z_ref[here, :]
 
     @pl.when(step >= steps)
     def _():
         tall = keep_ref.shape[0]
         rows = pl.ds(pl.multiple_of((step - steps) * tall, tall), tall)
-        put_tile(nt(z_ref[rows, :], half_ref[...]), sends, keep_ref)
+        put_tile(nt(z_ref[rows, :], half_ref[...]), relayed(place, line), sends, keep_ref)
 
 
 def own_tile(at, line, design, mine, theirs, facts, more):
@@ -381,7 +395,7 @@
                 whole,
             ],
             out_specs=[pl.BlockSpec(memory_space=pltpu.VMEM)]
-            + [pl.BlockSpec((tall, share), second)] * line,
+            + [pl.BlockSpec((tall, share), second)] * (line + 1),
             scratch_shapes=[
                 pltpu.VMEM((rows // 2, 2 * probes), BF16),
                 pltpu.VMEM((3 * K, probes), BF16),
@@ -389,7 +403,7 @@
             ],
         ),
         out_shape=[pltpu.VMEM((rows, 2 * probes), BF16)]
-        + [jax.ShapeDtypeStruct((rows, share), BF16)] * (line - 1)
+        + [jax.ShapeDtypeStruct((rows, share), BF16)] * line
         + [jax.ShapeDtypeStruct((rows, share), F32)],
         compiler_params=params("arbitrary"),
         cost_estimate=cost(2 * rows * rows * probes, 12 * rows * probes),
@@ -624,16 +638,23 @@
             if rounds is None or j in rounds
         ]
 
+    def near_round(by):
+        return [(i, to) for i, to in round_of(by) if line <= 3 or abs(to - i) < line - 1]
+
     zscore, *own_sends, own_keep = own_tile(at, line, design, methyl, theirs, facts, more)
     early = {1, line - 1}
     late = set(range(1, line)) - early
-    own_parts = arrivals(own_sends, rounds=early)
-    tops = arrivals([value[: rows // 2] for value in own_sends], rounds=late)
+    relay = on_line(own_sends[0], [(0, 1), (line - 1, line - 2)])
+    own_parts = [on_line(own_sends[j], near_round(j)) for j in sorted(early)]
     design_ends = jnp.concatenate([design_before[:quarter], design_before[line - quarter :]])
     *sends, keep = pair_tile(
         among_ends, at, line, design_ends, zscore, 0, [facts, more],
         [ends_mine, ends_theirs],
     )
+    joined = (own_sends[0].astype(F32) + relay.astype(F32)).astype(BF16)
+    for j in sorted(late):
+        passing = ((place == 1) & (j == line - 2)) | ((place == line - 2) & (j == 2))
+        own_parts.append(on_line(jnp.where(passing, joined, own_sends[j]), near_round(j)))
     pair_parts = [keep] + arrivals(sends, ends)
     design_inner = design_before[quarter : line - quarter]
     (partial,) = pair_tile(
@@ -650,11 +671,10 @@
     left, same, other = fold(at, line, pair_parts)
     same = to_panel(same, -1)
     other = to_panel_sibling(other, -1)
-    bottoms = arrivals([value[rows // 2 :] for value in own_sends], rounds=late)
     shifted = []
     for j in range(1, line):
         shifted.append(on_line(jnp.stack([same[j], other[j]]), round_of(j)))
-    tiles = scale(probes, own_keep, own_parts, tops, bottoms, left)
+    tiles = scale(probes, own_keep, own_parts, [], [], left)
     return finish(at, line, probes, tiles, same, other, shifted), scores
 
 

time: 220 us -> 216 us (0.982)
  waiting for transfers between devices: 116 us -> 102 us
  local copies, waits for them, and re-layouts: 6.02 us -> 9.76 us
  Pallas kernels: 41.5 us -> 44.8 us
  starting transfers between devices: 31.2 us -> 33.5 us
    ppermute x25, waiting for transfers between devices: 116 us -> 102 us  [along(): return lax.ppermute(value, axis, pairs)]
    unnamed x10 -> x24, local copies, waits for them, and re-layouts: 5.98 us -> 9.74 us
    ppermute x25, starting transfers between devices: 31.2 us -> 33.5 us  [along(): return lax.ppermute(value, axis, pairs)]
  transfers between devices with their start and end apart: 25 -> 25, of which waited for: 13 -> 10; matrix products, arithmetic and copies ran while one was open for 0% -> 1% of each run, Pallas kernels for 18% -> 20%
where the time goes in v11:
time: 216 us; the launch traced here: 215 us
  waiting for transfers between devices  102 us (47%)
  Pallas kernels  44.8 us (21%)
  starting transfers between devices  33.5 us (16%)
  blocking collectives  23.8 us (11%)
  local copies, waits for them, and re-layouts  9.76 us (5%)
    ppermute x25, waiting for transfers between devices, along(): return lax.ppermute(value, axis, pairs)  102 us
    ppermute x25, starting transfers between devices, along(): return lax.ppermute(value, axis, pairs)  33.5 us
    all_to_all x1, blocking collectives, body(): parts = lax.all_to_all(parts, 'probe', 0, 0)  15.5 us
    pallas_call x3, Pallas kernels, pair_tile(): pl.pallas_call(functools.partial(pair_kernel, index_of, line, first, side...  12.6 us
    pallas_call x1, Pallas kernels, own_tile(): pl.pallas_call(functools.partial(own_kernel, steps, line), grid_spec=pltp...  11.4 us
    unnamed x24, local copies, waits for them, and re-layouts  9.74 us
    all_to_all x1, blocking collectives, body(): design = lax.all_to_all(copies, 'probe', 0, 0)  8.28 us
    pallas_call x1, Pallas kernels, descend(): pl.pallas_call(descend_kernel, out_shape=(jax.ShapeDtypeStruct((K, share)...  6.61 us
  transfers between devices with their start and end apart: 25, of which 10 were waited for; matrix products, arithmetic and copies ran while one was open for 1% of the time, Pallas kernels for 20%

profile of v11, /device:TPU:0, one launch (start us, length us, event | category | flops | bytes accessed | tf_op | source)
XLA Modules:
  0.0 215.4 jit_solution(11759464549099655746)
XLA Ops:
  1.2 2.2 %copy-done = bf16[1024,2048]{1,0:T(8,128)(2,1)S(1)} copy-done((bf16[1024,2048]{1,0:T(8,128)(2,1)S(1)}, bf16[1024,2048]{1,0:T(8,128)(2,1)}, u32[]{:S(2)}) %copy-start) | copy-done | bytes 4194328
  5.0 4.5 %project.1 = (f32[8,64,128]{2,1,0:T(8,128)S(1)}, bf16[32,2048]{1,0:T(8,128)(2,1)S(1)}, bf16[256,2048]{1,0:T(8,128)(2,1)}, bf16[256,2048]{1,0:T(8,128)(2,1)}, bf16[256,2048]{1,0:T(8,128)(2,1)}) custom-call(s32[1]{0:T(128)} %bitcast.1.core_ref._, s32[64]{0:T(128)S(1)} %copy-done.9, bf16[64,2048]{1,0:T(8,128)(2,1)S(1)} %copy-done.5, bf16[1024,2048]{1,0:T(8,128)(2,1)S(1)} %copy-done), custom_call_target="tpu_custom_call" | custom-call | flops 134217728 | bytes 8388608 | tf_op jit(solution)/shard_map/project/pallas_call | solution.py:104
  9.5 15.5 %all_to_all.10.parts_ref = f32[8,64,128]{2,1,0:T(8,128)S(1)} all-to-all(f32[8,64,128]{2,1,0:T(8,128)S(1)} %get-tuple-element.26), channel_id=1, replica_groups=mesh['samp'=4,'probe'=8] {'probe'}, dimensions={0} | all-to-all | bytes 524288 | tf_op jit(solution)/shard_map/all_to_all | solution.py:618
  25.0 6.6 %descend.1 = (f32[32,128]{1,0:T(8,128)}, bf16[8,32,128]{2,1,0:T(8,128)(2,1)S(1)}) custom-call(f32[8,64,128]{2,1,0:T(8,128)S(1)} %all_to_all.10.parts_ref), custom_call_target="tpu_custom_call" | custom-call | flops 33554432 | bytes 16384 | tf_op jit(solution)/shard_map/descend/pallas_call | solution.py:198
  31.6 8.3 %all_to_all.11.design_ref = bf16[8,32,128]{2,1,0:T(8,128)(2,1)S(1)} all-to-all(bf16[8,32,128]{2,1,0:T(8,128)(2,1)S(1)} %get-tuple-element.27), channel_id=1, replica_groups=mesh['samp'=4,'probe'=8] {'probe'}, dimensions={0} | all-to-all | bytes 131072 | tf_op jit(solution)/shard_map/all_to_all | solution.py:620
  39.9 2.3 %cross.1.refs_0_ = f32[32,2176]{1,0:T(8,128)S(1)} custom-call(bf16[8,32,128]{2,1,0:T(8,128)(2,1)S(1)} %all_to_all.11.design_ref, bf16[1024,2048]{1,0:T(8,128)(2,1)S(1)} %copy-done.1, bf16[32,2048]{1,0:T(8,128)(2,1)S(1)} %get-tuple-element.28.panel_ref.refs_4_), custom_call_target="tpu_custom_call" | custom-call | flops 268435456 | bytes 4194304 | tf_op jit(solution)/shard_map/cross/pallas_call | solution.py:236
  42.2 1.5 collective-permute-start.1
  43.7 1.5 collective-permute-start.2
  45.7 6.0 %collective-permute-done.1.refs_1_ = f32[32,2176]{1,0:T(8,128)S(1)} collective-permute-done((f32[32,2176]{1,0:T(8,128)S(1)}, f32[32,2176]{1,0:T(8,128)S(1)}, u32[]{:S(2)}, u32[]{:S(2)}) %collective-permute-start.1) | collective-permute-done | bytes 278560 | tf_op jit(solution)/shard_map/ppermute | solution.py:581
  51.7 5.9 %collective-permute-done.2.refs_2_ = f32[32,2176]{1,0:T(8,128)S(1)} collective-permute-done((f32[32,2176]{1,0:T(8,128)S(1)}, f32[32,2176]{1,0:T(8,128)S(1)}, u32[]{:S(2)}, u32[]{:S(2)}) %collective-permute-start.2) | collective-permute-done | bytes 278560 | tf_op jit(solution)/shard_map/ppermute | solution.py:581
  57.6 3.8 %solve.1.facts_ref.refs_0_ = f32[40,2048]{1,0:T(8,128)S(1)} custom-call(f32[32,2176]{1,0:T(8,128)S(1)} %cross.1.refs_0_, f32[32,2176]{1,0:T(8,128)S(1)} %collective-permute-done.1.refs_1_, f32[32,2176]{1,0:T(8,128)S(1)} %collective-permute-done.2.refs_2_, f32[32,2176]{1,0:T(8,128)S(1)} %collective-permute-done.3.refs_3_, ...), custom_call_target="tpu_custom_call" | custom-call | flops 104857600 | bytes 1310720 | tf_op jit(solution)/shard_map/solve/pallas_call | solution.py:293
  62.8 1.5 collective-permute-start.15
  64.8 2.2 %copy-done.2 = bf16[1024,2048]{1,0:T(8,128)(2,1)S(1)} copy-done((bf16[1024,2048]{1,0:T(8,128)(2,1)S(1)}, bf16[1024,2048]{1,0:T(8,128)(2,1)}, u32[]{:S(2)}) %copy-start.2) | copy-done | bytes 4194328
  67.1 44.2 %collective-permute-done.9 = bf16[4,32,128]{2,1,0:T(8,128)(2,1)S(1)} collective-permute-done((bf16[4,32,128]{2,1,0:T(8,128)(2,1)S(1)}, bf16[4,32,128]{2,1,0:T(8,128)(2,1)S(1)}, u32[]{:S(2)}, u32[]{:S(2)}) %collective-permute-start.9) | collective-permute-done | bytes 32800 | tf_op jit(solution)/shard_map/ppermute | solution.py:581
  111.3 1.9 collective-permute-start.10
  113.2 11.4 %own.1 = (bf16[1024,4096]{1,0:T(8,128)(2,1)S(1)}, bf16[1024,128]{1,0:T(8,128)(2,1)}, bf16[1024,128]{1,0:T(8,128)(2,1)S(1)}, bf16[1024,128]{1,0:T(8,128)(2,1)S(1)...) custom-call(s32[1]{0:T(128)} %bitcast.place_ref, s32[1]{0:T(128)} %bitcast.1.core_ref._, ...), custom_call_target="tpu_custom_call" | custom-call | flops 4294967296 | bytes 25165824 | tf_op jit(solution)/shard_map/own/pallas_call | solution.py:385
  126.7 3.4 %shard_map.51.refs_2_ = f32[1024,256]{1,0:T(8,128)S(1)} custom-call(s32[1]{0:T(128)} %bitcast.place_ref, bf16[2,32,128]{2,1,0:T(8,128)(2,1)S(1)} %slice.38.design_ref, bf16[1024,4096]{1,0:T(8,128)(2,1)S(1)} %get-tuple-element.34.zscore_ref, f32[40,2048]{1,0:T(8,128)S(1)} %solve.1.facts_ref.refs_0_, bf16[256,2048]{1,0:T(8,128)(2,1)} %collective-permute-done.16.refs_1_), custom_call_target="tpu_custom_call" | custom-call | flops 1073741824 | bytes 8388608 | tf_op jit(solution)/shard_map/pallas_call | solution.py:464
  130.2 3.9 %shard_map.52 = (bf16[1024,128]{1,0:T(8,128)(2,1)S(1)}, bf16[1024,128]{1,0:T(8,128)(2,1)S(1)}, bf16[1024,128]{1,0:T(8,128)(2,1)}, f32[1024,128]{1,0:T(8,128)S(1)}) custom-call(s32[1]{0:T(128)} %bitcast.place_ref, bf16[2,32,128]{2,1,0:T(8,128)(2,1)S(1)} %slice.38.design_ref, bf16[1024,4096]{1,0:T(8,128)(2,1)S(1)} %get-tuple-element.34.zscore_ref, ...), custom_call_target="tpu_custom_call" | custom-call | flops 1073741824 | bytes 8388608 | tf_op jit(solution)/shard_map/pallas_call | solution.py:464
  134.1 2.4 %collective-permute-start.17 = (bf16[1024,128]{1,0:T(8,128)(2,1)S(1)}, bf16[1024,128]{1,0:T(8,128)(2,1)S(1)}, u32[]{:S(2)}, u32[]{:S(2)}) collective-permute-start(bf16[1024,128]{1,0:T(8,128)(2,1)S(1)} %get-tuple-element.43), channel_id=1, source_target_pairs={{0,4},{1,5},{6,2},{7,3},{8,12},{9,13},{14,10},{15,11},{16,20},{17,... | collective-permute-start | bytes 786440 | tf_op jit(solution)/shard_map/ppermute | solution.py:581
  136.5 1.6 collective-permute-start.18
  138.1 1.4 collective-permute-start.19
  139.5 19.9 %collective-permute-done.10.refs_2_ = bf16[256,2048]{1,0:T(8,128)(2,1)} collective-permute-done((bf16[256,2048]{1,0:T(8,128)(2,1)S(1)}, bf16[256,2048]{1,0:T(8,128)(2,1)}, u32[]{:S(2)}, u32[]{:S(2)}) %collective-permute-start.10) | collective-permute-done | bytes 1048608 | tf_op jit(solution)/shard_map/ppermute | solution.py:581
  159.4 5.3 %shard_map.50 = (bf16[1024,128]{1,0:T(8,128)(2,1)S(1)}, bf16[1024,128]{1,0:T(8,128)(2,1)S(1)}, bf16[1024,128]{1,0:T(8,128)(2,1)}, f32[1024,128]{1,0:T(8,128)S(1)}) custom-call(s32[1]{0:T(128)} %bitcast.place_ref, bf16[2,32,128]{2,1,0:T(8,128)(2,1)S(1)} %pad_maximum_fusion.3.design_ref, bf16[1024,4096]{1,0:T(8,128)(2,1)S(1)} %get-tuple-element.34.zscore_ref, ...), custom_call_target="tpu_custom_call" | custom-call | flops 2147483648 | bytes 8388608 | tf_op jit(solution)/shard_map/pallas_call | solution.py:464
  164.7 1.4 collective-permute-start.12
  167.4 6.3 %collective-permute-start.14 = (bf16[1024,128]{1,0:T(8,128)(2,1)}, bf16[1024,128]{1,0:T(8,128)(2,1)S(1)}, u32[]{:S(2)}, u32[]{:S(2)}) collective-permute-start(bf16[1024,128]{1,0:T(8,128)(2,1)} %get-tuple-element.39), channel_id=1, source_target_pairs={{0,6},{1,7},{2,0},{3,1},{8,14},{9,15},{10,8},{11,9},{16,22},{17,23... | collective-permute-start | bytes 786440 | tf_op jit(solution)/shard_map/ppermute | solution.py:581
  174.5 2.5 %collective-permute-start.7 = (bf16[1024,128]{1,0:T(8,128)(2,1)}, bf16[1024,128]{1,0:T(8,128)(2,1)S(1)}, u32[]{:S(2)}, u32[]{:S(2)}) collective-permute-start(bf16[1024,128]{1,0:T(8,128)(2,1)} %get-tuple-element.32), channel_id=1, source_target_pairs={{0,2},{1,3},{6,4},{7,5},{8,10},{9,11},{14,12},{15,13},{16,18},{17,... | collective-permute-start | bytes 786440 | tf_op jit(solution)/shard_map/ppermute | solution.py:581
  179.6 3.1 %collective-permute-done.13.refs_2_ = bf16[1024,128]{1,0:T(8,128)(2,1)S(1)} collective-permute-done((bf16[1024,128]{1,0:T(8,128)(2,1)S(1)}, bf16[1024,128]{1,0:T(8,128)(2,1)S(1)}, u32[]{:S(2)}, u32[]{:S(2)}) %collective-permute-start.13) | collective-permute-done | bytes 262176 | tf_op jit(solution)/shard_map/ppermute | solution.py:581
  182.8 5.6 %collective-permute-done.14.refs_3_ = bf16[1024,128]{1,0:T(8,128)(2,1)S(1)} collective-permute-done((bf16[1024,128]{1,0:T(8,128)(2,1)}, bf16[1024,128]{1,0:T(8,128)(2,1)S(1)}, u32[]{:S(2)}, u32[]{:S(2)}) %collective-permute-start.14) | collective-permute-done | bytes 262176 | tf_op jit(solution)/shard_map/ppermute | solution.py:581
  190.8 2.2 %collective-permute-start.21 = (bf16[4,128,128]{2,1,0:T(8,128)(2,1)S(1)}, bf16[4,128,128]{2,1,0:T(8,128)(2,1)S(1)}, u32[]{:S(2)}, u32[]{:S(2)}) collective-permute-start(bf16[4,128,128]{2,1,0:T(8,128)(2,1)S(1)} %get-tuple-element.48), channel_id=1, source_target_pairs={{0,25},{1,24},{2,27},{3,26},{4,29},{5,28},{6,31},{7,30},{8,1},{9,0... | collective-permute-start | bytes 393224 | tf_op jit(solution)/shard_map/ppermute | solution.py:581
  194.2 2.9 %collective-permute-done.20.same_ref = bf16[4,128,128]{2,1,0:T(8,128)(2,1)S(1)} collective-permute-done((bf16[4,128,128]{2,1,0:T(8,128)(2,1)S(1)}, bf16[4,128,128]{2,1,0:T(8,128)(2,1)S(1)}, u32[]{:S(2)}, u32[]{:S(2)}) %collective-permute-start.20) | collective-permute-done | bytes 131104 | tf_op jit(solution)/shard_map/ppermute | solution.py:581
  200.2 11.4 %collective-permute-done.8.refs_2_ = bf16[1024,128]{1,0:T(8,128)(2,1)S(1)} collective-permute-done((bf16[1024,128]{1,0:T(8,128)(2,1)S(1)}, bf16[1024,128]{1,0:T(8,128)(2,1)S(1)}, u32[]{:S(2)}, u32[]{:S(2)}) %collective-permute-start.8) | collective-permute-done | bytes 262176 | tf_op jit(solution)/shard_map/ppermute | solution.py:581
  212.7 1.7 collective-permute-done.23.refs_1_
  (66 shorter events, 20.0 us)
Async XLA Ops:
  0.6 112.6 %collective-permute-start = (bf16[1024,2048]{1,0:T(8,128)(2,1)}, bf16[1024,2048]{1,0:T(8,128)(2,1)}, u32[]{:S(2)}, u32[]{:S(2)}) collective-permute-start(bf16[1024,2048]{1,0:T(8,128)(2,1)} %from_ref.1), channel_id=1, source_target_pairs={{0,1},{1,0},{2,3},{3,2},{4,5},{5,4},{6,7},{7,6},{8,9},{9,8},{10,11... | collective-permute-start | bytes 12582920 | tf_op jit(solution)/shard_map/ppermute | solution.py:581
  1.2 2.2 %copy-start = (bf16[1024,2048]{1,0:T(8,128)(2,1)S(1)}, bf16[1024,2048]{1,0:T(8,128)(2,1)}, u32[]{:S(2)}) copy-start(bf16[1024,2048]{1,0:T(8,128)(2,1)} %from_ref.1) | copy-start | bytes 12582916
  3.4 0.9 copy-start.5
  5.0 34.9 %copy-start.1 = (bf16[1024,2048]{1,0:T(8,128)(2,1)S(1)}, bf16[1024,2048]{1,0:T(8,128)(2,1)}, u32[]{:S(2)}) copy-start(bf16[1024,2048]{1,0:T(8,128)(2,1)} %from_ref.1) | copy-start | bytes 12582916
  42.2 9.6 %collective-permute-start.1 = (f32[32,2176]{1,0:T(8,128)S(1)}, f32[32,2176]{1,0:T(8,128)S(1)}, u32[]{:S(2)}, u32[]{:S(2)}) collective-permute-start(f32[32,2176]{1,0:T(8,128)S(1)} %cross.1.refs_0_), channel_id=1, source_target_pairs={{0,8},{8,0},{16,24},{24,16},{1,9},{9,1},{17,25},{25,17},{2,10},{10... | collective-permute-start | bytes 835592 | tf_op jit(solution)/shard_map/ppermute | solution.py:581
  43.7 13.9 %collective-permute-start.2 = (f32[32,2176]{1,0:T(8,128)S(1)}, f32[32,2176]{1,0:T(8,128)S(1)}, u32[]{:S(2)}, u32[]{:S(2)}) collective-permute-start(f32[32,2176]{1,0:T(8,128)S(1)} %cross.1.refs_0_), channel_id=1, source_target_pairs={{0,16},{8,24},{16,0},{24,8},{1,17},{9,25},{17,1},{25,9},{2,18},{10... | collective-permute-start | bytes 835592 | tf_op jit(solution)/shard_map/ppermute | solution.py:581
  45.2 12.4 %collective-permute-start.3 = (f32[32,2176]{1,0:T(8,128)S(1)}, f32[32,2176]{1,0:T(8,128)S(1)}, u32[]{:S(2)}, u32[]{:S(2)}) collective-permute-start(f32[32,2176]{1,0:T(8,128)S(1)} %cross.1.refs_0_), channel_id=1, source_target_pairs={{0,24},{8,16},{16,8},{24,0},{1,25},{9,17},{17,9},{25,1},{2,26},{10... | collective-permute-start | bytes 835592 | tf_op jit(solution)/shard_map/ppermute | solution.py:581
  61.4 49.9 %collective-permute-start.4 = (f32[40,2048]{1,0:T(8,128)S(1)}, f32[40,2048]{1,0:T(8,128)S(1)}, u32[]{:S(2)}, u32[]{:S(2)}) collective-permute-start(f32[40,2048]{1,0:T(8,128)S(1)} %solve.1.facts_ref.refs_0_), channel_id=1, source_target_pairs={{0,1},{1,0},{2,3},{3,2},{4,5},{5,4},{6,7},{7,6},{8,9},{9,8},{10,11... | collective-permute-start | bytes 983048 | tf_op jit(solution)/shard_map/ppermute | solution.py:581
  61.5 65.2 %collective-permute-start.16 = (bf16[256,2048]{1,0:T(8,128)(2,1)}, bf16[256,2048]{1,0:T(8,128)(2,1)}, u32[]{:S(2)}, u32[]{:S(2)}) collective-permute-start(bf16[256,2048]{1,0:T(8,128)(2,1)} %get-tuple-element.41), channel_id=1, source_target_pairs={{0,8},{8,16},{16,24},{24,0},{1,9},{9,17},{17,25},{25,1},{2,10},{10... | collective-permute-start | bytes 3145736 | tf_op jit(solution)/shard_map/ppermute | solution.py:581
  62.8 67.4 %collective-permute-start.15 = (bf16[256,2048]{1,0:T(8,128)(2,1)}, bf16[256,2048]{1,0:T(8,128)(2,1)}, u32[]{:S(2)}, u32[]{:S(2)}) collective-permute-start(bf16[256,2048]{1,0:T(8,128)(2,1)} %get-tuple-element.40), channel_id=1, source_target_pairs={{0,9},{1,8},{2,11},{3,10},{4,13},{5,12},{6,15},{7,14},{8,17},{9,16... | collective-permute-start | bytes 3145736 | tf_op jit(solution)/shard_map/ppermute | solution.py:581
  64.3 47.0 %collective-permute-start.9 = (bf16[4,32,128]{2,1,0:T(8,128)(2,1)S(1)}, bf16[4,32,128]{2,1,0:T(8,128)(2,1)S(1)}, u32[]{:S(2)}, u32[]{:S(2)}) collective-permute-start(bf16[4,32,128]{2,1,0:T(8,128)(2,1)S(1)} %dynamic-slice_bitcast_fusion), channel_id=1, source_target_pairs={{0,8},{8,16},{16,24},{24,0},{1,9},{9,17},{17,25},{25,1},{2,10},{10... | collective-permute-start | bytes 98312 | tf_op jit(solution)/shard_map/ppermute | solution.py:581
  64.8 2.2 %copy-start.2 = (bf16[1024,2048]{1,0:T(8,128)(2,1)S(1)}, bf16[1024,2048]{1,0:T(8,128)(2,1)}, u32[]{:S(2)}) copy-start(bf16[1024,2048]{1,0:T(8,128)(2,1)} %from_ref.1) | copy-start | bytes 12582916
  111.3 28.2 %collective-permute-start.11 = (bf16[256,2048]{1,0:T(8,128)(2,1)}, bf16[256,2048]{1,0:T(8,128)(2,1)S(1)}, u32[]{:S(2)}, u32[]{:S(2)}) collective-permute-start(bf16[256,2048]{1,0:T(8,128)(2,1)} %get-tuple-element.35), channel_id=1, source_target_pairs={{0,9},{1,8},{2,11},{3,10},{4,13},{5,12},{6,15},{7,14},{8,17},{9,16... | collective-permute-start | bytes 3145736 | tf_op jit(solution)/shard_map/ppermute | solution.py:581
  111.3 48.1 %collective-permute-start.10 = (bf16[256,2048]{1,0:T(8,128)(2,1)S(1)}, bf16[256,2048]{1,0:T(8,128)(2,1)}, u32[]{:S(2)}, u32[]{:S(2)}) collective-permute-start(bf16[256,2048]{1,0:T(8,128)(2,1)S(1)} %pick_ends.1), channel_id=1, source_target_pairs={{0,8},{8,16},{16,24},{24,0},{1,9},{9,17},{17,25},{25,1},{2,10},{10... | collective-permute-start | bytes 3145736 | tf_op jit(solution)/shard_map/ppermute | solution.py:581
  126.7 3.4 %copy-start.3 = (f32[1024,128]{1,0:T(8,128)}, f32[1024,128]{1,0:T(8,128)S(1)}, u32[]{:S(2)}) copy-start(f32[1024,128]{1,0:T(8,128)S(1)} %get-tuple-element.29.own_ref) | copy-start | bytes 1572868
  134.1 33.3 %collective-permute-start.17 = (bf16[1024,128]{1,0:T(8,128)(2,1)S(1)}, bf16[1024,128]{1,0:T(8,128)(2,1)S(1)}, u32[]{:S(2)}, u32[]{:S(2)}) collective-permute-start(bf16[1024,128]{1,0:T(8,128)(2,1)S(1)} %get-tuple-element.43), channel_id=1, source_target_pairs={{0,4},{1,5},{6,2},{7,3},{8,12},{9,13},{14,10},{15,11},{16,20},{17,... | collective-permute-start | bytes 786440 | tf_op jit(solution)/shard_map/ppermute | solution.py:581
  136.5 37.3 %collective-permute-start.18 = (bf16[1024,128]{1,0:T(8,128)(2,1)S(1)}, bf16[1024,128]{1,0:T(8,128)(2,1)S(1)}, u32[]{:S(2)}, u32[]{:S(2)}) collective-permute-start(bf16[1024,128]{1,0:T(8,128)(2,1)S(1)} %get-tuple-element.44), channel_id=1, source_target_pairs={{0,2},{1,3},{2,4},{3,5},{8,10},{9,11},{10,12},{11,13},{16,18},{17,... | collective-permute-start | bytes 786440 | tf_op jit(solution)/shard_map/ppermute | solution.py:581
  138.1 38.9 %collective-permute-start.19 = (bf16[1024,128]{1,0:T(8,128)(2,1)}, bf16[1024,128]{1,0:T(8,128)(2,1)}, u32[]{:S(2)}, u32[]{:S(2)}) collective-permute-start(bf16[1024,128]{1,0:T(8,128)(2,1)} %get-tuple-element.45), channel_id=1, source_target_pairs={{4,2},{5,3},{6,4},{7,5},{12,10},{13,11},{14,12},{15,13},{20,18},{2... | collective-permute-start | bytes 786440 | tf_op jit(solution)/shard_map/ppermute | solution.py:581
  164.7 46.9 %copy-start.4 = (f32[1024,128]{1,0:T(8,128)S(1)}, f32[1024,128]{1,0:T(8,128)}, u32[]{:S(2)}) copy-start(f32[1024,128]{1,0:T(8,128)} %copy-done.3) | copy-start | bytes 1572868
  164.7 13.6 %collective-permute-start.12 = (bf16[1024,128]{1,0:T(8,128)(2,1)S(1)}, bf16[1024,128]{1,0:T(8,128)(2,1)S(1)}, u32[]{:S(2)}, u32[]{:S(2)}) collective-permute-start(bf16[1024,128]{1,0:T(8,128)(2,1)S(1)} %get-tuple-element.37), channel_id=1, source_target_pairs={{4,6},{5,7},{6,0},{7,1},{12,14},{13,15},{14,8},{15,9},{20,22},{21,... | collective-permute-start | bytes 786440 | tf_op jit(solution)/shard_map/ppermute | solution.py:581
  166.1 16.7 %collective-permute-start.13 = (bf16[1024,128]{1,0:T(8,128)(2,1)S(1)}, bf16[1024,128]{1,0:T(8,128)(2,1)S(1)}, u32[]{:S(2)}, u32[]{:S(2)}) collective-permute-start(bf16[1024,128]{1,0:T(8,128)(2,1)S(1)} %get-tuple-element.38), channel_id=1, source_target_pairs={{2,6},{3,7},{4,0},{5,1},{10,14},{11,15},{12,8},{13,9},{18,22},{19,... | collective-permute-start | bytes 786440 | tf_op jit(solution)/shard_map/ppermute | solution.py:581
  167.4 21.0 %collective-permute-start.14 = (bf16[1024,128]{1,0:T(8,128)(2,1)}, bf16[1024,128]{1,0:T(8,128)(2,1)S(1)}, u32[]{:S(2)}, u32[]{:S(2)}) collective-permute-start(bf16[1024,128]{1,0:T(8,128)(2,1)} %get-tuple-element.39), channel_id=1, source_target_pairs={{0,6},{1,7},{2,0},{3,1},{8,14},{9,15},{10,8},{11,9},{16,22},{17,23... | collective-permute-start | bytes 786440 | tf_op jit(solution)/shard_map/ppermute | solution.py:581
  174.5 18.5 %collective-permute-start.7 = (bf16[1024,128]{1,0:T(8,128)(2,1)}, bf16[1024,128]{1,0:T(8,128)(2,1)S(1)}, u32[]{:S(2)}, u32[]{:S(2)}) collective-permute-start(bf16[1024,128]{1,0:T(8,128)(2,1)} %get-tuple-element.32), channel_id=1, source_target_pairs={{0,2},{1,3},{6,4},{7,5},{8,10},{9,11},{14,12},{15,13},{16,18},{17,... | collective-permute-start | bytes 786440 | tf_op jit(solution)/shard_map/ppermute | solution.py:581
  177.0 22.1 %collective-permute-start.5 = (bf16[1024,128]{1,0:T(8,128)(2,1)}, bf16[1024,128]{1,0:T(8,128)(2,1)S(1)}, u32[]{:S(2)}, u32[]{:S(2)}) collective-permute-start(bf16[1024,128]{1,0:T(8,128)(2,1)} %copy-done.11), channel_id=1, source_target_pairs={{0,2},{1,3},{2,4},{3,5},{4,6},{5,7},{8,10},{9,11},{10,12},{11,13},... | collective-permute-start | bytes 786440 | tf_op jit(solution)/shard_map/ppermute | solution.py:581
  178.3 21.8 %collective-permute-start.6 = (bf16[1024,128]{1,0:T(8,128)(2,1)}, bf16[1024,128]{1,0:T(8,128)(2,1)S(1)}, u32[]{:S(2)}, u32[]{:S(2)}) collective-permute-start(bf16[1024,128]{1,0:T(8,128)(2,1)} %copy-done.10), channel_id=1, source_target_pairs={{2,0},{3,1},{4,2},{5,3},{6,4},{7,5},{10,8},{11,9},{12,10},{13,11},... | collective-permute-start | bytes 786440 | tf_op jit(solution)/shard_map/ppermute | solution.py:581
  188.4 1.0 copy-start.7
  190.7 6.4 %collective-permute-start.20 = (bf16[4,128,128]{2,1,0:T(8,128)(2,1)S(1)}, bf16[4,128,128]{2,1,0:T(8,128)(2,1)S(1)}, u32[]{:S(2)}, u32[]{:S(2)}) collective-permute-start(bf16[4,128,128]{2,1,0:T(8,128)(2,1)S(1)} %get-tuple-element.47), channel_id=1, source_target_pairs={{0,24},{8,0},{16,8},{24,16},{1,25},{9,1},{17,9},{25,17},{2,26},{10... | collective-permute-start | bytes 393224 | tf_op jit(solution)/shard_map/ppermute | solution.py:581
  190.8 7.1 %collective-permute-start.21 = (bf16[4,128,128]{2,1,0:T(8,128)(2,1)S(1)}, bf16[4,128,128]{2,1,0:T(8,128)(2,1)S(1)}, u32[]{:S(2)}, u32[]{:S(2)}) collective-permute-start(bf16[4,128,128]{2,1,0:T(8,128)(2,1)S(1)} %get-tuple-element.48), channel_id=1, source_target_pairs={{0,25},{1,24},{2,27},{3,26},{4,29},{5,28},{6,31},{7,30},{8,1},{9,0... | collective-permute-start | bytes 393224 | tf_op jit(solution)/shard_map/ppermute | solution.py:581
  194.2 17.5 %collective-permute-start.8 = (bf16[1024,128]{1,0:T(8,128)(2,1)S(1)}, bf16[1024,128]{1,0:T(8,128)(2,1)S(1)}, u32[]{:S(2)}, u32[]{:S(2)}) collective-permute-start(bf16[1024,128]{1,0:T(8,128)(2,1)S(1)} %fusion), channel_id=1, source_target_pairs={{0,4},{1,5},{2,6},{3,7},{4,0},{5,1},{6,2},{7,3},{8,12},{9,13},{10,... | collective-permute-start | bytes 786440 | tf_op jit(solution)/shard_map/ppermute | solution.py:581
  197.9 14.8 %collective-permute-start.24 = (bf16[2,128,128]{2,1,0:T(8,128)(2,1)S(1)}, bf16[2,128,128]{2,1,0:T(8,128)(2,1)S(1)}, u32[]{:S(2)}, u32[]{:S(2)}) collective-permute-start(bf16[2,128,128]{2,1,0:T(8,128)(2,1)S(1)} %pad_maximum_fusion.2), channel_id=1, source_target_pairs={{0,6},{1,7},{2,0},{3,1},{4,2},{5,3},{6,4},{7,5},{8,14},{9,15},{10,... | collective-permute-start | bytes 196616 | tf_op jit(solution)/shard_map/ppermute | solution.py:581
  198.0 16.4 %collective-permute-start.23 = (bf16[2,128,128]{2,1,0:T(8,128)(2,1)S(1)}, bf16[2,128,128]{2,1,0:T(8,128)(2,1)S(1)}, u32[]{:S(2)}, u32[]{:S(2)}) collective-permute-start(bf16[2,128,128]{2,1,0:T(8,128)(2,1)S(1)} %pad_maximum_fusion.1), channel_id=1, source_target_pairs={{0,4},{1,5},{2,6},{3,7},{4,0},{5,1},{6,2},{7,3},{8,12},{9,13},{10,... | collective-permute-start | bytes 196616 | tf_op jit(solution)/shard_map/ppermute | solution.py:581
  199.2 15.3 %collective-permute-start.22 = (bf16[2,128,128]{2,1,0:T(8,128)(2,1)S(1)}, bf16[2,128,128]{2,1,0:T(8,128)(2,1)S(1)}, u32[]{:S(2)}, u32[]{:S(2)}) collective-permute-start(bf16[2,128,128]{2,1,0:T(8,128)(2,1)S(1)} %pad_maximum_fusion), channel_id=1, source_target_pairs={{0,2},{1,3},{2,4},{3,5},{4,6},{5,7},{6,0},{7,1},{8,10},{9,11},{10,... | collective-permute-start | bytes 196616 | tf_op jit(solution)/shard_map/ppermute | solution.py:581
  (5 other events, 3.5 us)

commit v12 on v10

--- a/solution.py
+++ b/solution.py
@@ -403,7 +403,7 @@
     outs, (z_ref, *terms) = refs[: -1 - sides], refs[-1 - sides :]
     blocks, kk, share = design_ref.shape
     probes = facts[0].shape[1]
-    tall = outs[0].shape[0]
+    tall = outs[0].shape[-2]
     step, place = pl.program_id(0), place_ref[0]
 
     @pl.when(step == 0)
@@ -425,6 +425,15 @@
             part = part + given_ref[rows, :]
         if not last:
             outs[0][...] = part
+            return
+        if index_of is None:
+            swap_ref, keep_ref = outs
+            odd = lax.rem(place, 2) == 1
+            for k in range(blocks // 2):
+                low = part[:, 2 * k * share : (2 * k + 1) * share]
+                high = part[:, (2 * k + 1) * share : (2 * k + 2) * share]
+                swap_ref[k] = jnp.where(odd, low, high).astype(BF16)
+                keep_ref[k] = jnp.where(odd, high, low)
             return
         *sends, keep_ref = outs
         for j, ref in enumerate([keep_ref, *sends]):
@@ -447,17 +456,23 @@
     column = pl.BlockSpec((tall, width), lambda i, *_: (jnp.maximum(i - 1, 0), 0))
     whole = jax.ShapeDtypeStruct((rows, width), F32)
     sends = [jax.ShapeDtypeStruct((rows, share), BF16)] * (line - 1)
+    out_specs = [column] * line if last else [column]
+    out_shape = sends + [whole] if last else [whole]
+    if last and index_of is None:
+        halves = (blocks // 2, tall, share)
+        out_specs = [pl.BlockSpec(halves, lambda i, *_: (0, jnp.maximum(i - 1, 0), 0))] * 2
+        out_shape = [jax.ShapeDtypeStruct((blocks // 2, rows, share), t) for t in (BF16, F32)]
     return pl.pallas_call(
         functools.partial(pair_kernel, index_of, line, first, sides, bool(given), last),
         grid_spec=pltpu.PrefetchScalarGridSpec(
             num_scalar_prefetch=1,
             grid=(1 + rows // tall,),
             in_specs=[pl.BlockSpec(memory_space=pltpu.VMEM)] * (2 + 2 * sides + len(given)),
-            out_specs=[column] * line if last else [column],
+            out_specs=out_specs,
             scratch_shapes=[pltpu.VMEM((blocks * share, sides * probes), BF16)]
             + [pltpu.VMEM((3 * K, probes), BF16)] * sides,
         ),
-        out_shape=sends + [whole] if last else [whole],
+        out_shape=out_shape,
         compiler_params=params("arbitrary"),
         cost_estimate=cost(2 * rows * blocks * share * sides * probes, 4 * rows * probes),
     )(at[0], design, zscore, *facts, *raws, *given)
@@ -589,10 +604,6 @@
     quarter = line // 4
     ends = [*range(quarter), *range(line - quarter, line)]
     inner = [*range(quarter, line - quarter)]
-
-    def among_ends(to):
-        high = to >= line - quarter
-        return jnp.where(high, to - (line - 2 * quarter), to), (to < quarter) | high
 
     def among_inner(to):
         return to - quarter, (to >= quarter) & (to < line - quarter)
@@ -630,16 +641,27 @@
     own_parts = arrivals(own_sends, rounds=early)
     tops = arrivals([value[: rows // 2] for value in own_sends], rounds=late)
     design_ends = jnp.concatenate([design_before[:quarter], design_before[line - quarter :]])
-    *sends, keep = pair_tile(
-        among_ends, at, line, design_ends, zscore, 0, [facts, more],
+    swap, keep = pair_tile(
+        None, at, line, design_ends, zscore, 0, [facts, more],
         [ends_mine, ends_theirs],
     )
-    pair_parts = [keep] + arrivals(sends, ends)
+    given = on_line(swap, [(i, i ^ 1) for i in range(line)])
     design_inner = design_before[quarter : line - quarter]
     (partial,) = pair_tile(
         among_inner, at, line, design_inner, zscore, 0, [facts], [inner_mine],
         last=False,
     )
+    keep = keep + given.astype(F32)
+
+    def sum_for(to):
+        if quarter == 1:
+            return keep[0]
+        which = jnp.where(to >= line - quarter, to - line + 2 * quarter, to) // 2
+        return lax.dynamic_index_in_dim(keep, jnp.clip(which, 0, quarter - 1), 0, False)
+
+    pair_parts = [jnp.where((place < quarter) | (place >= line - quarter), sum_for(place), 0.0)]
+    for j in range(2, line, 2):
+        pair_parts.append(on_line(sum_for((place + j) % line).astype(BF16), round_of(j, ends)))
     *sends, keep = pair_tile(
         among_inner, at, line, design_inner, zscore, 1, [more], [inner_theirs],
         given=partial,

time: 220 us -> 217 us (0.986)
  starting transfers between devices: 31.2 us -> 25 us
  local copies, waits for them, and re-layouts: 6.02 us -> 9.38 us
    ppermute x25 -> x24, starting transfers between devices: 31.2 us -> 25 us  [along(): return lax.ppermute(value, axis, pairs)]
    unnamed x10 -> x28, local copies, waits for them, and re-layouts: 5.98 us -> 9.34 us
    ppermute x25 -> x24, waiting for transfers between devices: 116 us -> 116 us  [along(): return lax.ppermute(value, axis, pairs)]
  transfers between devices with their start and end apart: 25 -> 24, of which waited for: 13 -> 13; matrix products, arithmetic and copies ran while one was open for 0% -> 0% of each run, Pallas kernels for 18% -> 19%
where the time goes in v12:
time: 217 us; the launch traced here: 216 us
  waiting for transfers between devices  116 us (53%)
  Pallas kernels  41.4 us (19%)
  starting transfers between devices  25 us (12%)
  blocking collectives  23.8 us (11%)
  local copies, waits for them, and re-layouts  9.38 us (4%)
    ppermute x24, waiting for transfers between devices, along(): return lax.ppermute(value, axis, pairs)  116 us
    ppermute x24, starting transfers between devices, along(): return lax.ppermute(value, axis, pairs)  25 us
    all_to_all x1, blocking collectives, body(): parts = lax.all_to_all(parts, 'probe', 0, 0)  15.5 us
    pallas_call x3, Pallas kernels, pair_tile(): pl.pallas_call(functools.partial(pair_kernel, index_of, line, first, side...  11.9 us
    pallas_call x1, Pallas kernels, own_tile(): pl.pallas_call(functools.partial(own_kernel, steps, line), grid_spec=pltp...  10.7 us
    unnamed x28, local copies, waits for them, and re-layouts  9.34 us
    all_to_all x1, blocking collectives, body(): design = lax.all_to_all(copies, 'probe', 0, 0)  8.28 us
    pallas_call x1, Pallas kernels, descend(): pl.pallas_call(descend_kernel, out_shape=(jax.ShapeDtypeStruct((K, share)...  6.61 us
  transfers between devices with their start and end apart: 24, of which 13 were waited for; matrix products, arithmetic and copies ran while one was open for 0% of the time, Pallas kernels for 19%

profile of v12, /device:TPU:0, one launch (start us, length us, event | category | flops | bytes accessed | tf_op | source)
XLA Modules:
  0.0 216.2 jit_solution(17463774975870793066)
XLA Ops:
  1.2 2.2 %copy-done.2 = bf16[1024,2048]{1,0:T(8,128)(2,1)S(1)} copy-done((bf16[1024,2048]{1,0:T(8,128)(2,1)S(1)}, bf16[1024,2048]{1,0:T(8,128)(2,1)}, u32[]{:S(2)}) %copy-start.2) | copy-done | bytes 4194328
  5.0 3.7 %project.1 = (f32[8,64,128]{2,1,0:T(8,128)S(1)}, bf16[32,2048]{1,0:T(8,128)(2,1)S(1)}, bf16[256,2048]{1,0:T(8,128)(2,1)}, bf16[256,2048]{1,0:T(8,128)(2,1)S(1)}, bf16[256,2048]{1,0:T(8,128)(2,1)S(1)}) custom-call(s32[1]{0:T(128)} %bitcast.1.core_ref._, s32[64]{0:T(128)S(1)} %copy-done.7, bf16[64,2048]{1,0:T(8,128)(2,1)S(1)} %copy-done.4, ...), custom_call_target="tpu_custom_call" | custom-call | flops 134217728 | bytes 8388608 | tf_op jit(solution)/shard_map/project/pallas_call | solution.py:104
  8.7 15.5 %all_to_all.10.parts_ref = f32[8,64,128]{2,1,0:T(8,128)S(1)} all-to-all(f32[8,64,128]{2,1,0:T(8,128)S(1)} %get-tuple-element.23), channel_id=1, replica_groups=mesh['samp'=4,'probe'=8] {'probe'}, dimensions={0} | all-to-all | bytes 524288 | tf_op jit(solution)/shard_map/all_to_all | solution.py:615
  24.2 6.6 %descend.1 = (f32[32,128]{1,0:T(8,128)}, bf16[8,32,128]{2,1,0:T(8,128)(2,1)S(1)}) custom-call(f32[8,64,128]{2,1,0:T(8,128)S(1)} %all_to_all.10.parts_ref), custom_call_target="tpu_custom_call" | custom-call | flops 33554432 | bytes 16384 | tf_op jit(solution)/shard_map/descend/pallas_call | solution.py:198
  30.8 8.3 %all_to_all.11.design_ref = bf16[8,32,128]{2,1,0:T(8,128)(2,1)S(1)} all-to-all(bf16[8,32,128]{2,1,0:T(8,128)(2,1)S(1)} %get-tuple-element.24), channel_id=1, replica_groups=mesh['samp'=4,'probe'=8] {'probe'}, dimensions={0} | all-to-all | bytes 131072 | tf_op jit(solution)/shard_map/all_to_all | solution.py:617
  39.1 2.3 %cross.1.refs_0_ = f32[32,2176]{1,0:T(8,128)S(1)} custom-call(bf16[8,32,128]{2,1,0:T(8,128)(2,1)S(1)} %all_to_all.11.design_ref, bf16[1024,2048]{1,0:T(8,128)(2,1)S(1)} %copy-done.3, bf16[32,2048]{1,0:T(8,128)(2,1)S(1)} %get-tuple-element.25.panel_ref.refs_4_), custom_call_target="tpu_custom_call" | custom-call | flops 268435456 | bytes 4194304 | tf_op jit(solution)/shard_map/cross/pallas_call | solution.py:236
  41.4 1.5 collective-permute-start.1
  44.9 6.0 %collective-permute-done.1.refs_1_ = f32[32,2176]{1,0:T(8,128)S(1)} collective-permute-done((f32[32,2176]{1,0:T(8,128)S(1)}, f32[32,2176]{1,0:T(8,128)S(1)}, u32[]{:S(2)}, u32[]{:S(2)}) %collective-permute-start.1) | collective-permute-done | bytes 278560 | tf_op jit(solution)/shard_map/ppermute | solution.py:582
  50.9 5.8 %collective-permute-done.2.refs_2_ = f32[32,2176]{1,0:T(8,128)S(1)} collective-permute-done((f32[32,2176]{1,0:T(8,128)S(1)}, f32[32,2176]{1,0:T(8,128)S(1)}, u32[]{:S(2)}, u32[]{:S(2)}) %collective-permute-start.2) | collective-permute-done | bytes 278560 | tf_op jit(solution)/shard_map/ppermute | solution.py:582
  56.8 3.8 %solve.1.facts_ref.refs_0_ = f32[40,2048]{1,0:T(8,128)S(1)} custom-call(f32[32,2176]{1,0:T(8,128)S(1)} %cross.1.refs_0_, f32[32,2176]{1,0:T(8,128)S(1)} %collective-permute-done.1.refs_1_, f32[32,2176]{1,0:T(8,128)S(1)} %collective-permute-done.2.refs_2_, f32[32,2176]{1,0:T(8,128)S(1)} %collective-permute-done.3.refs_3_, ...), custom_call_target="tpu_custom_call" | custom-call | flops 104857600 | bytes 1310720 | tf_op jit(solution)/shard_map/solve/pallas_call | solution.py:293
  62.2 1.8 collective-permute-start.10
  64.5 46.0 %collective-permute-done.9 = bf16[4,32,128]{2,1,0:T(8,128)(2,1)S(1)} collective-permute-done((bf16[4,32,128]{2,1,0:T(8,128)(2,1)S(1)}, bf16[4,32,128]{2,1,0:T(8,128)(2,1)S(1)}, u32[]{:S(2)}, u32[]{:S(2)}) %collective-permute-start.9) | collective-permute-done | bytes 32800 | tf_op jit(solution)/shard_map/ppermute | solution.py:582
  110.8 1.6 collective-permute-start.14
  112.4 10.7 %own.1 = (bf16[1024,4096]{1,0:T(8,128)(2,1)S(1)}, bf16[1024,128]{1,0:T(8,128)(2,1)S(1)}, bf16[1024,128]{1,0:T(8,128)(2,1)S(1)}, bf16[1024,128]{1,0:T(8,128)(2,1)S(1)}, f32[1024,128]{1,0:T(8,128)S(1)}) custom-call(s32[1]{0:T(128)} %bitcast.place_ref, s32[1]{0:T(128)} %bitcast.1.core_ref._, bf16[8,32,128]{2,1,0:T(8,128)(2,1)S(1)} %all_to_all.11.design_ref, ...), custom_call_target="tpu_custom_call" | custom-call | flops 4294967296 | bytes 25165824 | tf_op jit(solution)/shard_map/own/pallas_call | solution.py:371
  125.2 5.4 %shard_map.50 = (bf16[1,1024,128]{2,1,0:T(8,128)(2,1)S(1)}, f32[1,1024,128]{2,1,0:T(8,128)S(1)}) custom-call(s32[1]{0:T(128)} %bitcast.place_ref, bf16[2,32,128]{2,1,0:T(8,128)(2,1)S(1)} %pad_maximum_fusion.3.design_ref, bf16[1024,4096]{1,0:T(8,128)(2,1)S(1)} %get-tuple-element.30.zscore_ref, f32[40,2048]{1,0:T(8,128)S(1)} %solve.1.facts_ref.refs_0_, ...), custom_call_target="tpu_custom_call" | custom-call | flops 2147483648 | bytes 8388608 | tf_op jit(solution)/shard_map/pallas_call | solution.py:465
  131.6 6.2 %collective-permute-done.15.refs_1_ = bf16[256,2048]{1,0:T(8,128)(2,1)} collective-permute-done((bf16[256,2048]{1,0:T(8,128)(2,1)}, bf16[256,2048]{1,0:T(8,128)(2,1)}, u32[]{:S(2)}, u32[]{:S(2)}) %collective-permute-start.15) | collective-permute-done | bytes 1048608 | tf_op jit(solution)/shard_map/ppermute | solution.py:582
  137.7 3.4 %copy-done.1 = bf16[1024,4096]{1,0:T(8,128)(2,1)S(1)} copy-done((bf16[1024,4096]{1,0:T(8,128)(2,1)S(1)}, bf16[1024,4096]{1,0:T(8,128)(2,1)}, u32[]{:S(2)}) %copy-start.1) | copy-done | bytes 8388632
  141.1 3.2 %shard_map.51.refs_2_ = f32[1024,256]{1,0:T(8,128)S(1)} custom-call(s32[1]{0:T(128)} %bitcast.place_ref, bf16[2,32,128]{2,1,0:T(8,128)(2,1)S(1)} %slice.46.design_ref, bf16[1024,4096]{1,0:T(8,128)(2,1)S(1)} %copy-done.1, f32[40,2048]{1,0:T(8,128)S(1)} %solve.1.facts_ref.refs_0_, bf16[256,2048]{1,0:T(8,128)(2,1)} %collective-permute-done.15.refs_1_), custom_call_target="tpu_custom_call" | custom-call | flops 1073741824 | bytes 8388608 | tf_op jit(solution)/shard_map/pallas_call | solution.py:465
  144.4 13.1 %collective-permute-done.14.refs_1_ = bf16[256,2048]{1,0:T(8,128)(2,1)} collective-permute-done((bf16[256,2048]{1,0:T(8,128)(2,1)}, bf16[256,2048]{1,0:T(8,128)(2,1)}, u32[]{:S(2)}, u32[]{:S(2)}) %collective-permute-start.14) | collective-permute-done | bytes 1048608 | tf_op jit(solution)/shard_map/ppermute | solution.py:582
  157.5 3.2 %shard_map.52 = (bf16[1024,128]{1,0:T(8,128)(2,1)S(1)}, bf16[1024,128]{1,0:T(8,128)(2,1)S(1)}, bf16[1024,128]{1,0:T(8,128)(2,1)S(1)}, f32[1024,128]{1,0:T(8,128)S(1)}) custom-call(s32[1]{0:T(128)} %bitcast.place_ref, bf16[2,32,128]{2,1,0:T(8,128)(2,1)S(1)} %slice.46.design_ref, bf16[1024,4096]{1,0:T(8,128)(2,1)S(1)} %copy-done.1, ...), custom_call_target="tpu_custom_call" | custom-call | flops 1073741824 | bytes 8388608 | tf_op jit(solution)/shard_map/pallas_call | solution.py:465
  160.7 2.5 %collective-permute-start.16 = (bf16[1024,128]{1,0:T(8,128)(2,1)S(1)}, bf16[1024,128]{1,0:T(8,128)(2,1)S(1)}, u32[]{:S(2)}, u32[]{:S(2)}) collective-permute-start(bf16[1024,128]{1,0:T(8,128)(2,1)S(1)} %get-tuple-element.37), channel_id=1, source_target_pairs={{0,4},{1,5},{6,2},{7,3},{8,12},{9,13},{14,10},{15,11},{16,20},{17,... | collective-permute-start | bytes 786440 | tf_op jit(solution)/shard_map/ppermute | solution.py:582
  163.3 1.6 collective-permute-start.17
  167.0 2.8 %collective-permute-done.16.refs_3_ = bf16[1024,128]{1,0:T(8,128)(2,1)S(1)} collective-permute-done((bf16[1024,128]{1,0:T(8,128)(2,1)S(1)}, bf16[1024,128]{1,0:T(8,128)(2,1)S(1)}, u32[]{:S(2)}, u32[]{:S(2)}) %collective-permute-start.16) | collective-permute-done | bytes 262176 | tf_op jit(solution)/shard_map/ppermute | solution.py:582
  169.7 5.6 %collective-permute-done.17.refs_4_ = bf16[1024,128]{1,0:T(8,128)(2,1)S(1)} collective-permute-done((bf16[1024,128]{1,0:T(8,128)(2,1)S(1)}, bf16[1024,128]{1,0:T(8,128)(2,1)S(1)}, u32[]{:S(2)}, u32[]{:S(2)}) %collective-permute-start.17) | collective-permute-done | bytes 262176 | tf_op jit(solution)/shard_map/ppermute | solution.py:582
  175.4 8.9 %collective-permute-done.13.refs_1_ = bf16[1024,128]{1,0:T(8,128)(2,1)S(1)} collective-permute-done((bf16[1024,128]{1,0:T(8,128)(2,1)S(1)}, bf16[1024,128]{1,0:T(8,128)(2,1)S(1)}, u32[]{:S(2)}, u32[]{:S(2)}) %collective-permute-start.13) | collective-permute-done | bytes 262176 | tf_op jit(solution)/shard_map/ppermute | solution.py:582
  185.3 2.9 %collective-permute-start.8 = (bf16[512,128]{1,0:T(8,128)(2,1)S(1)}, bf16[512,128]{1,0:T(8,128)(2,1)S(1)}, u32[]{:S(2)}, u32[]{:S(2)}) collective-permute-start(bf16[512,128]{1,0:T(8,128)(2,1)S(1)} %get-tuple-element.46), channel_id=1, source_target_pairs={{0,4},{1,5},{2,6},{3,7},{4,0},{5,1},{6,2},{7,3},{8,12},{9,13},{10,... | collective-permute-start | bytes 393224 | tf_op jit(solution)/shard_map/ppermute | solution.py:582
  188.3 3.8 %collective-permute-start.6 = (bf16[1024,128]{1,0:T(8,128)(2,1)S(1)}, bf16[1024,128]{1,0:T(8,128)(2,1)S(1)}, u32[]{:S(2)}, u32[]{:S(2)}) collective-permute-start(bf16[1024,128]{1,0:T(8,128)(2,1)S(1)} %copy-done.11), channel_id=1, source_target_pairs={{0,6},{1,7},{2,0},{3,1},{4,2},{5,3},{6,4},{7,5},{8,14},{9,15},{10,... | collective-permute-start | bytes 786440 | tf_op jit(solution)/shard_map/ppermute | solution.py:582
  192.8 5.1 %collective-permute-done.20.other_ref = bf16[4,128,128]{2,1,0:T(8,128)(2,1)S(1)} collective-permute-done((bf16[4,128,128]{2,1,0:T(8,128)(2,1)S(1)}, bf16[4,128,128]{2,1,0:T(8,128)(2,1)S(1)}, u32[]{:S(2)}, u32[]{:S(2)}) %collective-permute-start.20) | collective-permute-done | bytes 131104 | tf_op jit(solution)/shard_map/ppermute | solution.py:582
  198.0 3.3 %collective-permute-done.7.refs_2_ = bf16[512,128]{1,0:T(8,128)(2,1)S(1)} collective-permute-done((bf16[512,128]{1,0:T(8,128)(2,1)S(1)}, bf16[512,128]{1,0:T(8,128)(2,1)S(1)}, u32[]{:S(2)}, u32[]{:S(2)}) %collective-permute-start.7) | collective-permute-done | bytes 131104 | tf_op jit(solution)/shard_map/ppermute | solution.py:582
  201.3 2.8 %collective-permute-done.8.refs_3_ = bf16[512,128]{1,0:T(8,128)(2,1)S(1)} collective-permute-done((bf16[512,128]{1,0:T(8,128)(2,1)S(1)}, bf16[512,128]{1,0:T(8,128)(2,1)S(1)}, u32[]{:S(2)}, u32[]{:S(2)}) %collective-permute-start.8) | collective-permute-done | bytes 131104 | tf_op jit(solution)/shard_map/ppermute | solution.py:582
  204.1 3.5 %collective-permute-done.6.refs_1_ = bf16[1024,128]{1,0:T(8,128)(2,1)S(1)} collective-permute-done((bf16[1024,128]{1,0:T(8,128)(2,1)S(1)}, bf16[1024,128]{1,0:T(8,128)(2,1)S(1)}, u32[]{:S(2)}, u32[]{:S(2)}) %collective-permute-start.6) | collective-permute-done | bytes 262176 | tf_op jit(solution)/shard_map/ppermute | solution.py:582
  208.7 6.5 %collective-permute-done.22.refs_1_ = bf16[2,128,128]{2,1,0:T(8,128)(2,1)S(1)} collective-permute-done((bf16[2,128,128]{2,1,0:T(8,128)(2,1)S(1)}, bf16[2,128,128]{2,1,0:T(8,128)(2,1)S(1)}, u32[]{:S(2)}, u32[]{:S(2)}) %collective-permute-start.22) | collective-permute-done | bytes 65568 | tf_op jit(solution)/shard_map/ppermute | solution.py:582
  (69 shorter events, 15.7 us)
Async XLA Ops:
  0.6 111.8 %collective-permute-start = (bf16[1024,2048]{1,0:T(8,128)(2,1)}, bf16[1024,2048]{1,0:T(8,128)(2,1)}, u32[]{:S(2)}, u32[]{:S(2)}) collective-permute-start(bf16[1024,2048]{1,0:T(8,128)(2,1)} %from_ref.1), channel_id=1, source_target_pairs={{0,1},{1,0},{2,3},{3,2},{4,5},{5,4},{6,7},{7,6},{8,9},{9,8},{10,11... | collective-permute-start | bytes 12582920 | tf_op jit(solution)/shard_map/ppermute | solution.py:582
  5.0 34.1 %copy-start.3 = (bf16[1024,2048]{1,0:T(8,128)(2,1)S(1)}, bf16[1024,2048]{1,0:T(8,128)(2,1)}, u32[]{:S(2)}) copy-start(bf16[1024,2048]{1,0:T(8,128)(2,1)} %from_ref.1) | copy-start | bytes 12582916
  8.7 53.4 %copy-start.8 = (bf16[256,2048]{1,0:T(8,128)(2,1)}, bf16[256,2048]{1,0:T(8,128)(2,1)S(1)}, u32[]{:S(2)}) copy-start(bf16[256,2048]{1,0:T(8,128)(2,1)S(1)} %get-tuple-element.34) | copy-start | bytes 3145732
  8.7 53.4 %copy-start.9 = (bf16[256,2048]{1,0:T(8,128)(2,1)}, bf16[256,2048]{1,0:T(8,128)(2,1)S(1)}, u32[]{:S(2)}) copy-start(bf16[256,2048]{1,0:T(8,128)(2,1)S(1)} %get-tuple-element.35) | copy-start | bytes 3145732
  41.4 9.6 %collective-permute-start.1 = (f32[32,2176]{1,0:T(8,128)S(1)}, f32[32,2176]{1,0:T(8,128)S(1)}, u32[]{:S(2)}, u32[]{:S(2)}) collective-permute-start(f32[32,2176]{1,0:T(8,128)S(1)} %cross.1.refs_0_), channel_id=1, source_target_pairs={{0,8},{8,0},{16,24},{24,16},{1,9},{9,1},{17,25},{25,17},{2,10},{10... | collective-permute-start | bytes 835592 | tf_op jit(solution)/shard_map/ppermute | solution.py:582
  42.9 13.9 %collective-permute-start.2 = (f32[32,2176]{1,0:T(8,128)S(1)}, f32[32,2176]{1,0:T(8,128)S(1)}, u32[]{:S(2)}, u32[]{:S(2)}) collective-permute-start(f32[32,2176]{1,0:T(8,128)S(1)} %cross.1.refs_0_), channel_id=1, source_target_pairs={{0,16},{8,24},{16,0},{24,8},{1,17},{9,25},{17,1},{25,9},{2,18},{10... | collective-permute-start | bytes 835592 | tf_op jit(solution)/shard_map/ppermute | solution.py:582
  44.4 12.4 %collective-permute-start.3 = (f32[32,2176]{1,0:T(8,128)S(1)}, f32[32,2176]{1,0:T(8,128)S(1)}, u32[]{:S(2)}, u32[]{:S(2)}) collective-permute-start(f32[32,2176]{1,0:T(8,128)S(1)} %cross.1.refs_0_), channel_id=1, source_target_pairs={{0,24},{8,16},{16,8},{24,0},{1,25},{9,17},{17,9},{25,1},{2,26},{10... | collective-permute-start | bytes 835592 | tf_op jit(solution)/shard_map/ppermute | solution.py:582
  60.6 50.2 %collective-permute-start.4 = (f32[40,2048]{1,0:T(8,128)S(1)}, f32[40,2048]{1,0:T(8,128)S(1)}, u32[]{:S(2)}, u32[]{:S(2)}) collective-permute-start(f32[40,2048]{1,0:T(8,128)S(1)} %solve.1.facts_ref.refs_0_), channel_id=1, source_target_pairs={{0,1},{1,0},{2,3},{3,2},{4,5},{5,4},{6,7},{7,6},{8,9},{9,8},{10,11... | collective-permute-start | bytes 983048 | tf_op jit(solution)/shard_map/ppermute | solution.py:582
  60.7 64.5 %collective-permute-start.11 = (bf16[256,2048]{1,0:T(8,128)(2,1)}, bf16[256,2048]{1,0:T(8,128)(2,1)S(1)}, u32[]{:S(2)}, u32[]{:S(2)}) collective-permute-start(bf16[256,2048]{1,0:T(8,128)(2,1)} %get-tuple-element.31), channel_id=1, source_target_pairs={{0,9},{1,8},{2,11},{3,10},{4,13},{5,12},{6,15},{7,14},{8,17},{9,16... | collective-permute-start | bytes 3145736 | tf_op jit(solution)/shard_map/ppermute | solution.py:582
  62.2 63.1 %collective-permute-start.10 = (bf16[256,2048]{1,0:T(8,128)(2,1)S(1)}, bf16[256,2048]{1,0:T(8,128)(2,1)}, u32[]{:S(2)}, u32[]{:S(2)}) collective-permute-start(bf16[256,2048]{1,0:T(8,128)(2,1)S(1)} %pick_ends.1), channel_id=1, source_target_pairs={{0,8},{8,16},{16,24},{24,0},{1,9},{9,17},{17,25},{25,1},{2,10},{10... | collective-permute-start | bytes 3145736 | tf_op jit(solution)/shard_map/ppermute | solution.py:582
  64.0 46.5 %collective-permute-start.9 = (bf16[4,32,128]{2,1,0:T(8,128)(2,1)S(1)}, bf16[4,32,128]{2,1,0:T(8,128)(2,1)S(1)}, u32[]{:S(2)}, u32[]{:S(2)}) collective-permute-start(bf16[4,32,128]{2,1,0:T(8,128)(2,1)S(1)} %dynamic-slice_bitcast_fusion), channel_id=1, source_target_pairs={{0,8},{8,16},{16,24},{24,0},{1,9},{9,17},{17,25},{25,1},{2,10},{10... | collective-permute-start | bytes 98312 | tf_op jit(solution)/shard_map/ppermute | solution.py:582
  110.5 27.2 %collective-permute-start.15 = (bf16[256,2048]{1,0:T(8,128)(2,1)}, bf16[256,2048]{1,0:T(8,128)(2,1)}, u32[]{:S(2)}, u32[]{:S(2)}) collective-permute-start(bf16[256,2048]{1,0:T(8,128)(2,1)} %copy-done.9), channel_id=1, source_target_pairs={{0,8},{8,16},{16,24},{24,0},{1,9},{9,17},{17,25},{25,1},{2,10},{10... | collective-permute-start | bytes 3145736 | tf_op jit(solution)/shard_map/ppermute | solution.py:582
  110.8 46.6 %collective-permute-start.14 = (bf16[256,2048]{1,0:T(8,128)(2,1)}, bf16[256,2048]{1,0:T(8,128)(2,1)}, u32[]{:S(2)}, u32[]{:S(2)}) collective-permute-start(bf16[256,2048]{1,0:T(8,128)(2,1)} %copy-done.8), channel_id=1, source_target_pairs={{0,9},{1,8},{2,11},{3,10},{4,13},{5,12},{6,15},{7,14},{8,17},{9,16... | collective-permute-start | bytes 3145736 | tf_op jit(solution)/shard_map/ppermute | solution.py:582
  125.2 5.4 %copy-start = (bf16[1024,4096]{1,0:T(8,128)(2,1)}, bf16[1024,4096]{1,0:T(8,128)(2,1)S(1)}, u32[]{:S(2)}) copy-start(bf16[1024,4096]{1,0:T(8,128)(2,1)S(1)} %get-tuple-element.30.zscore_ref) | copy-start | bytes 25165828
  130.7 34.9 %collective-permute-start.12 = (bf16[1,1024,128]{2,1,0:T(8,128)(2,1)S(1)}, bf16[1,1024,128]{2,1,0:T(8,128)(2,1)S(1)}, u32[]{:S(2)}, u32[]{:S(2)}) collective-permute-start(bf16[1,1024,128]{2,1,0:T(8,128)(2,1)S(1)} %get-tuple-element.33), channel_id=1, source_target_pairs={{0,2},{1,3},{2,0},{3,1},{4,6},{5,7},{6,4},{7,5},{8,10},{9,11},{10,... | collective-permute-start | bytes 786440 | tf_op jit(solution)/shard_map/ppermute | solution.py:582
  137.7 3.4 %copy-start.1 = (bf16[1024,4096]{1,0:T(8,128)(2,1)S(1)}, bf16[1024,4096]{1,0:T(8,128)(2,1)}, u32[]{:S(2)}) copy-start(bf16[1024,4096]{1,0:T(8,128)(2,1)} %copy-done) | copy-start | bytes 25165828
  144.3 40.9 %copy-start.6 = (bf16[1024,128]{1,0:T(8,128)(2,1)S(1)}, bf16[1024,128]{1,0:T(8,128)(2,1)}, u32[]{:S(2)}) copy-start(bf16[1024,128]{1,0:T(8,128)(2,1)} %copy-done.5) | copy-start | bytes 786436
  160.7 27.6 %copy-start.13 = (bf16[1024,128]{1,0:T(8,128)(2,1)S(1)}, bf16[1024,128]{1,0:T(8,128)(2,1)}, u32[]{:S(2)}) copy-start(bf16[1024,128]{1,0:T(8,128)(2,1)} %copy-done.12) | copy-start | bytes 786436
  160.7 27.6 %copy-start.11 = (bf16[1024,128]{1,0:T(8,128)(2,1)S(1)}, bf16[1024,128]{1,0:T(8,128)(2,1)}, u32[]{:S(2)}) copy-start(bf16[1024,128]{1,0:T(8,128)(2,1)} %copy-done.10) | copy-start | bytes 786436
  160.7 9.0 %collective-permute-start.16 = (bf16[1024,128]{1,0:T(8,128)(2,1)S(1)}, bf16[1024,128]{1,0:T(8,128)(2,1)S(1)}, u32[]{:S(2)}, u32[]{:S(2)}) collective-permute-start(bf16[1024,128]{1,0:T(8,128)(2,1)S(1)} %get-tuple-element.37), channel_id=1, source_target_pairs={{0,4},{1,5},{6,2},{7,3},{8,12},{9,13},{14,10},{15,11},{16,20},{17,... | collective-permute-start | bytes 786440 | tf_op jit(solution)/shard_map/ppermute | solution.py:582
  163.3 12.1 %collective-permute-start.17 = (bf16[1024,128]{1,0:T(8,128)(2,1)S(1)}, bf16[1024,128]{1,0:T(8,128)(2,1)S(1)}, u32[]{:S(2)}, u32[]{:S(2)}) collective-permute-start(bf16[1024,128]{1,0:T(8,128)(2,1)S(1)} %get-tuple-element.38), channel_id=1, source_target_pairs={{0,2},{1,3},{2,4},{3,5},{8,10},{9,11},{10,12},{11,13},{16,18},{17,... | collective-permute-start | bytes 786440 | tf_op jit(solution)/shard_map/ppermute | solution.py:582
  164.9 10.5 %collective-permute-start.18 = (bf16[1024,128]{1,0:T(8,128)(2,1)S(1)}, bf16[1024,128]{1,0:T(8,128)(2,1)S(1)}, u32[]{:S(2)}, u32[]{:S(2)}) collective-permute-start(bf16[1024,128]{1,0:T(8,128)(2,1)S(1)} %get-tuple-element.39), channel_id=1, source_target_pairs={{4,2},{5,3},{6,4},{7,5},{12,10},{13,11},{14,12},{15,13},{20,18},{2... | collective-permute-start | bytes 786440 | tf_op jit(solution)/shard_map/ppermute | solution.py:582
  165.7 18.6 %collective-permute-start.13 = (bf16[1024,128]{1,0:T(8,128)(2,1)S(1)}, bf16[1024,128]{1,0:T(8,128)(2,1)S(1)}, u32[]{:S(2)}, u32[]{:S(2)}) collective-permute-start(bf16[1024,128]{1,0:T(8,128)(2,1)S(1)} %get-tuple-element.44), channel_id=1, source_target_pairs={{2,6},{3,7},{4,0},{5,1},{10,14},{11,15},{12,8},{13,9},{18,22},{19,... | collective-permute-start | bytes 786440 | tf_op jit(solution)/shard_map/ppermute | solution.py:582
  184.6 7.5 %collective-permute-start.19 = (bf16[4,128,128]{2,1,0:T(8,128)(2,1)S(1)}, bf16[4,128,128]{2,1,0:T(8,128)(2,1)S(1)}, u32[]{:S(2)}, u32[]{:S(2)}) collective-permute-start(bf16[4,128,128]{2,1,0:T(8,128)(2,1)S(1)} %get-tuple-element.41), channel_id=1, source_target_pairs={{0,24},{8,0},{16,8},{24,16},{1,25},{9,1},{17,9},{25,17},{2,26},{10... | collective-permute-start | bytes 393224 | tf_op jit(solution)/shard_map/ppermute | solution.py:582
  185.3 16.1 %collective-permute-start.7 = (bf16[512,128]{1,0:T(8,128)(2,1)S(1)}, bf16[512,128]{1,0:T(8,128)(2,1)S(1)}, u32[]{:S(2)}, u32[]{:S(2)}) collective-permute-start(bf16[512,128]{1,0:T(8,128)(2,1)S(1)} %get-tuple-element.47), channel_id=1, source_target_pairs={{0,4},{1,5},{2,6},{3,7},{4,0},{5,1},{6,2},{7,3},{8,12},{9,13},{10,... | collective-permute-start | bytes 393224 | tf_op jit(solution)/shard_map/ppermute | solution.py:582
  185.3 18.8 %collective-permute-start.8 = (bf16[512,128]{1,0:T(8,128)(2,1)S(1)}, bf16[512,128]{1,0:T(8,128)(2,1)S(1)}, u32[]{:S(2)}, u32[]{:S(2)}) collective-permute-start(bf16[512,128]{1,0:T(8,128)(2,1)S(1)} %get-tuple-element.46), channel_id=1, source_target_pairs={{0,4},{1,5},{2,6},{3,7},{4,0},{5,1},{6,2},{7,3},{8,12},{9,13},{10,... | collective-permute-start | bytes 393224 | tf_op jit(solution)/shard_map/ppermute | solution.py:582
  188.3 15.8 %collective-permute-start.5 = (bf16[1024,128]{1,0:T(8,128)(2,1)S(1)}, bf16[1024,128]{1,0:T(8,128)(2,1)S(1)}, u32[]{:S(2)}, u32[]{:S(2)}) collective-permute-start(bf16[1024,128]{1,0:T(8,128)(2,1)S(1)} %copy-done.13), channel_id=1, source_target_pairs={{0,2},{1,3},{2,4},{3,5},{4,6},{5,7},{6,0},{7,1},{8,10},{9,11},{10,... | collective-permute-start | bytes 786440 | tf_op jit(solution)/shard_map/ppermute | solution.py:582
  188.3 19.3 %collective-permute-start.6 = (bf16[1024,128]{1,0:T(8,128)(2,1)S(1)}, bf16[1024,128]{1,0:T(8,128)(2,1)S(1)}, u32[]{:S(2)}, u32[]{:S(2)}) collective-permute-start(bf16[1024,128]{1,0:T(8,128)(2,1)S(1)} %copy-done.11), channel_id=1, source_target_pairs={{0,6},{1,7},{2,0},{3,1},{4,2},{5,3},{6,4},{7,5},{8,14},{9,15},{10,... | collective-permute-start | bytes 786440 | tf_op jit(solution)/shard_map/ppermute | solution.py:582
  192.1 5.8 %collective-permute-start.20 = (bf16[4,128,128]{2,1,0:T(8,128)(2,1)S(1)}, bf16[4,128,128]{2,1,0:T(8,128)(2,1)S(1)}, u32[]{:S(2)}, u32[]{:S(2)}) collective-permute-start(bf16[4,128,128]{2,1,0:T(8,128)(2,1)S(1)} %get-tuple-element.42), channel_id=1, source_target_pairs={{0,25},{1,24},{2,27},{3,26},{4,29},{5,28},{6,31},{7,30},{8,1},{9,0... | collective-permute-start | bytes 393224 | tf_op jit(solution)/shard_map/ppermute | solution.py:582
  197.9 10.8 %collective-permute-start.23 = (bf16[2,128,128]{2,1,0:T(8,128)(2,1)S(1)}, bf16[2,128,128]{2,1,0:T(8,128)(2,1)S(1)}, u32[]{:S(2)}, u32[]{:S(2)}) collective-permute-start(bf16[2,128,128]{2,1,0:T(8,128)(2,1)S(1)} %pad_maximum_fusion.2), channel_id=1, source_target_pairs={{0,6},{1,7},{2,0},{3,1},{4,2},{5,3},{6,4},{7,5},{8,14},{9,15},{10,... | collective-permute-start | bytes 196616 | tf_op jit(solution)/shard_map/ppermute | solution.py:582
  201.3 13.9 %collective-permute-start.22 = (bf16[2,128,128]{2,1,0:T(8,128)(2,1)S(1)}, bf16[2,128,128]{2,1,0:T(8,128)(2,1)S(1)}, u32[]{:S(2)}, u32[]{:S(2)}) collective-permute-start(bf16[2,128,128]{2,1,0:T(8,128)(2,1)S(1)} %pad_maximum_fusion.1), channel_id=1, source_target_pairs={{0,4},{1,5},{2,6},{3,7},{4,0},{5,1},{6,2},{7,3},{8,12},{9,13},{10,... | collective-permute-start | bytes 196616 | tf_op jit(solution)/shard_map/ppermute | solution.py:582
  204.1 11.1 %collective-permute-start.21 = (bf16[2,128,128]{2,1,0:T(8,128)(2,1)S(1)}, bf16[2,128,128]{2,1,0:T(8,128)(2,1)S(1)}, u32[]{:S(2)}, u32[]{:S(2)}) collective-permute-start(bf16[2,128,128]{2,1,0:T(8,128)(2,1)S(1)} %pad_maximum_fusion), channel_id=1, source_target_pairs={{0,2},{1,3},{2,4},{3,5},{4,6},{5,7},{6,0},{7,1},{8,10},{9,11},{10,... | collective-permute-start | bytes 196616 | tf_op jit(solution)/shard_map/ppermute | solution.py:582
  (6 other events, 5.9 us)
